TPU v7x, 32 devices: a whole 2x2x4 slice. The times are simulated.
32 devices in a mesh: dp: 16 (over z, y, x), mp: 2 (over core).
Axes of the slice: x: 2, y: 2, z: 4, core: 2. Of those that a mesh axis runs over, the one named last changes fastest.
Arguments:
- tokens: bfloat16 [128, 256, 1152], P('dp'), may hold values from -6 to 6
- condition: bfloat16 [128, 1152], P('dp'), may hold values from -6 to 6
- counts: int32 [16], P('dp'), may hold values from 1 to 8, as said below
- w_qkv: bfloat16 [1152, 3, 1152], P(None, None, 'mp'), may hold values from -0.1875 to 0.1875
- b_qv: bfloat16 [2, 1152], P(None, 'mp'), may hold values from -3 to 3
- w_proj: bfloat16 [1152, 1152], P('mp'), may hold values from -0.75 to 0.75
- b_proj: bfloat16 [1152], replicated, may hold values from -3 to 3
- w_up: bfloat16 [1152, 4608], P(None, 'mp'), may hold values from -0.1875 to 0.1875
- b_up: bfloat16 [4608], P('mp'), may hold values from -3 to 3
- w_down: bfloat16 [4608, 1152], P('mp'), may hold values from -0.09375 to 0.09375
- b_down: bfloat16 [1152], replicated, may hold values from -3 to 3
- w_mod: bfloat16 [1152, 6912], P(None, 'mp'), may hold values from -0.1875 to 0.1875
- b_mod: bfloat16 [6912], P('mp'), may hold values from -3 to 3
- cotangent: bfloat16 [128, 256, 1152], P('dp'), may hold values from -6 to 6
Outputs:
- output: bfloat16 [128, 256, 1152], P('dp')
- grad_tokens: float32 [128, 256, 1152], P('dp')
- grad_condition: float32 [128, 1152], P('dp')
- grad_w_qkv: float32 [1152, 3, 1152], P(None, None, 'mp')
- grad_b_qv: float32 [2, 1152], P(None, 'mp')
- grad_w_proj: float32 [1152, 1152], P('mp')
- grad_b_proj: float32 [1152], replicated
- grad_w_up: float32 [1152, 4608], P(None, 'mp')
- grad_b_up: float32 [4608], P('mp')
- grad_w_down: float32 [4608, 1152], P('mp')
- grad_b_down: float32 [1152], replicated
- grad_w_mod: float32 [1152, 6912], P(None, 'mp')
- grad_b_mod: float32 [6912], P('mp')
Inputs may be any that keep to these rules, and one draw needn't show every extreme that they name: counts[g] of group g's 8 slots are live, its first ones; some group has all 8 live in every draw.
All inputs are finite; a program needn't handle non-finite values.
Results may differ from a plain program's by a relative error of at most 0.02.
Values may be sent and summed in bfloat16 or wider, within the bound.
No kernel may reach another device: no remote copies, remote signals or barrier semaphores. Data moves between devices by JAX's collectives and lax.ppermute only.
A program may use at most 256 MiB of HBM per device.

v0:
```python
import jax
import jax.numpy as jnp
from jax import lax
from jax.sharding import PartitionSpec as P

HEAD_DIM = 72


epsilon = 1e-06


def layer_norm(values):
    center = values - jnp.mean(values, axis=-1, keepdims=True)
    return center * lax.rsqrt(jnp.mean(center * center, axis=-1, keepdims=True) + epsilon)


def modulate(values, shift_part, scale_part):
    return layer_norm(values) * (1.0 + scale_part) + shift_part


def gelu_tanh(values):
    return (
        0.5
        * values
        * (1.0 + jnp.tanh(0.7978845608028654 * (values + 0.044715 * values * values * values)))
    )


def inner_rows(left, right):
    return lax.dot_general(
        left, right, (((0,), (0,)), ((), ())), preferred_element_type=jnp.float32
    )


def outer_cols(left, right):
    return lax.dot_general(
        left, right, (((1,), (1,)), ((), ())), preferred_element_type=jnp.float32
    )


def attention_forward(query_rows, key_rows, value_rows):
    factor = HEAD_DIM ** (-0.5)
    scores = (
        jnp.einsum("bqhd,bkhd->bhqk", query_rows, key_rows, preferred_element_type=jnp.float32)
        * factor
    )
    row_max = jnp.max(scores, axis=-1, keepdims=True)
    row_total = jnp.sum(jnp.exp(scores - row_max), axis=-1, keepdims=True)
    logsum = row_max + jnp.log(row_total)
    prob_b = jnp.exp(scores - logsum).astype(jnp.bfloat16)
    mixed_out = jnp.einsum(
        "bhqk,bkhd->bqhd", prob_b, value_rows, preferred_element_type=jnp.float32
    )
    return (mixed_out, logsum)


def attention_backward(query_rows, key_rows, value_rows, logsum, grad_mixed):
    factor = HEAD_DIM ** (-0.5)
    scores = (
        jnp.einsum("bqhd,bkhd->bhqk", query_rows, key_rows, preferred_element_type=jnp.float32)
        * factor
    )
    prob_f = jnp.exp(scores - logsum)
    prob_b = prob_f.astype(jnp.bfloat16)
    grad_prob = jnp.einsum(
        "bqhd,bkhd->bhqk", grad_mixed, value_rows, preferred_element_type=jnp.float32
    )
    row_delta = jnp.sum(prob_f * grad_prob, axis=-1, keepdims=True)
    grad_scores = (prob_f * (grad_prob - row_delta)).astype(jnp.bfloat16)
    grad_query = (
        jnp.einsum("bhqk,bkhd->bqhd", grad_scores, key_rows, preferred_element_type=jnp.float32)
        * factor
    )
    grad_key = (
        jnp.einsum("bhqk,bqhd->bkhd", grad_scores, query_rows, preferred_element_type=jnp.float32)
        * factor
    )
    grad_value = jnp.einsum(
        "bhqk,bqhd->bkhd", prob_b, grad_mixed, preferred_element_type=jnp.float32
    )
    return (
        grad_query.astype(jnp.bfloat16),
        grad_key.astype(jnp.bfloat16),
        grad_value.astype(jnp.bfloat16),
    )


def forward(tokens_f, spans, weights, repeat):
    w_qkv, b_qv, w_proj, b_proj, w_up, b_up, w_down, b_down = weights
    shift_attn, scale_attn, gate_attn, shift_mlp, scale_mlp, gate_mlp = spans
    slot_count, seq_len, model_dim = tokens_f.shape
    row_count = slot_count * seq_len
    head_cols = w_qkv.shape[2]
    head_count = head_cols // HEAD_DIM
    shape_four = (slot_count, seq_len, head_count, HEAD_DIM)
    normed = (
        modulate(tokens_f, shift_attn, scale_attn)
        .astype(jnp.bfloat16)
        .reshape(row_count, model_dim)
    )
    projected = jnp.dot(
        normed, w_qkv.reshape(model_dim, 3 * head_cols), preferred_element_type=jnp.float32
    )
    qkv_bias = jnp.stack([b_qv[0], jnp.zeros_like(b_qv[0]), b_qv[1]]).astype(jnp.float32)
    projected = (projected.reshape(row_count, 3, head_cols) + qkv_bias).astype(jnp.bfloat16)
    query_rows = projected[:, 0].reshape(shape_four)
    key_rows = projected[:, 1].reshape(shape_four)
    value_rows = projected[:, 2].reshape(shape_four)
    mixed_out, logsum = attention_forward(query_rows, key_rows, value_rows)
    mixed_b = mixed_out.astype(jnp.bfloat16).reshape(row_count, head_cols)
    partial_value = jnp.dot(mixed_b, w_proj, preferred_element_type=jnp.float32)
    if repeat:
        summed = lax.psum(partial_value.astype(jnp.bfloat16), "mp").astype(jnp.float32)
    else:
        summed = lax.psum(partial_value.astype(jnp.bfloat16), "mp").astype(jnp.float32)
    attn_out = (summed + b_proj.astype(jnp.float32)).reshape(slot_count, seq_len, model_dim)
    residual = tokens_f + gate_attn * attn_out
    normed_mlp = (
        modulate(residual, shift_mlp, scale_mlp).astype(jnp.bfloat16).reshape(row_count, model_dim)
    )
    hidden = jnp.dot(normed_mlp, w_up, preferred_element_type=jnp.float32) + b_up.astype(
        jnp.float32
    )
    act_bf = gelu_tanh(hidden).astype(jnp.bfloat16)
    partial_mlp = jnp.dot(act_bf, w_down, preferred_element_type=jnp.float32)
    if repeat:
        summed_mlp = lax.psum(partial_mlp.astype(jnp.bfloat16), "mp").astype(jnp.float32)
    else:
        summed_mlp = lax.psum(partial_mlp.astype(jnp.bfloat16), "mp").astype(jnp.float32)
    mlp_out = (summed_mlp + b_down.astype(jnp.float32)).reshape(slot_count, seq_len, model_dim)
    output = residual + gate_mlp * mlp_out
    return {
        "normed": normed,
        "query_rows": query_rows,
        "key_rows": key_rows,
        "value_rows": value_rows,
        "logsum": logsum,
        "mixed_b": mixed_b,
        "attn_out": attn_out,
        "residual": residual,
        "normed_mlp": normed_mlp,
        "hidden": hidden,
        "act_bf": act_bf,
        "mlp_out": mlp_out,
        "output": output,
    }


def image_pass(tokens_f, grad_out, spans, weights):
    w_qkv, b_qv, w_proj, b_proj, w_up, b_up, w_down, b_down = weights
    shift_attn, scale_attn, gate_attn, shift_mlp, scale_mlp, gate_mlp = spans
    slot_count, seq_len, model_dim = tokens_f.shape
    row_count = slot_count * seq_len
    head_cols = w_qkv.shape[2]
    head_count = head_cols // HEAD_DIM
    kept_fwd = forward(tokens_f, spans, weights, False)
    out_one = kept_fwd["output"]
    stored = forward(tokens_f, spans, weights, True)
    grad_gate_mlp = jnp.sum(grad_out * stored["mlp_out"], axis=1)
    grad_mlp = (gate_mlp * grad_out).astype(jnp.bfloat16).reshape(row_count, model_dim)
    grad_b_down = jnp.sum(grad_mlp.astype(jnp.float32), axis=0)
    grad_w_down = inner_rows(stored["act_bf"], grad_mlp)
    grad_act = outer_cols(grad_mlp, w_down)
    gelu_value, gelu_back = jax.vjp(gelu_tanh, stored["hidden"])
    grad_hidden = gelu_back(grad_act)[0].astype(jnp.bfloat16)
    grad_b_up = jnp.sum(grad_hidden.astype(jnp.float32), axis=0)
    grad_w_up = inner_rows(stored["normed_mlp"], grad_hidden)
    part_normed_mlp = outer_cols(grad_hidden, w_up)
    grad_normed_mlp = (
        lax.psum(part_normed_mlp.astype(jnp.bfloat16), "mp")
        .astype(jnp.float32)
        .reshape(slot_count, seq_len, model_dim)
    )
    norm_value, norm_back = jax.vjp(modulate, stored["residual"], shift_mlp, scale_mlp)
    grad_resid_norm, grad_shift_mlp, grad_scale_mlp = norm_back(grad_normed_mlp)
    grad_residual = grad_out + grad_resid_norm
    grad_gate_attn = jnp.sum(grad_residual * stored["attn_out"], axis=1)
    grad_attn = (gate_attn * grad_residual).astype(jnp.bfloat16).reshape(row_count, model_dim)
    grad_b_proj = jnp.sum(grad_attn.astype(jnp.float32), axis=0)
    grad_w_proj = inner_rows(stored["mixed_b"], grad_attn)
    grad_mixed = (
        outer_cols(grad_attn, w_proj)
        .astype(jnp.bfloat16)
        .reshape(slot_count, seq_len, head_count, HEAD_DIM)
    )
    grad_query, grad_key, grad_value = attention_backward(
        stored["query_rows"], stored["key_rows"], stored["value_rows"], stored["logsum"], grad_mixed
    )
    grad_qkv = jnp.stack(
        [
            grad_query.reshape(row_count, head_cols),
            grad_key.reshape(row_count, head_cols),
            grad_value.reshape(row_count, head_cols),
        ],
        axis=1,
    )
    grad_b_qv = jnp.stack(
        [
            jnp.sum(grad_qkv[:, 0].astype(jnp.float32), axis=0),
            jnp.sum(grad_qkv[:, 2].astype(jnp.float32), axis=0),
        ]
    )
    grad_w_qkv = inner_rows(stored["normed"], grad_qkv)
    part_normed = outer_cols(
        grad_qkv.reshape(row_count, 3 * head_cols), w_qkv.reshape(model_dim, 3 * head_cols)
    )
    grad_normed = (
        lax.psum(part_normed.astype(jnp.bfloat16), "mp")
        .astype(jnp.float32)
        .reshape(slot_count, seq_len, model_dim)
    )
    first_value, first_back = jax.vjp(modulate, tokens_f, shift_attn, scale_attn)
    grad_tok_norm, grad_shift_attn, grad_scale_attn = first_back(grad_normed)
    grad_tok_one = grad_residual + grad_tok_norm
    grad_mod_one = jnp.concatenate(
        [
            grad_shift_attn[:, 0],
            grad_scale_attn[:, 0],
            grad_gate_attn,
            grad_shift_mlp[:, 0],
            grad_scale_mlp[:, 0],
            grad_gate_mlp,
        ],
        axis=1,
    )
    grad_terms = (
        grad_w_qkv,
        grad_b_qv,
        grad_w_proj,
        grad_b_proj,
        grad_w_up,
        grad_b_up,
        grad_w_down,
        grad_b_down,
    )
    return (out_one, grad_tok_one, grad_mod_one, grad_terms)


def run_layer(tokens, condition, cotangent, live_count, turns, weights, w_mod, b_mod):
    slot_count, seq_len, model_dim = tokens.shape
    cond_f = condition.astype(jnp.float32)
    scaled = jax.nn.silu(cond_f).astype(jnp.bfloat16)
    own_mod = jnp.dot(scaled, w_mod, preferred_element_type=jnp.float32) + b_mod.astype(jnp.float32)
    modulation = lax.all_gather(own_mod, "mp", axis=1, tiled=True)
    tokens_f = tokens.astype(jnp.float32)
    cot_f = cotangent.astype(jnp.float32)

    def image_step(slot_idx, carry):
        out_buf, grad_buf, mod_buf, grad_sums = carry
        live_flag = (slot_idx < live_count).astype(jnp.float32)
        tok_one = lax.dynamic_slice_in_dim(tokens_f, slot_idx, 1, 0)
        cot_one = lax.dynamic_slice_in_dim(cot_f, slot_idx, 1, 0) * live_flag
        mod_row = lax.dynamic_slice_in_dim(modulation, slot_idx, 1, 0)
        spans = [
            mod_row[:, None, part_idx * model_dim : (part_idx + 1) * model_dim]
            for part_idx in range(6)
        ]
        out_one, grad_tok_one, grad_mod_one, grad_terms = image_pass(
            tok_one, cot_one, spans, weights
        )
        out_one = (out_one * live_flag).astype(jnp.bfloat16)
        out_buf = lax.dynamic_update_slice_in_dim(out_buf, out_one, slot_idx, 0)
        grad_buf = lax.dynamic_update_slice_in_dim(grad_buf, grad_tok_one, slot_idx, 0)
        mod_buf = lax.dynamic_update_slice_in_dim(mod_buf, grad_mod_one, slot_idx, 0)
        grad_sums = tuple((total_a + term_b for total_a, term_b in zip(grad_sums, grad_terms)))
        return (out_buf, grad_buf, mod_buf, grad_sums)

    start_sums = tuple((jnp.zeros(weight_in.shape, jnp.float32) for weight_in in weights))
    start_state = (
        jnp.zeros(tokens.shape, jnp.bfloat16),
        jnp.zeros(tokens.shape, jnp.float32),
        jnp.zeros((slot_count, 6 * model_dim), jnp.float32),
        start_sums,
    )
    out_buf, grad_buf, mod_buf, grad_sums = lax.fori_loop(0, turns, image_step, start_state)
    grad_modulation = mod_buf.astype(jnp.bfloat16)
    own_cols = w_mod.shape[1]
    grad_own = lax.dynamic_slice_in_dim(
        grad_modulation, lax.axis_index("mp") * own_cols, own_cols, 1
    )
    part_scaled = outer_cols(grad_own, w_mod)
    grad_scaled = lax.psum(part_scaled.astype(jnp.bfloat16), "mp").astype(jnp.float32)
    silu_value, silu_back = jax.vjp(jax.nn.silu, cond_f)
    grad_condition = silu_back(grad_scaled)[0]
    return (out_buf, grad_buf, grad_condition, grad_sums, scaled, grad_own)


def on_device(
    tokens,
    condition,
    counts,
    w_qkv,
    b_qv,
    w_proj,
    b_proj,
    w_up,
    b_up,
    w_down,
    b_down,
    w_mod,
    b_mod,
    cotangent,
):
    slot_count, seq_len, model_dim = tokens.shape
    weights = (w_qkv, b_qv, w_proj, b_proj, w_up, b_up, w_down, b_down)
    own_count = counts[0]
    output, grad_tokens, grad_condition, grad_sums, scaled, grad_own = run_layer(
        tokens, condition, cotangent, own_count, slot_count, weights, w_mod, b_mod
    )
    (
        grad_w_qkv,
        grad_b_qv,
        grad_w_proj,
        grad_b_proj,
        grad_w_up,
        grad_b_up,
        grad_w_down,
        grad_b_down,
    ) = grad_sums
    grad_w_mod = inner_rows(scaled, grad_own)
    grad_b_mod = jnp.sum(grad_own.astype(jnp.float32), axis=0)
    (
        grad_w_qkv,
        grad_b_qv,
        grad_w_proj,
        grad_b_proj,
        grad_w_up,
        grad_b_up,
        grad_w_down,
        grad_b_down,
        grad_w_mod,
        grad_b_mod,
    ) = (
        lax.psum(grad_w_qkv.astype(jnp.bfloat16), "dp").astype(jnp.float32),
        lax.psum(grad_b_qv.astype(jnp.bfloat16), "dp").astype(jnp.float32),
        lax.psum(grad_w_proj.astype(jnp.bfloat16), "dp").astype(jnp.float32),
        lax.psum(grad_b_proj.astype(jnp.bfloat16), "dp").astype(jnp.float32),
        lax.psum(grad_w_up.astype(jnp.bfloat16), "dp").astype(jnp.float32),
        lax.psum(grad_b_up.astype(jnp.bfloat16), "dp").astype(jnp.float32),
        lax.psum(grad_w_down.astype(jnp.bfloat16), "dp").astype(jnp.float32),
        lax.psum(grad_b_down.astype(jnp.bfloat16), "dp").astype(jnp.float32),
        lax.psum(grad_w_mod.astype(jnp.bfloat16), "dp").astype(jnp.float32),
        lax.psum(grad_b_mod.astype(jnp.bfloat16), "dp").astype(jnp.float32),
    )
    return (
        output,
        grad_tokens,
        grad_condition,
        grad_w_qkv,
        grad_b_qv,
        grad_w_proj,
        grad_b_proj,
        grad_w_up,
        grad_b_up,
        grad_w_down,
        grad_b_down,
        grad_w_mod,
        grad_b_mod,
    )


def solution(mesh):
    placed = (
        P("dp", None, None),
        P("dp", None),
        P("dp"),
        P(None, None, "mp"),
        P(None, "mp"),
        P("mp", None),
        P(),
        P(None, "mp"),
        P("mp"),
        P("mp", None),
        P(),
        P(None, "mp"),
        P("mp"),
        P("dp", None, None),
    )
    return jax.shard_map(
        on_device,
        mesh=mesh,
        in_specs=placed,
        out_specs=(
            P("dp", None, None),
            P("dp", None, None),
            P("dp", None),
            P(None, None, "mp"),
            P(None, "mp"),
            P("mp", None),
            P(),
            P(None, "mp"),
            P("mp"),
            P("mp", None),
            P(),
            P(None, "mp"),
            P("mp"),
        ),
        check_vma=False,
    )
```

profile of v0, /device:TPU:0, one launch (start us, length us, event | category | flops | bytes accessed | tf_op | source)
XLA Modules:
  0.0 1665.7 jit_solution(14494195875991652209)
XLA Ops:
  23.1 950.2 %while.34 = (s32[]{:T(128)}, bf16[8,256,1152]{2,1,0:T(8,128)(2,1)}, f32[8,256,1152]{2,1,0:T(8,128)}, bf16[8,6912]{1,0:T(8,128)(2,1)}, f32[1152,3,576]{0,2,1:T(8,...) while((s32[]{:T(128)}, bf16[8,256,1152]{2,1,0:T(8,128)(2,1)}, ...), condition=%wide.region_27.0_spmd.clone, body=%wide.region_0.27_spmd.clone.sunk | while | flops 12777392128 | bytes 295346112 | solution.py:275
  38.1 18.6 %all-reduce.12.cloned.1.call-done = bf16[256,1152]{1,0:T(8,128)(2,1)} async-done(((bf16[256,1152]{1,0:T(8,128)(2,1)}), bf16[256,1152]{1,0:T(8,128)(2,1)}) %all-reduce.12.cloned.1.call-update) | async-done | bytes 589840 | tf_op jit(solution)/shard_map/while/body/eval_jaxpr/psum | solution.py:115
  118.0 13.0 all-reduce.16.cloned.1.call-done
  157.3 17.2 %all-reduce.12.cloned.1.call-done = bf16[256,1152]{1,0:T(8,128)(2,1)} async-done(((bf16[256,1152]{1,0:T(8,128)(2,1)}), bf16[256,1152]{1,0:T(8,128)(2,1)}) %all-reduce.12.cloned.1.call-update) | async-done | bytes 589840 | tf_op jit(solution)/shard_map/while/body/eval_jaxpr/psum | solution.py:115
  191.2 10.4 convolution_add_fusion.11
  232.4 8.7 select_add_fusion.8
  276.0 17.2 %all-reduce.12.cloned.1.call-done = bf16[256,1152]{1,0:T(8,128)(2,1)} async-done(((bf16[256,1152]{1,0:T(8,128)(2,1)}), bf16[256,1152]{1,0:T(8,128)(2,1)}) %all-reduce.12.cloned.1.call-update) | async-done | bytes 589840 | tf_op jit(solution)/shard_map/while/body/eval_jaxpr/psum | solution.py:115
  309.9 10.4 convolution_add_fusion.11
  394.6 17.2 %all-reduce.12.cloned.1.call-done = bf16[256,1152]{1,0:T(8,128)(2,1)} async-done(((bf16[256,1152]{1,0:T(8,128)(2,1)}), bf16[256,1152]{1,0:T(8,128)(2,1)}) %all-reduce.12.cloned.1.call-update) | async-done | bytes 589840 | tf_op jit(solution)/shard_map/while/body/eval_jaxpr/psum | solution.py:115
  428.6 10.4 convolution_add_fusion.11
  469.8 8.7 select_add_fusion.8
  513.3 17.2 %all-reduce.12.cloned.1.call-done = bf16[256,1152]{1,0:T(8,128)(2,1)} async-done(((bf16[256,1152]{1,0:T(8,128)(2,1)}), bf16[256,1152]{1,0:T(8,128)(2,1)}) %all-reduce.12.cloned.1.call-update) | async-done | bytes 589840 | tf_op jit(solution)/shard_map/while/body/eval_jaxpr/psum | solution.py:115
  547.3 10.4 convolution_add_fusion.11
  632.0 17.2 %all-reduce.12.cloned.1.call-done = bf16[256,1152]{1,0:T(8,128)(2,1)} async-done(((bf16[256,1152]{1,0:T(8,128)(2,1)}), bf16[256,1152]{1,0:T(8,128)(2,1)}) %all-reduce.12.cloned.1.call-update) | async-done | bytes 589840 | tf_op jit(solution)/shard_map/while/body/eval_jaxpr/psum | solution.py:115
  665.9 10.4 convolution_add_fusion.11
  707.2 8.7 select_add_fusion.8
  750.7 17.2 %all-reduce.12.cloned.1.call-done = bf16[256,1152]{1,0:T(8,128)(2,1)} async-done(((bf16[256,1152]{1,0:T(8,128)(2,1)}), bf16[256,1152]{1,0:T(8,128)(2,1)}) %all-reduce.12.cloned.1.call-update) | async-done | bytes 589840 | tf_op jit(solution)/shard_map/while/body/eval_jaxpr/psum | solution.py:115
  784.6 10.4 convolution_add_fusion.11
  869.4 17.2 %all-reduce.12.cloned.1.call-done = bf16[256,1152]{1,0:T(8,128)(2,1)} async-done(((bf16[256,1152]{1,0:T(8,128)(2,1)}), bf16[256,1152]{1,0:T(8,128)(2,1)}) %all-reduce.12.cloned.1.call-update) | async-done | bytes 589840 | tf_op jit(solution)/shard_map/while/body/eval_jaxpr/psum | solution.py:115
  903.3 10.4 convolution_add_fusion.11
  944.5 8.7 select_add_fusion.8
  996.8 81.0 %all-reduce.1 = (bf16[2,576]{1,0:T(2,128)(2,1)S(1)}, bf16[1152]{0:T(1024)(128)(2,1)S(1)}, bf16[2304]{0:T(1024)(128)(2,1)S(1)}, bf16[1152]{0:T(1024)(128)(2,1)S(1)}, bf16[3456]{0:T(1024)(128)(2,1)S(1)}) all-reduce(bf16[2,576]{1,0:T(2,128)(2,1)S(1)} %convert_element_type.383, ...), channel_id=1, replica_groups=mesh['dp'=16,'mp'=2] {'dp'}, use_global_device_ids=true, to_apply=%region_30.0 | all-reduce | flops 9216 | bytes 36864 | tf_op jit(solution)/shard_map/psum | solution.py:335
  1090.5 541.9 %all-reduce.10.cloned.1.call-done = (bf16[1152,3,576]{0,2,1:T(8,128)(2,1)}, bf16[576,1152]{1,0:T(8,128)(2,1)}, bf16[1152,2304]{1,0:T(8,128)(2,1)}, bf16[2304,1152]{1,0:T(8,128)(2,1)}, bf16[1152,3456]{1,0:T(8,128)(2,1)}) async-done(((bf16[1152,3,576]{0,2,1:T(8,128)(2,1)}, bf16[576,1152]{1,0:T(8,128)(2,1)}, bf16[1152,2304]{1,0:T(8,128)(2,1)}, bf16[2304,1152]{1,0:T(8,128)(2,1)}, bf16[1152,3456]{1,0:T(8,128)(2,1)}), ...) | async-done | bytes 23887888 | tf_op jit(solution)/shard_map/psum | solution.py:334
  1632.4 10.3 convert_element_type.398
  (1146 shorter events, 747.2 us)
Async XLA Ops:
  23.4 33.4 %all-reduce.12.cloned.1.call-start = ((), (), s32[]{:S(2)}) async-start(), calls=%async_computation.1 | async-start | bytes 1179648 | tf_op jit(solution)/shard_map/while/body/eval_jaxpr/psum | solution.py:115
  35.1 58.4 %all-reduce.14.cloned.1.call-start = ((), (), s32[]{:S(2)}) async-start(), calls=%async_computation.2 | async-start | bytes 1179648 | tf_op jit(solution)/shard_map/while/body/eval_jaxpr/psum | solution.py:170
  73.4 57.6 %all-reduce.16.cloned.1.call-start = ((), (), s32[]{:S(2)}) async-start(), calls=%async_computation.3 | async-start | bytes 2359296 | tf_op jit(solution)/shard_map/while/body/eval_jaxpr/psum | solution.py:129
  154.3 57.9 %all-reduce.14.cloned.1.call-start = ((), (), s32[]{:S(2)}) async-start(), calls=%async_computation.2 | async-start | bytes 1179648 | tf_op jit(solution)/shard_map/while/body/eval_jaxpr/psum | solution.py:170
  191.1 58.5 %all-reduce.16.cloned.1.call-start = ((), (), s32[]{:S(2)}) async-start(), calls=%async_computation.3 | async-start | bytes 2359296 | tf_op jit(solution)/shard_map/while/body/eval_jaxpr/psum | solution.py:129
  261.2 32.0 %all-reduce.12.cloned.1.call-start = ((), (), s32[]{:S(2)}) async-start(), calls=%async_computation.1 | async-start | bytes 1179648 | tf_op jit(solution)/shard_map/while/body/eval_jaxpr/psum | solution.py:115
  273.0 57.9 %all-reduce.14.cloned.1.call-start = ((), (), s32[]{:S(2)}) async-start(), calls=%async_computation.2 | async-start | bytes 1179648 | tf_op jit(solution)/shard_map/while/body/eval_jaxpr/psum | solution.py:170
  309.8 58.5 %all-reduce.16.cloned.1.call-start = ((), (), s32[]{:S(2)}) async-start(), calls=%async_computation.3 | async-start | bytes 2359296 | tf_op jit(solution)/shard_map/while/body/eval_jaxpr/psum | solution.py:129
  379.9 32.0 %all-reduce.12.cloned.1.call-start = ((), (), s32[]{:S(2)}) async-start(), calls=%async_computation.1 | async-start | bytes 1179648 | tf_op jit(solution)/shard_map/while/body/eval_jaxpr/psum | solution.py:115
  391.7 57.9 %all-reduce.14.cloned.1.call-start = ((), (), s32[]{:S(2)}) async-start(), calls=%async_computation.2 | async-start | bytes 1179648 | tf_op jit(solution)/shard_map/while/body/eval_jaxpr/psum | solution.py:170
  428.5 58.5 %all-reduce.16.cloned.1.call-start = ((), (), s32[]{:S(2)}) async-start(), calls=%async_computation.3 | async-start | bytes 2359296 | tf_op jit(solution)/shard_map/while/body/eval_jaxpr/psum | solution.py:129
  498.6 32.0 %all-reduce.12.cloned.1.call-start = ((), (), s32[]{:S(2)}) async-start(), calls=%async_computation.1 | async-start | bytes 1179648 | tf_op jit(solution)/shard_map/while/body/eval_jaxpr/psum | solution.py:115
  510.4 57.9 %all-reduce.14.cloned.1.call-start = ((), (), s32[]{:S(2)}) async-start(), calls=%async_computation.2 | async-start | bytes 1179648 | tf_op jit(solution)/shard_map/while/body/eval_jaxpr/psum | solution.py:170
  547.2 58.5 %all-reduce.16.cloned.1.call-start = ((), (), s32[]{:S(2)}) async-start(), calls=%async_computation.3 | async-start | bytes 2359296 | tf_op jit(solution)/shard_map/while/body/eval_jaxpr/psum | solution.py:129
  617.3 32.0 %all-reduce.12.cloned.1.call-start = ((), (), s32[]{:S(2)}) async-start(), calls=%async_computation.1 | async-start | bytes 1179648 | tf_op jit(solution)/shard_map/while/body/eval_jaxpr/psum | solution.py:115
  629.0 57.9 %all-reduce.14.cloned.1.call-start = ((), (), s32[]{:S(2)}) async-start(), calls=%async_computation.2 | async-start | bytes 1179648 | tf_op jit(solution)/shard_map/while/body/eval_jaxpr/psum | solution.py:170
  665.9 58.5 %all-reduce.16.cloned.1.call-start = ((), (), s32[]{:S(2)}) async-start(), calls=%async_computation.3 | async-start | bytes 2359296 | tf_op jit(solution)/shard_map/while/body/eval_jaxpr/psum | solution.py:129
  735.9 32.0 %all-reduce.12.cloned.1.call-start = ((), (), s32[]{:S(2)}) async-start(), calls=%async_computation.1 | async-start | bytes 1179648 | tf_op jit(solution)/shard_map/while/body/eval_jaxpr/psum | solution.py:115
  747.7 57.9 %all-reduce.14.cloned.1.call-start = ((), (), s32[]{:S(2)}) async-start(), calls=%async_computation.2 | async-start | bytes 1179648 | tf_op jit(solution)/shard_map/while/body/eval_jaxpr/psum | solution.py:170
  784.5 58.5 %all-reduce.16.cloned.1.call-start = ((), (), s32[]{:S(2)}) async-start(), calls=%async_computation.3 | async-start | bytes 2359296 | tf_op jit(solution)/shard_map/while/body/eval_jaxpr/psum | solution.py:129
  854.6 32.0 %all-reduce.12.cloned.1.call-start = ((), (), s32[]{:S(2)}) async-start(), calls=%async_computation.1 | async-start | bytes 1179648 | tf_op jit(solution)/shard_map/while/body/eval_jaxpr/psum | solution.py:115
  866.4 57.9 %all-reduce.14.cloned.1.call-start = ((), (), s32[]{:S(2)}) async-start(), calls=%async_computation.2 | async-start | bytes 1179648 | tf_op jit(solution)/shard_map/while/body/eval_jaxpr/psum | solution.py:170
  903.2 58.5 %all-reduce.16.cloned.1.call-start = ((), (), s32[]{:S(2)}) async-start(), calls=%async_computation.3 | async-start | bytes 2359296 | tf_op jit(solution)/shard_map/while/body/eval_jaxpr/psum | solution.py:129
  973.3 659.1 %all-reduce.10.cloned.1.call-start = ((), (), s32[]{:S(2)}) async-start(), calls=%async_computation | async-start | bytes 47775744 | tf_op jit(solution)/shard_map/psum | solution.py:334
  (267 other events, 2213.8 us)
Sparse Core Ops, SparseCore 0:
  35.3 21.4 all-reduce.11
  73.5 20.0 all-reduce.13
  109.9 21.0 all-reduce.15
  154.4 20.0 all-reduce.11
  191.3 20.0 all-reduce.13
  228.6 21.0 all-reduce.15
  273.1 20.0 all-reduce.11
  309.9 20.0 all-reduce.13
  347.2 21.0 all-reduce.15
  391.8 20.0 all-reduce.11
  428.6 20.0 all-reduce.13
  465.9 21.0 all-reduce.15
  510.5 20.0 all-reduce.11
  547.3 20.0 all-reduce.13
  584.6 21.0 all-reduce.15
  629.2 20.0 all-reduce.11
  666.0 20.0 all-reduce.13
  703.3 21.0 all-reduce.15
  747.8 20.0 all-reduce.11
  784.7 20.0 all-reduce.13
  822.0 21.0 all-reduce.15
  866.5 20.0 all-reduce.11
  903.3 20.0 all-reduce.13
  940.7 21.0 all-reduce.15
Sparse Core Ops, SparseCore 1:
  996.8 635.5 all-reduce.9
where the time goes:
time: 1670 us
  waiting for transfers between devices  759 us (45%)
  matrix products  505 us (30%)
  other arithmetic  245 us (15%)
  blocking collectives  86.5 us (5%)
  local copies, waits for them, and re-layouts  44.8 us (3%)
    psum x1, waiting for transfers between devices, on_device(): lax.psum(grad_w_qkv.astype(jnp.bfloat16), 'dp').astype(jnp.float32)  542 us
    dot_general x33, matrix products, inner_rows(): lax.dot_general(left, right, (((0,), (0,)), ((), ())), preferred_element_...  243 us
    psum x8, waiting for transfers between devices, forward(): lax.psum(partial_value.astype(jnp.bfloat16), 'mp').astype(jnp.float32)  139 us
    dot_general x33, matrix products, outer_cols(): lax.dot_general(left, right, (((1,), (1,)), ((), ())), preferred_element_...  120 us
    psum x1, blocking collectives, on_device(): lax.psum(grad_b_qv.astype(jnp.bfloat16), 'dp').astype(jnp.float32)  81 us
    psum x8, waiting for transfers between devices, forward(): lax.psum(partial_mlp.astype(jnp.bfloat16), 'mp').astype(jnp.float32)  72.8 us
    dot_general x8, matrix products, forward(): jnp.dot(normed_mlp, w_up, preferred_element_type=jnp.float32)  35.7 us
  transfers between devices with their start and end apart: 25, of which 18 were waited for; matrix products, arithmetic and copies ran while one was open for 17% of the time, Pallas kernels for 0%

commit v1 on v0

--- a/solution.py
+++ b/solution.py
@@ -1,12 +1,877 @@
+import functools
+
 import jax
 import jax.numpy as jnp
 from jax import lax
+from jax.experimental import pallas as pl
+from jax.experimental.pallas import tpu as pltpu
 from jax.sharding import PartitionSpec as P
 
 HEAD_DIM = 72
 
 
 epsilon = 1e-06
+
+f32 = jnp.float32
+bf16 = jnp.bfloat16
+
+
+def dot_nn(left, right):
+    return lax.dot_general(left, right, (((1,), (0,)), ((), ())), preferred_element_type=f32)
+
+
+def dot_nt(left, right):
+    return lax.dot_general(left, right, (((1,), (1,)), ((), ())), preferred_element_type=f32)
+
+
+def dot_tn(left, right):
+    return lax.dot_general(left, right, (((0,), (0,)), ((), ())), preferred_element_type=f32)
+
+
+def normalize(values):
+    center = values - jnp.mean(values, axis=-1, keepdims=True)
+    recip = lax.rsqrt(jnp.mean(center * center, axis=-1, keepdims=True) + epsilon)
+    return center * recip, recip
+
+
+def norm_pullback(grad_normed, unit, recip, scale_row):
+    scaled_grad = grad_normed * (1.0 + scale_row)
+    mean_grad = jnp.mean(scaled_grad, axis=-1, keepdims=True)
+    mean_unit = jnp.mean(scaled_grad * unit, axis=-1, keepdims=True)
+    return recip * (scaled_grad - mean_grad - unit * mean_unit)
+
+
+def column(rows):
+    return rows[...].T[:, 0:1]
+
+
+def token_sum(values):
+    return jnp.sum(values, axis=0, keepdims=True)
+
+
+def entry_kernel(own_images, sc, tok, cot, mod, normed, grad_mlp, sums):
+    image = sc[0] * own_images + pl.program_id(0)
+    live = jnp.where(image < sc[1], 1.0, 0.0).astype(f32)
+    unit, _ = normalize(tok[0].astype(f32))
+    normed[0] = (unit * (1.0 + mod[0, 1:2, :]) + mod[0, 0:1, :]).astype(bf16)
+    grad = (mod[0, 5:6, :] * (cot[0].astype(f32) * live)).astype(bf16)
+    grad_mlp[0] = grad
+    sums[0] = token_sum(grad.astype(f32))
+
+
+def attention_kernel(parts, sc, tok, normed, mod, b_proj, *refs):
+    w_qkv, w_proj, bias = refs[:parts], refs[parts : 2 * parts], refs[2 * parts : 3 * parts]
+    qkv, prob, mixed, attn_out, residual, normed_mlp = refs[3 * parts :]
+    cols = w_proj[0].shape[0]
+    pairs = cols // (2 * HEAD_DIM)
+    span = 2 * HEAD_DIM
+    factor = HEAD_DIM ** (-0.5)
+    rows = normed[0]
+    total = b_proj[...]
+    for part in range(parts):
+        base = part * 3 * cols
+        shift = column(bias[part])
+        for proj in range(3):
+            lo = proj * cols
+            value = dot_nt(w_qkv[part][lo : lo + cols, :], rows) + shift[lo : lo + cols, :]
+            qkv[0, base + lo : base + lo + cols, :] = value.astype(bf16)
+
+        def pair_step(pair, carry, base=base, part=part):
+            at = pl.multiple_of(base + pair * span, 16)
+            query = qkv[0, pl.ds(at, span), :].astype(f32)
+            key = qkv[0, pl.ds(at + cols, span), :].astype(f32)
+            value = qkv[0, pl.ds(at + 2 * cols, span), :].astype(f32)
+            outs = []
+            for one in range(2):
+                rows_of = slice(one * HEAD_DIM, (one + 1) * HEAD_DIM)
+                scores = dot_tn(key[rows_of].astype(bf16), query[rows_of].astype(bf16)) * factor
+                raised = jnp.exp(scores - jnp.max(scores, axis=0, keepdims=True))
+                share = 1.0 / jnp.sum(raised, axis=0, keepdims=True)
+                prob_b = (raised * share).astype(bf16)
+                prob[0, part * 2 * pairs + 2 * pair + one] = prob_b
+                outs.append(dot_nn(value[rows_of].astype(bf16), prob_b))
+            to = pl.multiple_of(part * cols + pair * span, 16)
+            mixed[0, pl.ds(to, span), :] = jnp.concatenate(outs, axis=0).astype(bf16)
+            return carry
+
+        lax.fori_loop(0, pairs, pair_step, 0, unroll=True)
+        total = total + dot_tn(mixed[0, part * cols : (part + 1) * cols, :], w_proj[part][...])
+    attn_out[0] = total
+    summed = tok[0].astype(f32) + mod[0, 2:3, :] * total
+    residual[0] = summed
+    unit, _ = normalize(summed)
+    normed_mlp[0] = (unit * (1.0 + mod[0, 4:5, :]) + mod[0, 3:4, :]).astype(bf16)
+
+
+def mlp_kernel(per, sc, rows, grad_mlp, w_up, w_down, bias, act_in, back_in, act, back, grads, sums):
+    step = pl.program_id(0)
+    here = w_down.shape[0] // per
+    hidden = lax.dot_general(
+        w_up[...], rows[...], (((0,), (1,)), ((), ())), preferred_element_type=f32
+    ) + column(bias)
+    square = hidden * hidden
+    bend = jnp.tanh(0.7978845608028654 * hidden * (1.0 + 0.044715 * square))
+    half = 0.5 * (1.0 + bend)
+    act_b = (hidden * half).astype(bf16)
+    slope = half + 0.5 * hidden * (1.0 - bend * bend) * (
+        0.7978845608028654 * (1.0 + 3.0 * 0.044715 * square)
+    )
+    back_b = (dot_nt(w_down[...], grad_mlp[...]) * slope).astype(bf16)
+    act[0] = act_b
+    back[0] = back_b
+    sums[...] = dot_nt(jnp.ones((8, rows.shape[0]), bf16), back_b)
+    grad_down = dot_nn(act_b, grad_mlp[...]).astype(bf16)
+    grad_up = dot_nn(back_b, rows[...]).astype(bf16)
+    for piece in range(here):
+        at = jnp.bitwise_xor(step * here + piece, sc[2])
+        lo = piece * per
+        grads[at, 0:per, :] = grad_down[lo : lo + per]
+        grads[at, per : 2 * per, :] = grad_up[lo : lo + per]
+
+
+def norm_back_kernel(
+    images, own_images, sc, back, w_up0, w_up1, residual, cot, mod, attn_out,
+    grad_residual, grad_attn, sums, total
+):
+    step, steps = pl.program_id(0), pl.num_programs(0)
+    seq = residual.shape[1]
+
+    def term(w_up):
+        return lax.dot_general(
+            back[0], w_up[...], (((0,), (1,)), ((), ())), preferred_element_type=f32
+        )
+
+    @pl.when(step == 0)
+    def _():
+        total[...] = term(w_up0)
+
+    @pl.when(jnp.logical_and(step > 0, step < steps // 2))
+    def _():
+        total[...] += term(w_up0)
+
+    @pl.when(step >= steps // 2)
+    def _():
+        total[...] += term(w_up1)
+
+    @pl.when(step == steps - 1)
+    def _():
+        for one in range(images):
+            live = jnp.where(sc[0] * own_images + one < sc[1], 1.0, 0.0).astype(f32)
+            grad_normed = total[one * seq : (one + 1) * seq, :]
+            unit, recip = normalize(residual[one])
+            sums[one, 0:1, :] = token_sum(grad_normed)
+            sums[one, 1:2, :] = token_sum(grad_normed * unit)
+            grad_res = cot[one].astype(f32) * live + norm_pullback(
+                grad_normed, unit, recip, mod[one, 4:5, :]
+            )
+            grad_residual[one] = grad_res
+            sums[one, 2:3, :] = token_sum(grad_res * attn_out[one])
+            grad_att = (mod[one, 2:3, :] * grad_res).astype(bf16)
+            grad_attn[one] = grad_att
+            sums[one, 3:4, :] = token_sum(grad_att.astype(f32))
+
+
+def back_kernel(parts, sc, grad_attn, qkv, prob, *refs):
+    w_proj = refs[:parts]
+    grad_qkv, grad_mixed = refs[parts:]
+    cols = w_proj[0].shape[0]
+    pairs = cols // (2 * HEAD_DIM)
+    span = 2 * HEAD_DIM
+    factor = HEAD_DIM ** (-0.5)
+    grad_att = grad_attn[0]
+    for part in range(parts):
+        base = part * 3 * cols
+        grad_mixed[part * cols : (part + 1) * cols, :] = dot_nt(w_proj[part][...], grad_att).astype(bf16)
+
+        def pair_step(pair, carry, base=base, part=part):
+            at = pl.multiple_of(base + pair * span, 16)
+            query = qkv[0, pl.ds(at, span), :].astype(f32)
+            key = qkv[0, pl.ds(at + cols, span), :].astype(f32)
+            value = qkv[0, pl.ds(at + 2 * cols, span), :].astype(f32)
+            grads = grad_mixed[pl.ds(pl.multiple_of(part * cols + pair * span, 16), span), :].astype(f32)
+            to_query, to_key, to_value = [], [], []
+            for one in range(2):
+                rows_of = slice(one * HEAD_DIM, (one + 1) * HEAD_DIM)
+                prob_b = prob[0, part * 2 * pairs + 2 * pair + one]
+                prob_f = prob_b.astype(f32)
+                grad_b = grads[rows_of].astype(bf16)
+                grad_prob = dot_tn(value[rows_of].astype(bf16), grad_b)
+                delta = jnp.sum(prob_f * grad_prob, axis=0, keepdims=True)
+                grad_scores = (prob_f * (grad_prob - delta)).astype(bf16)
+                to_query.append(dot_nn(key[rows_of].astype(bf16), grad_scores) * factor)
+                to_key.append(dot_nt(query[rows_of].astype(bf16), grad_scores) * factor)
+                to_value.append(dot_nt(grad_b, prob_b))
+            grad_qkv[0, pl.ds(at, span), :] = jnp.concatenate(to_query, axis=0).astype(bf16)
+            grad_qkv[0, pl.ds(at + cols, span), :] = jnp.concatenate(to_key, axis=0).astype(bf16)
+            grad_qkv[0, pl.ds(at + 2 * cols, span), :] = jnp.concatenate(to_value, axis=0).astype(bf16)
+            return carry
+
+        lax.fori_loop(0, pairs, pair_step, 0, unroll=True)
+
+
+def attn_grad_kernel(pieces, per, sc, *refs):
+    grad_qkv, mixed, normed, grad_attn = refs[:pieces], refs[pieces], refs[pieces + 1], refs[pieces + 2]
+    grads, sums = refs[pieces + 3 :]
+    step = pl.program_id(0)
+    here = mixed.shape[1] // per
+    images = mixed.shape[0]
+    each = images // pieces
+
+    def spread(total):
+        total = total.astype(bf16)
+        for piece in range(here):
+            at = jnp.bitwise_xor(step * here + piece, sc[2])
+            grads[at] = total[piece * per : (piece + 1) * per]
+
+    @pl.when(step < 3)
+    def _():
+        ones = jnp.ones((8, mixed.shape[2]), bf16)
+        total = count = None
+        for image in range(images):
+            left = grad_qkv[image // each][image % each]
+            term, one = dot_nn(left, normed[image]), dot_nt(ones, left)
+            total = term if image == 0 else total + term
+            count = one if image == 0 else count + one
+        sums[0] = count
+        spread(total)
+
+    @pl.when(step == 3)
+    def _():
+        total = dot_nn(mixed[0], grad_attn[0])
+        for image in range(1, images):
+            total = total + dot_nn(mixed[image], grad_attn[image])
+        spread(total)
+
+
+def first_back_kernel(pieces, images, sc, *refs):
+    grad_qkv = refs[:pieces]
+    w_qkv0, w_qkv1, tok, mod, grad_residual = refs[pieces : pieces + 5]
+    grad_tokens, sums = refs[pieces + 5 :]
+    step, steps = pl.program_id(0), pl.num_programs(0)
+    each = images // pieces
+
+    def add(w_qkv, fresh):
+        for one in range(images):
+            term = dot_tn(grad_qkv[one // each][one % each], w_qkv[...])
+            if fresh:
+                grad_tokens[one] = term
+            else:
+                grad_tokens[one] += term
+
+    @pl.when(step == 0)
+    def _():
+        add(w_qkv0, True)
+
+    @pl.when(jnp.logical_and(step > 0, step < steps // 2))
+    def _():
+        add(w_qkv0, False)
+
+    @pl.when(step >= steps // 2)
+    def _():
+        add(w_qkv1, False)
+
+    @pl.when(step == steps - 1)
+    def _():
+        for one in range(images):
+            grad_normed = grad_tokens[one]
+            unit, recip = normalize(tok[one].astype(f32))
+            sums[one, 0:1, :] = token_sum(grad_normed)
+            sums[one, 1:2, :] = token_sum(grad_normed * unit)
+            grad_tokens[one] = grad_residual[one] + norm_pullback(
+                grad_normed, unit, recip, mod[one, 1:2, :]
+            )
+
+
+def output_kernel(images, own_images, sc, act, w_down0, w_down1, residual, cot, mod, b_down, output, sums, total):
+    step, steps = pl.program_id(0), pl.num_programs(0)
+    seq = residual.shape[1]
+
+    @pl.when(step == 0)
+    def _():
+        total[...] = dot_tn(act[0], w_down0[...])
+
+    @pl.when(jnp.logical_and(step > 0, step < steps // 2))
+    def _():
+        total[...] += dot_tn(act[0], w_down0[...])
+
+    @pl.when(step >= steps // 2)
+    def _():
+        total[...] += dot_tn(act[0], w_down1[...])
+
+    @pl.when(step == steps - 1)
+    def _():
+        for one in range(images):
+            live = jnp.where(sc[0] * own_images + one < sc[1], 1.0, 0.0).astype(f32)
+            mlp_out = total[one * seq : (one + 1) * seq, :] + b_down[...]
+            sums[one] = token_sum((cot[one].astype(f32) * live) * mlp_out)
+            output[one] = ((residual[one] + mod[one, 5:6, :] * mlp_out) * live).astype(bf16)
+
+
+def final_piece(sc, halves, piece, store):
+    rel = jnp.bitwise_xor(piece, sc[2])
+    for low, high, bit, lo, hi in halves:
+        index = ((rel >> (bit + 1)) << bit) | (rel & ((1 << bit) - 1))
+        side = (rel >> bit) & 1
+
+        @pl.when(side == 0)
+        def _(low=low, index=index, lo=lo, hi=hi):
+            store(low[index].astype(f32), lo, hi)
+
+        @pl.when(side == 1)
+        def _(high=high, index=index, lo=lo, hi=hi):
+            store(high[index].astype(f32), lo, hi)
+
+
+def final_mlp_kernel(cuts, per, sc, *refs):
+    count = 2 * len(cuts)
+    arrays, (_, _, down, up, turned) = refs[:count], refs[count:]
+    here = down.shape[0] // per
+    halves = [(arrays[2 * k], arrays[2 * k + 1]) + cut for k, cut in enumerate(cuts)]
+    for piece in range(here):
+
+        def store(value, lo, hi, piece=piece):
+            down[piece * per : (piece + 1) * per, lo:hi] = value[0:per]
+            turned[piece * per : (piece + 1) * per, lo:hi] = value[per : 2 * per]
+
+        final_piece(sc, halves, pl.program_id(0) * here + piece, store)
+    up[...] = turned[...].T
+
+
+def final_attn_kernel(cuts, per, sc, *refs):
+    count = 2 * len(cuts)
+    arrays, (qkv, proj) = refs[:count], refs[count:]
+    here = proj.shape[0] // per
+    halves = [(arrays[2 * k], arrays[2 * k + 1]) + cut for k, cut in enumerate(cuts)]
+    for target, wanted in ((qkv, True), (proj, False)):
+
+        @pl.when((pl.program_id(0) < 3) == wanted)
+        def _(target=target):
+            for piece in range(here):
+
+                def store(value, lo, hi, piece=piece):
+                    target[piece * per : (piece + 1) * per, lo:hi] = value
+
+                final_piece(sc, halves, pl.program_id(0) * here + piece, store)
+
+
+VMEM_LIMIT = 60 << 20
+
+
+def run_kernel(body, sc, args, in_specs, out_specs, out_shape, grid, flops, scratch=(), alias=None):
+    size = sum(a.size * a.dtype.itemsize for a in args) + sum(
+        s.size * s.dtype.itemsize for s in out_shape
+    )
+    return pl.pallas_call(
+        body,
+        out_shape=out_shape,
+        grid_spec=pltpu.PrefetchScalarGridSpec(
+            num_scalar_prefetch=1,
+            grid=grid,
+            in_specs=in_specs,
+            out_specs=out_specs,
+            scratch_shapes=list(scratch),
+        ),
+        compiler_params=pltpu.CompilerParams(vmem_limit_bytes=VMEM_LIMIT),
+        cost_estimate=pl.CostEstimate(flops=int(flops), bytes_accessed=int(size), transcendentals=0),
+        input_output_aliases=alias or {},
+    )(sc, *args)
+
+
+def whole_block(array):
+    zeros = (0,) * array.ndim
+    return pl.BlockSpec(array.shape, lambda *_: zeros, pipeline_mode=pl.Buffered(1))
+
+
+def shape_of(dims, kind):
+    return jax.ShapeDtypeStruct(dims, kind)
+
+
+SWAP = [(0, 1), (1, 0)]
+
+
+def swap_cores(value):
+    return lax.ppermute(value, "mp", SWAP)
+
+
+def bit_pairs(bit):
+    return [(index, index ^ (1 << bit)) for index in range(16)]
+
+
+MLP_WAYS = ((0, 640, (0, 1, 2, 3)), (640, 1152, (1, 0, 2, 3)))
+ATTN_WAYS = ((0, 512, (0, 1, 2, 3)), (512, 896, (1, 0, 2, 3)), (896, 1152, (2, 3, 0, 1)))
+
+
+def cut(array, bits, bit, side, cols=None):
+    lo = [0] * array.ndim
+    hi = list(array.shape)
+    place = bits.index(bit)
+    lo[place], hi[place] = side, side + 1
+    if cols is not None:
+        lo[-1], hi[-1] = cols
+    out = lax.slice(array, lo, hi)
+    return out.reshape(out.shape[:place] + out.shape[place + 1 :])
+
+
+class Flow:
+    def __init__(self, ways, own, other):
+        self.ways = ways
+        self.shape = (2, 2, 2, 2) + other.shape[1:]
+        self.own, self.other = own, other
+        self.stage = 0
+        self.halves = None
+
+    def set_own(self, own):
+        self.own = own
+
+    def pending(self):
+        if self.stage == 0:
+            return [self.other]
+        if self.stage == 1:
+            return [self.own, self.came]
+        return [self.keeps, self.comes]
+
+    def step(self, fence):
+        if self.stage == 0:
+            (other,) = fence([self.other])
+            self.came = swap_cores(other)
+        elif self.stage <= 5:
+            first, second = fence(self.pending())
+            if self.stage == 1:
+                first = [first.reshape(self.shape)] * len(self.ways)
+                second = [second.reshape(self.shape)] * len(self.ways)
+            sends, keeps = [], []
+            for (lo, hi, order), one, two in zip(self.ways, first, second):
+                if self.stage == 5:
+                    keeps.append(one + two)
+                    sends.append(one + two)
+                    continue
+                bits = [bit for bit in (3, 2, 1, 0) if bit not in order[: self.stage - 1]]
+                bit = order[self.stage - 1]
+                cols = (lo, hi) if self.stage == 1 else None
+                sends.append(cut(one, bits, bit, 1, cols) + cut(two, bits, bit, 1, cols))
+                keeps.append(cut(one, bits, bit, 0, cols) + cut(two, bits, bit, 0, cols))
+            if self.stage == 5:
+                self.sets = [[] for _ in self.ways]
+                (keeps,) = fence([keeps])
+                self.send(keeps, keeps)
+            else:
+                sends, keeps = fence([sends, keeps])
+                self.send(sends, keeps)
+        else:
+            haves, comes = fence(self.pending())
+            joined = []
+            for (lo, hi, order), bits, have, got in zip(self.ways, self.sets, haves, comes):
+                bit = order[8 - self.stage + 1]
+                if self.stage == 9:
+                    continue
+                place = sum(1 for other in bits if other > bit)
+                joined.append(jnp.stack([have, got], axis=place))
+                bits.insert(place, bit)
+            if self.stage == 9:
+                self.halves = [
+                    part.reshape((8,) + part.shape[-2:]) for pair in zip(haves, comes) for part in pair
+                ]
+            else:
+                (joined,) = fence([joined])
+                self.send(joined, joined)
+        self.stage += 1
+
+    def send(self, sends, keeps):
+        self.keeps = keeps
+        which = self.stage - 1 if self.stage <= 4 else 8 - self.stage
+        self.comes = [
+            lax.ppermute(value, "dp", bit_pairs(order[which]))
+            for value, (_, _, order) in zip(sends, self.ways)
+        ]
+
+
+class Order:
+    def __init__(self, sc):
+        self.sc = sc
+
+    def fence(self, values):
+        self.sc, values = lax.optimization_barrier((self.sc, values))
+        return values
+
+    def after(self, value):
+        self.sc, _ = lax.optimization_barrier((self.sc, value))
+
+    def tick(self, *flows):
+        for flow in flows:
+            if flow.halves is None:
+                flow.step(self.fence)
+
+
+CHUNKS = 3
+
+
+def fast_device(
+    tokens, condition, counts, w_qkv, b_qv, w_proj, b_proj, w_up, b_up, w_down, b_down, w_mod, b_mod,
+    cotangent,
+):
+    slots, seq, dim = tokens.shape
+    images = slots // 2
+    count = images * seq
+    cols = w_qkv.shape[2]
+    ff = w_up.shape[1]
+    own_cols = w_mod.shape[1]
+    heads = cols // HEAD_DIM
+    core = lax.axis_index("mp")
+    order = Order(jnp.stack([core, counts[0], lax.axis_index("dp")]).astype(jnp.int32))
+
+    qkv_rows = jnp.transpose(w_qkv, (1, 2, 0)).reshape(3 * cols, dim)
+    wq = [qkv_rows, swap_cores(qkv_rows)]
+    wp = [w_proj, swap_cores(w_proj)]
+    wu = [w_up, swap_cores(w_up)]
+    wd = [w_down, swap_cores(w_down)]
+
+    cond_f = condition.astype(f32)
+    scaled = jax.nn.silu(cond_f).astype(bf16)
+    own_mod = jnp.dot(scaled, w_mod, preferred_element_type=f32) + b_mod.astype(f32)
+    own_bias = jnp.concatenate([b_qv.reshape(-1), b_up]).astype(f32)[None]
+    gathered = lax.all_gather(jnp.concatenate([own_mod, own_bias]), "mp", axis=0, tiled=False)
+    modulation = jnp.concatenate([gathered[0, :slots], gathered[1, :slots]], axis=1).reshape(slots, 6, dim)
+    zero_bias = jnp.zeros((cols,), f32)
+    qkv_bias, up_bias = [], []
+    for part in range(2):
+        row = lax.dynamic_index_in_dim(gathered[:, slots], core ^ part, 0, keepdims=False)
+        qkv_row = jnp.concatenate([row[:cols], zero_bias, row[cols : 2 * cols]])
+        qkv_bias.append(jnp.broadcast_to(qkv_row, (8, 3 * cols)))
+        up_bias.append(jnp.broadcast_to(row[2 * cols :], (8, ff)))
+    proj_bias = b_proj.astype(f32)[None]
+    down_bias = b_down.astype(f32)[None]
+
+    local = lambda i, s: (s[0] * images + i, 0, 0)
+    mine = lambda i, s: (i, 0, 0)
+    tok_spec = pl.BlockSpec((1, seq, dim), local)
+    own_spec = pl.BlockSpec((1, seq, dim), mine)
+    mod_spec = pl.BlockSpec((1, 6, dim), local)
+    group = lambda i, s: (s[0], 0, 0)
+    once = pl.Buffered(1)
+    all_tok_spec = pl.BlockSpec((images, seq, dim), group, pipeline_mode=once)
+    all_mod_spec = pl.BlockSpec((images, 6, dim), group, pipeline_mode=once)
+
+    normed, grad_mlp, down_sums = run_kernel(
+        functools.partial(entry_kernel, images),
+        order.sc,
+        [tokens, cotangent, modulation],
+        [tok_spec, tok_spec, mod_spec],
+        [own_spec, own_spec, pl.BlockSpec((1, 1, dim), mine)],
+        [shape_of((images, seq, dim), bf16)] * 2 + [shape_of((images, 1, dim), f32)],
+        (images,),
+        count * dim * 20,
+    )
+    order.after(down_sums)
+    qkv_spec = pl.BlockSpec((1, 6 * cols, seq), mine)
+    prob_spec = pl.BlockSpec((1, 2 * heads, seq, seq), lambda i, s: (i, 0, 0, 0))
+    mixed_spec = pl.BlockSpec((1, 2 * cols, seq), mine)
+    attn_args = wq + wp + qkv_bias
+    qkv, prob, mixed, attn_out, residual, normed_mlp = run_kernel(
+        functools.partial(attention_kernel, 2),
+        order.sc,
+        [tokens, normed, modulation, proj_bias] + attn_args,
+        [tok_spec, own_spec, mod_spec, whole_block(proj_bias)] + [whole_block(a) for a in attn_args],
+        [qkv_spec, prob_spec, mixed_spec, own_spec, own_spec, own_spec],
+        [
+            shape_of((images, 6 * cols, seq), bf16),
+            shape_of((images, 2 * heads, seq, seq), bf16),
+            shape_of((images, 2 * cols, seq), bf16),
+            shape_of((images, seq, dim), f32),
+            shape_of((images, seq, dim), f32),
+            shape_of((images, seq, dim), bf16),
+        ],
+        (images,),
+        2 * count * dim * 8 * cols + 8 * count * seq * dim,
+    )
+
+    rows_flat = normed_mlp.reshape(count, dim)
+    grad_flat = grad_mlp.reshape(count, dim)
+    width = ff // CHUNKS
+    per = width // 16
+    steps = 2
+    block = width // steps
+    anywhere = pl.BlockSpec(memory_space=pl.ANY)
+    act = back = None
+    up_sums = [[None] * CHUNKS, [None] * CHUNKS]
+
+    def mlp_part(chunk, part):
+        nonlocal act, back
+        first = act is None
+        if first:
+            act = back = jnp.zeros((8, 128), bf16)
+        at = chunk * steps
+        spread = pl.BlockSpec((1, block, count), lambda s, c: (part, at + s, 0))
+        act, back, grads, sums = run_kernel(
+            functools.partial(mlp_kernel, per),
+            order.sc,
+            [rows_flat, grad_flat, wu[part], wd[part], up_bias[part], act, back],
+            [
+                whole_block(rows_flat),
+                whole_block(grad_flat),
+                pl.BlockSpec((dim, block), lambda s, c: (0, at + s)),
+                pl.BlockSpec((block, dim), lambda s, c: (at + s, 0)),
+                pl.BlockSpec((8, block), lambda s, c: (0, at + s)),
+                anywhere,
+                anywhere,
+            ],
+            [
+                spread,
+                spread,
+                pl.BlockSpec((16, 2 * per, dim), lambda s, c: (0, 0, 0)),
+                pl.BlockSpec((8, block), lambda s, c: (0, s)),
+            ],
+            [shape_of((2, ff, count), bf16)] * 2
+            + [shape_of((16, 2 * per, dim), bf16), shape_of((8, width), f32)],
+            (steps,),
+            8 * count * dim * width,
+            alias=None if first else {6: 0, 7: 1},
+        )
+        up_sums[part][chunk] = sums[0]
+        order.after(sums)
+        return grads
+
+    other = mlp_part(0, 1)
+    first = Flow(MLP_WAYS, None, other)
+    order.tick(first)
+    first.set_own(mlp_part(0, 0))
+    order.tick(first)
+    second = Flow(MLP_WAYS, None, mlp_part(1, 1))
+    order.tick(second)
+    second.set_own(mlp_part(1, 0))
+    order.tick(first, second)
+    third = Flow(MLP_WAYS, None, mlp_part(2, 1))
+    order.tick(first, third)
+    third.set_own(mlp_part(2, 0))
+    order.tick(first, second, third)
+
+    reach = 768
+    per_part = ff // reach
+    every = lambda s, c: (0, 0, 0)
+    own_whole = pl.BlockSpec((images, seq, dim), every, pipeline_mode=once)
+    grad_residual, grad_attn, mid_sums = run_kernel(
+        functools.partial(norm_back_kernel, images, images),
+        order.sc,
+        [back] + wu + [residual, cotangent, modulation, attn_out],
+        [
+            pl.BlockSpec((1, reach, count), lambda s, c: (s // per_part, s % per_part, 0)),
+            pl.BlockSpec((dim, reach), lambda s, c: (0, jnp.minimum(s, per_part - 1))),
+            pl.BlockSpec((dim, reach), lambda s, c: (0, jnp.maximum(s - per_part, 0))),
+            own_whole,
+            all_tok_spec,
+            all_mod_spec,
+            own_whole,
+        ],
+        [own_whole, own_whole, pl.BlockSpec((images, 4, dim), every)],
+        [
+            shape_of((images, seq, dim), f32),
+            shape_of((images, seq, dim), bf16),
+            shape_of((images, 4, dim), f32),
+        ],
+        (2 * per_part,),
+        2 * count * dim * 2 * ff,
+        scratch=[pltpu.VMEM((count, dim), f32)],
+    )
+    order.after(mid_sums)
+    order.tick(first, second, third)
+    pieces = 2
+    each = images // pieces
+    grad_qkv = []
+    for piece in range(pieces):
+        there = lambda i, s, piece=piece: (piece * each + i, 0, 0)
+        (grad_piece,) = run_kernel(
+            functools.partial(back_kernel, 2),
+            order.sc,
+            [grad_attn, qkv, prob] + wp,
+            [
+                pl.BlockSpec((1, seq, dim), there),
+                pl.BlockSpec((1, 6 * cols, seq), there),
+                pl.BlockSpec((1, 2 * heads, seq, seq), lambda i, s, piece=piece: (piece * each + i, 0, 0, 0)),
+            ]
+            + [whole_block(a) for a in wp],
+            [qkv_spec],
+            [shape_of((each, 6 * cols, seq), bf16)],
+            (each,),
+            (2 * count * dim * 2 * cols + 10 * count * seq * dim) // pieces,
+            scratch=[pltpu.VMEM((2 * cols, seq), bf16)],
+        )
+        grad_qkv.append(grad_piece)
+        order.after(grad_piece)
+        order.tick(first, second, third)
+
+    attn_per = 4 * cols // 16
+    qv_sums = [None, None]
+
+    def attn_part(part):
+        grads, sums = run_kernel(
+            functools.partial(attn_grad_kernel, pieces, attn_per),
+            order.sc,
+            grad_qkv + [mixed, normed, grad_attn],
+            [
+                pl.BlockSpec((each, cols, seq), lambda s, c: (0, 3 * part + jnp.minimum(s, 2), 0))
+                for _ in range(pieces)
+            ]
+            + [pl.BlockSpec((images, cols, seq), lambda s, c: (0, part, 0))]
+            + [whole_block(normed), whole_block(grad_attn)],
+            [
+                pl.BlockSpec((16, attn_per, dim), every),
+                pl.BlockSpec((1, 8, cols), lambda s, c: (jnp.minimum(s, 2), 0, 0)),
+            ],
+            [shape_of((16, attn_per, dim), bf16), shape_of((3, 8, cols), f32)],
+            (4,),
+            2 * count * dim * 4 * cols,
+        )
+        qv_sums[part] = sums[:, 0]
+        order.after(sums)
+        return grads
+
+    last = Flow(ATTN_WAYS, None, attn_part(1))
+    order.tick(last, first, second, third)
+    last.set_own(attn_part(0))
+    order.tick(last, first, second, third)
+
+    per_part = 3
+    rows = cols
+    grad_tokens, low_sums = run_kernel(
+        functools.partial(first_back_kernel, pieces, images),
+        order.sc,
+        grad_qkv + wq + [tokens, modulation, grad_residual],
+        [pl.BlockSpec((each, rows, seq), lambda s, c: (0, s, 0)) for _ in range(pieces)]
+        + [
+            pl.BlockSpec((rows, dim), lambda s, c: (jnp.minimum(s, 2), 0)),
+            pl.BlockSpec((rows, dim), lambda s, c: (jnp.maximum(s - 3, 0), 0)),
+            all_tok_spec,
+            all_mod_spec,
+            own_whole,
+        ],
+        [own_whole, pl.BlockSpec((images, 2, dim), every)],
+        [shape_of((images, seq, dim), f32), shape_of((images, 2, dim), f32)],
+        (6,),
+        2 * count * dim * 6 * cols,
+    )
+    order.after(low_sums)
+    order.tick(last, first, second, third)
+    per_part = ff // reach
+    output, gate_sums = run_kernel(
+        functools.partial(output_kernel, images, images),
+        order.sc,
+        [act] + wd + [residual, cotangent, modulation, down_bias],
+        [
+            pl.BlockSpec((1, reach, count), lambda s, c: (s // per_part, s % per_part, 0)),
+            pl.BlockSpec((reach, dim), lambda s, c: (jnp.minimum(s, per_part - 1), 0)),
+            pl.BlockSpec((reach, dim), lambda s, c: (jnp.maximum(s - per_part, 0), 0)),
+            own_whole,
+            all_tok_spec,
+            all_mod_spec,
+            whole_block(down_bias),
+        ],
+        [own_whole, pl.BlockSpec((images, 1, dim), every)],
+        [shape_of((images, seq, dim), bf16), shape_of((images, 1, dim), f32)],
+        (2 * per_part,),
+        2 * count * dim * 2 * ff,
+        scratch=[pltpu.VMEM((count, dim), f32)],
+    )
+    order.after(gate_sums)
+    order.tick(last, first, second, third)
+    output = lax.all_gather(output, "mp", axis=0, tiled=True)
+    grad_tokens = lax.all_gather(grad_tokens, "mp", axis=0, tiled=True)
+
+    grad_modulation = jnp.concatenate([low_sums, mid_sums[:, 2:3], mid_sums[:, 0:2], gate_sums], axis=1)
+    grad_modulation = grad_modulation.reshape(images, 6 * dim).astype(bf16)
+    bias_sums = [
+        jnp.concatenate([qv_sums[part][0], qv_sums[part][2]] + up_sums[part]) for part in range(2)
+    ]
+    shared = jnp.concatenate([jnp.sum(mid_sums[:, 3], axis=0), jnp.sum(down_sums[:, 0], axis=0)])
+    shared = jnp.pad(shared, (0, own_cols - 2 * dim))
+    packed = jnp.concatenate(
+        [grad_modulation.astype(f32).reshape(2 * images, own_cols), jnp.stack(bias_sums + [shared])]
+    )
+    both = lax.all_gather(packed, "mp", axis=0, tiled=False)
+    group_mod = both[:, : 2 * images].reshape(2, images, 2, own_cols)
+    group_mod = lax.dynamic_index_in_dim(group_mod, core, 2, keepdims=False).reshape(slots, own_cols)
+    group_mod = group_mod.astype(bf16)
+    own_bias_sum = lax.dynamic_index_in_dim(both[:, 2 * images], core, 0) + lax.dynamic_index_in_dim(
+        both[:, 2 * images + 1], 1 - core, 0
+    )
+    shared_sum = both[0, -1:] + both[1, -1:]
+    part_scaled = outer_cols(group_mod, w_mod).astype(bf16)
+    grad_scaled = part_scaled.astype(f32) + swap_cores(part_scaled).astype(f32)
+    _, silu_back = jax.vjp(jax.nn.silu, cond_f)
+    grad_condition = silu_back(grad_scaled)[0]
+    wide_scaled = jnp.pad(scaled.reshape(-1), (0, 3 * own_cols - slots * dim)).reshape(3, own_cols)
+    packed_rows = jnp.concatenate(
+        [group_mod, own_bias_sum.astype(bf16), shared_sum.astype(bf16), wide_scaled]
+    )
+    all_rows = lax.all_gather(packed_rows, "dp", axis=0, tiled=False)
+    all_mod = all_rows[:, :slots].reshape(-1, own_cols)
+    all_scaled = all_rows[:, slots + 2 :].reshape(16, -1)[:, : slots * dim].reshape(-1, dim)
+    grad_w_mod = inner_rows(all_scaled, all_mod)
+    grad_b_mod = jnp.sum(all_mod.astype(f32), axis=0)
+    bias_total = jnp.sum(all_rows[:, slots : slots + 2].astype(f32), axis=0)
+    grad_b_qv = bias_total[0, : 2 * cols].reshape(2, cols)
+    grad_b_up = bias_total[0, 2 * cols :]
+    grad_b_proj = bias_total[1, :dim]
+    grad_b_down = bias_total[1, dim : 2 * dim]
+
+    while first.halves is None or second.halves is None or third.halves is None:
+        order.tick(last, *[flow for flow in (first, second, third) if flow.halves is None])
+
+    def cuts(ways):
+        return tuple((way[0], lo, hi) for lo, hi, way in ways)
+
+    grad_w_down = grad_w_up = jnp.zeros((8, 128), f32)
+    for chunk, flow in enumerate((first, second, third)):
+        args = flow.halves
+        spot = len(args) + 1
+        grad_w_down, grad_w_up = run_kernel(
+            functools.partial(final_mlp_kernel, cuts(MLP_WAYS), per),
+            order.sc,
+            list(args) + [grad_w_down, grad_w_up],
+            [whole_block(a) for a in args] + [anywhere, anywhere],
+            [
+                pl.BlockSpec((block, dim), lambda s, c, chunk=chunk: (chunk * steps + s, 0)),
+                pl.BlockSpec((dim, block), lambda s, c, chunk=chunk: (0, chunk * steps + s)),
+            ],
+            [shape_of((ff, dim), f32), shape_of((dim, ff), f32)],
+            (steps,),
+            width * dim,
+            scratch=[pltpu.VMEM((block, dim), f32)],
+            alias=None if chunk == 0 else {spot: 0, spot + 1: 1},
+        )
+        if last.halves is None:
+            order.after(grad_w_down[0, :1])
+            order.tick(last)
+    while last.halves is None:
+        order.tick(last)
+    args = last.halves
+    grad_qkv_rows, grad_w_proj = run_kernel(
+        functools.partial(final_attn_kernel, cuts(ATTN_WAYS), attn_per),
+        order.sc,
+        list(args),
+        [whole_block(a) for a in args],
+        [
+            pl.BlockSpec((cols, dim), lambda s, c: (jnp.minimum(s, 2), 0)),
+            pl.BlockSpec((cols, dim), lambda s, c: (0, 0)),
+        ],
+        [shape_of((3 * cols, dim), f32), shape_of((cols, dim), f32)],
+        (4,),
+        cols * dim,
+    )
+    grad_w_qkv = jnp.transpose(grad_qkv_rows.reshape(3, cols, dim), (2, 0, 1))
+    return (
+        output,
+        grad_tokens,
+        grad_condition,
+        grad_w_qkv,
+        grad_b_qv,
+        grad_w_proj,
+        grad_b_proj,
+        grad_w_up,
+        grad_b_up,
+        grad_w_down,
+        grad_b_down,
+        grad_w_mod,
+        grad_b_mod,
+    )
 
 
 def layer_norm(values):
@@ -376,8 +1241,9 @@
         P("mp"),
         P("dp", None, None),
     )
+    fast = mesh.shape["dp"] == 16 and mesh.shape["mp"] == 2
     return jax.shard_map(
-        on_device,
+        fast_device if fast else on_device,
         mesh=mesh,
         in_specs=placed,
         out_specs=(

time: 1670 us -> 702 us (0.42)
  waiting for transfers between devices: 759 us -> 125 us
  matrix products: 505 us -> 19.2 us
  Pallas kernels: 0 us -> 319 us
  other arithmetic: 245 us -> 69 us
  starting transfers between devices: 0.75 us -> 82.7 us
  blocking collectives: 86.5 us -> 6.34 us
    psum x25 -> x0, waiting for transfers between devices: 759 us -> none  [the longest x1 542 us: on_device(): lax.psum(grad_w_qkv.astype(jnp.bfloat16), 'dp').astype(jnp.float32)]
    pallas_call x0 -> x19, Pallas kernels: none -> 319 us  [run_kernel(): pl.pallas_call(body, out_shape=out_shape, grid_spec=pltpu.PrefetchScalarG...]
    dot_general x33 -> x1, matrix products: 243 us -> 9.31 us  [inner_rows(): lax.dot_general(left, right, (((0,), (0,)), ((), ())), preferred_element_...]
    reduce_sum x105 -> x4, other arithmetic: 171 us -> 3.34 us  [the longest x1 1.91 us: fast_device(): grad_b_mod = jnp.sum(all_mod.astype(f32), axis=0)]
    dot_general x81 -> x1, matrix products: 143 us -> 4.42 us  [fast_device(): jnp.dot(scaled, w_mod, preferred_element_type=f32) + b_mod.astype(f32)]
    ppermute x0 -> x81, waiting for transfers between devices: none -> 124 us  [the longest x72 120 us: send(): lax.ppermute(value, 'dp', bit_pairs(order[which]))]
    dot_general x33 -> x1, matrix products: 120 us -> 5.42 us  [outer_cols(): lax.dot_general(left, right, (((1,), (1,)), ((), ())), preferred_element_...]
    psum x2 -> x0, blocking collectives: 84.4 us -> none  [the longest x1 81 us: on_device(): lax.psum(grad_b_qv.astype(jnp.bfloat16), 'dp').astype(jnp.float32)]
  transfers between devices with their start and end apart: 25 -> 84, of which waited for: 18 -> 28; matrix products, arithmetic and copies ran while one was open for 17% -> 15% of each run, Pallas kernels for 0% -> 36%
where the time goes in v1:
time: 702 us; the launch traced here: 690 us
  Pallas kernels  319 us (45%)
  waiting for transfers between devices  125 us (18%)
  starting transfers between devices  82.7 us (12%)
  other arithmetic  69 us (10%)
  local copies, waits for them, and re-layouts  52.3 us (7%)
  matrix products  19.2 us (3%)
  between operations  15.8 us (2%)
    pallas_call x19, Pallas kernels, run_kernel(): pl.pallas_call(body, out_shape=out_shape, grid_spec=pltpu.PrefetchScalarG...  319 us
    ppermute x72, waiting for transfers between devices, send(): lax.ppermute(value, 'dp', bit_pairs(order[which]))  120 us
    ppermute x72, starting transfers between devices, send(): lax.ppermute(value, 'dp', bit_pairs(order[which]))  80.4 us
    add x36, other arithmetic, step(): keeps.append(cut(one, bits, bit, 0, cols) + cut(two, bits, bit, 0, cols))  31 us
    slice x18, local copies, waits for them, and re-layouts, cut(): out = lax.slice(array, lo, hi)  20.6 us
    another operation x27, other arithmetic, step(): joined.append(jnp.stack([have, got], axis=place))  15.7 us
  transfers between devices with their start and end apart: 84, of which 28 were waited for; matrix products, arithmetic and copies ran while one was open for 15% of the time, Pallas kernels for 36%

profile of v1, /device:TPU:0, one launch (start us, length us, event | category | flops | bytes accessed | tf_op | source)
XLA Modules:
  0.0 689.5 jit_solution(8179724134416972277)
XLA Ops:
  22.1 6.6 shard_map.237
  33.2 45.3 %shard_map.238 = (bf16[4,3456,256]{2,1,0:T(8,128)(2,1)}, bf16[4,16,256,256]{3,2,1,0:T(8,128)(2,1)}, bf16[4,1152,256]{2,1,0:T(8,128)(2,1)}, f32[4,256,1152]{2,1,0...) custom-call(s32[3]{0:T(128)} %pad_add_fusion.sc, bf16[8,256,1152]{2,1,0:T(8,128)(2,1)} %refs_4_.1, ...), custom_call_target="tpu_custom_call" | custom-call | flops 13287555072 | bytes 47653376 | tf_op jit(solution)/shard_map/pallas_call | solution.py:364
  79.8 15.8 %shard_map.239 = (bf16[2,2304,1024]{2,1,0:T(8,128)(2,1)}, bf16[2,2304,1024]{2,1,0:T(8,128)(2,1)}, bf16[16,96,1152]{2,1,0:T(8,128)(2,1)}, f32[8,768]{1,0:T(8,128)}) custom-call(s32[3]{0:T(128)} %pad_add_fusion.sc, bf16[1024,1152]{1,0:T(8,128)(2,1)} %bitcast.295, bf16[1024,1152]{1,0:T(8,128)(2,1)} %bitcast.289, ...), custom_call_target="tpu_custom_call" | custom-call | flops 7247757312 | bytes 37851136 | tf_op jit(solution)/shard_map/pallas_call | solution.py:364
  96.6 16.0 %shard_map.240 = (bf16[2,2304,1024]{2,1,0:T(8,128)(2,1)}, bf16[2,2304,1024]{2,1,0:T(8,128)(2,1)}, bf16[16,96,1152]{2,1,0:T(8,128)(2,1)}, f32[8,768]{1,0:T(8,128)}) custom-call(s32[3]{0:T(128)} %pad_add_fusion.sc, bf16[1024,1152]{1,0:T(8,128)(2,1)} %bitcast.296, bf16[1024,1152]{1,0:T(8,128)(2,1)} %bitcast.290, ...), custom_call_target="tpu_custom_call", output_to_operand_aliasing={{0}: (6, {}), {1}: (7, {})} | custom-call | flops 7247757312 | bytes 56721408 | tf_op jit(solution)/shard_map/pallas_call | solution.py:364
  117.5 15.6 %shard_map.241 = (bf16[2,2304,1024]{2,1,0:T(8,128)(2,1)}, bf16[2,2304,1024]{2,1,0:T(8,128)(2,1)}, bf16[16,96,1152]{2,1,0:T(8,128)(2,1)}, f32[8,768]{1,0:T(8,128)}) custom-call(s32[3]{0:T(128)} %pad_add_fusion.sc, bf16[1024,1152]{1,0:T(8,128)(2,1)} %bitcast.297, bf16[1024,1152]{1,0:T(8,128)(2,1)} %bitcast.291, ...), custom_call_target="tpu_custom_call", output_to_operand_aliasing={{0}: (6, {}), {1}: (7, {})} | custom-call | flops 7247757312 | bytes 56721408 | tf_op jit(solution)/shard_map/pallas_call | solution.py:364
  137.7 15.9 %shard_map.242 = (bf16[2,2304,1024]{2,1,0:T(8,128)(2,1)}, bf16[2,2304,1024]{2,1,0:T(8,128)(2,1)}, bf16[16,96,1152]{2,1,0:T(8,128)(2,1)}, f32[8,768]{1,0:T(8,128)}) custom-call(s32[3]{0:T(128)} %pad_add_fusion.sc, bf16[1024,1152]{1,0:T(8,128)(2,1)} %bitcast.298, bf16[1024,1152]{1,0:T(8,128)(2,1)} %bitcast.292, ...), custom_call_target="tpu_custom_call", output_to_operand_aliasing={{0}: (6, {}), {1}: (7, {})} | custom-call | flops 7247757312 | bytes 56721408 | tf_op jit(solution)/shard_map/pallas_call | solution.py:364
  168.6 15.6 %shard_map.243 = (bf16[2,2304,1024]{2,1,0:T(8,128)(2,1)}, bf16[2,2304,1024]{2,1,0:T(8,128)(2,1)}, bf16[16,96,1152]{2,1,0:T(8,128)(2,1)}, f32[8,768]{1,0:T(8,128)}) custom-call(s32[3]{0:T(128)} %pad_add_fusion.sc, bf16[1024,1152]{1,0:T(8,128)(2,1)} %bitcast.299, bf16[1024,1152]{1,0:T(8,128)(2,1)} %bitcast.293, ...), custom_call_target="tpu_custom_call", output_to_operand_aliasing={{0}: (6, {}), {1}: (7, {})} | custom-call | flops 7247757312 | bytes 56721408 | tf_op jit(solution)/shard_map/pallas_call | solution.py:364
  190.0 15.7 %shard_map.244 = (bf16[2,2304,1024]{2,1,0:T(8,128)(2,1)}, bf16[2,2304,1024]{2,1,0:T(8,128)(2,1)}, bf16[16,96,1152]{2,1,0:T(8,128)(2,1)}, f32[8,768]{1,0:T(8,128)}) custom-call(s32[3]{0:T(128)} %pad_add_fusion.sc, bf16[1024,1152]{1,0:T(8,128)(2,1)} %bitcast.300, bf16[1024,1152]{1,0:T(8,128)(2,1)} %bitcast.294, ...), custom_call_target="tpu_custom_call", output_to_operand_aliasing={{0}: (6, {}), {1}: (7, {})} | custom-call | flops 7247757312 | bytes 56721408 | tf_op jit(solution)/shard_map/pallas_call | solution.py:364
  224.7 29.1 %shard_map.245 = (f32[4,256,1152]{2,1,0:T(8,128)}, bf16[4,256,1152]{2,1,0:T(8,128)(2,1)}, f32[4,4,1152]{2,1,0:T(4,128)}) custom-call(s32[3]{0:T(128)} %pad_add_fusion.sc, bf16[2,2304,1024]{2,1,0:T(8,128)(2,1)} %get-tuple-element.506.back, bf16[1152,2304]{1,0:T(8,128)(2,1)} %w_up0.1, bf16[1152,2304]{1,0:T(8,128)(2,1)} %collective-permute-done.2.w_up.w_up1, ...), custom_call_target="tpu_custom_call" | custom-call | flops 10871635968 | bytes 41582592 | tf_op jit(solution)/shard_map/pallas_call | solution.py:364
  269.3 20.3 %shard_map.246.refs_0_ = bf16[2,3456,256]{2,1,0:T(8,128)(2,1)} custom-call(s32[3]{0:T(128)} %pad_add_fusion.sc, bf16[4,256,1152]{2,1,0:T(8,128)(2,1)} %get-tuple-element.541.grad_attn.refs_4_, bf16[4,3456,256]{2,1,0:T(8,128)(2,1)} %get-tuple-element.542.qkv, bf16[4,16,256,256]{3,2,1,0:T(8,128)(2,1)} %get-tuple-element.543.prob, bf16[576,1152]{1,0:T(8,128)(2,1)} %refs_0_.3, ...), custom_call_target="tpu_custom_call" | custom-call | flops 2868903936 | bytes 24018944 | tf_op jit(solution)/shard_map/pallas_call | solution.py:364
  301.6 20.1 %shard_map.247.refs_1_ = bf16[2,3456,256]{2,1,0:T(8,128)(2,1)} custom-call(s32[3]{0:T(128)} %pad_add_fusion.sc, bf16[4,256,1152]{2,1,0:T(8,128)(2,1)} %get-tuple-element.541.grad_attn.refs_4_, bf16[4,3456,256]{2,1,0:T(8,128)(2,1)} %get-tuple-element.542.qkv, bf16[4,16,256,256]{3,2,1,0:T(8,128)(2,1)} %get-tuple-element.543.prob, bf16[576,1152]{1,0:T(8,128)(2,1)} %refs_0_.3, ...), custom_call_target="tpu_custom_call" | custom-call | flops 2868903936 | bytes 24018944 | tf_op jit(solution)/shard_map/pallas_call | solution.py:364
  331.5 14.3 %shard_map.248 = (bf16[16,144,1152]{2,1,0:T(8,128)(2,1)}, f32[3,8,576]{2,1,0:T(8,128)}) custom-call(s32[3]{0:T(128)} %pad_add_fusion.sc, bf16[2,3456,256]{2,1,0:T(8,128)(2,1)} %shard_map.246.refs_0_, bf16[2,3456,256]{2,1,0:T(8,128)(2,1)} %shard_map.247.refs_1_, bf16[4,1152,256]{2,1,0:T(8,128)(2,1)} %get-tuple-element.602.refs_2_, ...), custom_call_target="tpu_custom_call" | custom-call | flops 5435817984 | bytes 19519488 | tf_op jit(solution)/shard_map/pallas_call | solution.py:364
  378.4 13.9 %shard_map.249 = (bf16[16,144,1152]{2,1,0:T(8,128)(2,1)}, f32[3,8,576]{2,1,0:T(8,128)}) custom-call(s32[3]{0:T(128)} %pad_add_fusion.sc, bf16[2,3456,256]{2,1,0:T(8,128)(2,1)} %shard_map.246.refs_0_, bf16[2,3456,256]{2,1,0:T(8,128)(2,1)} %shard_map.247.refs_1_, bf16[4,1152,256]{2,1,0:T(8,128)(2,1)} %get-tuple-element.602.refs_2_, ...), custom_call_target="tpu_custom_call" | custom-call | flops 5435817984 | bytes 19519488 | tf_op jit(solution)/shard_map/pallas_call | solution.py:364
  428.2 24.6 %shard_map.250 = (f32[4,256,1152]{2,1,0:T(8,128)}, f32[4,2,1152]{2,1,0:T(2,128)}) custom-call(s32[3]{0:T(128)} %pad_add_fusion.sc, bf16[2,3456,256]{2,1,0:T(8,128)(2,1)} %shard_map.246.refs_0_, bf16[2,3456,256]{2,1,0:T(8,128)(2,1)} %shard_map.247.refs_1_, bf16[1728,1152]{1,0:T(8,128)(2,1)} %bitcast.377, ...), custom_call_target="tpu_custom_call" | custom-call | flops 8153726976 | bytes 29454336 | tf_op jit(solution)/shard_map/pallas_call | solution.py:364
  470.1 23.4 %shard_map.251 = (bf16[4,256,1152]{2,1,0:T(8,128)(2,1)}, f32[4,1,1152]{2,1,0:T(1,128)}) custom-call(s32[3]{0:T(128)} %pad_add_fusion.sc, bf16[2,2304,1024]{2,1,0:T(8,128)(2,1)} %get-tuple-element.693.act, bf16[2304,1152]{1,0:T(8,128)(2,1)} %w_down0.1, bf16[2304,1152]{1,0:T(8,128)(2,1)} %collective-permute-done.3.w_down.w_down1, ...), custom_call_target="tpu_custom_call" | custom-call | flops 10871635968 | bytes 32094720 | tf_op jit(solution)/shard_map/pallas_call | solution.py:364
  513.2 15.2 %collective-permute-done.56 = bf16[2,2,144,256]{3,2,0,1:T(8,128)(2,1)S(1)} collective-permute-done((bf16[2,2,144,256]{3,2,0,1:T(8,128)(2,1)}, bf16[2,2,144,256]{3,2,0,1:T(8,128)(2,1)S(1)}, u32[]{:S(2)}, u32[]{:S(2)}) %collective-permute-start.56) | collective-permute-done | bytes 294944 | tf_op jit(solution)/shard_map/ppermute | solution.py:483
  533.0 11.1 %collective-permute-done.58 = bf16[2,2,2,96,512]{4,3,2,1,0:T(8,128)(2,1)S(1)} collective-permute-done((bf16[2,2,2,96,512]{4,3,2,1,0:T(8,128)(2,1)S(1)}, bf16[2,2,2,96,512]{4,3,2,1,0:T(8,128)(2,1)S(1)}, u32[]{:S(2)}, u32[]{:S(2)}) %collective-permute-start.58) | collective-permute-done | bytes 786464 | tf_op jit(solution)/shard_map/ppermute | solution.py:483
  548.3 9.4 %collective-permute-done.60 = bf16[2,2,96,512]{3,2,1,0:T(8,128)(2,1)S(1)} collective-permute-done((bf16[2,2,96,512]{3,2,1,0:T(8,128)(2,1)}, bf16[2,2,96,512]{3,2,1,0:T(8,128)(2,1)S(1)}, u32[]{:S(2)}, u32[]{:S(2)}) %collective-permute-start.60) | collective-permute-done | bytes 393248 | tf_op jit(solution)/shard_map/ppermute | solution.py:483
  569.2 11.0 %collective-permute-done.65 = bf16[2,2,2,96,512]{4,3,2,1,0:T(8,128)(2,1)S(1)} collective-permute-done((bf16[2,2,2,96,512]{4,3,2,1,0:T(8,128)(2,1)S(1)}, bf16[2,2,2,96,512]{4,3,2,1,0:T(8,128)(2,1)S(1)}, u32[]{:S(2)}, u32[]{:S(2)}) %collective-permute-start.65) | collective-permute-done | bytes 786464 | tf_op jit(solution)/shard_map/ppermute | solution.py:483
  593.0 6.3 collective-permute-done.70
  606.7 6.4 collective-permute-done.73
  628.1 6.1 shard_map.255
  646.3 9.3 %fusion.10 = f32[1152,3456]{1,0:T(8,128)} fusion(bf16[128,1152]{1,0:T(8,128)(2,1)S(1)} %reshape.502, bf16[16,13,3456]{2,1,0:T(8,128)(2,1)} %all-gather.14.cloned.1.call-done), kind=kOutput, calls=%fused_computation.28 | convolution fusion | flops 1019215872 | bytes 17104896 | tf_op jit(solution)/shard_map/dot_general | solution.py:895
  663.7 8.5 %shard_map.252 = (f32[1728,1152]{1,0:T(8,128)}, f32[576,1152]{1,0:T(8,128)}) custom-call(s32[3]{0:T(128)} %pad_add_fusion.sc, bf16[8,144,512]{2,1,0:T(8,128)(2,1)} %bitcast.304, bf16[8,144,512]{2,1,0:T(8,128)(2,1)} %bitcast.161.refs_1_, bf16[8,144,384]{2,1,0:T(8,128)(2,1)} %bitcast.316, bf16[8,144,384]{2,1,0:T(8,128)(2,1)} %bitcast.339, ...), custom_call_target="tpu_custom_call" | custom-call | flops 663552 | bytes 15925248 | tf_op jit(solution)/shard_map/pallas_call | solution.py:364
  (433 shorter events, 298.1 us)
Async XLA Ops:
  7.2 631.0 %all-gather.14.cloned.1.call-start = ((), (), s32[]{:S(2)}) async-start(), calls=%async_computation.2 | async-start | bytes 1880064 | tf_op jit(solution)/shard_map/all_gather | solution.py:804
  7.2 71.3 %collective-permute-start.2 = (bf16[1152,2304]{1,0:T(8,128)(2,1)}, bf16[1152,2304]{1,0:T(8,128)(2,1)}, u32[]{:S(2)}, u32[]{:S(2)}) collective-permute-start(bf16[1152,2304]{1,0:T(8,128)(2,1)} %w_up0.1), channel_id=1, source_target_pairs={{0,1},{1,0},{2,3},{3,2},{4,5},{5,4},{6,7},{7,6},{8,9},{9,8},{10,11... | collective-permute-start | bytes 15925256 | tf_op jit(solution)/shard_map/ppermute | solution.py:393
  7.7 70.8 %collective-permute-start.3 = (bf16[2304,1152]{1,0:T(8,128)(2,1)}, bf16[2304,1152]{1,0:T(8,128)(2,1)}, u32[]{:S(2)}, u32[]{:S(2)}) collective-permute-start(bf16[2304,1152]{1,0:T(8,128)(2,1)} %w_down0.1), channel_id=1, source_target_pairs={{0,1},{1,0},{2,3},{3,2},{4,5},{5,4},{6,7},{7,6},{8,9},{9,8},{10,11... | collective-permute-start | bytes 15925256 | tf_op jit(solution)/shard_map/ppermute | solution.py:393
  133.1 30.5 %collective-permute-start.7 = (bf16[16,96,1152]{2,1,0:T(8,128)(2,1)}, bf16[16,96,1152]{2,1,0:T(8,128)(2,1)}, u32[]{:S(2)}, u32[]{:S(2)}) collective-permute-start(bf16[16,96,1152]{2,1,0:T(8,128)(2,1)} %get-tuple-element.455), channel_id=1, source_target_pairs={{0,1},{1,0},{2,3},{3,2},{4,5},{5,4},{6,7},{7,6},{8,9},{9,8},{10,11... | collective-permute-start | bytes 10616840 | tf_op jit(solution)/shard_map/ppermute | solution.py:393
  187.0 30.6 %collective-permute-start.14 = (bf16[16,96,1152]{2,1,0:T(8,128)(2,1)}, bf16[16,96,1152]{2,1,0:T(8,128)(2,1)}, u32[]{:S(2)}, u32[]{:S(2)}) collective-permute-start(bf16[16,96,1152]{2,1,0:T(8,128)(2,1)} %get-tuple-element.501), channel_id=1, source_target_pairs={{0,1},{1,0},{2,3},{3,2},{4,5},{5,4},{6,7},{7,6},{8,9},{9,8},{10,11... | collective-permute-start | bytes 10616840 | tf_op jit(solution)/shard_map/ppermute | solution.py:393
  209.9 43.9 %collective-permute-start.15 = (bf16[96,640]{1,0:T(8,128)(2,1)}, bf16[96,640]{1,0:T(8,128)(2,1)}, u32[]{:S(2)}, u32[]{:S(2)}) collective-permute-start(bf16[96,640]{1,0:T(8,128)(2,1)} %get-tuple-element.513), channel_id=1, source_target_pairs={{0,16},{2,18},{4,20},{6,22},{8,24},{10,26},{12,28},{14,30},{16,0},... | collective-permute-start | bytes 368648 | tf_op jit(solution)/shard_map/ppermute | solution.py:483
  215.6 41.4 %collective-permute-start.18 = (bf16[2,2,96,512]{3,2,0,1:T(8,128)(2,1)}, bf16[2,2,96,512]{3,2,0,1:T(8,128)(2,1)}, u32[]{:S(2)}, u32[]{:S(2)}) collective-permute-start(bf16[2,2,96,512]{3,2,0,1:T(8,128)(2,1)} %get-tuple-element.524), channel_id=1, source_target_pairs={{0,2},{2,0},{4,6},{6,4},{8,10},{10,8},{12,14},{14,12},{16,18},{18,... | collective-permute-start | bytes 1179656 | tf_op jit(solution)/shard_map/ppermute | solution.py:483
  215.9 41.1 %collective-permute-start.17 = (bf16[2,2,96,640]{3,2,0,1:T(8,128)(2,1)}, bf16[2,2,96,640]{3,2,0,1:T(8,128)(2,1)S(1)}, u32[]{:S(2)}, u32[]{:S(2)}) collective-permute-start(bf16[2,2,96,640]{3,2,0,1:T(8,128)(2,1)} %get-tuple-element.523), channel_id=1, source_target_pairs={{0,4},{2,6},{4,0},{6,2},{8,12},{10,14},{12,8},{14,10},{16,20},{18,... | collective-permute-start | bytes 1474568 | tf_op jit(solution)/shard_map/ppermute | solution.py:483
  222.6 42.3 %collective-permute-start.20 = (bf16[2,2,2,96,512]{4,3,0,1,2:T(8,128)(2,1)}, bf16[2,2,2,96,512]{4,3,0,1,2:T(8,128)(2,1)}, u32[]{:S(2)}, u32[]{:S(2)}) collective-permute-start(bf16[2,2,2,96,512]{4,3,0,1,2:T(8,128)(2,1)} %fusion.13), channel_id=1, source_target_pairs={{0,4},{2,6},{4,0},{6,2},{8,12},{10,14},{12,8},{14,10},{16,20},{18,... | collective-permute-start | bytes 2359304 | tf_op jit(solution)/shard_map/ppermute | solution.py:483
  222.9 42.4 %collective-permute-start.19 = (bf16[2,2,2,96,640]{4,3,0,1,2:T(8,128)(2,1)S(1)}, bf16[2,2,2,96,640]{4,3,0,1,2:T(8,128)(2,1)}, u32[]{:S(2)}, u32[]{:S(2)}) collective-permute-start(bf16[2,2,2,96,640]{4,3,0,1,2:T(8,128)(2,1)S(1)} %fusion.3), channel_id=1, source_target_pairs={{0,2},{2,0},{4,6},{6,4},{8,10},{10,8},{12,14},{14,12},{16,18},{18,... | collective-permute-start | bytes 2949128 | tf_op jit(solution)/shard_map/ppermute | solution.py:483
  257.0 32.6 %collective-permute-start.22 = (bf16[96,512]{1,0:T(8,128)(2,1)}, bf16[96,512]{1,0:T(8,128)(2,1)}, u32[]{:S(2)}, u32[]{:S(2)}) collective-permute-start(bf16[96,512]{1,0:T(8,128)(2,1)} %add.581), channel_id=1, source_target_pairs={{0,16},{2,18},{4,20},{6,22},{8,24},{10,26},{12,28},{14,30},{16,0},... | collective-permute-start | bytes 294920 | tf_op jit(solution)/shard_map/ppermute | solution.py:483
  259.7 31.5 %collective-permute-start.21 = (bf16[96,640]{1,0:T(8,128)(2,1)}, bf16[96,640]{1,0:T(8,128)(2,1)}, u32[]{:S(2)}, u32[]{:S(2)}) collective-permute-start(bf16[96,640]{1,0:T(8,128)(2,1)} %add.580), channel_id=1, source_target_pairs={{0,16},{2,18},{4,20},{6,22},{8,24},{10,26},{12,28},{14,30},{16,0},... | collective-permute-start | bytes 368648 | tf_op jit(solution)/shard_map/ppermute | solution.py:483
  263.2 29.8 %collective-permute-start.24 = (bf16[2,96,512]{2,1,0:T(8,128)(2,1)}, bf16[2,96,512]{2,1,0:T(8,128)(2,1)}, u32[]{:S(2)}, u32[]{:S(2)}) collective-permute-start(bf16[2,96,512]{2,1,0:T(8,128)(2,1)} %get-tuple-element.556), channel_id=1, source_target_pairs={{0,8},{2,10},{4,12},{6,14},{8,0},{10,2},{12,4},{14,6},{16,24},{18,... | collective-permute-start | bytes 589832 | tf_op jit(solution)/shard_map/ppermute | solution.py:483
  268.6 31.1 %collective-permute-start.26 = (bf16[2,2,96,512]{3,2,0,1:T(8,128)(2,1)}, bf16[2,2,96,512]{3,2,0,1:T(8,128)(2,1)S(1)}, u32[]{:S(2)}, u32[]{:S(2)}) collective-permute-start(bf16[2,2,96,512]{3,2,0,1:T(8,128)(2,1)} %get-tuple-element.566), channel_id=1, source_target_pairs={{0,2},{2,0},{4,6},{6,4},{8,10},{10,8},{12,14},{14,12},{16,18},{18,... | collective-permute-start | bytes 1179656 | tf_op jit(solution)/shard_map/ppermute | solution.py:483
  345.7 52.7 %collective-permute-start.39 = (bf16[16,144,1152]{2,1,0:T(8,128)(2,1)}, bf16[16,144,1152]{2,1,0:T(8,128)(2,1)}, u32[]{:S(2)}, u32[]{:S(2)}) collective-permute-start(bf16[16,144,1152]{2,1,0:T(8,128)(2,1)} %get-tuple-element.636), channel_id=1, source_target_pairs={{0,1},{1,0},{2,3},{3,2},{4,5},{5,4},{6,7},{7,6},{8,9},{9,8},{10,11... | collective-permute-start | bytes 15925256 | tf_op jit(solution)/shard_map/ppermute | solution.py:393
  421.1 37.4 %collective-permute-start.46 = (bf16[2,2,2,144,512]{4,3,0,1,2:T(8,128)(2,1)}, bf16[2,2,2,144,512]{4,3,0,1,2:T(8,128)(2,1)}, u32[]{:S(2)}, u32[]{:S(2)}) collective-permute-start(bf16[2,2,2,144,512]{4,3,0,1,2:T(8,128)(2,1)} %fusion.1), channel_id=1, source_target_pairs={{0,2},{2,0},{4,6},{6,4},{8,10},{10,8},{12,14},{14,12},{16,18},{18,... | collective-permute-start | bytes 3538952 | tf_op jit(solution)/shard_map/ppermute | solution.py:483
  423.4 34.1 %collective-permute-start.47 = (bf16[2,2,2,144,384]{4,3,0,1,2:T(8,128)(2,1)}, bf16[2,2,2,144,384]{4,3,0,1,2:T(8,128)(2,1)}, u32[]{:S(2)}, u32[]{:S(2)}) collective-permute-start(bf16[2,2,2,144,384]{4,3,0,1,2:T(8,128)(2,1)} %fusion.9), channel_id=1, source_target_pairs={{0,4},{2,6},{4,0},{6,2},{8,12},{10,14},{12,8},{14,10},{16,20},{18,... | collective-permute-start | bytes 2654216 | tf_op jit(solution)/shard_map/ppermute | solution.py:483
  426.6 29.7 %collective-permute-start.48 = (bf16[2,2,2,144,256]{4,3,1,2,0:T(8,128)(2,1)}, bf16[2,2,2,144,256]{4,3,1,2,0:T(8,128)(2,1)S(1)}, u32[]{:S(2)}, u32[]{:S(2)}) collective-permute-start(bf16[2,2,2,144,256]{4,3,1,2,0:T(8,128)(2,1)} %fusion.20), channel_id=1, source_target_pairs={{0,8},{2,10},{4,12},{6,14},{8,0},{10,2},{12,4},{14,6},{16,24},{18,... | collective-permute-start | bytes 1769480 | tf_op jit(solution)/shard_map/ppermute | solution.py:483
  507.0 165.2 %all-gather.10.cloned.1.call-start = ((), (), s32[]{:S(2)}) async-start(), calls=%async_computation | async-start | bytes 7077888 | tf_op jit(solution)/shard_map/all_gather | solution.py:775
  507.7 164.5 %all-gather.12.cloned.1.call-start = ((), (), s32[]{:S(2)}) async-start(), calls=%async_computation.1 | async-start | bytes 14155776 | tf_op jit(solution)/shard_map/all_gather | solution.py:776
  511.5 36.1 %collective-permute-start.57 = (bf16[2,2,2,96,640]{4,3,2,1,0:T(8,128)(2,1)S(1)}, bf16[2,2,2,96,640]{4,3,2,1,0:T(8,128)(2,1)S(1)}, u32[]{:S(2)}, u32[]{:S(2)}) collective-permute-start(bf16[2,2,2,96,640]{4,3,2,1,0:T(8,128)(2,1)S(1)} %pad_maximum_fusion.2), channel_id=1, source_target_pairs={{0,2},{2,0},{4,6},{6,4},{8,10},{10,8},{12,14},{14,12},{16,18},{18,... | collective-permute-start | bytes 2949128 | tf_op jit(solution)/shard_map/ppermute | solution.py:483
  512.0 32.1 %collective-permute-start.58 = (bf16[2,2,2,96,512]{4,3,2,1,0:T(8,128)(2,1)S(1)}, bf16[2,2,2,96,512]{4,3,2,1,0:T(8,128)(2,1)S(1)}, u32[]{:S(2)}, u32[]{:S(2)}) collective-permute-start(bf16[2,2,2,96,512]{4,3,2,1,0:T(8,128)(2,1)S(1)} %pad_maximum_fusion.6), channel_id=1, source_target_pairs={{0,4},{2,6},{4,0},{6,2},{8,12},{10,14},{12,8},{14,10},{16,20},{18,... | collective-permute-start | bytes 2359304 | tf_op jit(solution)/shard_map/ppermute | solution.py:483
  528.4 29.3 %collective-permute-start.60 = (bf16[2,2,96,512]{3,2,1,0:T(8,128)(2,1)}, bf16[2,2,96,512]{3,2,1,0:T(8,128)(2,1)S(1)}, u32[]{:S(2)}, u32[]{:S(2)}) collective-permute-start(bf16[2,2,96,512]{3,2,1,0:T(8,128)(2,1)} %pad_maximum_fusion.16), channel_id=1, source_target_pairs={{0,2},{2,0},{4,6},{6,4},{8,10},{10,8},{12,14},{14,12},{16,18},{18,... | collective-permute-start | bytes 1179656 | tf_op jit(solution)/shard_map/ppermute | solution.py:483
  532.1 32.0 %collective-permute-start.63 = (bf16[2,144,256]{2,1,0:T(8,128)(2,1)S(1)}, bf16[2,144,256]{2,1,0:T(8,128)(2,1)S(1)}, u32[]{:S(2)}, u32[]{:S(2)}) collective-permute-start(bf16[2,144,256]{2,1,0:T(8,128)(2,1)S(1)} %get-tuple-element.728), channel_id=1, source_target_pairs={{0,2},{2,0},{4,6},{6,4},{8,10},{10,8},{12,14},{14,12},{16,18},{18,... | collective-permute-start | bytes 442376 | tf_op jit(solution)/shard_map/ppermute | solution.py:483
  (107 other events, 1968.3 us)
Sparse Core Ops, SparseCore 0:
  507.1 70.4 all-gather.13
  579.2 12.4 all-gather.9
  593.9 23.0 all-gather.11

commit v2 on v1

--- a/solution.py
+++ b/solution.py
@@ -41,27 +41,24 @@
     return recip * (scaled_grad - mean_grad - unit * mean_unit)
 
 
-def column(rows):
-    return rows[...].T[:, 0:1]
+def column(row):
+    return jnp.broadcast_to(row[...].astype(f32), (8, row.shape[1])).T[:, 0:1]
 
 
 def token_sum(values):
     return jnp.sum(values, axis=0, keepdims=True)
 
 
-def entry_kernel(own_images, sc, tok, cot, mod, normed, grad_mlp, sums):
+def attention_kernel(parts, own_images, sc, tok, cot, mod, b_proj, *refs):
+    w_qkv, w_proj, bias = refs[:parts], refs[parts : 2 * parts], refs[2 * parts : 3 * parts]
+    qkv, prob, mixed, attn_out, residual, normed_mlp, normed, grad_mlp, down_sums = refs[3 * parts :]
     image = sc[0] * own_images + pl.program_id(0)
     live = jnp.where(image < sc[1], 1.0, 0.0).astype(f32)
     unit, _ = normalize(tok[0].astype(f32))
     normed[0] = (unit * (1.0 + mod[0, 1:2, :]) + mod[0, 0:1, :]).astype(bf16)
     grad = (mod[0, 5:6, :] * (cot[0].astype(f32) * live)).astype(bf16)
     grad_mlp[0] = grad
-    sums[0] = token_sum(grad.astype(f32))
-
-
-def attention_kernel(parts, sc, tok, normed, mod, b_proj, *refs):
-    w_qkv, w_proj, bias = refs[:parts], refs[parts : 2 * parts], refs[2 * parts : 3 * parts]
-    qkv, prob, mixed, attn_out, residual, normed_mlp = refs[3 * parts :]
+    down_sums[0] = token_sum(grad.astype(f32))
     cols = w_proj[0].shape[0]
     pairs = cols // (2 * HEAD_DIM)
     span = 2 * HEAD_DIM
@@ -70,10 +67,12 @@
     total = b_proj[...]
     for part in range(parts):
         base = part * 3 * cols
-        shift = column(bias[part])
+        shift = bias[part][...].astype(f32).T
         for proj in range(3):
             lo = proj * cols
-            value = dot_nt(w_qkv[part][lo : lo + cols, :], rows) + shift[lo : lo + cols, :]
+            value = dot_nt(w_qkv[part][lo : lo + cols, :], rows)
+            if proj != 1:
+                value = value + shift[:, proj // 2 : proj // 2 + 1]
             qkv[0, base + lo : base + lo + cols, :] = value.astype(bf16)
 
         def pair_step(pair, carry, base=base, part=part):
@@ -103,8 +102,22 @@
     normed_mlp[0] = (unit * (1.0 + mod[0, 4:5, :]) + mod[0, 3:4, :]).astype(bf16)
 
 
-def mlp_kernel(per, sc, rows, grad_mlp, w_up, w_down, bias, act_in, back_in, act, back, grads, sums):
-    step = pl.program_id(0)
+def mlp_kernel(
+    per, steps, sc, rows, grad_mlp, w_up0, w_up1, w_down0, w_down1, bias0, bias1, act_in, back_in,
+    act, back, grad_own, grad_other, sums
+):
+    part, step = pl.program_id(0), pl.program_id(1)
+
+    @pl.when(part == 0)
+    def _():
+        mlp_block(per, step, sc, rows, grad_mlp, w_up0, w_down0, bias0, act, back, grad_own, sums)
+
+    @pl.when(part == 1)
+    def _():
+        mlp_block(per, step, sc, rows, grad_mlp, w_up1, w_down1, bias1, act, back, grad_other, sums)
+
+
+def mlp_block(per, step, sc, rows, grad_mlp, w_up, w_down, bias, act, back, grads, sums):
     here = w_down.shape[0] // per
     hidden = lax.dot_general(
         w_up[...], rows[...], (((0,), (1,)), ((), ())), preferred_element_type=f32
@@ -119,7 +132,7 @@
     back_b = (dot_nt(w_down[...], grad_mlp[...]) * slope).astype(bf16)
     act[0] = act_b
     back[0] = back_b
-    sums[...] = dot_nt(jnp.ones((8, rows.shape[0]), bf16), back_b)
+    sums[0] = dot_nt(jnp.ones((8, rows.shape[0]), bf16), back_b)
     grad_down = dot_nn(act_b, grad_mlp[...]).astype(bf16)
     grad_up = dot_nn(back_b, rows[...]).astype(bf16)
     for piece in range(here):
@@ -129,46 +142,46 @@
         grads[at, per : 2 * per, :] = grad_up[lo : lo + per]
 
 
+def grow(total, part_steps, left, rights, dims):
+    step = pl.program_id(0)
+
+    def term(right):
+        return lax.dot_general(left, right[...], (dims, ((), ())), preferred_element_type=f32)
+
+    @pl.when(step == 0)
+    def _():
+        total[...] = term(rights[0])
+
+    @pl.when(jnp.logical_and(step > 0, step < part_steps))
+    def _():
+        total[...] += term(rights[0])
+
+    @pl.when(jnp.logical_and(step >= part_steps, step < 2 * part_steps))
+    def _():
+        total[...] += term(rights[1])
+
+
 def norm_back_kernel(
-    images, own_images, sc, back, w_up0, w_up1, residual, cot, mod, attn_out,
+    part_steps, own_images, sc, back, w_up0, w_up1, residual, cot, mod, attn_out,
     grad_residual, grad_attn, sums, total
 ):
-    step, steps = pl.program_id(0), pl.num_programs(0)
+    grow(total, part_steps, back[0], (w_up0, w_up1), ((0,), (1,)))
+    one = pl.program_id(0) - 2 * part_steps
     seq = residual.shape[1]
 
-    def term(w_up):
-        return lax.dot_general(
-            back[0], w_up[...], (((0,), (1,)), ((), ())), preferred_element_type=f32
-        )
-
-    @pl.when(step == 0)
+    @pl.when(one >= 0)
     def _():
-        total[...] = term(w_up0)
-
-    @pl.when(jnp.logical_and(step > 0, step < steps // 2))
-    def _():
-        total[...] += term(w_up0)
-
-    @pl.when(step >= steps // 2)
-    def _():
-        total[...] += term(w_up1)
-
-    @pl.when(step == steps - 1)
-    def _():
-        for one in range(images):
-            live = jnp.where(sc[0] * own_images + one < sc[1], 1.0, 0.0).astype(f32)
-            grad_normed = total[one * seq : (one + 1) * seq, :]
-            unit, recip = normalize(residual[one])
-            sums[one, 0:1, :] = token_sum(grad_normed)
-            sums[one, 1:2, :] = token_sum(grad_normed * unit)
-            grad_res = cot[one].astype(f32) * live + norm_pullback(
-                grad_normed, unit, recip, mod[one, 4:5, :]
-            )
-            grad_residual[one] = grad_res
-            sums[one, 2:3, :] = token_sum(grad_res * attn_out[one])
-            grad_att = (mod[one, 2:3, :] * grad_res).astype(bf16)
-            grad_attn[one] = grad_att
-            sums[one, 3:4, :] = token_sum(grad_att.astype(f32))
+        live = jnp.where(sc[0] * own_images + one < sc[1], 1.0, 0.0).astype(f32)
+        grad_normed = total[pl.ds(pl.multiple_of(one * seq, seq), seq), :]
+        unit, recip = normalize(residual[0])
+        sums[0, 0:1, :] = token_sum(grad_normed)
+        sums[0, 1:2, :] = token_sum(grad_normed * unit)
+        grad_res = cot[0].astype(f32) * live + norm_pullback(grad_normed, unit, recip, mod[0, 4:5, :])
+        grad_residual[0] = grad_res
+        sums[0, 2:3, :] = token_sum(grad_res * attn_out[0])
+        grad_att = (mod[0, 2:3, :] * grad_res).astype(bf16)
+        grad_attn[0] = grad_att
+        sums[0, 3:4, :] = token_sum(grad_att.astype(f32))
 
 
 def back_kernel(parts, sc, grad_attn, qkv, prob, *refs):
@@ -246,65 +259,57 @@
 def first_back_kernel(pieces, images, sc, *refs):
     grad_qkv = refs[:pieces]
     w_qkv0, w_qkv1, tok, mod, grad_residual = refs[pieces : pieces + 5]
-    grad_tokens, sums = refs[pieces + 5 :]
-    step, steps = pl.program_id(0), pl.num_programs(0)
+    grad_tokens, grad_own, sums, total = refs[pieces + 5 :]
+    step = pl.program_id(0)
     each = images // pieces
+    seq = tok.shape[1]
 
     def add(w_qkv, fresh):
         for one in range(images):
             term = dot_tn(grad_qkv[one // each][one % each], w_qkv[...])
             if fresh:
-                grad_tokens[one] = term
+                total[one * seq : (one + 1) * seq, :] = term
             else:
-                grad_tokens[one] += term
+                total[one * seq : (one + 1) * seq, :] += term
 
     @pl.when(step == 0)
     def _():
         add(w_qkv0, True)
 
-    @pl.when(jnp.logical_and(step > 0, step < steps // 2))
+    @pl.when(jnp.logical_and(step > 0, step < 3))
     def _():
         add(w_qkv0, False)
 
-    @pl.when(step >= steps // 2)
+    @pl.when(jnp.logical_and(step >= 3, step < 6))
     def _():
         add(w_qkv1, False)
 
-    @pl.when(step == steps - 1)
+    @pl.when(step >= 6)
     def _():
-        for one in range(images):
-            grad_normed = grad_tokens[one]
-            unit, recip = normalize(tok[one].astype(f32))
-            sums[one, 0:1, :] = token_sum(grad_normed)
-            sums[one, 1:2, :] = token_sum(grad_normed * unit)
-            grad_tokens[one] = grad_residual[one] + norm_pullback(
-                grad_normed, unit, recip, mod[one, 1:2, :]
-            )
-
-
-def output_kernel(images, own_images, sc, act, w_down0, w_down1, residual, cot, mod, b_down, output, sums, total):
-    step, steps = pl.program_id(0), pl.num_programs(0)
+        grad_normed = total[pl.ds(pl.multiple_of((step - 6) * seq, seq), seq), :]
+        unit, recip = normalize(tok[0].astype(f32))
+        sums[0, 0:1, :] = token_sum(grad_normed)
+        sums[0, 1:2, :] = token_sum(grad_normed * unit)
+        grad = grad_residual[0] + norm_pullback(grad_normed, unit, recip, mod[0, 1:2, :])
+        grad_tokens[0] = grad
+        grad_own[0] = grad
+
+
+def output_kernel(
+    part_steps, own_images, sc, act, w_down0, w_down1, residual, cot, mod, b_down, output, own, sums, total
+):
+    grow(total, part_steps, act[0], (w_down0, w_down1), ((0,), (0,)))
+    one = pl.program_id(0) - 2 * part_steps
     seq = residual.shape[1]
 
-    @pl.when(step == 0)
+    @pl.when(one >= 0)
     def _():
-        total[...] = dot_tn(act[0], w_down0[...])
-
-    @pl.when(jnp.logical_and(step > 0, step < steps // 2))
-    def _():
-        total[...] += dot_tn(act[0], w_down0[...])
-
-    @pl.when(step >= steps // 2)
-    def _():
-        total[...] += dot_tn(act[0], w_down1[...])
-
-    @pl.when(step == steps - 1)
-    def _():
-        for one in range(images):
-            live = jnp.where(sc[0] * own_images + one < sc[1], 1.0, 0.0).astype(f32)
-            mlp_out = total[one * seq : (one + 1) * seq, :] + b_down[...]
-            sums[one] = token_sum((cot[one].astype(f32) * live) * mlp_out)
-            output[one] = ((residual[one] + mod[one, 5:6, :] * mlp_out) * live).astype(bf16)
+        live = jnp.where(sc[0] * own_images + one < sc[1], 1.0, 0.0).astype(f32)
+        mlp_out = total[pl.ds(pl.multiple_of(one * seq, seq), seq), :] + b_down[...]
+        sums[0] = token_sum((cot[0].astype(f32) * live) * mlp_out)
+        rows = ((residual[0] + mod[0, 5:6, :] * mlp_out) * live).astype(bf16)
+        output[0] = rows
+        own[0] = rows
 
 
 def final_piece(sc, halves, piece, store):
@@ -324,7 +329,7 @@
 
 def final_mlp_kernel(cuts, per, sc, *refs):
     count = 2 * len(cuts)
-    arrays, (_, _, down, up, turned) = refs[:count], refs[count:]
+    arrays, (_, _, down, up, mark, turned) = refs[:count], refs[count:]
     here = down.shape[0] // per
     halves = [(arrays[2 * k], arrays[2 * k + 1]) + cut for k, cut in enumerate(cuts)]
     for piece in range(here):
@@ -335,6 +340,7 @@
 
         final_piece(sc, halves, pl.program_id(0) * here + piece, store)
     up[...] = turned[...].T
+    mark[...] = jnp.zeros_like(mark)
 
 
 def final_attn_kernel(cuts, per, sc, *refs):
@@ -354,10 +360,9 @@
                 final_piece(sc, halves, pl.program_id(0) * here + piece, store)
 
 
-VMEM_LIMIT = 60 << 20
-
-
-def run_kernel(body, sc, args, in_specs, out_specs, out_shape, grid, flops, scratch=(), alias=None):
+def run_kernel(
+    body, sc, args, in_specs, out_specs, out_shape, grid, micros, scratch=(), alias=None, room=60
+):
     size = sum(a.size * a.dtype.itemsize for a in args) + sum(
         s.size * s.dtype.itemsize for s in out_shape
     )
@@ -371,8 +376,10 @@
             out_specs=out_specs,
             scratch_shapes=list(scratch),
         ),
-        compiler_params=pltpu.CompilerParams(vmem_limit_bytes=VMEM_LIMIT),
-        cost_estimate=pl.CostEstimate(flops=int(flops), bytes_accessed=int(size), transcendentals=0),
+        compiler_params=pltpu.CompilerParams(vmem_limit_bytes=room << 20),
+        cost_estimate=pl.CostEstimate(
+            flops=int(micros * 1.15e9), bytes_accessed=int(size), transcendentals=0
+        ),
         input_output_aliases=alias or {},
     )(sc, *args)
 
@@ -412,82 +419,78 @@
     return out.reshape(out.shape[:place] + out.shape[place + 1 :])
 
 
-class Flow:
-    def __init__(self, ways, own, other):
-        self.ways = ways
-        self.shape = (2, 2, 2, 2) + other.shape[1:]
-        self.own, self.other = own, other
-        self.stage = 0
-        self.halves = None
-
-    def set_own(self, own):
-        self.own = own
-
-    def pending(self):
-        if self.stage == 0:
-            return [self.other]
-        if self.stage == 1:
-            return [self.own, self.came]
-        return [self.keeps, self.comes]
-
-    def step(self, fence):
-        if self.stage == 0:
-            (other,) = fence([self.other])
-            self.came = swap_cores(other)
-        elif self.stage <= 5:
-            first, second = fence(self.pending())
-            if self.stage == 1:
-                first = [first.reshape(self.shape)] * len(self.ways)
-                second = [second.reshape(self.shape)] * len(self.ways)
-            sends, keeps = [], []
-            for (lo, hi, order), one, two in zip(self.ways, first, second):
-                if self.stage == 5:
-                    keeps.append(one + two)
-                    sends.append(one + two)
-                    continue
-                bits = [bit for bit in (3, 2, 1, 0) if bit not in order[: self.stage - 1]]
-                bit = order[self.stage - 1]
-                cols = (lo, hi) if self.stage == 1 else None
-                sends.append(cut(one, bits, bit, 1, cols) + cut(two, bits, bit, 1, cols))
-                keeps.append(cut(one, bits, bit, 0, cols) + cut(two, bits, bit, 0, cols))
-            if self.stage == 5:
-                self.sets = [[] for _ in self.ways]
-                (keeps,) = fence([keeps])
-                self.send(keeps, keeps)
-            else:
-                sends, keeps = fence([sends, keeps])
-                self.send(sends, keeps)
-        else:
-            haves, comes = fence(self.pending())
-            joined = []
-            for (lo, hi, order), bits, have, got in zip(self.ways, self.sets, haves, comes):
-                bit = order[8 - self.stage + 1]
-                if self.stage == 9:
-                    continue
-                place = sum(1 for other in bits if other > bit)
-                joined.append(jnp.stack([have, got], axis=place))
-                bits.insert(place, bit)
-            if self.stage == 9:
-                self.halves = [
-                    part.reshape((8,) + part.shape[-2:]) for pair in zip(haves, comes) for part in pair
-                ]
-            else:
-                (joined,) = fence([joined])
-                self.send(joined, joined)
-        self.stage += 1
-
-    def send(self, sends, keeps):
-        self.keeps = keeps
-        which = self.stage - 1 if self.stage <= 4 else 8 - self.stage
-        self.comes = [
-            lax.ppermute(value, "dp", bit_pairs(order[which]))
-            for value, (_, _, order) in zip(sends, self.ways)
-        ]
+def left_bits(done):
+    return [bit for bit in (3, 2, 1, 0) if bit not in done]
+
+
+def exchange(values, bits):
+    return [lax.ppermute(value, "dp", bit_pairs(bit)) for value, bit in zip(values, bits)]
+
+
+def reduce_flow(ways, get_own, other):
+    shape = (2, 2, 2, 2) + other.shape[1:]
+    (other,) = yield [other]
+    came = swap_cores(other)
+    yield None
+    own, came = yield [get_own(), came]
+    firsts, seconds = [own.reshape(shape)] * len(ways), [came.reshape(shape)] * len(ways)
+    routes = [way for _, _, way in ways]
+    for stage in range(4):
+        sends, keeps = [], []
+        for (lo, hi, _), route, one, two in zip(ways, routes, firsts, seconds):
+            bits = left_bits(route[:stage])
+            cols = (lo, hi) if stage == 0 else None
+            for side, into in ((1, sends), (0, keeps)):
+                into.append(
+                    cut(one, bits, route[stage], side, cols) + cut(two, bits, route[stage], side, cols)
+                )
+        if stage == 2 and routes[0][2:] == routes[1][2:]:
+            sends = [jnp.concatenate(sends[:2], axis=-1)] + sends[2:]
+            keeps = [jnp.concatenate(keeps[:2], axis=-1)] + keeps[2:]
+            routes = [routes[0]] + routes[2:]
+            ways = [(0, 0, way) for way in routes]
+        sends, keeps = yield [sends, keeps]
+        comes = exchange(sends, [route[stage] for route in routes])
+        yield None
+        firsts, seconds = yield [keeps, comes]
+    return [one + two for one, two in zip(firsts, seconds)]
+
+
+def gather_flow(ways, have):
+    routes = [ways[0][2]] + [way for _, _, way in ways[2:]]
+    middle = ways[0][1]
+    known = [[] for _ in routes]
+    (have,) = yield [have]
+    comes = exchange(have, [route[3] for route in routes])
+    yield None
+    for stage in (2, 1, 0):
+        have, comes = yield [have, comes]
+        joined = []
+        for route, bits, one, two in zip(routes, known, have, comes):
+            bit = route[stage + 1]
+            place = sum(1 for other in bits if other > bit)
+            joined.append(jnp.stack([one, two], axis=place))
+            bits.insert(place, bit)
+        if stage == 1:
+            joined = [joined[0][..., :middle], joined[0][..., middle:]] + joined[1:]
+            routes = [way for _, _, way in ways]
+            known = [list(known[0]), list(known[0])] + known[1:]
+        (have,) = yield [joined]
+        comes = exchange(have, [route[stage] for route in routes])
+        yield None
+    have, comes = yield [have, comes]
+    return [part.reshape((8,) + part.shape[-2:]) for pair in zip(have, comes) for part in pair]
+
+
+def sum_flow(ways, get_own, other):
+    have = yield from reduce_flow(ways, get_own, other)
+    return (yield from gather_flow(ways, have))
 
 
 class Order:
     def __init__(self, sc):
         self.sc = sc
+        self.results = {}
 
     def fence(self, values):
         self.sc, values = lax.optimization_barrier((self.sc, values))
@@ -497,12 +500,31 @@
         self.sc, _ = lax.optimization_barrier((self.sc, value))
 
     def tick(self, *flows):
-        for flow in flows:
-            if flow.halves is None:
-                flow.step(self.fence)
+        replies = {flow: None for flow in flows if flow not in self.results}
+        while replies:
+            wants = {}
+            for flow, reply in replies.items():
+                try:
+                    want = flow.send(reply)
+                except StopIteration as stop:
+                    self.results[flow] = stop.value
+                    continue
+                if want is not None:
+                    wants[flow] = want
+            replies = dict(zip(wants, self.fence(list(wants.values())))) if wants else {}
+
+    def finish(self, flow):
+        while flow not in self.results:
+            self.tick(flow)
+        return self.results[flow]
 
 
 CHUNKS = 3
+
+
+def fill_other(both, came, core):
+    size = came.shape[0]
+    return lax.dynamic_update_slice_in_dim(both, came, (1 - core) * size, 0)
 
 
 def fast_device(
@@ -522,67 +544,56 @@
     qkv_rows = jnp.transpose(w_qkv, (1, 2, 0)).reshape(3 * cols, dim)
     wq = [qkv_rows, swap_cores(qkv_rows)]
     wp = [w_proj, swap_cores(w_proj)]
-    wu = [w_up, swap_cores(w_up)]
-    wd = [w_down, swap_cores(w_down)]
+    qkv_bias = [b_qv, swap_cores(b_qv)]
 
     cond_f = condition.astype(f32)
     scaled = jax.nn.silu(cond_f).astype(bf16)
     own_mod = jnp.dot(scaled, w_mod, preferred_element_type=f32) + b_mod.astype(f32)
-    own_bias = jnp.concatenate([b_qv.reshape(-1), b_up]).astype(f32)[None]
-    gathered = lax.all_gather(jnp.concatenate([own_mod, own_bias]), "mp", axis=0, tiled=False)
-    modulation = jnp.concatenate([gathered[0, :slots], gathered[1, :slots]], axis=1).reshape(slots, 6, dim)
-    zero_bias = jnp.zeros((cols,), f32)
-    qkv_bias, up_bias = [], []
-    for part in range(2):
-        row = lax.dynamic_index_in_dim(gathered[:, slots], core ^ part, 0, keepdims=False)
-        qkv_row = jnp.concatenate([row[:cols], zero_bias, row[cols : 2 * cols]])
-        qkv_bias.append(jnp.broadcast_to(qkv_row, (8, 3 * cols)))
-        up_bias.append(jnp.broadcast_to(row[2 * cols :], (8, ff)))
+    other_mod = swap_cores(own_mod)
+    sides = [jnp.where(core == side, own_mod, other_mod) for side in range(2)]
+    modulation = jnp.concatenate(sides, axis=1).reshape(slots, 6, dim)
     proj_bias = b_proj.astype(f32)[None]
     down_bias = b_down.astype(f32)[None]
+
+    late_up, late_down, late_bias = lax.optimization_barrier((wq[1], w_up, w_down, b_up, modulation))[1:4]
+    wu = [w_up, swap_cores(late_up)]
+    wd = [w_down, swap_cores(late_down)]
+    up_bias = [b_up[None], swap_cores(late_bias[None])]
 
     local = lambda i, s: (s[0] * images + i, 0, 0)
     mine = lambda i, s: (i, 0, 0)
     tok_spec = pl.BlockSpec((1, seq, dim), local)
     own_spec = pl.BlockSpec((1, seq, dim), mine)
     mod_spec = pl.BlockSpec((1, 6, dim), local)
-    group = lambda i, s: (s[0], 0, 0)
-    once = pl.Buffered(1)
-    all_tok_spec = pl.BlockSpec((images, seq, dim), group, pipeline_mode=once)
-    all_mod_spec = pl.BlockSpec((images, 6, dim), group, pipeline_mode=once)
-
-    normed, grad_mlp, down_sums = run_kernel(
-        functools.partial(entry_kernel, images),
-        order.sc,
-        [tokens, cotangent, modulation],
-        [tok_spec, tok_spec, mod_spec],
-        [own_spec, own_spec, pl.BlockSpec((1, 1, dim), mine)],
-        [shape_of((images, seq, dim), bf16)] * 2 + [shape_of((images, 1, dim), f32)],
-        (images,),
-        count * dim * 20,
-    )
-    order.after(down_sums)
+    row_spec = pl.BlockSpec((1, 1, dim), mine)
     qkv_spec = pl.BlockSpec((1, 6 * cols, seq), mine)
     prob_spec = pl.BlockSpec((1, 2 * heads, seq, seq), lambda i, s: (i, 0, 0, 0))
     mixed_spec = pl.BlockSpec((1, 2 * cols, seq), mine)
+    token_f = shape_of((images, seq, dim), f32)
+    token_b = shape_of((images, seq, dim), bf16)
     attn_args = wq + wp + qkv_bias
-    qkv, prob, mixed, attn_out, residual, normed_mlp = run_kernel(
-        functools.partial(attention_kernel, 2),
+    qkv, prob, mixed, attn_out, residual, normed_mlp, normed, grad_mlp, down_sums = run_kernel(
+        functools.partial(attention_kernel, 2, images),
         order.sc,
-        [tokens, normed, modulation, proj_bias] + attn_args,
-        [tok_spec, own_spec, mod_spec, whole_block(proj_bias)] + [whole_block(a) for a in attn_args],
-        [qkv_spec, prob_spec, mixed_spec, own_spec, own_spec, own_spec],
+        [tokens, cotangent, modulation, proj_bias] + attn_args,
+        [tok_spec, tok_spec, mod_spec, whole_block(proj_bias)] + [whole_block(a) for a in attn_args],
+        [qkv_spec, prob_spec, mixed_spec] + [own_spec] * 5 + [row_spec],
         [
             shape_of((images, 6 * cols, seq), bf16),
             shape_of((images, 2 * heads, seq, seq), bf16),
             shape_of((images, 2 * cols, seq), bf16),
-            shape_of((images, seq, dim), f32),
-            shape_of((images, seq, dim), f32),
-            shape_of((images, seq, dim), bf16),
+            token_f,
+            token_f,
+            token_b,
+            token_b,
+            token_b,
+            shape_of((images, 1, dim), f32),
         ],
         (images,),
-        2 * count * dim * 8 * cols + 8 * count * seq * dim,
-    )
+        45,
+        room=44,
+    )
+    order.after(down_sums)
 
     rows_flat = normed_mlp.reshape(count, dim)
     grad_flat = grad_mlp.reshape(count, dim)
@@ -591,88 +602,87 @@
     steps = 2
     block = width // steps
     anywhere = pl.BlockSpec(memory_space=pl.ANY)
-    act = back = None
-    up_sums = [[None] * CHUNKS, [None] * CHUNKS]
-
-    def mlp_part(chunk, part):
-        nonlocal act, back
-        first = act is None
-        if first:
-            act = back = jnp.zeros((8, 128), bf16)
+    act = back = jnp.zeros((8, 128), bf16)
+    flows, up_sums = [], []
+    for chunk in range(CHUNKS):
         at = chunk * steps
-        spread = pl.BlockSpec((1, block, count), lambda s, c: (part, at + s, 0))
-        act, back, grads, sums = run_kernel(
-            functools.partial(mlp_kernel, per),
+
+        def pick(which, at=at):
+            rest = (steps - 1) * (1 - which)
+            return lambda p, s, c: at + jnp.where(p == which, s, rest)
+
+        def up_map(which):
+            return lambda p, s, c: (0, pick(which)(p, s, c))
+
+        def down_map(which):
+            return lambda p, s, c: (pick(which)(p, s, c), 0)
+
+        spread = pl.BlockSpec((1, block, count), lambda p, s, c, at=at: (p, at + s, 0))
+        act, back, grad_own, grad_other, sums = run_kernel(
+            functools.partial(mlp_kernel, per, steps),
             order.sc,
-            [rows_flat, grad_flat, wu[part], wd[part], up_bias[part], act, back],
-            [
-                whole_block(rows_flat),
-                whole_block(grad_flat),
-                pl.BlockSpec((dim, block), lambda s, c: (0, at + s)),
-                pl.BlockSpec((block, dim), lambda s, c: (at + s, 0)),
-                pl.BlockSpec((8, block), lambda s, c: (0, at + s)),
-                anywhere,
-                anywhere,
-            ],
-            [
-                spread,
-                spread,
-                pl.BlockSpec((16, 2 * per, dim), lambda s, c: (0, 0, 0)),
-                pl.BlockSpec((8, block), lambda s, c: (0, s)),
-            ],
+            [rows_flat, grad_flat] + wu + wd + up_bias + [act, back],
+            [whole_block(rows_flat), whole_block(grad_flat)]
+            + [pl.BlockSpec((dim, block), up_map(which)) for which in range(2)]
+            + [pl.BlockSpec((block, dim), down_map(which)) for which in range(2)]
+            + [pl.BlockSpec((1, block), up_map(which)) for which in range(2)]
+            + [anywhere, anywhere],
+            [spread, spread]
+            + [pl.BlockSpec((16, 2 * per, dim), lambda p, s, c: (0, 0, 0))] * 2
+            + [pl.BlockSpec((1, 8, block), lambda p, s, c: (p, 0, s))],
             [shape_of((2, ff, count), bf16)] * 2
-            + [shape_of((16, 2 * per, dim), bf16), shape_of((8, width), f32)],
-            (steps,),
-            8 * count * dim * width,
-            alias=None if first else {6: 0, 7: 1},
+            + [shape_of((16, 2 * per, dim), bf16)] * 2
+            + [shape_of((2, 8, width), f32)],
+            (2, steps),
+            28,
+            alias=None if chunk == 0 else {9: 0, 10: 1},
+            room=48,
         )
-        up_sums[part][chunk] = sums[0]
+        up_sums.append(sums)
         order.after(sums)
-        return grads
-
-    other = mlp_part(0, 1)
-    first = Flow(MLP_WAYS, None, other)
-    order.tick(first)
-    first.set_own(mlp_part(0, 0))
-    order.tick(first)
-    second = Flow(MLP_WAYS, None, mlp_part(1, 1))
-    order.tick(second)
-    second.set_own(mlp_part(1, 0))
-    order.tick(first, second)
-    third = Flow(MLP_WAYS, None, mlp_part(2, 1))
-    order.tick(first, third)
-    third.set_own(mlp_part(2, 0))
-    order.tick(first, second, third)
+        flows.append(sum_flow(MLP_WAYS, lambda grad_own=grad_own: grad_own, grad_other))
+        order.tick(*flows)
 
     reach = 768
-    per_part = ff // reach
+    turns = ff // reach
     every = lambda s, c: (0, 0, 0)
-    own_whole = pl.BlockSpec((images, seq, dim), every, pipeline_mode=once)
+    tail = lambda first: lambda s, c: (jnp.maximum(s - first, 0), 0, 0)
+    tail_local = lambda first: lambda s, c: (c[0] * images + jnp.maximum(s - first, 0), 0, 0)
+
+    def image_spec(first, where=tail):
+        return pl.BlockSpec((1, seq, dim), where(first))
+
+    def rows_of(part, size):
+        if part == 0:
+            return lambda s, c: jnp.minimum(s, size - 1)
+        return lambda s, c: jnp.clip(s - size, 0, size - 1)
+
+    span_spec = pl.BlockSpec(
+        (1, reach, count),
+        lambda s, c: (jnp.minimum(s // turns, 1), jnp.where(s < 2 * turns, s % turns, turns - 1), 0),
+    )
     grad_residual, grad_attn, mid_sums = run_kernel(
-        functools.partial(norm_back_kernel, images, images),
+        functools.partial(norm_back_kernel, turns, images),
         order.sc,
         [back] + wu + [residual, cotangent, modulation, attn_out],
         [
-            pl.BlockSpec((1, reach, count), lambda s, c: (s // per_part, s % per_part, 0)),
-            pl.BlockSpec((dim, reach), lambda s, c: (0, jnp.minimum(s, per_part - 1))),
-            pl.BlockSpec((dim, reach), lambda s, c: (0, jnp.maximum(s - per_part, 0))),
-            own_whole,
-            all_tok_spec,
-            all_mod_spec,
-            own_whole,
+            span_spec,
+            pl.BlockSpec((dim, reach), lambda s, c: (0, rows_of(0, turns)(s, c))),
+            pl.BlockSpec((dim, reach), lambda s, c: (0, rows_of(1, turns)(s, c))),
+            image_spec(2 * turns),
+            image_spec(2 * turns, tail_local),
+            pl.BlockSpec((1, 6, dim), tail_local(2 * turns)),
+            image_spec(2 * turns),
         ],
-        [own_whole, own_whole, pl.BlockSpec((images, 4, dim), every)],
-        [
-            shape_of((images, seq, dim), f32),
-            shape_of((images, seq, dim), bf16),
-            shape_of((images, 4, dim), f32),
-        ],
-        (2 * per_part,),
-        2 * count * dim * 2 * ff,
+        [image_spec(2 * turns)] * 2 + [pl.BlockSpec((1, 4, dim), tail(2 * turns))],
+        [token_f, token_b, shape_of((images, 4, dim), f32)],
+        (2 * turns + images,),
+        24,
         scratch=[pltpu.VMEM((count, dim), f32)],
+        room=44,
     )
     order.after(mid_sums)
-    order.tick(first, second, third)
+    order.tick(*flows)
     pieces = 2
     each = images // pieces
     grad_qkv = []
@@ -691,12 +701,13 @@
             [qkv_spec],
             [shape_of((each, 6 * cols, seq), bf16)],
             (each,),
-            (2 * count * dim * 2 * cols + 10 * count * seq * dim) // pieces,
+            20,
             scratch=[pltpu.VMEM((2 * cols, seq), bf16)],
+            room=40,
         )
         grad_qkv.append(grad_piece)
         order.after(grad_piece)
-        order.tick(first, second, third)
+        order.tick(*flows)
 
     attn_per = 4 * cols // 16
     qv_sums = [None, None]
@@ -718,81 +729,89 @@
             ],
             [shape_of((16, attn_per, dim), bf16), shape_of((3, 8, cols), f32)],
             (4,),
-            2 * count * dim * 4 * cols,
+            14,
+            room=40,
         )
-        qv_sums[part] = sums[:, 0]
+        qv_sums[part] = sums
         order.after(sums)
         return grads
 
-    last = Flow(ATTN_WAYS, None, attn_part(1))
-    order.tick(last, first, second, third)
-    last.set_own(attn_part(0))
-    order.tick(last, first, second, third)
-
-    per_part = 3
-    rows = cols
-    grad_tokens, low_sums = run_kernel(
+    grad_other = attn_part(1)
+    made = []
+    last = sum_flow(ATTN_WAYS, lambda: made[0], grad_other)
+    order.tick(last, *flows)
+    made.append(attn_part(0))
+    order.tick(last, *flows)
+
+    first_spec = lambda part: pl.BlockSpec((cols, dim), lambda s, c: (rows_of(part, 3)(s, c), 0))
+    grad_tokens, grad_own_tokens, low_sums = run_kernel(
         functools.partial(first_back_kernel, pieces, images),
         order.sc,
         grad_qkv + wq + [tokens, modulation, grad_residual],
-        [pl.BlockSpec((each, rows, seq), lambda s, c: (0, s, 0)) for _ in range(pieces)]
-        + [
-            pl.BlockSpec((rows, dim), lambda s, c: (jnp.minimum(s, 2), 0)),
-            pl.BlockSpec((rows, dim), lambda s, c: (jnp.maximum(s - 3, 0), 0)),
-            all_tok_spec,
-            all_mod_spec,
-            own_whole,
-        ],
-        [own_whole, pl.BlockSpec((images, 2, dim), every)],
-        [shape_of((images, seq, dim), f32), shape_of((images, 2, dim), f32)],
-        (6,),
-        2 * count * dim * 6 * cols,
+        [pl.BlockSpec((each, cols, seq), lambda s, c: (0, jnp.minimum(s, 5), 0)) for _ in range(pieces)]
+        + [first_spec(0), first_spec(1)]
+        + [image_spec(6, tail_local), pl.BlockSpec((1, 6, dim), tail_local(6)), image_spec(6)],
+        [image_spec(6, tail_local), image_spec(6), pl.BlockSpec((1, 2, dim), tail(6))],
+        [shape_of((slots, seq, dim), f32), token_f, shape_of((images, 2, dim), f32)],
+        (6 + images,),
+        20,
+        scratch=[pltpu.VMEM((count, dim), f32)],
+        room=40,
     )
     order.after(low_sums)
-    order.tick(last, first, second, third)
-    per_part = ff // reach
-    output, gate_sums = run_kernel(
-        functools.partial(output_kernel, images, images),
+    order.tick(last, *flows)
+    other_tokens = swap_cores(grad_own_tokens)
+    down_spec = lambda part: pl.BlockSpec((reach, dim), lambda s, c: (rows_of(part, turns)(s, c), 0))
+    output, own_output, gate_sums = run_kernel(
+        functools.partial(output_kernel, turns, images),
         order.sc,
         [act] + wd + [residual, cotangent, modulation, down_bias],
         [
-            pl.BlockSpec((1, reach, count), lambda s, c: (s // per_part, s % per_part, 0)),
-            pl.BlockSpec((reach, dim), lambda s, c: (jnp.minimum(s, per_part - 1), 0)),
-            pl.BlockSpec((reach, dim), lambda s, c: (jnp.maximum(s - per_part, 0), 0)),
-            own_whole,
-            all_tok_spec,
-            all_mod_spec,
+            span_spec,
+            down_spec(0),
+            down_spec(1),
+            image_spec(2 * turns),
+            image_spec(2 * turns, tail_local),
+            pl.BlockSpec((1, 6, dim), tail_local(2 * turns)),
             whole_block(down_bias),
         ],
-        [own_whole, pl.BlockSpec((images, 1, dim), every)],
-        [shape_of((images, seq, dim), bf16), shape_of((images, 1, dim), f32)],
-        (2 * per_part,),
-        2 * count * dim * 2 * ff,
+        [image_spec(2 * turns, tail_local), image_spec(2 * turns), pl.BlockSpec((1, 1, dim), tail(2 * turns))],
+        [shape_of((slots, seq, dim), bf16), token_b, shape_of((images, 1, dim), f32)],
+        (2 * turns + images,),
+        22,
         scratch=[pltpu.VMEM((count, dim), f32)],
+        room=40,
     )
     order.after(gate_sums)
-    order.tick(last, first, second, third)
-    output = lax.all_gather(output, "mp", axis=0, tiled=True)
-    grad_tokens = lax.all_gather(grad_tokens, "mp", axis=0, tiled=True)
+    order.tick(last, *flows)
+    other_output = swap_cores(own_output)
 
     grad_modulation = jnp.concatenate([low_sums, mid_sums[:, 2:3], mid_sums[:, 0:2], gate_sums], axis=1)
     grad_modulation = grad_modulation.reshape(images, 6 * dim).astype(bf16)
     bias_sums = [
-        jnp.concatenate([qv_sums[part][0], qv_sums[part][2]] + up_sums[part]) for part in range(2)
+        jnp.concatenate(
+            [qv_sums[part][0, 0:1], qv_sums[part][2, 0:1]] + [sums[part, 0:1] for sums in up_sums], axis=1
+        )
+        for part in range(2)
     ]
-    shared = jnp.concatenate([jnp.sum(mid_sums[:, 3], axis=0), jnp.sum(down_sums[:, 0], axis=0)])
-    shared = jnp.pad(shared, (0, own_cols - 2 * dim))
-    packed = jnp.concatenate(
-        [grad_modulation.astype(f32).reshape(2 * images, own_cols), jnp.stack(bias_sums + [shared])]
-    )
-    both = lax.all_gather(packed, "mp", axis=0, tiled=False)
-    group_mod = both[:, : 2 * images].reshape(2, images, 2, own_cols)
-    group_mod = lax.dynamic_index_in_dim(group_mod, core, 2, keepdims=False).reshape(slots, own_cols)
-    group_mod = group_mod.astype(bf16)
-    own_bias_sum = lax.dynamic_index_in_dim(both[:, 2 * images], core, 0) + lax.dynamic_index_in_dim(
-        both[:, 2 * images + 1], 1 - core, 0
-    )
-    shared_sum = both[0, -1:] + both[1, -1:]
+    shared = jnp.concatenate(
+        [
+            jnp.sum(mid_sums[:, 3], axis=0, keepdims=True),
+            jnp.sum(down_sums[:, 0], axis=0, keepdims=True),
+            jnp.zeros((1, own_cols - 2 * dim), f32),
+        ],
+        axis=1,
+    )
+    halves = grad_modulation.reshape(images, 2, own_cols)
+    kept = lax.dynamic_index_in_dim(halves, core, 1, keepdims=False)
+    given = lax.dynamic_index_in_dim(halves, 1 - core, 1, keepdims=False)
+    got = swap_cores(jnp.concatenate([given.astype(f32), bias_sums[1], shared]))
+    came = got[:images].astype(bf16)
+    group_mod = jnp.where(
+        core == 0, jnp.concatenate([kept, came]), jnp.concatenate([came, kept])
+    )
+    own_bias_sum = bias_sums[0] + got[images : images + 1]
+    shared_sum = shared + got[images + 1 :]
     part_scaled = outer_cols(group_mod, w_mod).astype(bf16)
     grad_scaled = part_scaled.astype(f32) + swap_cores(part_scaled).astype(f32)
     _, silu_back = jax.vjp(jax.nn.silu, cond_f)
@@ -802,6 +821,38 @@
         [group_mod, own_bias_sum.astype(bf16), shared_sum.astype(bf16), wide_scaled]
     )
     all_rows = lax.all_gather(packed_rows, "dp", axis=0, tiled=False)
+    order.tick(last, *flows)
+    output = fill_other(output, order.fence(other_output), core)
+    order.after(output[0, 0, :1])
+
+    def cuts(ways):
+        return tuple((way[0], lo, hi) for lo, hi, way in ways)
+
+    grad_w_down = grad_w_up = jnp.zeros((8, 128), f32)
+    for chunk, flow in enumerate(flows):
+        args = order.finish(flow)
+        spot = len(args) + 1
+        grad_w_down, grad_w_up, mark = run_kernel(
+            functools.partial(final_mlp_kernel, cuts(MLP_WAYS), per),
+            order.sc,
+            list(args) + [grad_w_down, grad_w_up],
+            [whole_block(a) for a in args] + [anywhere, anywhere],
+            [
+                pl.BlockSpec((block, dim), lambda s, c, chunk=chunk: (chunk * steps + s, 0)),
+                pl.BlockSpec((dim, block), lambda s, c, chunk=chunk: (0, chunk * steps + s)),
+                pl.BlockSpec((8, 128), lambda s, c: (0, 0)),
+            ],
+            [shape_of((ff, dim), f32), shape_of((dim, ff), f32), shape_of((8, 128), f32)],
+            (steps,),
+            6,
+            scratch=[pltpu.VMEM((block, dim), f32)],
+            alias=None if chunk == 0 else {spot: 0, spot + 1: 1},
+            room=32,
+        )
+        order.after(mark)
+        order.tick(last)
+    grad_tokens = fill_other(grad_tokens, order.fence(other_tokens), core)
+    all_rows = order.fence(all_rows)
     all_mod = all_rows[:, :slots].reshape(-1, own_cols)
     all_scaled = all_rows[:, slots + 2 :].reshape(16, -1)[:, : slots * dim].reshape(-1, dim)
     grad_w_mod = inner_rows(all_scaled, all_mod)
@@ -811,38 +862,8 @@
     grad_b_up = bias_total[0, 2 * cols :]
     grad_b_proj = bias_total[1, :dim]
     grad_b_down = bias_total[1, dim : 2 * dim]
-
-    while first.halves is None or second.halves is None or third.halves is None:
-        order.tick(last, *[flow for flow in (first, second, third) if flow.halves is None])
-
-    def cuts(ways):
-        return tuple((way[0], lo, hi) for lo, hi, way in ways)
-
-    grad_w_down = grad_w_up = jnp.zeros((8, 128), f32)
-    for chunk, flow in enumerate((first, second, third)):
-        args = flow.halves
-        spot = len(args) + 1
-        grad_w_down, grad_w_up = run_kernel(
-            functools.partial(final_mlp_kernel, cuts(MLP_WAYS), per),
-            order.sc,
-            list(args) + [grad_w_down, grad_w_up],
-            [whole_block(a) for a in args] + [anywhere, anywhere],
-            [
-                pl.BlockSpec((block, dim), lambda s, c, chunk=chunk: (chunk * steps + s, 0)),
-                pl.BlockSpec((dim, block), lambda s, c, chunk=chunk: (0, chunk * steps + s)),
-            ],
-            [shape_of((ff, dim), f32), shape_of((dim, ff), f32)],
-            (steps,),
-            width * dim,
-            scratch=[pltpu.VMEM((block, dim), f32)],
-            alias=None if chunk == 0 else {spot: 0, spot + 1: 1},
-        )
-        if last.halves is None:
-            order.after(grad_w_down[0, :1])
-            order.tick(last)
-    while last.halves is None:
-        order.tick(last)
-    args = last.halves
+    order.after((grad_tokens[0, 0, :1], grad_w_mod[0, :1], grad_b_mod[:1], bias_total[0, :1]))
+    args = order.finish(last)
     grad_qkv_rows, grad_w_proj = run_kernel(
         functools.partial(final_attn_kernel, cuts(ATTN_WAYS), attn_per),
         order.sc,
@@ -854,7 +875,8 @@
         ],
         [shape_of((3 * cols, dim), f32), shape_of((cols, dim), f32)],
         (4,),
-        cols * dim,
+        9,
+        room=32,
     )
     grad_w_qkv = jnp.transpose(grad_qkv_rows.reshape(3, cols, dim), (2, 0, 1))
     return (

time: 702 us -> 645 us (0.919)
  Pallas kernels: 319 us -> 271 us
  waiting for transfers between devices: 125 us -> 148 us
  other arithmetic: 69 us -> 51.2 us
  starting transfers between devices: 82.7 us -> 65.4 us
  local copies, waits for them, and re-layouts: 52.3 us -> 66.7 us
    pallas_call x19 -> x15, Pallas kernels: 319 us -> 271 us  [run_kernel(): pl.pallas_call(body, out_shape=out_shape, grid_spec=pltpu.PrefetchScalarG...]
    ppermute x72 -> x56, starting transfers between devices: 80.4 us -> 61.9 us  [exchange(): lax.ppermute(value, 'dp', bit_pairs(bit))]
    all_gather x1, waiting for transfers between devices: 0.01 us -> 18.4 us  [fast_device(): all_rows = lax.all_gather(packed_rows, 'dp', axis=0, tiled=False)]
    add x52 -> x44, other arithmetic: 42.7 us -> 25.8 us  [the longest x39 23 us: reduce_flow(): cut(one, bits, route[stage], side, cols)]
    unnamed x96 -> x134, local copies, waits for them, and re-layouts: 11.7 us -> 27.4 us
    ppermute x72 -> x56, waiting for transfers between devices: 120 us -> 123 us  [exchange(): lax.ppermute(value, 'dp', bit_pairs(bit))]
    another operation x30 -> x26, other arithmetic: 17.8 us -> 17.3 us  [the longest x23 17.3 us: gather_flow(): joined.append(jnp.stack([one, two], axis=place))]
  transfers between devices with their start and end apart: 84 -> 72, of which waited for: 28 -> 30; matrix products, arithmetic and copies ran while one was open for 15% -> 9% of each run, Pallas kernels for 36% -> 34%
where the time goes in v2:
time: 645 us; the launch traced here: 637 us
  Pallas kernels  271 us (42%)
  waiting for transfers between devices  148 us (23%)
  local copies, waits for them, and re-layouts  66.7 us (10%)
  starting transfers between devices  65.4 us (10%)
  other arithmetic  51.2 us (8%)
  matrix products  18.1 us (3%)
  between operations  16.5 us (3%)
    pallas_call x15, Pallas kernels, run_kernel(): pl.pallas_call(body, out_shape=out_shape, grid_spec=pltpu.PrefetchScalarG...  271 us
    ppermute x56, waiting for transfers between devices, exchange(): lax.ppermute(value, 'dp', bit_pairs(bit))  123 us
    ppermute x56, starting transfers between devices, exchange(): lax.ppermute(value, 'dp', bit_pairs(bit))  61.9 us
    unnamed x134, local copies, waits for them, and re-layouts  27.4 us
    add x39, other arithmetic, reduce_flow(): cut(one, bits, route[stage], side, cols)  23 us
    slice x18, local copies, waits for them, and re-layouts, cut(): out = lax.slice(array, lo, hi)  21 us
    all_gather x1, waiting for transfers between devices, fast_device(): all_rows = lax.all_gather(packed_rows, 'dp', axis=0, tiled=False)  18.4 us
    another operation x23, other arithmetic, gather_flow(): joined.append(jnp.stack([one, two], axis=place))  17.3 us
  transfers between devices with their start and end apart: 72, of which 30 were waited for; matrix products, arithmetic and copies ran while one was open for 9% of the time, Pallas kernels for 34%

profile of v2, /device:TPU:0, one launch (start us, length us, event | category | flops | bytes accessed | tf_op | source)
XLA Modules:
  0.0 636.9 jit_solution(15666455651036118277)
XLA Ops:
  20.9 47.4 %shard_map.237 = (bf16[4,3456,256]{2,1,0:T(8,128)(2,1)}, bf16[4,16,256,256]{3,2,1,0:T(8,128)(2,1)}, bf16[4,1152,256]{2,1,0:T(8,128)(2,1)S(1)}, f32[4,256,1152]{2...) custom-call(s32[3]{0:T(128)S(1)} %pad_add_fusion.sc, ...), custom_call_target="tpu_custom_call" | custom-call | flops 51749998592 | bytes 54643712 | tf_op jit(solution)/shard_map/pallas_call | solution.py:369
  72.2 25.7 %shard_map.238 = (bf16[2,2304,1024]{2,1,0:T(8,128)(2,1)}, bf16[2,2304,1024]{2,1,0:T(8,128)(2,1)}, bf16[16,96,1152]{2,1,0:T(8,128)(2,1)}, bf16[16,96,1152]{2,1,0:T(8,128)(2,1)}, f32[2,8,768]{2,1,0:T(8,128)S(1)}) custom-call(s32[3]{0:T(128)S(1)} %pad_add_fusion.sc, bf16[1024,1152]{1,0:T(8,128)(2,1)S(1)} %bitcast.283, bf16[1024,1152]{1,0:T(8,128)(2,1)S(1)} %bitcast.286, ...), custom_call_target="tpu_custom_call" | custom-call | flops 32199999488 | bytes 51966976 | tf_op jit(solution)/shard_map/pallas_call | solution.py:369
  98.2 25.8 %shard_map.239 = (bf16[2,2304,1024]{2,1,0:T(8,128)(2,1)}, bf16[2,2304,1024]{2,1,0:T(8,128)(2,1)}, bf16[16,96,1152]{2,1,0:T(8,128)(2,1)}, bf16[16,96,1152]{2,1,0:T(8,128)(2,1)}, f32[2,8,768]{2,1,0:T(8,128)S(1)}) custom-call(s32[3]{0:T(128)S(1)} %pad_add_fusion.sc, bf16[1024,1152]{1,0:T(8,128)(2,1)S(1)} %bitcast.284, ...), custom_call_target="tpu_custom_call", output_to_operand_aliasing={{0}: (9, {}), {1}: (10, {})} | custom-call | flops 32199999488 | bytes 70837248 | tf_op jit(solution)/shard_map/pallas_call | solution.py:369
  137.1 26.0 %shard_map.240 = (bf16[2,2304,1024]{2,1,0:T(8,128)(2,1)}, bf16[2,2304,1024]{2,1,0:T(8,128)(2,1)}, bf16[16,96,1152]{2,1,0:T(8,128)(2,1)}, bf16[16,96,1152]{2,1,0:T(8,128)(2,1)}, f32[2,8,768]{2,1,0:T(8,128)S(1)}) custom-call(s32[3]{0:T(128)S(1)} %pad_add_fusion.sc, bf16[1024,1152]{1,0:T(8,128)(2,1)S(1)} %bitcast.285, ...), custom_call_target="tpu_custom_call", output_to_operand_aliasing={{0}: (9, {}), {1}: (10, {})} | custom-call | flops 32199999488 | bytes 70837248 | tf_op jit(solution)/shard_map/pallas_call | solution.py:369
  175.2 25.4 %shard_map.241 = (f32[4,256,1152]{2,1,0:T(8,128)S(1)}, bf16[4,256,1152]{2,1,0:T(8,128)(2,1)S(1)}, f32[4,4,1152]{2,1,0:T(4,128)S(1)}) custom-call(s32[3]{0:T(128)S(1)} %pad_add_fusion.sc, bf16[2,2304,1024]{2,1,0:T(8,128)(2,1)} %get-tuple-element.358.back, bf16[1152,2304]{1,0:T(8,128)(2,1)} %w_up0.7, bf16[1152,2304]{1,0:T(8,128)(2,1)} %collective-permute-done.4.w_up1, ...), custom_call_target="tpu_custom_call" | custom-call | flops 27599998976 | bytes 41582592 | tf_op jit(solution)/shard_map/pallas_call | solution.py:369
  216.3 17.6 %shard_map.242.refs_0_ = bf16[2,3456,256]{2,1,0:T(8,128)(2,1)S(1)} custom-call(s32[3]{0:T(128)S(1)} %pad_add_fusion.sc, bf16[4,256,1152]{2,1,0:T(8,128)(2,1)S(1)} %get-tuple-element.385.grad_attn.refs_4_, bf16[4,3456,256]{2,1,0:T(8,128)(2,1)} %get-tuple-element.386.qkv, bf16[4,16,256,256]{3,2,1,0:T(8,128)(2,1)} %get-tuple-element.387.prob, ...), custom_call_target="tpu_custom_call" | custom-call | flops 23000000512 | bytes 24018944 | tf_op jit(solution)/shard_map/pallas_call | solution.py:369
  233.9 8.0 %collective-permute-done.20 = bf16[2,2,2,96,512]{4,3,0,1,2:T(8,128)(2,1)S(1)} collective-permute-done((bf16[2,2,2,96,512]{4,3,0,1,2:T(8,128)(2,1)S(1)}, bf16[2,2,2,96,512]{4,3,0,1,2:T(8,128)(2,1)S(1)}, u32[]{:S(2)}, u32[]{:S(2)}) %collective-permute-start.20) | collective-permute-done | bytes 786464 | tf_op jit(solution)/shard_map/ppermute | solution.py:427
  248.2 17.4 %shard_map.243.refs_1_ = bf16[2,3456,256]{2,1,0:T(8,128)(2,1)S(1)} custom-call(s32[3]{0:T(128)S(1)} %pad_add_fusion.sc, bf16[4,256,1152]{2,1,0:T(8,128)(2,1)S(1)} %get-tuple-element.385.grad_attn.refs_4_, bf16[4,3456,256]{2,1,0:T(8,128)(2,1)} %get-tuple-element.386.qkv, bf16[4,16,256,256]{3,2,1,0:T(8,128)(2,1)} %get-tuple-element.387.prob, ...), custom_call_target="tpu_custom_call" | custom-call | flops 23000000512 | bytes 24018944 | tf_op jit(solution)/shard_map/pallas_call | solution.py:369
  269.9 11.4 %shard_map.244 = (bf16[16,144,1152]{2,1,0:T(8,128)(2,1)}, f32[3,8,576]{2,1,0:T(8,128)S(1)}) custom-call(s32[3]{0:T(128)S(1)} %pad_add_fusion.sc, bf16[2,3456,256]{2,1,0:T(8,128)(2,1)S(1)} %shard_map.242.refs_0_, bf16[2,3456,256]{2,1,0:T(8,128)(2,1)S(1)} %shard_map.243.refs_1_, bf16[4,1152,256]{2,1,0:T(8,128)(2,1)S(1)} %get-tuple-element.430.refs_2_, ...), custom_call_target="tpu_custom_call" | custom-call | flops 16099999744 | bytes 19519488 | tf_op jit(solution)/shard_map/pallas_call | solution.py:369
  300.4 11.0 %shard_map.245 = (bf16[16,144,1152]{2,1,0:T(8,128)(2,1)}, f32[3,8,576]{2,1,0:T(8,128)S(1)}) custom-call(s32[3]{0:T(128)S(1)} %pad_add_fusion.sc, bf16[2,3456,256]{2,1,0:T(8,128)(2,1)S(1)} %copy-done.9, bf16[2,3456,256]{2,1,0:T(8,128)(2,1)S(1)} %copy-done.12, bf16[4,1152,256]{2,1,0:T(8,128)(2,1)S(1)} %copy-done.17, bf16[4,256,1152]{2,1,0:T(8,128)(2,1)S(1)} %copy-done.20, ...), custom_call_target="tpu_custom_call" | custom-call | flops 16099999744 | bytes 19519488 | tf_op jit(solution)/shard_map/pallas_call | solution.py:369
  334.8 8.5 %collective-permute-done.38 = bf16[96,1152]{1,0:T(8,128)(2,1)} collective-permute-done((bf16[96,1152]{1,0:T(8,128)(2,1)}, bf16[96,1152]{1,0:T(8,128)(2,1)}, u32[]{:S(2)}, u32[]{:S(2)}) %collective-permute-start.38) | collective-permute-done | bytes 221216 | tf_op jit(solution)/shard_map/ppermute | solution.py:427
  351.5 23.9 %shard_map.246 = (f32[8,256,1152]{2,1,0:T(8,128)}, f32[4,256,1152]{2,1,0:T(8,128)}, f32[4,2,1152]{2,1,0:T(2,128)S(1)}) custom-call(s32[3]{0:T(128)S(1)} %pad_add_fusion.sc, bf16[2,3456,256]{2,1,0:T(8,128)(2,1)S(1)} %copy-done.10, bf16[2,3456,256]{2,1,0:T(8,128)(2,1)S(1)} %copy-done.13, bf16[1728,1152]{1,0:T(8,128)(2,1)S(1)} %bitcast.277, ...), custom_call_target="tpu_custom_call" | custom-call | flops 23000000512 | bytes 38891520 | tf_op jit(solution)/shard_map/pallas_call | solution.py:369
  386.6 21.5 %shard_map.247 = (bf16[8,256,1152]{2,1,0:T(8,128)(2,1)}, bf16[4,256,1152]{2,1,0:T(8,128)(2,1)S(1)}, f32[4,1,1152]{2,1,0:T(1,128)S(1)}) custom-call(s32[3]{0:T(128)S(1)} %pad_add_fusion.sc, bf16[2,2304,1024]{2,1,0:T(8,128)(2,1)} %get-tuple-element.495.act, bf16[2304,1152]{1,0:T(8,128)(2,1)} %w_down0.7, bf16[2304,1152]{1,0:T(8,128)(2,1)} %collective-permute-done.5.w_down1, ...), custom_call_target="tpu_custom_call" | custom-call | flops 25300000768 | bytes 36813312 | tf_op jit(solution)/shard_map/pallas_call | solution.py:369
  415.7 8.2 %collective-permute-done.41 = bf16[2,2,144,256]{3,2,0,1:T(8,128)(2,1)} collective-permute-done((bf16[2,2,144,256]{3,2,0,1:T(8,128)(2,1)}, bf16[2,2,144,256]{3,2,0,1:T(8,128)(2,1)}, u32[]{:S(2)}, u32[]{:S(2)}) %collective-permute-start.41) | collective-permute-done | bytes 294944 | tf_op jit(solution)/shard_map/ppermute | solution.py:427
  433.4 6.8 %collective-permute-done.46 = bf16[2,96,1152]{2,1,0:T(8,128)(2,1)S(1)} collective-permute-done((bf16[2,96,1152]{2,1,0:T(8,128)(2,1)S(1)}, bf16[2,96,1152]{2,1,0:T(8,128)(2,1)S(1)}, u32[]{:S(2)}, u32[]{:S(2)}) %collective-permute-start.46) | collective-permute-done | bytes 442400 | tf_op jit(solution)/shard_map/ppermute | solution.py:427
  440.2 17.8 %collective-permute-done.44 = bf16[2,2,96,640]{3,2,1,0:T(8,128)(2,1)} collective-permute-done((bf16[2,2,96,640]{3,2,1,0:T(8,128)(2,1)}, bf16[2,2,96,640]{3,2,1,0:T(8,128)(2,1)}, u32[]{:S(2)}, u32[]{:S(2)}) %collective-permute-start.44) | collective-permute-done | bytes 491552 | tf_op jit(solution)/shard_map/ppermute | solution.py:427
  470.0 5.4 convolution_convert_fusion
  489.1 6.8 %collective-permute-done.47 = bf16[2,144,896]{2,1,0:T(8,128)(2,1)} collective-permute-done((bf16[2,144,896]{2,1,0:T(8,128)(2,1)}, bf16[2,144,896]{2,1,0:T(8,128)(2,1)}, u32[]{:S(2)}, u32[]{:S(2)}) %collective-permute-start.47) | collective-permute-done | bytes 516128 | tf_op jit(solution)/shard_map/ppermute | solution.py:427
  495.9 6.6 %collective-permute-done.50 = bf16[2,2,2,96,512]{4,3,2,1,0:T(8,128)(2,1)S(1)} collective-permute-done((bf16[2,2,2,96,512]{4,3,2,1,0:T(8,128)(2,1)S(1)}, bf16[2,2,2,96,512]{4,3,2,1,0:T(8,128)(2,1)S(1)}, u32[]{:S(2)}, u32[]{:S(2)}) %collective-permute-start.50) | collective-permute-done | bytes 786464 | tf_op jit(solution)/shard_map/ppermute | solution.py:427
  554.9 8.5 %collective-permute-done.60 = bf16[2,144,896]{2,1,0:T(8,128)(2,1)S(1)} collective-permute-done((bf16[2,144,896]{2,1,0:T(8,128)(2,1)S(1)}, bf16[2,144,896]{2,1,0:T(8,128)(2,1)S(1)}, u32[]{:S(2)}, u32[]{:S(2)}) %collective-permute-start.60) | collective-permute-done | bytes 516128 | tf_op jit(solution)/shard_map/ppermute | solution.py:427
  570.5 18.4 %all-gather.4.cloned.1.call-done = bf16[16,13,3456]{2,1,0:T(8,128)(2,1)} async-done(((bf16[1,13,3456]{2,1,0:T(8,128)(2,1)}), bf16[16,13,3456]{2,1,0:T(8,128)(2,1)}) %all-gather.4.cloned.1.call-update) | async-done | bytes 1437712 | tf_op jit(solution)/shard_map/all_gather | solution.py:823
  604.9 8.1 %fusion.10 = f32[1152,3456]{1,0:T(8,128)} fusion(bf16[128,1152]{1,0:T(8,128)(2,1)S(1)} %reshape.367, bf16[16,13,3456]{2,1,0:T(8,128)(2,1)S(1)} %copy-done.31), kind=kOutput, calls=%fused_computation.36 | convolution fusion | flops 1019215872 | bytes 17104896 | tf_op jit(solution)/shard_map/dot_general | solution.py:917
  613.0 6.5 %collective-permute-done.70 = bf16[2,2,2,144,256]{4,3,2,1,0:T(8,128)(2,1)S(1)} collective-permute-done((bf16[2,2,2,144,256]{4,3,2,1,0:T(8,128)(2,1)S(1)}, bf16[2,2,2,144,256]{4,3,2,1,0:T(8,128)(2,1)S(1)}, u32[]{:S(2)}, u32[]{:S(2)}) %collective-permute-start.70) | collective-permute-done | bytes 589856 | tf_op jit(solution)/shard_map/ppermute | solution.py:427
  623.7 5.9 shard_map.248
  (427 shorter events, 251.6 us)
Async XLA Ops:
  7.2 581.7 %all-gather.4.cloned.1.call-start = ((), (), s32[]{:S(2)}) async-start(), calls=%async_computation | async-start | bytes 1880064 | tf_op jit(solution)/shard_map/all_gather | solution.py:823
  14.6 55.1 %collective-permute-start.4 = (bf16[1152,2304]{1,0:T(8,128)(2,1)}, bf16[1152,2304]{1,0:T(8,128)(2,1)}, u32[]{:S(2)}, u32[]{:S(2)}) collective-permute-start(bf16[1152,2304]{1,0:T(8,128)(2,1)} %w_up0.7), channel_id=1, source_target_pairs={{0,1},{1,0},{2,3},{3,2},{4,5},{5,4},{6,7},{7,6},{8,9},{9,8},{10,11... | collective-permute-start | bytes 15925256 | tf_op jit(solution)/shard_map/ppermute | solution.py:400
  14.9 54.8 %collective-permute-start.5 = (bf16[2304,1152]{1,0:T(8,128)(2,1)}, bf16[2304,1152]{1,0:T(8,128)(2,1)}, u32[]{:S(2)}, u32[]{:S(2)}) collective-permute-start(bf16[2304,1152]{1,0:T(8,128)(2,1)} %w_down0.7), channel_id=1, source_target_pairs={{0,1},{1,0},{2,3},{3,2},{4,5},{5,4},{6,7},{7,6},{8,9},{9,8},{10,11... | collective-permute-start | bytes 15925256 | tf_op jit(solution)/shard_map/ppermute | solution.py:400
  16.3 53.4 %collective-permute-start.6 = (bf16[1,2304]{1,0:T(2,128)(2,1)S(1)}, bf16[1,2304]{1,0:T(2,128)(2,1)S(1)}, u32[]{:S(2)}, u32[]{:S(2)}) collective-permute-start(bf16[1,2304]{1,0:T(2,128)(2,1)S(1)} %broadcast_in_dim.35), channel_id=1, source_target_pairs={{0,1},{1,0},{2,3},{3,2},{4,5},{5,4},{6,7},{7,6},{8,9},{9,8},{10,11... | collective-permute-start | bytes 13832 | tf_op jit(solution)/shard_map/ppermute | solution.py:400
  130.0 33.1 %collective-permute-start.10 = (bf16[16,96,1152]{2,1,0:T(8,128)(2,1)}, bf16[16,96,1152]{2,1,0:T(8,128)(2,1)}, u32[]{:S(2)}, u32[]{:S(2)}) collective-permute-start(bf16[16,96,1152]{2,1,0:T(8,128)(2,1)} %get-tuple-element.348), channel_id=1, source_target_pairs={{0,1},{1,0},{2,3},{3,2},{4,5},{5,4},{6,7},{7,6},{8,9},{9,8},{10,11... | collective-permute-start | bytes 10616840 | tf_op jit(solution)/shard_map/ppermute | solution.py:400
  132.9 30.2 %collective-permute-start.9 = (bf16[2,2,2,96,512]{4,3,0,1,2:T(8,128)(2,1)}, bf16[2,2,2,96,512]{4,3,0,1,2:T(8,128)(2,1)}, u32[]{:S(2)}, u32[]{:S(2)}) collective-permute-start(bf16[2,2,2,96,512]{4,3,0,1,2:T(8,128)(2,1)} %get-tuple-element.346), channel_id=1, source_target_pairs={{0,4},{2,6},{4,0},{6,2},{8,12},{10,14},{12,8},{14,10},{16,20},{18,... | collective-permute-start | bytes 2359304 | tf_op jit(solution)/shard_map/ppermute | solution.py:427
  165.1 38.8 %collective-permute-start.15 = (bf16[16,96,1152]{2,1,0:T(8,128)(2,1)}, bf16[16,96,1152]{2,1,0:T(8,128)(2,1)}, u32[]{:S(2)}, u32[]{:S(2)}) collective-permute-start(bf16[16,96,1152]{2,1,0:T(8,128)(2,1)} %get-tuple-element.372), channel_id=1, source_target_pairs={{0,1},{1,0},{2,3},{3,2},{4,5},{5,4},{6,7},{7,6},{8,9},{9,8},{10,11... | collective-permute-start | bytes 10616840 | tf_op jit(solution)/shard_map/ppermute | solution.py:400
  171.1 29.6 %collective-permute-start.12 = (bf16[2,2,96,512]{3,2,0,1:T(8,128)(2,1)}, bf16[2,2,96,512]{3,2,0,1:T(8,128)(2,1)}, u32[]{:S(2)}, u32[]{:S(2)}) collective-permute-start(bf16[2,2,96,512]{3,2,0,1:T(8,128)(2,1)} %get-tuple-element.366), channel_id=1, source_target_pairs={{0,2},{2,0},{4,6},{6,4},{8,10},{10,8},{12,14},{14,12},{16,18},{18,... | collective-permute-start | bytes 1179656 | tf_op jit(solution)/shard_map/ppermute | solution.py:427
  171.8 30.4 %collective-permute-start.14 = (bf16[2,2,2,96,512]{4,3,0,1,2:T(8,128)(2,1)}, bf16[2,2,2,96,512]{4,3,0,1,2:T(8,128)(2,1)S(1)}, u32[]{:S(2)}, u32[]{:S(2)}) collective-permute-start(bf16[2,2,2,96,512]{4,3,0,1,2:T(8,128)(2,1)} %fusion.15), channel_id=1, source_target_pairs={{0,4},{2,6},{4,0},{6,2},{8,12},{10,14},{12,8},{14,10},{16,20},{18,... | collective-permute-start | bytes 2359304 | tf_op jit(solution)/shard_map/ppermute | solution.py:427
  173.8 30.2 %collective-permute-start.13 = (bf16[2,2,2,96,640]{4,3,0,1,2:T(8,128)(2,1)S(1)}, bf16[2,2,2,96,640]{4,3,0,1,2:T(8,128)(2,1)S(1)}, u32[]{:S(2)}, u32[]{:S(2)}) collective-permute-start(bf16[2,2,2,96,640]{4,3,0,1,2:T(8,128)(2,1)S(1)} %fusion.5), channel_id=1, source_target_pairs={{0,2},{2,0},{4,6},{6,4},{8,10},{10,8},{12,14},{14,12},{16,18},{18,... | collective-permute-start | bytes 2949128 | tf_op jit(solution)/shard_map/ppermute | solution.py:427
  331.2 44.2 %collective-permute-start.37 = (bf16[2,96,1152]{2,1,0:T(8,128)(2,1)S(1)}, bf16[2,96,1152]{2,1,0:T(8,128)(2,1)S(1)}, u32[]{:S(2)}, u32[]{:S(2)}) collective-permute-start(bf16[2,96,1152]{2,1,0:T(8,128)(2,1)S(1)} %pad_maximum_fusion.20), channel_id=1, source_target_pairs={{0,8},{2,10},{4,12},{6,14},{8,0},{10,2},{12,4},{14,6},{16,24},{18,... | collective-permute-start | bytes 1327112 | tf_op jit(solution)/shard_map/ppermute | solution.py:427
  332.0 43.5 %collective-permute-start.35 = (bf16[2,2,96,640]{3,2,1,0:T(8,128)(2,1)S(1)}, bf16[2,2,96,640]{3,2,1,0:T(8,128)(2,1)S(1)}, u32[]{:S(2)}, u32[]{:S(2)}) collective-permute-start(bf16[2,2,96,640]{3,2,1,0:T(8,128)(2,1)S(1)} %fusion.24), channel_id=1, source_target_pairs={{0,4},{2,6},{4,0},{6,2},{8,12},{10,14},{12,8},{14,10},{16,20},{18,... | collective-permute-start | bytes 1474568 | tf_op jit(solution)/shard_map/ppermute | solution.py:427
  333.4 42.0 %collective-permute-start.34 = (bf16[2,2,2,144,256]{4,3,1,2,0:T(8,128)(2,1)}, bf16[2,2,2,144,256]{4,3,1,2,0:T(8,128)(2,1)S(1)}, u32[]{:S(2)}, u32[]{:S(2)}) collective-permute-start(bf16[2,2,2,144,256]{4,3,1,2,0:T(8,128)(2,1)} %fusion.21), channel_id=1, source_target_pairs={{0,8},{2,10},{4,12},{6,14},{8,0},{10,2},{12,4},{14,6},{16,24},{18,... | collective-permute-start | bytes 1769480 | tf_op jit(solution)/shard_map/ppermute | solution.py:427
  343.3 32.1 %collective-permute-start.33 = (bf16[2,2,2,144,384]{4,3,0,1,2:T(8,128)(2,1)}, bf16[2,2,2,144,384]{4,3,0,1,2:T(8,128)(2,1)S(1)}, u32[]{:S(2)}, u32[]{:S(2)}) collective-permute-start(bf16[2,2,2,144,384]{4,3,0,1,2:T(8,128)(2,1)} %fusion.9), channel_id=1, source_target_pairs={{0,4},{2,6},{4,0},{6,2},{8,12},{10,14},{12,8},{14,10},{16,20},{18,... | collective-permute-start | bytes 2654216 | tf_op jit(solution)/shard_map/ppermute | solution.py:427
  344.8 30.7 %collective-permute-start.32 = (bf16[2,2,2,144,512]{4,3,0,1,2:T(8,128)(2,1)}, bf16[2,2,2,144,512]{4,3,0,1,2:T(8,128)(2,1)S(1)}, u32[]{:S(2)}, u32[]{:S(2)}) collective-permute-start(bf16[2,2,2,144,512]{4,3,0,1,2:T(8,128)(2,1)} %fusion.1), channel_id=1, source_target_pairs={{0,2},{2,0},{4,6},{6,4},{8,10},{10,8},{12,14},{14,12},{16,18},{18,... | collective-permute-start | bytes 3538952 | tf_op jit(solution)/shard_map/ppermute | solution.py:427
  412.1 45.9 %collective-permute-start.42 = (bf16[2,2,2,96,640]{4,3,1,0,2:T(8,128)(2,1)S(1)}, bf16[2,2,2,96,640]{4,3,1,0,2:T(8,128)(2,1)}, u32[]{:S(2)}, u32[]{:S(2)}) collective-permute-start(bf16[2,2,2,96,640]{4,3,1,0,2:T(8,128)(2,1)S(1)} %copy-done.23), channel_id=1, source_target_pairs={{0,2},{2,0},{4,6},{6,4},{8,10},{10,8},{12,14},{14,12},{16,18},{18,... | collective-permute-start | bytes 2949128 | tf_op jit(solution)/shard_map/ppermute | solution.py:427
  415.1 42.9 %collective-permute-start.43 = (bf16[2,2,2,96,512]{4,3,2,1,0:T(8,128)(2,1)S(1)}, bf16[2,2,2,96,512]{4,3,2,1,0:T(8,128)(2,1)S(1)}, u32[]{:S(2)}, u32[]{:S(2)}) collective-permute-start(bf16[2,2,2,96,512]{4,3,2,1,0:T(8,128)(2,1)S(1)} %pad_maximum_fusion.5), channel_id=1, source_target_pairs={{0,4},{2,6},{4,0},{6,2},{8,12},{10,14},{12,8},{14,10},{16,20},{18,... | collective-permute-start | bytes 2359304 | tf_op jit(solution)/shard_map/ppermute | solution.py:427
  423.9 34.1 %collective-permute-start.39 = (bf16[2,2,144,512]{3,2,0,1:T(8,128)(2,1)}, bf16[2,2,144,512]{3,2,0,1:T(8,128)(2,1)}, u32[]{:S(2)}, u32[]{:S(2)}) collective-permute-start(bf16[2,2,144,512]{3,2,0,1:T(8,128)(2,1)} %get-tuple-element.502), channel_id=1, source_target_pairs={{0,4},{2,6},{4,0},{6,2},{8,12},{10,14},{12,8},{14,10},{16,20},{18,... | collective-permute-start | bytes 1769480 | tf_op jit(solution)/shard_map/ppermute | solution.py:427
  424.4 33.6 %collective-permute-start.44 = (bf16[2,2,96,640]{3,2,1,0:T(8,128)(2,1)}, bf16[2,2,96,640]{3,2,1,0:T(8,128)(2,1)}, u32[]{:S(2)}, u32[]{:S(2)}) collective-permute-start(bf16[2,2,96,640]{3,2,1,0:T(8,128)(2,1)} %fusion.23), channel_id=1, source_target_pairs={{0,4},{2,6},{4,0},{6,2},{8,12},{10,14},{12,8},{14,10},{16,20},{18,... | collective-permute-start | bytes 1474568 | tf_op jit(solution)/shard_map/ppermute | solution.py:427
  477.1 93.4 %collective-permute-start.62 = (f32[4,256,1152]{2,1,0:T(8,128)}, f32[4,256,1152]{2,1,0:T(8,128)}, u32[]{:S(2)}, u32[]{:S(2)}) collective-permute-start(f32[4,256,1152]{2,1,0:T(8,128)} %get-tuple-element.575), channel_id=1, source_target_pairs={{0,1},{1,0},{2,3},{3,2},{4,5},{5,4},{6,7},{7,6},{8,9},{9,8},{10,11... | collective-permute-start | bytes 14155784 | tf_op jit(solution)/shard_map/ppermute | solution.py:400
  477.3 45.6 %collective-permute-start.53 = (bf16[4,256,1152]{2,1,0:T(8,128)(2,1)}, bf16[4,256,1152]{2,1,0:T(8,128)(2,1)}, u32[]{:S(2)}, u32[]{:S(2)}) collective-permute-start(bf16[4,256,1152]{2,1,0:T(8,128)(2,1)} %copy-done.1), channel_id=1, source_target_pairs={{0,1},{1,0},{2,3},{3,2},{4,5},{5,4},{6,7},{7,6},{8,9},{9,8},{10,11... | collective-permute-start | bytes 7077896 | tf_op jit(solution)/shard_map/ppermute | solution.py:400
  520.6 32.2 %collective-permute-start.59 = (bf16[2,2,2,96,512]{4,3,2,1,0:T(8,128)(2,1)S(1)}, bf16[2,2,2,96,512]{4,3,2,1,0:T(8,128)(2,1)S(1)}, u32[]{:S(2)}, u32[]{:S(2)}) collective-permute-start(bf16[2,2,2,96,512]{4,3,2,1,0:T(8,128)(2,1)S(1)} %pad_maximum_fusion.7), channel_id=1, source_target_pairs={{0,4},{2,6},{4,0},{6,2},{8,12},{10,14},{12,8},{14,10},{16,20},{18,... | collective-permute-start | bytes 2359304 | tf_op jit(solution)/shard_map/ppermute | solution.py:427
  523.0 29.9 %collective-permute-start.58 = (bf16[2,2,2,96,640]{4,3,1,0,2:T(8,128)(2,1)S(1)}, bf16[2,2,2,96,640]{4,3,1,0,2:T(8,128)(2,1)S(1)}, u32[]{:S(2)}, u32[]{:S(2)}) collective-permute-start(bf16[2,2,2,96,640]{4,3,1,0,2:T(8,128)(2,1)S(1)} %copy-done.25), channel_id=1, source_target_pairs={{0,2},{2,0},{4,6},{6,4},{8,10},{10,8},{12,14},{14,12},{16,18},{18,... | collective-permute-start | bytes 2949128 | tf_op jit(solution)/shard_map/ppermute | solution.py:427
  563.6 29.6 %collective-permute-start.67 = (bf16[2,2,144,256]{3,2,1,0:T(8,128)(2,1)S(1)}, bf16[2,2,144,256]{3,2,1,0:T(8,128)(2,1)}, u32[]{:S(2)}, u32[]{:S(2)}) collective-permute-start(bf16[2,2,144,256]{3,2,1,0:T(8,128)(2,1)S(1)} %pad_maximum_fusion.25), channel_id=1, source_target_pairs={{0,16},{2,18},{4,20},{6,22},{8,24},{10,26},{12,28},{14,30},{16,0},... | collective-permute-start | bytes 884744 | tf_op jit(solution)/shard_map/ppermute | solution.py:427
  (115 other events, 2136.9 us)
Sparse Core Ops, SparseCore 0:
  518.0 70.8 all-gather.3

commit v3 on v2

--- a/solution.py
+++ b/solution.py
@@ -103,21 +103,21 @@
 
 
 def mlp_kernel(
-    per, steps, sc, rows, grad_mlp, w_up0, w_up1, w_down0, w_down1, bias0, bias1, act_in, back_in,
+    per, natural, sc, rows, grad_mlp, w_up0, w_up1, w_down0, w_down1, bias0, bias1, act_in, back_in,
     act, back, grad_own, grad_other, sums
 ):
     part, step = pl.program_id(0), pl.program_id(1)
 
     @pl.when(part == 0)
     def _():
-        mlp_block(per, step, sc, rows, grad_mlp, w_up0, w_down0, bias0, act, back, grad_own, sums)
+        mlp_block(per, natural, step, sc, rows, grad_mlp, w_up0, w_down0, bias0, act, back, grad_own, sums)
 
     @pl.when(part == 1)
     def _():
-        mlp_block(per, step, sc, rows, grad_mlp, w_up1, w_down1, bias1, act, back, grad_other, sums)
-
-
-def mlp_block(per, step, sc, rows, grad_mlp, w_up, w_down, bias, act, back, grads, sums):
+        mlp_block(per, natural, step, sc, rows, grad_mlp, w_up1, w_down1, bias1, act, back, grad_other, sums)
+
+
+def mlp_block(per, natural, step, sc, rows, grad_mlp, w_up, w_down, bias, act, back, grads, sums):
     here = w_down.shape[0] // per
     hidden = lax.dot_general(
         w_up[...], rows[...], (((0,), (1,)), ((), ())), preferred_element_type=f32
@@ -136,7 +136,9 @@
     grad_down = dot_nn(act_b, grad_mlp[...]).astype(bf16)
     grad_up = dot_nn(back_b, rows[...]).astype(bf16)
     for piece in range(here):
-        at = jnp.bitwise_xor(step * here + piece, sc[2])
+        at = step * here + piece
+        if not natural:
+            at = jnp.bitwise_xor(at, sc[2])
         lo = piece * per
         grads[at, 0:per, :] = grad_down[lo : lo + per]
         grads[at, per : 2 * per, :] = grad_up[lo : lo + per]
@@ -343,6 +345,15 @@
     mark[...] = jnp.zeros_like(mark)
 
 
+def final_plain_kernel(per, sc, summed, down_in, up_in, down, up, mark, turned):
+    for piece in range(summed.shape[0]):
+        lo = piece * per
+        down[lo : lo + per, :] = summed[piece, 0:per, :].astype(f32)
+        turned[lo : lo + per, :] = summed[piece, per : 2 * per, :].astype(f32)
+    up[...] = turned[...].T
+    mark[...] = jnp.zeros_like(mark)
+
+
 def final_attn_kernel(cuts, per, sc, *refs):
     count = 2 * len(cuts)
     arrays, (qkv, proj) = refs[:count], refs[count:]
@@ -378,7 +389,7 @@
         ),
         compiler_params=pltpu.CompilerParams(vmem_limit_bytes=room << 20),
         cost_estimate=pl.CostEstimate(
-            flops=int(micros * 1.15e9), bytes_accessed=int(size), transcendentals=0
+            flops=int(micros * 1.15e9), bytes_accessed=int(min(size, micros * 1e6)), transcendentals=0
         ),
         input_output_aliases=alias or {},
     )(sc, *args)
@@ -487,6 +498,25 @@
     return (yield from gather_flow(ways, have))
 
 
+def core_flow(own, other):
+    (other,) = yield [other]
+    came = swap_cores(other)
+    yield None
+    own, came = yield [own, came]
+    (total,) = yield [own + came]
+    return total
+
+
+def rows_flow(rows):
+    for bit in range(4):
+        (rows,) = yield [rows]
+        came = lax.ppermute(rows, "dp", bit_pairs(bit))
+        yield None
+        rows, came = yield [rows, came]
+        rows = jnp.concatenate([rows, came])
+    return rows
+
+
 class Order:
     def __init__(self, sc):
         self.sc = sc
@@ -520,6 +550,7 @@
 
 
 CHUNKS = 3
+PLAIN = 2
 
 
 def fill_other(both, came, core):
@@ -603,7 +634,7 @@
     block = width // steps
     anywhere = pl.BlockSpec(memory_space=pl.ANY)
     act = back = jnp.zeros((8, 128), bf16)
-    flows, up_sums = [], []
+    plain, flows, up_sums = [], [], []
     for chunk in range(CHUNKS):
         at = chunk * steps
 
@@ -619,7 +650,7 @@
 
         spread = pl.BlockSpec((1, block, count), lambda p, s, c, at=at: (p, at + s, 0))
         act, back, grad_own, grad_other, sums = run_kernel(
-            functools.partial(mlp_kernel, per, steps),
+            functools.partial(mlp_kernel, per, chunk < PLAIN),
             order.sc,
             [rows_flat, grad_flat] + wu + wd + up_bias + [act, back],
             [whole_block(rows_flat), whole_block(grad_flat)]
@@ -640,8 +671,15 @@
         )
         up_sums.append(sums)
         order.after(sums)
-        flows.append(sum_flow(MLP_WAYS, lambda grad_own=grad_own: grad_own, grad_other))
-        order.tick(*flows)
+        if chunk < PLAIN:
+            flow = core_flow(grad_own, grad_other)
+            plain.append(flow)
+        else:
+            flow = sum_flow(MLP_WAYS, lambda grad_own=grad_own: grad_own, grad_other)
+            flows.append(flow)
+        order.tick(*plain, *flows)
+
+    plain_sums = lax.psum([order.results[flow] for flow in plain], "dp")
 
     reach = 768
     turns = ff // reach
@@ -677,7 +715,7 @@
         [image_spec(2 * turns)] * 2 + [pl.BlockSpec((1, 4, dim), tail(2 * turns))],
         [token_f, token_b, shape_of((images, 4, dim), f32)],
         (2 * turns + images,),
-        24,
+        60,
         scratch=[pltpu.VMEM((count, dim), f32)],
         room=44,
     )
@@ -701,7 +739,7 @@
             [qkv_spec],
             [shape_of((each, 6 * cols, seq), bf16)],
             (each,),
-            20,
+            60,
             scratch=[pltpu.VMEM((2 * cols, seq), bf16)],
             room=40,
         )
@@ -729,7 +767,7 @@
             ],
             [shape_of((16, attn_per, dim), bf16), shape_of((3, 8, cols), f32)],
             (4,),
-            14,
+            60,
             room=40,
         )
         qv_sums[part] = sums
@@ -754,7 +792,7 @@
         [image_spec(6, tail_local), image_spec(6), pl.BlockSpec((1, 2, dim), tail(6))],
         [shape_of((slots, seq, dim), f32), token_f, shape_of((images, 2, dim), f32)],
         (6 + images,),
-        20,
+        60,
         scratch=[pltpu.VMEM((count, dim), f32)],
         room=40,
     )
@@ -778,7 +816,7 @@
         [image_spec(2 * turns, tail_local), image_spec(2 * turns), pl.BlockSpec((1, 1, dim), tail(2 * turns))],
         [shape_of((slots, seq, dim), bf16), token_b, shape_of((images, 1, dim), f32)],
         (2 * turns + images,),
-        22,
+        60,
         scratch=[pltpu.VMEM((count, dim), f32)],
         room=40,
     )
@@ -820,39 +858,19 @@
     packed_rows = jnp.concatenate(
         [group_mod, own_bias_sum.astype(bf16), shared_sum.astype(bf16), wide_scaled]
     )
-    all_rows = lax.all_gather(packed_rows, "dp", axis=0, tiled=False)
-    order.tick(last, *flows)
+    small = rows_flow(packed_rows)
+    order.tick(last, *flows, small)
     output = fill_other(output, order.fence(other_output), core)
     order.after(output[0, 0, :1])
 
     def cuts(ways):
         return tuple((way[0], lo, hi) for lo, hi, way in ways)
 
-    grad_w_down = grad_w_up = jnp.zeros((8, 128), f32)
-    for chunk, flow in enumerate(flows):
-        args = order.finish(flow)
-        spot = len(args) + 1
-        grad_w_down, grad_w_up, mark = run_kernel(
-            functools.partial(final_mlp_kernel, cuts(MLP_WAYS), per),
-            order.sc,
-            list(args) + [grad_w_down, grad_w_up],
-            [whole_block(a) for a in args] + [anywhere, anywhere],
-            [
-                pl.BlockSpec((block, dim), lambda s, c, chunk=chunk: (chunk * steps + s, 0)),
-                pl.BlockSpec((dim, block), lambda s, c, chunk=chunk: (0, chunk * steps + s)),
-                pl.BlockSpec((8, 128), lambda s, c: (0, 0)),
-            ],
-            [shape_of((ff, dim), f32), shape_of((dim, ff), f32), shape_of((8, 128), f32)],
-            (steps,),
-            6,
-            scratch=[pltpu.VMEM((block, dim), f32)],
-            alias=None if chunk == 0 else {spot: 0, spot + 1: 1},
-            room=32,
-        )
-        order.after(mark)
-        order.tick(last)
+    order.tick(last, *flows, small)
     grad_tokens = fill_other(grad_tokens, order.fence(other_tokens), core)
-    all_rows = order.fence(all_rows)
+    order.after(grad_tokens[0, 0, :1])
+    order.tick(last, *flows, small)
+    all_rows = order.finish(small).reshape(16, slots + 5, own_cols)
     all_mod = all_rows[:, :slots].reshape(-1, own_cols)
     all_scaled = all_rows[:, slots + 2 :].reshape(16, -1)[:, : slots * dim].reshape(-1, dim)
     grad_w_mod = inner_rows(all_scaled, all_mod)
@@ -862,7 +880,40 @@
     grad_b_up = bias_total[0, 2 * cols :]
     grad_b_proj = bias_total[1, :dim]
     grad_b_down = bias_total[1, dim : 2 * dim]
-    order.after((grad_tokens[0, 0, :1], grad_w_mod[0, :1], grad_b_mod[:1], bias_total[0, :1]))
+    order.after((grad_w_mod[0, :1], grad_b_mod[:1], bias_total[0, :1]))
+    order.tick(last, *flows)
+    grad_w_down = grad_w_up = jnp.zeros((8, 128), f32)
+
+    def final_mlp(chunk, body, args):
+        nonlocal grad_w_down, grad_w_up
+        spot = len(args) + 1
+        grad_w_down, grad_w_up, mark = run_kernel(
+            body,
+            order.sc,
+            list(args) + [grad_w_down, grad_w_up],
+            [
+                whole_block(a) if a.shape[0] == 8 else pl.BlockSpec((16 // steps,) + a.shape[1:], lambda s, c: (s, 0, 0))
+                for a in args
+            ]
+            + [anywhere, anywhere],
+            [
+                pl.BlockSpec((block, dim), lambda s, c: (chunk * steps + s, 0)),
+                pl.BlockSpec((dim, block), lambda s, c: (0, chunk * steps + s)),
+                pl.BlockSpec((8, 128), lambda s, c: (0, 0)),
+            ],
+            [shape_of((ff, dim), f32), shape_of((dim, ff), f32), shape_of((8, 128), f32)],
+            (steps,),
+            2,
+            scratch=[pltpu.VMEM((block, dim), f32)],
+            alias=None if spot == len(args) + 1 and grad_w_down.shape[0] == 8 else {spot: 0, spot + 1: 1},
+            room=32,
+        )
+        order.after(mark)
+
+    for chunk, flow in enumerate(flows):
+        body = functools.partial(final_mlp_kernel, cuts(MLP_WAYS), per)
+        final_mlp(PLAIN + chunk, body, order.finish(flow))
+        order.tick(last)
     args = order.finish(last)
     grad_qkv_rows, grad_w_proj = run_kernel(
         functools.partial(final_attn_kernel, cuts(ATTN_WAYS), attn_per),
@@ -875,10 +926,13 @@
         ],
         [shape_of((3 * cols, dim), f32), shape_of((cols, dim), f32)],
         (4,),
-        9,
+        2,
         room=32,
     )
     grad_w_qkv = jnp.transpose(grad_qkv_rows.reshape(3, cols, dim), (2, 0, 1))
+    order.after(grad_w_proj[0, :1])
+    for chunk, summed in enumerate(plain_sums):
+        final_mlp(chunk, functools.partial(final_plain_kernel, per), [summed])
     return (
         output,
         grad_tokens,

time: 645 us -> 618 us (0.958)
  starting transfers between devices: 65.4 us -> 50.1 us
  local copies, waits for them, and re-layouts: 66.7 us -> 57 us
    ppermute x0 -> x4, waiting for transfers between devices: none -> 32.1 us  [rows_flow(): came = lax.ppermute(rows, 'dp', bit_pairs(bit))]
    ppermute x56 -> x32, starting transfers between devices: 61.9 us -> 42 us  [exchange(): lax.ppermute(value, 'dp', bit_pairs(bit))]
    all_gather x1 -> x0, waiting for transfers between devices: 18.4 us -> none  [fast_device(): all_rows = lax.all_gather(packed_rows, 'dp', axis=0, tiled=False)]
    ppermute x56 -> x32, waiting for transfers between devices: 123 us -> 110 us  [exchange(): lax.ppermute(value, 'dp', bit_pairs(bit))]
    add x0 -> x2, other arithmetic: none -> 10.5 us  [core_flow(): total, = (yield [own + came])]
    slice x18 -> x10, local copies, waits for them, and re-layouts: 21 us -> 11.7 us  [cut(): out = lax.slice(array, lo, hi)]
    add x39 -> x21, other arithmetic: 23 us -> 15.4 us  [reduce_flow(): cut(one, bits, route[stage], side, cols)]
    another operation x23 -> x13, other arithmetic: 17.3 us -> 10.4 us  [gather_flow(): joined.append(jnp.stack([one, two], axis=place))]
  transfers between devices with their start and end apart: 72 -> 52, of which waited for: 30 -> 23; matrix products, arithmetic and copies ran while one was open for 9% -> 16% of each run, Pallas kernels for 34% -> 38%
where the time goes in v3:
time: 618 us; the launch traced here: 610 us
  Pallas kernels  272 us (44%)
  waiting for transfers between devices  148 us (24%)
  local copies, waits for them, and re-layouts  57 us (9%)
  starting transfers between devices  50.1 us (8%)
  other arithmetic  47.8 us (8%)
  matrix products  18.8 us (3%)
  between operations  16.2 us (3%)
    pallas_call x15, Pallas kernels, run_kernel(): pl.pallas_call(body, out_shape=out_shape, grid_spec=pltpu.PrefetchScalarG...  272 us
    ppermute x32, waiting for transfers between devices, exchange(): lax.ppermute(value, 'dp', bit_pairs(bit))  110 us
    ppermute x32, starting transfers between devices, exchange(): lax.ppermute(value, 'dp', bit_pairs(bit))  42 us
    ppermute x4, waiting for transfers between devices, rows_flow(): came = lax.ppermute(rows, 'dp', bit_pairs(bit))  32.1 us
    unnamed x132, local copies, waits for them, and re-layouts  21.6 us
    add x21, other arithmetic, reduce_flow(): cut(one, bits, route[stage], side, cols)  15.4 us
  transfers between devices with their start and end apart: 52, of which 23 were waited for; matrix products, arithmetic and copies ran while one was open for 16% of the time, Pallas kernels for 38%

profile of v3, /device:TPU:0, one launch (start us, length us, event | category | flops | bytes accessed | tf_op | source)
XLA Modules:
  0.0 609.9 jit_solution(8511549561909639719)
XLA Ops:
  20.9 47.4 %shard_map.237 = (bf16[4,3456,256]{2,1,0:T(8,128)(2,1)}, bf16[4,16,256,256]{3,2,1,0:T(8,128)(2,1)}, bf16[4,1152,256]{2,1,0:T(8,128)(2,1)S(1)}, f32[4,256,1152]{2...) custom-call(s32[3]{0:T(128)S(1)} %pad_add_fusion.sc, ...), custom_call_target="tpu_custom_call" | custom-call | flops 51749998592 | bytes 45000000 | tf_op jit(solution)/shard_map/pallas_call | solution.py:380
  73.1 25.9 %shard_map.238 = (bf16[2,2304,1024]{2,1,0:T(8,128)(2,1)}, bf16[2,2304,1024]{2,1,0:T(8,128)(2,1)}, bf16[16,96,1152]{2,1,0:T(8,128)(2,1)}, bf16[16,96,1152]{2,1,0:T(8,128)(2,1)}, f32[2,8,768]{2,1,0:T(8,128)S(1)}) custom-call(s32[3]{0:T(128)S(1)} %pad_add_fusion.sc, bf16[1024,1152]{1,0:T(8,128)(2,1)S(1)} %bitcast.180, bf16[1024,1152]{1,0:T(8,128)(2,1)S(1)} %bitcast.183, ...), custom_call_target="tpu_custom_call" | custom-call | flops 32199999488 | bytes 28000000 | tf_op jit(solution)/shard_map/pallas_call | solution.py:380
  99.2 25.6 %shard_map.239 = (bf16[2,2304,1024]{2,1,0:T(8,128)(2,1)}, bf16[2,2304,1024]{2,1,0:T(8,128)(2,1)}, bf16[16,96,1152]{2,1,0:T(8,128)(2,1)}, bf16[16,96,1152]{2,1,0:T(8,128)(2,1)}, f32[2,8,768]{2,1,0:T(8,128)S(1)}) custom-call(s32[3]{0:T(128)S(1)} %pad_add_fusion.sc, bf16[1024,1152]{1,0:T(8,128)(2,1)S(1)} %bitcast.181, ...), custom_call_target="tpu_custom_call", output_to_operand_aliasing={{0}: (9, {}), {1}: (10, {})} | custom-call | flops 32199999488 | bytes 28000000 | tf_op jit(solution)/shard_map/pallas_call | solution.py:380
  126.5 5.9 add.275
  132.4 25.9 %shard_map.240 = (bf16[2,2304,1024]{2,1,0:T(8,128)(2,1)}, bf16[2,2304,1024]{2,1,0:T(8,128)(2,1)}, bf16[16,96,1152]{2,1,0:T(8,128)(2,1)}, bf16[16,96,1152]{2,1,0:T(8,128)(2,1)}, f32[2,8,768]{2,1,0:T(8,128)S(1)}) custom-call(s32[3]{0:T(128)S(1)} %pad_add_fusion.sc, bf16[1024,1152]{1,0:T(8,128)(2,1)S(1)} %bitcast.182, ...), custom_call_target="tpu_custom_call", output_to_operand_aliasing={{0}: (9, {}), {1}: (10, {})} | custom-call | flops 32199999488 | bytes 28000000 | tf_op jit(solution)/shard_map/pallas_call | solution.py:380
  163.7 25.1 %shard_map.241 = (f32[4,256,1152]{2,1,0:T(8,128)S(1)}, bf16[4,256,1152]{2,1,0:T(8,128)(2,1)S(1)}, f32[4,4,1152]{2,1,0:T(4,128)S(1)}) custom-call(s32[3]{0:T(128)S(1)} %pad_add_fusion.sc, bf16[2,2304,1024]{2,1,0:T(8,128)(2,1)} %get-tuple-element.280.back, bf16[1152,2304]{1,0:T(8,128)(2,1)} %w_up0.7, bf16[1152,2304]{1,0:T(8,128)(2,1)} %collective-permute-done.4.w_up1, ...), custom_call_target="tpu_custom_call" | custom-call | flops 69000003584 | bytes 41582592 | tf_op jit(solution)/shard_map/pallas_call | solution.py:380
  203.7 17.8 %shard_map.242.refs_0_ = bf16[2,3456,256]{2,1,0:T(8,128)(2,1)S(1)} custom-call(s32[3]{0:T(128)S(1)} %pad_add_fusion.sc, bf16[4,256,1152]{2,1,0:T(8,128)(2,1)S(1)} %copy-done.34, bf16[4,3456,256]{2,1,0:T(8,128)(2,1)} %get-tuple-element.292.qkv, bf16[4,16,256,256]{3,2,1,0:T(8,128)(2,1)} %get-tuple-element.293.prob, bf16[576,1152]{1,0:T(8,128)(2,1)S(1)} %copy-done.8, ...), custom_call_target="tpu_custom_call" | custom-call | flops 69000003584 | bytes 24018944 | tf_op jit(solution)/shard_map/pallas_call | solution.py:380
  221.6 7.5 %collective-permute-done.11 = bf16[2,2,2,96,512]{4,3,0,1,2:T(8,128)(2,1)S(1)} collective-permute-done((bf16[2,2,2,96,512]{4,3,0,1,2:T(8,128)(2,1)S(1)}, bf16[2,2,2,96,512]{4,3,0,1,2:T(8,128)(2,1)S(1)}, u32[]{:S(2)}, u32[]{:S(2)}) %collective-permute-start.11) | collective-permute-done | bytes 786464 | tf_op jit(solution)/shard_map/ppermute | solution.py:438
  238.5 17.8 %shard_map.243.refs_1_ = bf16[2,3456,256]{2,1,0:T(8,128)(2,1)S(1)} custom-call(s32[3]{0:T(128)S(1)} %pad_add_fusion.sc, bf16[4,256,1152]{2,1,0:T(8,128)(2,1)S(1)} %copy-done.34, bf16[4,3456,256]{2,1,0:T(8,128)(2,1)} %get-tuple-element.292.qkv, bf16[4,16,256,256]{3,2,1,0:T(8,128)(2,1)} %get-tuple-element.293.prob, bf16[576,1152]{1,0:T(8,128)(2,1)S(1)} %copy-done.8, ...), custom_call_target="tpu_custom_call" | custom-call | flops 69000003584 | bytes 24018944 | tf_op jit(solution)/shard_map/pallas_call | solution.py:380
  260.1 11.1 %shard_map.244 = (bf16[16,144,1152]{2,1,0:T(8,128)(2,1)}, f32[3,8,576]{2,1,0:T(8,128)S(1)}) custom-call(s32[3]{0:T(128)S(1)} %pad_add_fusion.sc, bf16[2,3456,256]{2,1,0:T(8,128)(2,1)S(1)} %shard_map.242.refs_0_, bf16[2,3456,256]{2,1,0:T(8,128)(2,1)S(1)} %shard_map.243.refs_1_, bf16[4,1152,256]{2,1,0:T(8,128)(2,1)S(1)} %copy-done.23, ...), custom_call_target="tpu_custom_call" | custom-call | flops 69000003584 | bytes 19519488 | tf_op jit(solution)/shard_map/pallas_call | solution.py:380
  284.4 10.9 %shard_map.245 = (bf16[16,144,1152]{2,1,0:T(8,128)(2,1)}, f32[3,8,576]{2,1,0:T(8,128)S(1)}) custom-call(s32[3]{0:T(128)S(1)} %pad_add_fusion.sc, bf16[2,3456,256]{2,1,0:T(8,128)(2,1)S(1)} %copy-done.28, bf16[2,3456,256]{2,1,0:T(8,128)(2,1)S(1)} %copy-done.31, bf16[4,1152,256]{2,1,0:T(8,128)(2,1)S(1)} %copy-done.23, bf16[4,256,1152]{2,1,0:T(8,128)(2,1)S(1)} %copy-done.26, ...), custom_call_target="tpu_custom_call" | custom-call | flops 69000003584 | bytes 19519488 | tf_op jit(solution)/shard_map/pallas_call | solution.py:380
  312.0 24.4 %shard_map.246 = (f32[8,256,1152]{2,1,0:T(8,128)}, f32[4,256,1152]{2,1,0:T(8,128)}, f32[4,2,1152]{2,1,0:T(2,128)S(1)}) custom-call(s32[3]{0:T(128)S(1)} %pad_add_fusion.sc, bf16[2,3456,256]{2,1,0:T(8,128)(2,1)S(1)} %copy-done.29, bf16[2,3456,256]{2,1,0:T(8,128)(2,1)S(1)} %copy-done.32, bf16[1728,1152]{1,0:T(8,128)(2,1)S(1)} %bitcast.177, ...), custom_call_target="tpu_custom_call" | custom-call | flops 69000003584 | bytes 38891520 | tf_op jit(solution)/shard_map/pallas_call | solution.py:380
  347.4 21.6 %shard_map.247 = (bf16[8,256,1152]{2,1,0:T(8,128)(2,1)}, bf16[4,256,1152]{2,1,0:T(8,128)(2,1)S(1)}, f32[4,1,1152]{2,1,0:T(1,128)S(1)}) custom-call(s32[3]{0:T(128)S(1)} %pad_add_fusion.sc, bf16[2,2304,1024]{2,1,0:T(8,128)(2,1)} %get-tuple-element.359.act, bf16[2304,1152]{1,0:T(8,128)(2,1)} %w_down0.7, bf16[2304,1152]{1,0:T(8,128)(2,1)} %collective-permute-done.5.w_down1, ...), custom_call_target="tpu_custom_call" | custom-call | flops 69000003584 | bytes 36813312 | tf_op jit(solution)/shard_map/pallas_call | solution.py:380
  380.8 6.1 %convolution_convert_fusion = bf16[8,1152]{1,0:T(8,128)(2,1)S(1)} fusion(bf16[8,3456]{1,0:T(8,128)(2,1)S(1)} %maximum_select_fusion, bf16[1152,3456]{1,0:T(8,128)(2,1)} %param.25), kind=kOutput, calls=%fused_computation.1 | convolution fusion | flops 63710208 | bytes 8036352 | tf_op jit(solution)/shard_map/dot_general | solution.py:977
  387.0 9.6 %collective-permute-done.23 = bf16[2,2,144,256]{3,2,0,1:T(8,128)(2,1)S(1)} collective-permute-done((bf16[2,2,144,256]{3,2,0,1:T(8,128)(2,1)}, bf16[2,2,144,256]{3,2,0,1:T(8,128)(2,1)S(1)}, u32[]{:S(2)}, u32[]{:S(2)}) %collective-permute-start.23) | collective-permute-done | bytes 294944 | tf_op jit(solution)/shard_map/ppermute | solution.py:438
  397.1 10.2 %collective-permute-done.24 = bf16[2,96,1152]{2,1,0:T(8,128)(2,1)S(1)} collective-permute-done((bf16[2,96,1152]{2,1,0:T(8,128)(2,1)S(1)}, bf16[2,96,1152]{2,1,0:T(8,128)(2,1)S(1)}, u32[]{:S(2)}, u32[]{:S(2)}) %collective-permute-start.24) | collective-permute-done | bytes 442400 | tf_op jit(solution)/shard_map/ppermute | solution.py:438
  419.4 7.3 %collective-permute-done.28 = bf16[2,2,96,512]{3,2,1,0:T(8,128)(2,1)S(1)} collective-permute-done((bf16[2,2,96,512]{3,2,1,0:T(8,128)(2,1)S(1)}, bf16[2,2,96,512]{3,2,1,0:T(8,128)(2,1)S(1)}, u32[]{:S(2)}, u32[]{:S(2)}) %collective-permute-start.28) | collective-permute-done | bytes 393248 | tf_op jit(solution)/shard_map/ppermute | solution.py:438
  426.7 22.5 %collective-permute-done.25 = bf16[2,144,896]{2,1,0:T(8,128)(2,1)} collective-permute-done((bf16[2,144,896]{2,1,0:T(8,128)(2,1)}, bf16[2,144,896]{2,1,0:T(8,128)(2,1)}, u32[]{:S(2)}, u32[]{:S(2)}) %collective-permute-start.25) | collective-permute-done | bytes 516128 | tf_op jit(solution)/shard_map/ppermute | solution.py:438
  455.1 10.8 %collective-permute-done.32 = bf16[144,256]{1,0:T(8,128)(2,1)S(1)} collective-permute-done((bf16[144,256]{1,0:T(8,128)(2,1)S(1)}, bf16[144,256]{1,0:T(8,128)(2,1)S(1)}, u32[]{:S(2)}, u32[]{:S(2)}) %collective-permute-start.32) | collective-permute-done | bytes 73760 | tf_op jit(solution)/shard_map/ppermute | solution.py:438
  470.6 8.5 %collective-permute-done.31 = bf16[144,896]{1,0:T(8,128)(2,1)S(1)} collective-permute-done((bf16[144,896]{1,0:T(8,128)(2,1)S(1)}, bf16[144,896]{1,0:T(8,128)(2,1)S(1)}, u32[]{:S(2)}, u32[]{:S(2)}) %collective-permute-start.31) | collective-permute-done | bytes 258080 | tf_op jit(solution)/shard_map/ppermute | solution.py:438
  492.3 14.0 %collective-permute-done.41 = bf16[52,3456]{1,0:T(8,128)(2,1)S(1)} collective-permute-done((bf16[52,3456]{1,0:T(8,128)(2,1)S(1)}, bf16[52,3456]{1,0:T(8,128)(2,1)S(1)}, u32[]{:S(2)}, u32[]{:S(2)}) %collective-permute-start.41) | collective-permute-done | bytes 359456 | tf_op jit(solution)/shard_map/ppermute | solution.py:513
  518.0 14.9 %collective-permute-done.42 = bf16[104,3456]{1,0:T(8,128)(2,1)S(1)} collective-permute-done((bf16[104,3456]{1,0:T(8,128)(2,1)S(1)}, bf16[104,3456]{1,0:T(8,128)(2,1)S(1)}, u32[]{:S(2)}, u32[]{:S(2)}) %collective-permute-start.42) | collective-permute-done | bytes 718880 | tf_op jit(solution)/shard_map/ppermute | solution.py:513
  573.9 8.1 %fusion.6 = f32[1152,3456]{1,0:T(8,128)} fusion(bf16[128,1152]{1,0:T(8,128)(2,1)S(1)} %reshape.239, bf16[16,13,3456]{2,1,0:T(8,128)(2,1)S(1)} %copy-done.37), kind=kOutput, calls=%fused_computation.23 | convolution fusion | flops 1019215872 | bytes 17104896 | tf_op jit(solution)/shard_map/dot_general | solution.py:971
  595.5 7.1 %shard_map.248 = (f32[1728,1152]{1,0:T(8,128)}, f32[576,1152]{1,0:T(8,128)}) custom-call(s32[3]{0:T(128)S(1)} %pad_add_fusion.sc, bf16[8,144,512]{2,1,0:T(8,128)(2,1)S(1)} %bitcast.166, bf16[8,144,512]{2,1,0:T(8,128)(2,1)S(1)} %bitcast.167, bf16[8,144,384]{2,1,0:T(8,128)(2,1)S(1)} %bitcast.170, bf16[8,144,384]{2,1,0:T(8,128)(2,1)} %bitcast.89.refs_3_, ...), custom_call_target="tpu_custom_call" | custom-call | flops 2300000000 | bytes 2000000 | tf_op jit(solution)/shard_map/pallas_call | solution.py:380
  (346 shorter events, 207.6 us)
Async XLA Ops:
  7.2 578.5 %all-reduce.4.cloned.1.call-start = ((), (), s32[]{:S(2)}) async-start(), calls=%async_computation | async-start | bytes 14155776 | tf_op jit(solution)/shard_map/psum | solution.py:682
  14.6 55.1 %collective-permute-start.4 = (bf16[1152,2304]{1,0:T(8,128)(2,1)}, bf16[1152,2304]{1,0:T(8,128)(2,1)}, u32[]{:S(2)}, u32[]{:S(2)}) collective-permute-start(bf16[1152,2304]{1,0:T(8,128)(2,1)} %w_up0.7), channel_id=1, source_target_pairs={{0,1},{1,0},{2,3},{3,2},{4,5},{5,4},{6,7},{7,6},{8,9},{9,8},{10,11... | collective-permute-start | bytes 15925256 | tf_op jit(solution)/shard_map/ppermute | solution.py:411
  14.9 54.8 %collective-permute-start.5 = (bf16[2304,1152]{1,0:T(8,128)(2,1)}, bf16[2304,1152]{1,0:T(8,128)(2,1)}, u32[]{:S(2)}, u32[]{:S(2)}) collective-permute-start(bf16[2304,1152]{1,0:T(8,128)(2,1)} %w_down0.7), channel_id=1, source_target_pairs={{0,1},{1,0},{2,3},{3,2},{4,5},{5,4},{6,7},{7,6},{8,9},{9,8},{10,11... | collective-permute-start | bytes 15925256 | tf_op jit(solution)/shard_map/ppermute | solution.py:411
  16.3 53.4 %collective-permute-start.6 = (bf16[1,2304]{1,0:T(2,128)(2,1)S(1)}, bf16[1,2304]{1,0:T(2,128)(2,1)S(1)}, u32[]{:S(2)}, u32[]{:S(2)}) collective-permute-start(bf16[1,2304]{1,0:T(2,128)(2,1)S(1)} %broadcast_in_dim.35), channel_id=1, source_target_pairs={{0,1},{1,0},{2,3},{3,2},{4,5},{5,4},{6,7},{7,6},{8,9},{9,8},{10,11... | collective-permute-start | bytes 13832 | tf_op jit(solution)/shard_map/ppermute | solution.py:411
  99.0 25.8 %collective-permute-start.7 = (bf16[16,96,1152]{2,1,0:T(8,128)(2,1)}, bf16[16,96,1152]{2,1,0:T(8,128)(2,1)}, u32[]{:S(2)}, u32[]{:S(2)}) collective-permute-start(bf16[16,96,1152]{2,1,0:T(8,128)(2,1)} %get-tuple-element.263), channel_id=1, source_target_pairs={{0,1},{1,0},{2,3},{3,2},{4,5},{5,4},{6,7},{7,6},{8,9},{9,8},{10,11... | collective-permute-start | bytes 10616840 | tf_op jit(solution)/shard_map/ppermute | solution.py:411
  124.8 34.1 %collective-permute-start.8 = (bf16[16,96,1152]{2,1,0:T(8,128)(2,1)}, bf16[16,96,1152]{2,1,0:T(8,128)(2,1)}, u32[]{:S(2)}, u32[]{:S(2)}) collective-permute-start(bf16[16,96,1152]{2,1,0:T(8,128)(2,1)} %get-tuple-element.274), channel_id=1, source_target_pairs={{0,1},{1,0},{2,3},{3,2},{4,5},{5,4},{6,7},{7,6},{8,9},{9,8},{10,11... | collective-permute-start | bytes 10616840 | tf_op jit(solution)/shard_map/ppermute | solution.py:411
  163.6 28.8 %collective-permute-start.9 = (bf16[16,96,1152]{2,1,0:T(8,128)(2,1)}, bf16[16,96,1152]{2,1,0:T(8,128)(2,1)}, u32[]{:S(2)}, u32[]{:S(2)}) collective-permute-start(bf16[16,96,1152]{2,1,0:T(8,128)(2,1)} %get-tuple-element.286), channel_id=1, source_target_pairs={{0,1},{1,0},{2,3},{3,2},{4,5},{5,4},{6,7},{7,6},{8,9},{9,8},{10,11... | collective-permute-start | bytes 10616840 | tf_op jit(solution)/shard_map/ppermute | solution.py:411
  199.3 29.8 %collective-permute-start.11 = (bf16[2,2,2,96,512]{4,3,0,1,2:T(8,128)(2,1)S(1)}, bf16[2,2,2,96,512]{4,3,0,1,2:T(8,128)(2,1)S(1)}, u32[]{:S(2)}, u32[]{:S(2)}) collective-permute-start(bf16[2,2,2,96,512]{4,3,0,1,2:T(8,128)(2,1)S(1)} %get-tuple-element.298), channel_id=1, source_target_pairs={{0,4},{2,6},{4,0},{6,2},{8,12},{10,14},{12,8},{14,10},{16,20},{18,... | collective-permute-start | bytes 2359304 | tf_op jit(solution)/shard_map/ppermute | solution.py:438
  202.2 32.3 %collective-permute-start.10 = (bf16[2,2,2,96,640]{4,3,0,1,2:T(8,128)(2,1)S(1)}, bf16[2,2,2,96,640]{4,3,0,1,2:T(8,128)(2,1)S(1)}, u32[]{:S(2)}, u32[]{:S(2)}) collective-permute-start(bf16[2,2,2,96,640]{4,3,0,1,2:T(8,128)(2,1)S(1)} %get-tuple-element.297), channel_id=1, source_target_pairs={{0,2},{2,0},{4,6},{6,4},{8,10},{10,8},{12,14},{14,12},{16,18},{18,... | collective-permute-start | bytes 2949128 | tf_op jit(solution)/shard_map/ppermute | solution.py:438
  309.0 27.5 %collective-permute-start.20 = (bf16[96,1152]{1,0:T(8,128)(2,1)S(1)}, bf16[96,1152]{1,0:T(8,128)(2,1)}, u32[]{:S(2)}, u32[]{:S(2)}) collective-permute-start(bf16[96,1152]{1,0:T(8,128)(2,1)S(1)} %add.317), channel_id=1, source_target_pairs={{0,16},{2,18},{4,20},{6,22},{8,24},{10,26},{12,28},{14,30},{16,0},... | collective-permute-start | bytes 663560 | tf_op jit(solution)/shard_map/ppermute | solution.py:438
  309.0 27.5 %collective-permute-start.19 = (bf16[2,2,2,144,256]{4,3,1,2,0:T(8,128)(2,1)}, bf16[2,2,2,144,256]{4,3,1,2,0:T(8,128)(2,1)}, u32[]{:S(2)}, u32[]{:S(2)}) collective-permute-start(bf16[2,2,2,144,256]{4,3,1,2,0:T(8,128)(2,1)} %fusion.13), channel_id=1, source_target_pairs={{0,8},{2,10},{4,12},{6,14},{8,0},{10,2},{12,4},{14,6},{16,24},{18,... | collective-permute-start | bytes 1769480 | tf_op jit(solution)/shard_map/ppermute | solution.py:438
  310.2 26.3 %collective-permute-start.18 = (bf16[2,2,2,144,384]{4,3,0,1,2:T(8,128)(2,1)}, bf16[2,2,2,144,384]{4,3,0,1,2:T(8,128)(2,1)S(1)}, u32[]{:S(2)}, u32[]{:S(2)}) collective-permute-start(bf16[2,2,2,144,384]{4,3,0,1,2:T(8,128)(2,1)} %fusion.5), channel_id=1, source_target_pairs={{0,4},{2,6},{4,0},{6,2},{8,12},{10,14},{12,8},{14,10},{16,20},{18,... | collective-permute-start | bytes 2654216 | tf_op jit(solution)/shard_map/ppermute | solution.py:438
  311.4 28.5 %collective-permute-start.17 = (bf16[2,2,2,144,512]{4,3,0,1,2:T(8,128)(2,1)}, bf16[2,2,2,144,512]{4,3,0,1,2:T(8,128)(2,1)}, u32[]{:S(2)}, u32[]{:S(2)}) collective-permute-start(bf16[2,2,2,144,512]{4,3,0,1,2:T(8,128)(2,1)} %fusion.1), channel_id=1, source_target_pairs={{0,2},{2,0},{4,6},{6,4},{8,10},{10,8},{12,14},{14,12},{16,18},{18,... | collective-permute-start | bytes 3538952 | tf_op jit(solution)/shard_map/ppermute | solution.py:438
  371.0 111.3 %collective-permute-start.36 = (f32[4,256,1152]{2,1,0:T(8,128)}, f32[4,256,1152]{2,1,0:T(8,128)}, u32[]{:S(2)}, u32[]{:S(2)}) collective-permute-start(f32[4,256,1152]{2,1,0:T(8,128)} %get-tuple-element.415), channel_id=1, source_target_pairs={{0,1},{1,0},{2,3},{3,2},{4,5},{5,4},{6,7},{7,6},{8,9},{9,8},{10,11... | collective-permute-start | bytes 14155784 | tf_op jit(solution)/shard_map/ppermute | solution.py:411
  371.6 25.0 %collective-permute-start.23 = (bf16[2,2,144,256]{3,2,0,1:T(8,128)(2,1)}, bf16[2,2,144,256]{3,2,0,1:T(8,128)(2,1)S(1)}, u32[]{:S(2)}, u32[]{:S(2)}) collective-permute-start(bf16[2,2,144,256]{3,2,0,1:T(8,128)(2,1)} %get-tuple-element.368), channel_id=1, source_target_pairs={{0,16},{2,18},{4,20},{6,22},{8,24},{10,26},{12,28},{14,30},{16,0},... | collective-permute-start | bytes 884744 | tf_op jit(solution)/shard_map/ppermute | solution.py:438
  374.7 32.6 %collective-permute-start.24 = (bf16[2,96,1152]{2,1,0:T(8,128)(2,1)S(1)}, bf16[2,96,1152]{2,1,0:T(8,128)(2,1)S(1)}, u32[]{:S(2)}, u32[]{:S(2)}) collective-permute-start(bf16[2,96,1152]{2,1,0:T(8,128)(2,1)S(1)} %pad_maximum_fusion.13), channel_id=1, source_target_pairs={{0,8},{2,10},{4,12},{6,14},{8,0},{10,2},{12,4},{14,6},{16,24},{18,... | collective-permute-start | bytes 1327112 | tf_op jit(solution)/shard_map/ppermute | solution.py:438
  376.4 30.9 %collective-permute-start.21 = (bf16[2,2,144,512]{3,2,0,1:T(8,128)(2,1)}, bf16[2,2,144,512]{3,2,0,1:T(8,128)(2,1)S(1)}, u32[]{:S(2)}, u32[]{:S(2)}) collective-permute-start(bf16[2,2,144,512]{3,2,0,1:T(8,128)(2,1)} %get-tuple-element.366), channel_id=1, source_target_pairs={{0,4},{2,6},{4,0},{6,2},{8,12},{10,14},{12,8},{14,10},{16,20},{18,... | collective-permute-start | bytes 1769480 | tf_op jit(solution)/shard_map/ppermute | solution.py:438
  396.6 69.3 %collective-permute-start.30 = (bf16[4,256,1152]{2,1,0:T(8,128)(2,1)S(1)}, bf16[4,256,1152]{2,1,0:T(8,128)(2,1)}, u32[]{:S(2)}, u32[]{:S(2)}) collective-permute-start(bf16[4,256,1152]{2,1,0:T(8,128)(2,1)S(1)} %get-tuple-element.396), channel_id=1, source_target_pairs={{0,1},{1,0},{2,3},{3,2},{4,5},{5,4},{6,7},{7,6},{8,9},{9,8},{10,11... | collective-permute-start | bytes 7077896 | tf_op jit(solution)/shard_map/ppermute | solution.py:411
  413.9 35.4 %collective-permute-start.25 = (bf16[2,144,896]{2,1,0:T(8,128)(2,1)}, bf16[2,144,896]{2,1,0:T(8,128)(2,1)}, u32[]{:S(2)}, u32[]{:S(2)}) collective-permute-start(bf16[2,144,896]{2,1,0:T(8,128)(2,1)} %pad_maximum_fusion.7), channel_id=1, source_target_pairs={{0,8},{2,10},{4,12},{6,14},{8,0},{10,2},{12,4},{14,6},{16,24},{18,... | collective-permute-start | bytes 1548296 | tf_op jit(solution)/shard_map/ppermute | solution.py:438
  452.6 27.4 %collective-permute-start.33 = (bf16[2,2,2,96,640]{4,3,1,0,2:T(8,128)(2,1)S(1)}, bf16[2,2,2,96,640]{4,3,1,0,2:T(8,128)(2,1)}, u32[]{:S(2)}, u32[]{:S(2)}) collective-permute-start(bf16[2,2,2,96,640]{4,3,1,0,2:T(8,128)(2,1)S(1)} %pad_maximum_fusion.2), channel_id=1, source_target_pairs={{0,2},{2,0},{4,6},{6,4},{8,10},{10,8},{12,14},{14,12},{16,18},{18,... | collective-permute-start | bytes 2949128 | tf_op jit(solution)/shard_map/ppermute | solution.py:438
  453.1 26.1 %collective-permute-start.34 = (bf16[2,2,2,96,512]{4,3,2,1,0:T(8,128)(2,1)S(1)}, bf16[2,2,2,96,512]{4,3,2,1,0:T(8,128)(2,1)S(1)}, u32[]{:S(2)}, u32[]{:S(2)}) collective-permute-start(bf16[2,2,2,96,512]{4,3,2,1,0:T(8,128)(2,1)S(1)} %pad_maximum_fusion.4), channel_id=1, source_target_pairs={{0,4},{2,6},{4,0},{6,2},{8,12},{10,14},{12,8},{14,10},{16,20},{18,... | collective-permute-start | bytes 2359304 | tf_op jit(solution)/shard_map/ppermute | solution.py:438
  490.4 42.5 %collective-permute-start.43 = (bf16[2,144,896]{2,1,0:T(8,128)(2,1)S(1)}, bf16[2,144,896]{2,1,0:T(8,128)(2,1)S(1)}, u32[]{:S(2)}, u32[]{:S(2)}) collective-permute-start(bf16[2,144,896]{2,1,0:T(8,128)(2,1)S(1)} %pad_maximum_fusion.9), channel_id=1, source_target_pairs={{0,8},{2,10},{4,12},{6,14},{8,0},{10,2},{12,4},{14,6},{16,24},{18,... | collective-permute-start | bytes 1548296 | tf_op jit(solution)/shard_map/ppermute | solution.py:438
  506.4 26.5 %collective-permute-start.42 = (bf16[104,3456]{1,0:T(8,128)(2,1)S(1)}, bf16[104,3456]{1,0:T(8,128)(2,1)S(1)}, u32[]{:S(2)}, u32[]{:S(2)}) collective-permute-start(bf16[104,3456]{1,0:T(8,128)(2,1)S(1)} %pad_maximum_fusion.5), channel_id=1, source_target_pairs={{0,16},{2,18},{4,20},{6,22},{8,24},{10,26},{12,28},{14,30},{16,0},... | collective-permute-start | bytes 2156552 | tf_op jit(solution)/shard_map/ppermute | solution.py:513
  557.9 25.0 %collective-permute-start.48 = (bf16[2,2,2,144,512]{4,3,1,0,2:T(8,128)(2,1)}, bf16[2,2,2,144,512]{4,3,1,0,2:T(8,128)(2,1)}, u32[]{:S(2)}, u32[]{:S(2)}) collective-permute-start(bf16[2,2,2,144,512]{4,3,1,0,2:T(8,128)(2,1)} %pad_maximum_fusion.1), channel_id=1, source_target_pairs={{0,2},{2,0},{4,6},{6,4},{8,10},{10,8},{12,14},{14,12},{16,18},{18,... | collective-permute-start | bytes 3538952 | tf_op jit(solution)/shard_map/ppermute | solution.py:438
  (94 other events, 1280.7 us)
Sparse Core Ops, SparseCore 0:
  192.5 269.7 all-reduce.3

commit v4 on v2

--- a/solution.py
+++ b/solution.py
@@ -102,22 +102,27 @@
     normed_mlp[0] = (unit * (1.0 + mod[0, 4:5, :]) + mod[0, 3:4, :]).astype(bf16)
 
 
-def mlp_kernel(
-    per, steps, sc, rows, grad_mlp, w_up0, w_up1, w_down0, w_down1, bias0, bias1, act_in, back_in,
-    act, back, grad_own, grad_other, sums
-):
-    part, step = pl.program_id(0), pl.program_id(1)
-
-    @pl.when(part == 0)
-    def _():
-        mlp_block(per, step, sc, rows, grad_mlp, w_up0, w_down0, bias0, act, back, grad_own, sums)
-
-    @pl.when(part == 1)
-    def _():
-        mlp_block(per, step, sc, rows, grad_mlp, w_up1, w_down1, bias1, act, back, grad_other, sums)
-
-
-def mlp_block(per, step, sc, rows, grad_mlp, w_up, w_down, bias, act, back, grads, sums):
+def mlp_kernel(per, jobs, sc, rows, grad_mlp, *refs):
+    count = len(jobs)
+    weights = [refs[3 * k : 3 * k + 3] for k in range(count)]
+    refs = refs[3 * count :]
+    came = []
+    for _, summed in jobs:
+        came.append(refs[0] if summed else None)
+        refs = refs[1:] if summed else refs
+    act, back = refs[2], refs[3]
+    grads, sums = refs[4 : 4 + count], refs[4 + count :]
+    job, step = pl.program_id(0), pl.program_id(1)
+    for k in range(count):
+
+        @pl.when(job == k)
+        def _(k=k):
+            mlp_block(
+                per, jobs[k][0], step, sc, rows, grad_mlp, *weights[k], act, back, grads[k], sums[k], came[k]
+            )
+
+
+def mlp_block(per, natural, step, sc, rows, grad_mlp, w_up, w_down, bias, act, back, grads, sums, came):
     here = w_down.shape[0] // per
     hidden = lax.dot_general(
         w_up[...], rows[...], (((0,), (1,)), ((), ())), preferred_element_type=f32
@@ -132,14 +137,18 @@
     back_b = (dot_nt(w_down[...], grad_mlp[...]) * slope).astype(bf16)
     act[0] = act_b
     back[0] = back_b
-    sums[0] = dot_nt(jnp.ones((8, rows.shape[0]), bf16), back_b)
-    grad_down = dot_nn(act_b, grad_mlp[...]).astype(bf16)
-    grad_up = dot_nn(back_b, rows[...]).astype(bf16)
-    for piece in range(here):
-        at = jnp.bitwise_xor(step * here + piece, sc[2])
-        lo = piece * per
-        grads[at, 0:per, :] = grad_down[lo : lo + per]
-        grads[at, per : 2 * per, :] = grad_up[lo : lo + per]
+    sums[...] = dot_nt(jnp.ones((8, rows.shape[0]), bf16), back_b)
+    for lo_row, left, right in ((0, act_b, grad_mlp), (per, back_b, rows)):
+        grad = dot_nn(left, right[...])
+        for piece in range(here):
+            value = grad[piece * per : (piece + 1) * per]
+            if natural:
+                if came is not None:
+                    value = value + came[piece, lo_row : lo_row + per, :].astype(f32)
+                grads[piece, lo_row : lo_row + per, :] = value.astype(bf16)
+            else:
+                at = jnp.bitwise_xor(step * here + piece, sc[2])
+                grads[at, lo_row : lo_row + per, :] = value.astype(bf16)
 
 
 def grow(total, part_steps, left, rights, dims):
@@ -343,6 +352,15 @@
     mark[...] = jnp.zeros_like(mark)
 
 
+def final_plain_kernel(per, sc, summed, down_in, up_in, down, up, mark, turned):
+    for piece in range(summed.shape[0]):
+        lo = piece * per
+        down[lo : lo + per, :] = summed[piece, 0:per, :].astype(f32)
+        turned[lo : lo + per, :] = summed[piece, per : 2 * per, :].astype(f32)
+    up[...] = turned[...].T
+    mark[...] = jnp.zeros_like(mark)
+
+
 def final_attn_kernel(cuts, per, sc, *refs):
     count = 2 * len(cuts)
     arrays, (qkv, proj) = refs[:count], refs[count:]
@@ -378,7 +396,7 @@
         ),
         compiler_params=pltpu.CompilerParams(vmem_limit_bytes=room << 20),
         cost_estimate=pl.CostEstimate(
-            flops=int(micros * 1.15e9), bytes_accessed=int(size), transcendentals=0
+            flops=int(micros * 1.15e9), bytes_accessed=int(min(size, micros * 1e6)), transcendentals=0
         ),
         input_output_aliases=alias or {},
     )(sc, *args)
@@ -487,6 +505,24 @@
     return (yield from gather_flow(ways, have))
 
 
+def swap_flow(other):
+    (other,) = yield [other]
+    came = swap_cores(other)
+    yield None
+    (came,) = yield [came]
+    return came
+
+
+def rows_flow(rows):
+    for bit in (3, 2, 1, 0):
+        (rows,) = yield [rows]
+        came = lax.ppermute(rows, "dp", bit_pairs(bit))
+        yield None
+        rows, came = yield [rows, came]
+        rows = jnp.concatenate([rows, came])
+    return rows
+
+
 class Order:
     def __init__(self, sc):
         self.sc = sc
@@ -520,6 +556,7 @@
 
 
 CHUNKS = 3
+PLAIN = 2
 
 
 def fill_other(both, came, core):
@@ -591,7 +628,6 @@
         ],
         (images,),
         45,
-        room=44,
     )
     order.after(down_sums)
 
@@ -603,45 +639,82 @@
     block = width // steps
     anywhere = pl.BlockSpec(memory_space=pl.ANY)
     act = back = jnp.zeros((8, 128), bf16)
-    flows, up_sums = [], []
-    for chunk in range(CHUNKS):
-        at = chunk * steps
-
-        def pick(which, at=at):
-            rest = (steps - 1) * (1 - which)
-            return lambda p, s, c: at + jnp.where(p == which, s, rest)
-
-        def up_map(which):
-            return lambda p, s, c: (0, pick(which)(p, s, c))
-
-        def down_map(which):
-            return lambda p, s, c: (pick(which)(p, s, c), 0)
-
-        spread = pl.BlockSpec((1, block, count), lambda p, s, c, at=at: (p, at + s, 0))
-        act, back, grad_own, grad_other, sums = run_kernel(
-            functools.partial(mlp_kernel, per, steps),
+    up_sums = {}
+
+    def mlp_call(jobs, came, micros):
+        nonlocal act, back
+        first = act.shape[0] == 8
+        kinds = tuple((chunk < PLAIN, (chunk, part) in came) for chunk, part in jobs)
+
+        def turn(k):
+            return lambda p, s, c: jnp.clip((p - k) * steps + s, 0, steps - 1)
+
+        def pick(values):
+            return lambda p: sum(jnp.where(p == k, value, 0) for k, value in enumerate(values))
+
+        parts = pick([part for _, part in jobs])
+        starts = pick([chunk * steps for chunk, _ in jobs])
+        spread = pl.BlockSpec((1, block, count), lambda p, s, c: (parts(p), starts(p) + s, 0))
+        args, specs = [], []
+        for k, (chunk, part) in enumerate(jobs):
+            at = chunk * steps
+            wide = lambda p, s, c, k=k, at=at: (0, at + turn(k)(p, s, c))
+            tall = lambda p, s, c, k=k, at=at: (at + turn(k)(p, s, c), 0)
+            args += [wu[part], wd[part], up_bias[part]]
+            specs += [
+                pl.BlockSpec((dim, block), wide),
+                pl.BlockSpec((block, dim), tall),
+                pl.BlockSpec((1, block), wide),
+            ]
+        grad_specs = []
+        for k, (natural, _) in enumerate(kinds):
+            own = lambda p, s, c, k=k: (turn(k)(p, s, c), 0, 0)
+            fixed = lambda p, s, c: (0, 0, 0)
+            grad_specs.append(
+                pl.BlockSpec((16 // steps, 2 * per, dim), own)
+                if natural
+                else pl.BlockSpec((16, 2 * per, dim), fixed)
+            )
+        for k, job in enumerate(jobs):
+            if job in came:
+                args.append(came[job])
+                specs.append(grad_specs[k])
+        args += [act, back]
+        spot = len(args) + 1
+        outs = run_kernel(
+            functools.partial(mlp_kernel, per, kinds),
             order.sc,
-            [rows_flat, grad_flat] + wu + wd + up_bias + [act, back],
-            [whole_block(rows_flat), whole_block(grad_flat)]
-            + [pl.BlockSpec((dim, block), up_map(which)) for which in range(2)]
-            + [pl.BlockSpec((block, dim), down_map(which)) for which in range(2)]
-            + [pl.BlockSpec((1, block), up_map(which)) for which in range(2)]
-            + [anywhere, anywhere],
+            [rows_flat, grad_flat] + args,
+            [whole_block(rows_flat), whole_block(grad_flat)] + specs + [anywhere, anywhere],
             [spread, spread]
-            + [pl.BlockSpec((16, 2 * per, dim), lambda p, s, c: (0, 0, 0))] * 2
-            + [pl.BlockSpec((1, 8, block), lambda p, s, c: (p, 0, s))],
+            + grad_specs
+            + [pl.BlockSpec((8, block), lambda p, s, c, k=k: (0, turn(k)(p, s, c))) for k in range(len(jobs))],
             [shape_of((2, ff, count), bf16)] * 2
-            + [shape_of((16, 2 * per, dim), bf16)] * 2
-            + [shape_of((2, 8, width), f32)],
-            (2, steps),
-            28,
-            alias=None if chunk == 0 else {9: 0, 10: 1},
-            room=48,
+            + [shape_of((16, 2 * per, dim), bf16)] * len(jobs)
+            + [shape_of((8, width), f32)] * len(jobs),
+            (len(jobs), steps),
+            micros,
+            alias=None if first else {spot: 0, spot + 1: 1},
         )
-        up_sums.append(sums)
-        order.after(sums)
-        flows.append(sum_flow(MLP_WAYS, lambda grad_own=grad_own: grad_own, grad_other))
-        order.tick(*flows)
+        act, back = outs[:2]
+        grads = outs[2 : 2 + len(jobs)]
+        for job, sums in zip(jobs, outs[2 + len(jobs) :]):
+            up_sums[job] = sums[0:1]
+        order.after(outs[-1])
+        return grads
+
+    summed = range(PLAIN)
+    swaps = [swap_flow(grad) for grad in mlp_call([(chunk, 1) for chunk in summed], {}, 26)]
+    order.tick(*swaps)
+    rest = [(chunk, part) for chunk in range(PLAIN, CHUNKS) for part in (1, 0)]
+    grads = mlp_call(rest, {}, 26)
+    flows = [
+        sum_flow(MLP_WAYS, lambda own=own: own, other) for other, own in zip(grads[0::2], grads[1::2])
+    ]
+    order.tick(*swaps, *flows)
+    came = {(chunk, 0): order.results[swap] for chunk, swap in zip(summed, swaps)}
+    plain_sums = lax.psum(mlp_call([(chunk, 0) for chunk in summed], came, 26), "dp")
+    order.tick(*flows)
 
     reach = 768
     turns = ff // reach
@@ -677,9 +750,8 @@
         [image_spec(2 * turns)] * 2 + [pl.BlockSpec((1, 4, dim), tail(2 * turns))],
         [token_f, token_b, shape_of((images, 4, dim), f32)],
         (2 * turns + images,),
-        24,
+        60,
         scratch=[pltpu.VMEM((count, dim), f32)],
-        room=44,
     )
     order.after(mid_sums)
     order.tick(*flows)
@@ -701,10 +773,9 @@
             [qkv_spec],
             [shape_of((each, 6 * cols, seq), bf16)],
             (each,),
-            20,
+            60,
             scratch=[pltpu.VMEM((2 * cols, seq), bf16)],
-            room=40,
-        )
+            )
         grad_qkv.append(grad_piece)
         order.after(grad_piece)
         order.tick(*flows)
@@ -729,9 +800,8 @@
             ],
             [shape_of((16, attn_per, dim), bf16), shape_of((3, 8, cols), f32)],
             (4,),
-            14,
-            room=40,
-        )
+            60,
+            )
         qv_sums[part] = sums
         order.after(sums)
         return grads
@@ -754,9 +824,8 @@
         [image_spec(6, tail_local), image_spec(6), pl.BlockSpec((1, 2, dim), tail(6))],
         [shape_of((slots, seq, dim), f32), token_f, shape_of((images, 2, dim), f32)],
         (6 + images,),
-        20,
+        60,
         scratch=[pltpu.VMEM((count, dim), f32)],
-        room=40,
     )
     order.after(low_sums)
     order.tick(last, *flows)
@@ -778,19 +847,21 @@
         [image_spec(2 * turns, tail_local), image_spec(2 * turns), pl.BlockSpec((1, 1, dim), tail(2 * turns))],
         [shape_of((slots, seq, dim), bf16), token_b, shape_of((images, 1, dim), f32)],
         (2 * turns + images,),
-        22,
+        60,
         scratch=[pltpu.VMEM((count, dim), f32)],
-        room=40,
     )
     order.after(gate_sums)
     order.tick(last, *flows)
     other_output = swap_cores(own_output)
 
+    low_sums, mid_sums, gate_sums, down_sums = order.fence((low_sums, mid_sums, gate_sums, down_sums))
     grad_modulation = jnp.concatenate([low_sums, mid_sums[:, 2:3], mid_sums[:, 0:2], gate_sums], axis=1)
     grad_modulation = grad_modulation.reshape(images, 6 * dim).astype(bf16)
     bias_sums = [
         jnp.concatenate(
-            [qv_sums[part][0, 0:1], qv_sums[part][2, 0:1]] + [sums[part, 0:1] for sums in up_sums], axis=1
+            [qv_sums[part][0, 0:1], qv_sums[part][2, 0:1]]
+            + [up_sums[chunk, part] for chunk in range(CHUNKS)],
+            axis=1,
         )
         for part in range(2)
     ]
@@ -807,52 +878,68 @@
     given = lax.dynamic_index_in_dim(halves, 1 - core, 1, keepdims=False)
     got = swap_cores(jnp.concatenate([given.astype(f32), bias_sums[1], shared]))
     came = got[:images].astype(bf16)
-    group_mod = jnp.where(
-        core == 0, jnp.concatenate([kept, came]), jnp.concatenate([came, kept])
-    )
+    group_mod = jnp.where(core == 0, jnp.concatenate([kept, came]), jnp.concatenate([came, kept]))
     own_bias_sum = bias_sums[0] + got[images : images + 1]
     shared_sum = shared + got[images + 1 :]
-    part_scaled = outer_cols(group_mod, w_mod).astype(bf16)
-    grad_scaled = part_scaled.astype(f32) + swap_cores(part_scaled).astype(f32)
-    _, silu_back = jax.vjp(jax.nn.silu, cond_f)
-    grad_condition = silu_back(grad_scaled)[0]
     wide_scaled = jnp.pad(scaled.reshape(-1), (0, 3 * own_cols - slots * dim)).reshape(3, own_cols)
     packed_rows = jnp.concatenate(
         [group_mod, own_bias_sum.astype(bf16), shared_sum.astype(bf16), wide_scaled]
     )
-    all_rows = lax.all_gather(packed_rows, "dp", axis=0, tiled=False)
-    order.tick(last, *flows)
+    (packed_rows,) = order.fence([packed_rows])
+    small = rows_flow(packed_rows)
+    order.tick(last, small, *flows)
+    (group_mod,) = order.fence([group_mod])
+    part_scaled = outer_cols(group_mod, w_mod).astype(bf16)
+    came_scaled = swap_cores(part_scaled)
     output = fill_other(output, order.fence(other_output), core)
-    order.after(output[0, 0, :1])
+    order.after((output[0, 0, :1], part_scaled[0, :1]))
+    order.tick(last, small, *flows)
+    grad_tokens = fill_other(grad_tokens, order.fence(other_tokens), core)
+    part_scaled, came_scaled = order.fence((part_scaled, came_scaled))
+    grad_scaled = part_scaled.astype(f32) + came_scaled.astype(f32)
+    _, silu_back = jax.vjp(jax.nn.silu, cond_f)
+    grad_condition = silu_back(grad_scaled)[0]
+    order.after((grad_tokens[0, 0, :1], grad_condition[0, :1]))
+    order.tick(last, small, *flows)
 
     def cuts(ways):
         return tuple((way[0], lo, hi) for lo, hi, way in ways)
 
     grad_w_down = grad_w_up = jnp.zeros((8, 128), f32)
-    for chunk, flow in enumerate(flows):
-        args = order.finish(flow)
+
+    def final_mlp(chunk, body, args):
+        nonlocal grad_w_down, grad_w_up
+        first = grad_w_down.shape[0] == 8
         spot = len(args) + 1
         grad_w_down, grad_w_up, mark = run_kernel(
-            functools.partial(final_mlp_kernel, cuts(MLP_WAYS), per),
+            body,
             order.sc,
             list(args) + [grad_w_down, grad_w_up],
-            [whole_block(a) for a in args] + [anywhere, anywhere],
             [
-                pl.BlockSpec((block, dim), lambda s, c, chunk=chunk: (chunk * steps + s, 0)),
-                pl.BlockSpec((dim, block), lambda s, c, chunk=chunk: (0, chunk * steps + s)),
+                whole_block(a)
+                if a.shape[0] == 8
+                else pl.BlockSpec((16 // steps,) + a.shape[1:], lambda s, c: (s, 0, 0))
+                for a in args
+            ]
+            + [anywhere, anywhere],
+            [
+                pl.BlockSpec((block, dim), lambda s, c: (chunk * steps + s, 0)),
+                pl.BlockSpec((dim, block), lambda s, c: (0, chunk * steps + s)),
                 pl.BlockSpec((8, 128), lambda s, c: (0, 0)),
             ],
             [shape_of((ff, dim), f32), shape_of((dim, ff), f32), shape_of((8, 128), f32)],
             (steps,),
-            6,
+            4,
             scratch=[pltpu.VMEM((block, dim), f32)],
-            alias=None if chunk == 0 else {spot: 0, spot + 1: 1},
-            room=32,
+            alias=None if first else {spot: 0, spot + 1: 1},
         )
         order.after(mark)
-        order.tick(last)
-    grad_tokens = fill_other(grad_tokens, order.fence(other_tokens), core)
-    all_rows = order.fence(all_rows)
+
+    for chunk, flow in enumerate(flows):
+        body = functools.partial(final_mlp_kernel, cuts(MLP_WAYS), per)
+        final_mlp(PLAIN + chunk, body, order.finish(flow))
+    order.tick(last, small)
+    all_rows = order.fence(order.finish(small)).reshape(16, slots + 5, own_cols)
     all_mod = all_rows[:, :slots].reshape(-1, own_cols)
     all_scaled = all_rows[:, slots + 2 :].reshape(16, -1)[:, : slots * dim].reshape(-1, dim)
     grad_w_mod = inner_rows(all_scaled, all_mod)
@@ -862,7 +949,7 @@
     grad_b_up = bias_total[0, 2 * cols :]
     grad_b_proj = bias_total[1, :dim]
     grad_b_down = bias_total[1, dim : 2 * dim]
-    order.after((grad_tokens[0, 0, :1], grad_w_mod[0, :1], grad_b_mod[:1], bias_total[0, :1]))
+    order.after((grad_w_mod[0, :1], grad_b_mod[:1], bias_total[0, :1]))
     args = order.finish(last)
     grad_qkv_rows, grad_w_proj = run_kernel(
         functools.partial(final_attn_kernel, cuts(ATTN_WAYS), attn_per),
@@ -876,9 +963,11 @@
         [shape_of((3 * cols, dim), f32), shape_of((cols, dim), f32)],
         (4,),
         9,
-        room=32,
     )
     grad_w_qkv = jnp.transpose(grad_qkv_rows.reshape(3, cols, dim), (2, 0, 1))
+    order.after(grad_w_proj[0, :1])
+    for chunk, total in enumerate(plain_sums):
+        final_mlp(chunk, functools.partial(final_plain_kernel, per), [total])
     return (
         output,
         grad_tokens,

time: 645 us -> 586 us (0.909)
  waiting for transfers between devices: 148 us -> 107 us
  Pallas kernels: 271 us -> 302 us
  other arithmetic: 51.2 us -> 33.3 us
  starting transfers between devices: 65.4 us -> 49 us
  local copies, waits for them, and re-layouts: 66.7 us -> 52 us
    ppermute x56 -> x32, waiting for transfers between devices: 123 us -> 86.4 us  [exchange(): lax.ppermute(value, 'dp', bit_pairs(bit))]
    pallas_call x15, Pallas kernels: 271 us -> 302 us  [run_kernel(): pl.pallas_call(body, out_shape=out_shape, grid_spec=pltpu.PrefetchScalarG...]
    unnamed x134 -> x56, local copies, waits for them, and re-layouts: 27.4 us -> 4.73 us
    ppermute x56 -> x32, starting transfers between devices: 61.9 us -> 42.5 us  [exchange(): lax.ppermute(value, 'dp', bit_pairs(bit))]
    all_gather x1 -> x0, waiting for transfers between devices: 18.4 us -> none  [fast_device(): all_rows = lax.all_gather(packed_rows, 'dp', axis=0, tiled=False)]
    ppermute x0 -> x4, waiting for transfers between devices: none -> 17.3 us  [rows_flow(): came = lax.ppermute(rows, 'dp', bit_pairs(bit))]
    another operation x23 -> x13, other arithmetic: 17.3 us -> 7.45 us  [gather_flow(): joined.append(jnp.stack([one, two], axis=place))]
    add x39 -> x21, other arithmetic: 23 us -> 14.3 us  [reduce_flow(): cut(one, bits, route[stage], side, cols)]
  transfers between devices with their start and end apart: 72 -> 52, of which waited for: 30 -> 21; matrix products, arithmetic and copies ran while one was open for 9% -> 17% of each run, Pallas kernels for 34% -> 44%
where the time goes in v4:
time: 586 us; the launch traced here: 577 us
  Pallas kernels  302 us (52%)
  waiting for transfers between devices  107 us (18%)
  local copies, waits for them, and re-layouts  52 us (9%)
  starting transfers between devices  49 us (8%)
  other arithmetic  33.3 us (6%)
  matrix products  18.1 us (3%)
  between operations  15.7 us (3%)
    pallas_call x15, Pallas kernels, run_kernel(): pl.pallas_call(body, out_shape=out_shape, grid_spec=pltpu.PrefetchScalarG...  302 us
    ppermute x32, waiting for transfers between devices, exchange(): lax.ppermute(value, 'dp', bit_pairs(bit))  86.4 us
    ppermute x32, starting transfers between devices, exchange(): lax.ppermute(value, 'dp', bit_pairs(bit))  42.5 us
    ppermute x4, waiting for transfers between devices, rows_flow(): came = lax.ppermute(rows, 'dp', bit_pairs(bit))  17.3 us
    add x21, other arithmetic, reduce_flow(): cut(one, bits, route[stage], side, cols)  14.3 us
    slice x10, local copies, waits for them, and re-layouts, cut(): out = lax.slice(array, lo, hi)  13.6 us
  transfers between devices with their start and end apart: 52, of which 21 were waited for; matrix products, arithmetic and copies ran while one was open for 17% of the time, Pallas kernels for 44%

profile of v4, /device:TPU:0, one launch (start us, length us, event | category | flops | bytes accessed | tf_op | source)
XLA Modules:
  0.0 576.9 jit_solution(10599812512304258181)
XLA Ops:
  22.5 49.0 %shard_map.237 = (bf16[4,3456,256]{2,1,0:T(8,128)(2,1)}, bf16[4,16,256,256]{3,2,1,0:T(8,128)(2,1)}, bf16[4,1152,256]{2,1,0:T(8,128)(2,1)}, f32[4,256,1152]{2,1,0...) custom-call(s32[3]{0:T(128)} %pad_add_fusion.sc, ...), custom_call_target="tpu_custom_call" | custom-call | flops 51749998592 | bytes 45000000 | tf_op jit(solution)/shard_map/pallas_call | solution.py:387
  72.2 26.1 %shard_map.238 = (bf16[2,2304,1024]{2,1,0:T(8,128)(2,1)}, bf16[2,2304,1024]{2,1,0:T(8,128)(2,1)}, bf16[16,96,1152]{2,1,0:T(8,128)(2,1)}, bf16[16,96,1152]{2,1,0:...) custom-call(s32[3]{0:T(128)} %pad_add_fusion.sc, bf16[1024,1152]{1,0:T(8,128)(2,1)} %bitcast.195, ...), custom_call_target="tpu_custom_call" | custom-call | flops 29899999232 | bytes 26000000 | tf_op jit(solution)/shard_map/pallas_call | solution.py:387
  99.5 27.5 %shard_map.239 = (bf16[2,2304,1024]{2,1,0:T(8,128)(2,1)}, bf16[2,2304,1024]{2,1,0:T(8,128)(2,1)}, bf16[16,96,1152]{2,1,0:T(8,128)(2,1)}, bf16[16,96,1152]{2,1,0:...) custom-call(s32[3]{0:T(128)} %pad_add_fusion.sc, ...), custom_call_target="tpu_custom_call", output_to_operand_aliasing={{0}: (9, {}), {1}: (10, {})} | custom-call | flops 29899999232 | bytes 26000000 | tf_op jit(solution)/shard_map/pallas_call | solution.py:387
  133.9 27.2 %shard_map.240 = (bf16[2,2304,1024]{2,1,0:T(8,128)(2,1)}, bf16[2,2304,1024]{2,1,0:T(8,128)(2,1)}, bf16[16,96,1152]{2,1,0:T(8,128)(2,1)}, bf16[16,96,1152]{2,1,0:...) custom-call(s32[3]{0:T(128)} %pad_add_fusion.sc, ...), custom_call_target="tpu_custom_call", output_to_operand_aliasing={{0}: (11, {}), {1}: (12, {})} | custom-call | flops 29899999232 | bytes 26000000 | tf_op jit(solution)/shard_map/pallas_call | solution.py:387
  174.9 27.5 %shard_map.241 = (f32[4,256,1152]{2,1,0:T(8,128)}, bf16[4,256,1152]{2,1,0:T(8,128)(2,1)}, f32[4,4,1152]{2,1,0:T(4,128)}) custom-call(s32[3]{0:T(128)} %pad_add_fusion.sc, bf16[2,2304,1024]{2,1,0:T(8,128)(2,1)} %get-tuple-element.289.back, bf16[1152,2304]{1,0:T(8,128)(2,1)} %w_up0.1, bf16[1152,2304]{1,0:T(8,128)(2,1)} %collective-permute-done.4.refs_0_.refs_3_.w_up1, ...), custom_call_target="tpu_custom_call" | custom-call | flops 69000003584 | bytes 41582592 | tf_op jit(solution)/shard_map/pallas_call | solution.py:387
  211.1 20.4 %shard_map.242.refs_0_ = bf16[2,3456,256]{2,1,0:T(8,128)(2,1)} custom-call(s32[3]{0:T(128)} %pad_add_fusion.sc, bf16[4,256,1152]{2,1,0:T(8,128)(2,1)} %get-tuple-element.304.grad_attn.refs_4_, bf16[4,3456,256]{2,1,0:T(8,128)(2,1)} %get-tuple-element.305.qkv, bf16[4,16,256,256]{3,2,1,0:T(8,128)(2,1)} %get-tuple-element.306.prob, bf16[576,1152]{1,0:T(8,128)(2,1)} %refs_0_.5, ...), custom_call_target="tpu_custom_call" | custom-call | flops 69000003584 | bytes 24018944 | tf_op jit(solution)/shard_map/pallas_call | solution.py:387
  234.7 20.3 %shard_map.243.refs_1_ = bf16[2,3456,256]{2,1,0:T(8,128)(2,1)} custom-call(s32[3]{0:T(128)} %pad_add_fusion.sc, bf16[4,256,1152]{2,1,0:T(8,128)(2,1)} %get-tuple-element.304.grad_attn.refs_4_, bf16[4,3456,256]{2,1,0:T(8,128)(2,1)} %get-tuple-element.305.qkv, bf16[4,16,256,256]{3,2,1,0:T(8,128)(2,1)} %get-tuple-element.306.prob, bf16[576,1152]{1,0:T(8,128)(2,1)} %refs_0_.5, ...), custom_call_target="tpu_custom_call" | custom-call | flops 69000003584 | bytes 24018944 | tf_op jit(solution)/shard_map/pallas_call | solution.py:387
  257.6 14.1 %shard_map.244 = (bf16[16,144,1152]{2,1,0:T(8,128)(2,1)}, f32[3,8,576]{2,1,0:T(8,128)}) custom-call(s32[3]{0:T(128)} %pad_add_fusion.sc, bf16[2,3456,256]{2,1,0:T(8,128)(2,1)} %shard_map.242.refs_0_, bf16[2,3456,256]{2,1,0:T(8,128)(2,1)} %shard_map.243.refs_1_, bf16[4,1152,256]{2,1,0:T(8,128)(2,1)} %get-tuple-element.325.refs_2_, ...), custom_call_target="tpu_custom_call" | custom-call | flops 69000003584 | bytes 19519488 | tf_op jit(solution)/shard_map/pallas_call | solution.py:387
  273.8 14.6 %shard_map.245 = (bf16[16,144,1152]{2,1,0:T(8,128)(2,1)}, f32[3,8,576]{2,1,0:T(8,128)}) custom-call(s32[3]{0:T(128)} %pad_add_fusion.sc, bf16[2,3456,256]{2,1,0:T(8,128)(2,1)} %shard_map.242.refs_0_, bf16[2,3456,256]{2,1,0:T(8,128)(2,1)} %shard_map.243.refs_1_, bf16[4,1152,256]{2,1,0:T(8,128)(2,1)} %get-tuple-element.325.refs_2_, ...), custom_call_target="tpu_custom_call" | custom-call | flops 69000003584 | bytes 19519488 | tf_op jit(solution)/shard_map/pallas_call | solution.py:387
  309.2 24.3 %shard_map.246 = (f32[8,256,1152]{2,1,0:T(8,128)}, f32[4,256,1152]{2,1,0:T(8,128)}, f32[4,2,1152]{2,1,0:T(2,128)}) custom-call(s32[3]{0:T(128)} %pad_add_fusion.sc, bf16[2,3456,256]{2,1,0:T(8,128)(2,1)} %shard_map.242.refs_0_, bf16[2,3456,256]{2,1,0:T(8,128)(2,1)} %shard_map.243.refs_1_, bf16[1728,1152]{1,0:T(8,128)(2,1)} %bitcast.192, ...), custom_call_target="tpu_custom_call" | custom-call | flops 69000003584 | bytes 38891520 | tf_op jit(solution)/shard_map/pallas_call | solution.py:387
  333.5 8.6 %collective-permute-done.20 = bf16[2,2,2,144,256]{4,3,1,2,0:T(8,128)(2,1)} collective-permute-done((bf16[2,2,2,144,256]{4,3,1,2,0:T(8,128)(2,1)}, bf16[2,2,2,144,256]{4,3,1,2,0:T(8,128)(2,1)}, u32[]{:S(2)}, u32[]{:S(2)}) %collective-permute-start.20) | collective-permute-done | bytes 589856 | tf_op jit(solution)/shard_map/ppermute | solution.py:445
  355.9 24.9 %shard_map.247 = (bf16[8,256,1152]{2,1,0:T(8,128)(2,1)}, bf16[4,256,1152]{2,1,0:T(8,128)(2,1)}, f32[4,1,1152]{2,1,0:T(1,128)}) custom-call(s32[3]{0:T(128)} %pad_add_fusion.sc, bf16[2,2304,1024]{2,1,0:T(8,128)(2,1)} %get-tuple-element.367.act, bf16[2304,1152]{1,0:T(8,128)(2,1)} %w_down0.1, bf16[2304,1152]{1,0:T(8,128)(2,1)} %collective-permute-done.5.refs_1_.refs_4_.w_down1, ...), custom_call_target="tpu_custom_call" | custom-call | flops 69000003584 | bytes 36813312 | tf_op jit(solution)/shard_map/pallas_call | solution.py:387
  381.0 5.9 %collective-permute-done.22 = bf16[2,2,144,512]{3,2,0,1:T(8,128)(2,1)S(1)} collective-permute-done((bf16[2,2,144,512]{3,2,0,1:T(8,128)(2,1)S(1)}, bf16[2,2,144,512]{3,2,0,1:T(8,128)(2,1)S(1)}, u32[]{:S(2)}, u32[]{:S(2)}) %collective-permute-start.22) | collective-permute-done | bytes 589856 | tf_op jit(solution)/shard_map/ppermute | solution.py:445
  407.1 25.9 %collective-permute-done.28 = bf16[2,144,896]{2,1,0:T(8,128)(2,1)S(1)} collective-permute-done((bf16[2,144,896]{2,1,0:T(8,128)(2,1)}, bf16[2,144,896]{2,1,0:T(8,128)(2,1)S(1)}, u32[]{:S(2)}, u32[]{:S(2)}) %collective-permute-start.28) | collective-permute-done | bytes 516128 | tf_op jit(solution)/shard_map/ppermute | solution.py:445
  442.5 11.8 %collective-permute-done.35 = bf16[13,3456]{1,0:T(8,128)(2,1)S(1)} collective-permute-done((bf16[13,3456]{1,0:T(8,128)(2,1)S(1)}, bf16[13,3456]{1,0:T(8,128)(2,1)S(1)}, u32[]{:S(2)}, u32[]{:S(2)}) %collective-permute-start.35) | collective-permute-done | bytes 89888 | tf_op jit(solution)/shard_map/ppermute | solution.py:519
  459.3 5.4 convolution_convert_fusion
  494.5 6.2 %shard_map.249 = (f32[2304,1152]{1,0:T(8,128)}, f32[1152,2304]{1,0:T(8,128)}, f32[8,128]{1,0:T(8,128)}) custom-call(s32[3]{0:T(128)} %pad_add_fusion.sc, bf16[8,96,640]{2,1,0:T(8,128)(2,1)} %bitcast.175, bf16[8,96,640]{2,1,0:T(8,128)(2,1)} %bitcast.176, bf16[8,96,512]{2,1,0:T(8,128)(2,1)} %bitcast.179, bf16[8,96,512]{2,1,0:T(8,128)(2,1)} %bitcast.193, ...), custom_call_target="tpu_custom_call" | custom-call | flops 4600000000 | bytes 4000000 | tf_op jit(solution)/shard_map/pallas_call | solution.py:387
  505.1 9.2 %collective-permute-done.47 = bf16[2,2,144,256]{3,2,1,0:T(8,128)(2,1)S(1)} collective-permute-done((bf16[2,2,144,256]{3,2,1,0:T(8,128)(2,1)S(1)}, bf16[2,2,144,256]{3,2,1,0:T(8,128)(2,1)S(1)}, u32[]{:S(2)}, u32[]{:S(2)}) %collective-permute-start.47) | collective-permute-done | bytes 294944 | tf_op jit(solution)/shard_map/ppermute | solution.py:445
  523.1 8.1 %fusion.6 = f32[1152,3456]{1,0:T(8,128)} fusion(bf16[128,1152]{1,0:T(8,128)(2,1)S(1)} %reshape.239, bf16[16,13,3456]{2,1,0:T(8,128)(2,1)S(1)} %reshape.233), kind=kOutput, calls=%fused_computation.23 | convolution fusion | flops 1019215872 | bytes 17104896 | tf_op jit(solution)/shard_map/dot_general | solution.py:1006
  532.5 6.3 %collective-permute-done.49 = bf16[2,2,2,144,384]{4,3,2,1,0:T(8,128)(2,1)} collective-permute-done((bf16[2,2,2,144,384]{4,3,2,1,0:T(8,128)(2,1)}, bf16[2,2,2,144,384]{4,3,2,1,0:T(8,128)(2,1)}, u32[]{:S(2)}, u32[]{:S(2)}) %collective-permute-start.49) | collective-permute-done | bytes 884768 | tf_op jit(solution)/shard_map/ppermute | solution.py:445
  538.8 6.7 %collective-permute-done.48 = bf16[2,2,2,144,512]{4,3,1,0,2:T(8,128)(2,1)} collective-permute-done((bf16[2,2,2,144,512]{4,3,1,0,2:T(8,128)(2,1)}, bf16[2,2,2,144,512]{4,3,1,0,2:T(8,128)(2,1)}, u32[]{:S(2)}, u32[]{:S(2)}) %collective-permute-start.48) | collective-permute-done | bytes 1179680 | tf_op jit(solution)/shard_map/ppermute | solution.py:445
  550.3 5.5 shard_map.250
  555.8 5.5 shard_map.251
  561.2 8.5 %shard_map.248 = (f32[1728,1152]{1,0:T(8,128)}, f32[576,1152]{1,0:T(8,128)}) custom-call(s32[3]{0:T(128)} %pad_add_fusion.sc, bf16[8,144,512]{2,1,0:T(8,128)(2,1)} %bitcast.172, bf16[8,144,512]{2,1,0:T(8,128)(2,1)} %bitcast.173, bf16[8,144,384]{2,1,0:T(8,128)(2,1)} %bitcast.82.refs_2_, bf16[8,144,384]{2,1,0:T(8,128)(2,1)} %bitcast.83.refs_3_, ...), custom_call_target="tpu_custom_call" | custom-call | flops 10350000128 | bytes 9000000 | tf_op jit(solution)/shard_map/pallas_call | solution.py:387
  (270 shorter events, 171.7 us)
Async XLA Ops:
  7.2 543.2 %all-reduce.4.cloned.1.call-start = ((), (), s32[]{:S(2)}) async-start(), calls=%async_computation | async-start | bytes 14155776 | tf_op jit(solution)/shard_map/psum | solution.py:716
  14.6 57.0 %collective-permute-start.4 = (bf16[1152,2304]{1,0:T(8,128)(2,1)}, bf16[1152,2304]{1,0:T(8,128)(2,1)}, u32[]{:S(2)}, u32[]{:S(2)}) collective-permute-start(bf16[1152,2304]{1,0:T(8,128)(2,1)} %w_up0.1), channel_id=1, source_target_pairs={{0,1},{1,0},{2,3},{3,2},{4,5},{5,4},{6,7},{7,6},{8,9},{9,8},{10,11... | collective-permute-start | bytes 15925256 | tf_op jit(solution)/shard_map/ppermute | solution.py:418
  14.9 56.6 %collective-permute-start.5 = (bf16[2304,1152]{1,0:T(8,128)(2,1)}, bf16[2304,1152]{1,0:T(8,128)(2,1)}, u32[]{:S(2)}, u32[]{:S(2)}) collective-permute-start(bf16[2304,1152]{1,0:T(8,128)(2,1)} %w_down0.1), channel_id=1, source_target_pairs={{0,1},{1,0},{2,3},{3,2},{4,5},{5,4},{6,7},{7,6},{8,9},{9,8},{10,11... | collective-permute-start | bytes 15925256 | tf_op jit(solution)/shard_map/ppermute | solution.py:418
  18.1 53.4 %collective-permute-start.6 = (bf16[1,2304]{1,0:T(2,128)(2,1)S(1)}, bf16[1,2304]{1,0:T(2,128)(2,1)S(1)}, u32[]{:S(2)}, u32[]{:S(2)}) collective-permute-start(bf16[1,2304]{1,0:T(2,128)(2,1)S(1)} %broadcast_in_dim.34), channel_id=1, source_target_pairs={{0,1},{1,0},{2,3},{3,2},{4,5},{5,4},{6,7},{7,6},{8,9},{9,8},{10,11... | collective-permute-start | bytes 13832 | tf_op jit(solution)/shard_map/ppermute | solution.py:418
  98.3 28.7 %collective-permute-start.7 = (bf16[16,96,1152]{2,1,0:T(8,128)(2,1)}, bf16[16,96,1152]{2,1,0:T(8,128)(2,1)}, u32[]{:S(2)}, u32[]{:S(2)}) collective-permute-start(bf16[16,96,1152]{2,1,0:T(8,128)(2,1)} %get-tuple-element.273), channel_id=1, source_target_pairs={{0,1},{1,0},{2,3},{3,2},{4,5},{5,4},{6,7},{7,6},{8,9},{9,8},{10,11... | collective-permute-start | bytes 10616840 | tf_op jit(solution)/shard_map/ppermute | solution.py:418
  98.5 28.5 %collective-permute-start.8 = (bf16[16,96,1152]{2,1,0:T(8,128)(2,1)}, bf16[16,96,1152]{2,1,0:T(8,128)(2,1)}, u32[]{:S(2)}, u32[]{:S(2)}) collective-permute-start(bf16[16,96,1152]{2,1,0:T(8,128)(2,1)} %get-tuple-element.274), channel_id=1, source_target_pairs={{0,1},{1,0},{2,3},{3,2},{4,5},{5,4},{6,7},{7,6},{8,9},{9,8},{10,11... | collective-permute-start | bytes 10616840 | tf_op jit(solution)/shard_map/ppermute | solution.py:418
  127.1 36.7 %collective-permute-start.9 = (bf16[16,96,1152]{2,1,0:T(8,128)(2,1)}, bf16[16,96,1152]{2,1,0:T(8,128)(2,1)}, u32[]{:S(2)}, u32[]{:S(2)}) collective-permute-start(bf16[16,96,1152]{2,1,0:T(8,128)(2,1)} %get-tuple-element.284), channel_id=1, source_target_pairs={{0,1},{1,0},{2,3},{3,2},{4,5},{5,4},{6,7},{7,6},{8,9},{9,8},{10,11... | collective-permute-start | bytes 10616840 | tf_op jit(solution)/shard_map/ppermute | solution.py:418
  170.6 31.8 %collective-permute-start.11 = (bf16[2,2,2,96,512]{4,3,0,1,2:T(8,128)(2,1)}, bf16[2,2,2,96,512]{4,3,0,1,2:T(8,128)(2,1)}, u32[]{:S(2)}, u32[]{:S(2)}) collective-permute-start(bf16[2,2,2,96,512]{4,3,0,1,2:T(8,128)(2,1)} %get-tuple-element.297), channel_id=1, source_target_pairs={{0,4},{2,6},{4,0},{6,2},{8,12},{10,14},{12,8},{14,10},{16,20},{18,... | collective-permute-start | bytes 2359304 | tf_op jit(solution)/shard_map/ppermute | solution.py:445
  173.5 32.5 %collective-permute-start.10 = (bf16[2,2,2,96,640]{4,3,0,1,2:T(8,128)(2,1)S(1)}, bf16[2,2,2,96,640]{4,3,0,1,2:T(8,128)(2,1)S(1)}, u32[]{:S(2)}, u32[]{:S(2)}) collective-permute-start(bf16[2,2,2,96,640]{4,3,0,1,2:T(8,128)(2,1)S(1)} %get-tuple-element.296), channel_id=1, source_target_pairs={{0,2},{2,0},{4,6},{6,4},{8,10},{10,8},{12,14},{14,12},{16,18},{18,... | collective-permute-start | bytes 2949128 | tf_op jit(solution)/shard_map/ppermute | solution.py:445
  305.3 28.2 %collective-permute-start.21 = (bf16[2,96,1152]{2,1,0:T(8,128)(2,1)S(1)}, bf16[2,96,1152]{2,1,0:T(8,128)(2,1)S(1)}, u32[]{:S(2)}, u32[]{:S(2)}) collective-permute-start(bf16[2,96,1152]{2,1,0:T(8,128)(2,1)S(1)} %pad_maximum_fusion.13), channel_id=1, source_target_pairs={{0,8},{2,10},{4,12},{6,14},{8,0},{10,2},{12,4},{14,6},{16,24},{18,... | collective-permute-start | bytes 1327112 | tf_op jit(solution)/shard_map/ppermute | solution.py:445
  305.3 36.8 %collective-permute-start.20 = (bf16[2,2,2,144,256]{4,3,1,2,0:T(8,128)(2,1)}, bf16[2,2,2,144,256]{4,3,1,2,0:T(8,128)(2,1)}, u32[]{:S(2)}, u32[]{:S(2)}) collective-permute-start(bf16[2,2,2,144,256]{4,3,1,2,0:T(8,128)(2,1)} %fusion.13), channel_id=1, source_target_pairs={{0,8},{2,10},{4,12},{6,14},{8,0},{10,2},{12,4},{14,6},{16,24},{18,... | collective-permute-start | bytes 1769480 | tf_op jit(solution)/shard_map/ppermute | solution.py:445
  307.3 34.8 %collective-permute-start.19 = (bf16[2,2,2,144,384]{4,3,0,1,2:T(8,128)(2,1)}, bf16[2,2,2,144,384]{4,3,0,1,2:T(8,128)(2,1)}, u32[]{:S(2)}, u32[]{:S(2)}) collective-permute-start(bf16[2,2,2,144,384]{4,3,0,1,2:T(8,128)(2,1)} %fusion.5), channel_id=1, source_target_pairs={{0,4},{2,6},{4,0},{6,2},{8,12},{10,14},{12,8},{14,10},{16,20},{18,... | collective-permute-start | bytes 2654216 | tf_op jit(solution)/shard_map/ppermute | solution.py:445
  307.6 36.8 %collective-permute-start.18 = (bf16[2,2,2,144,512]{4,3,0,1,2:T(8,128)(2,1)}, bf16[2,2,2,144,512]{4,3,0,1,2:T(8,128)(2,1)}, u32[]{:S(2)}, u32[]{:S(2)}) collective-permute-start(bf16[2,2,2,144,512]{4,3,0,1,2:T(8,128)(2,1)} %fusion.1), channel_id=1, source_target_pairs={{0,2},{2,0},{4,6},{6,4},{8,10},{10,8},{12,14},{14,12},{16,18},{18,... | collective-permute-start | bytes 3538952 | tf_op jit(solution)/shard_map/ppermute | solution.py:445
  350.5 30.4 %collective-permute-start.24 = (bf16[2,2,144,256]{3,2,0,1:T(8,128)(2,1)}, bf16[2,2,144,256]{3,2,0,1:T(8,128)(2,1)S(1)}, u32[]{:S(2)}, u32[]{:S(2)}) collective-permute-start(bf16[2,2,144,256]{3,2,0,1:T(8,128)(2,1)} %get-tuple-element.376), channel_id=1, source_target_pairs={{0,16},{2,18},{4,20},{6,22},{8,24},{10,26},{12,28},{14,30},{16,0},... | collective-permute-start | bytes 884744 | tf_op jit(solution)/shard_map/ppermute | solution.py:445
  351.9 29.1 %collective-permute-start.26 = (bf16[2,2,96,512]{3,2,1,0:T(8,128)(2,1)}, bf16[2,2,96,512]{3,2,1,0:T(8,128)(2,1)}, u32[]{:S(2)}, u32[]{:S(2)}) collective-permute-start(bf16[2,2,96,512]{3,2,1,0:T(8,128)(2,1)} %pad_maximum_fusion.14), channel_id=1, source_target_pairs={{0,2},{2,0},{4,6},{6,4},{8,10},{10,8},{12,14},{14,12},{16,18},{18,... | collective-permute-start | bytes 1179656 | tf_op jit(solution)/shard_map/ppermute | solution.py:445
  353.0 28.0 %collective-permute-start.23 = (bf16[2,2,144,384]{3,2,0,1:T(8,128)(2,1)}, bf16[2,2,144,384]{3,2,0,1:T(8,128)(2,1)}, u32[]{:S(2)}, u32[]{:S(2)}) collective-permute-start(bf16[2,2,144,384]{3,2,0,1:T(8,128)(2,1)} %get-tuple-element.375), channel_id=1, source_target_pairs={{0,2},{2,0},{4,6},{6,4},{8,10},{10,8},{12,14},{14,12},{16,18},{18,... | collective-permute-start | bytes 1327112 | tf_op jit(solution)/shard_map/ppermute | solution.py:445
  353.9 27.0 %collective-permute-start.25 = (bf16[2,2,96,640]{3,2,1,0:T(8,128)(2,1)S(1)}, bf16[2,2,96,640]{3,2,1,0:T(8,128)(2,1)S(1)}, u32[]{:S(2)}, u32[]{:S(2)}) collective-permute-start(bf16[2,2,96,640]{3,2,1,0:T(8,128)(2,1)S(1)} %fusion.14), channel_id=1, source_target_pairs={{0,4},{2,6},{4,0},{6,2},{8,12},{10,14},{12,8},{14,10},{16,20},{18,... | collective-permute-start | bytes 1474568 | tf_op jit(solution)/shard_map/ppermute | solution.py:445
  355.1 31.8 %collective-permute-start.22 = (bf16[2,2,144,512]{3,2,0,1:T(8,128)(2,1)S(1)}, bf16[2,2,144,512]{3,2,0,1:T(8,128)(2,1)S(1)}, u32[]{:S(2)}, u32[]{:S(2)}) collective-permute-start(bf16[2,2,144,512]{3,2,0,1:T(8,128)(2,1)S(1)} %get-tuple-element.374), channel_id=1, source_target_pairs={{0,4},{2,6},{4,0},{6,2},{8,12},{10,14},{12,8},{14,10},{16,20},{18,... | collective-permute-start | bytes 1769480 | tf_op jit(solution)/shard_map/ppermute | solution.py:445
  380.9 87.2 %collective-permute-start.36 = (f32[4,256,1152]{2,1,0:T(8,128)}, f32[4,256,1152]{2,1,0:T(8,128)}, u32[]{:S(2)}, u32[]{:S(2)}) collective-permute-start(f32[4,256,1152]{2,1,0:T(8,128)} %get-tuple-element.431), channel_id=1, source_target_pairs={{0,1},{1,0},{2,3},{3,2},{4,5},{5,4},{6,7},{7,6},{8,9},{9,8},{10,11... | collective-permute-start | bytes 14155784 | tf_op jit(solution)/shard_map/ppermute | solution.py:418
  395.6 44.3 %collective-permute-start.32 = (bf16[4,256,1152]{2,1,0:T(8,128)(2,1)}, bf16[4,256,1152]{2,1,0:T(8,128)(2,1)S(1)}, u32[]{:S(2)}, u32[]{:S(2)}) collective-permute-start(bf16[4,256,1152]{2,1,0:T(8,128)(2,1)} %get-tuple-element.414), channel_id=1, source_target_pairs={{0,1},{1,0},{2,3},{3,2},{4,5},{5,4},{6,7},{7,6},{8,9},{9,8},{10,11... | collective-permute-start | bytes 7077896 | tf_op jit(solution)/shard_map/ppermute | solution.py:418
  397.2 35.8 %collective-permute-start.28 = (bf16[2,144,896]{2,1,0:T(8,128)(2,1)}, bf16[2,144,896]{2,1,0:T(8,128)(2,1)S(1)}, u32[]{:S(2)}, u32[]{:S(2)}) collective-permute-start(bf16[2,144,896]{2,1,0:T(8,128)(2,1)} %pad_maximum_fusion.7), channel_id=1, source_target_pairs={{0,8},{2,10},{4,12},{6,14},{8,0},{10,2},{12,4},{14,6},{16,24},{18,... | collective-permute-start | bytes 1548296 | tf_op jit(solution)/shard_map/ppermute | solution.py:445
  398.8 34.3 %collective-permute-start.30 = (bf16[2,2,2,96,640]{4,3,1,0,2:T(8,128)(2,1)S(1)}, bf16[2,2,2,96,640]{4,3,1,0,2:T(8,128)(2,1)}, u32[]{:S(2)}, u32[]{:S(2)}) collective-permute-start(bf16[2,2,2,96,640]{4,3,1,0,2:T(8,128)(2,1)S(1)} %pad_maximum_fusion.2), channel_id=1, source_target_pairs={{0,2},{2,0},{4,6},{6,4},{8,10},{10,8},{12,14},{14,12},{16,18},{18,... | collective-permute-start | bytes 2949128 | tf_op jit(solution)/shard_map/ppermute | solution.py:445
  405.6 27.4 %collective-permute-start.31 = (bf16[2,2,2,96,512]{4,3,2,1,0:T(8,128)(2,1)}, bf16[2,2,2,96,512]{4,3,2,1,0:T(8,128)(2,1)S(1)}, u32[]{:S(2)}, u32[]{:S(2)}) collective-permute-start(bf16[2,2,2,96,512]{4,3,2,1,0:T(8,128)(2,1)} %pad_maximum_fusion.4), channel_id=1, source_target_pairs={{0,4},{2,6},{4,0},{6,2},{8,12},{10,14},{12,8},{14,10},{16,20},{18,... | collective-permute-start | bytes 2359304 | tf_op jit(solution)/shard_map/ppermute | solution.py:445
  518.3 27.3 %collective-permute-start.48 = (bf16[2,2,2,144,512]{4,3,1,0,2:T(8,128)(2,1)}, bf16[2,2,2,144,512]{4,3,1,0,2:T(8,128)(2,1)}, u32[]{:S(2)}, u32[]{:S(2)}) collective-permute-start(bf16[2,2,2,144,512]{4,3,1,0,2:T(8,128)(2,1)} %pad_maximum_fusion.1), channel_id=1, source_target_pairs={{0,2},{2,0},{4,6},{6,4},{8,10},{10,8},{12,14},{14,12},{16,18},{18,... | collective-permute-start | bytes 3538952 | tf_op jit(solution)/shard_map/ppermute | solution.py:445
  (55 other events, 573.0 us)
Sparse Core Ops, SparseCore 0:
  163.9 270.3 all-reduce.3

commit v5 on v4

--- a/solution.py
+++ b/solution.py
@@ -556,7 +556,6 @@
 
 
 CHUNKS = 3
-PLAIN = 2
 
 
 def fill_other(both, came, core):
@@ -644,7 +643,7 @@
     def mlp_call(jobs, came, micros):
         nonlocal act, back
         first = act.shape[0] == 8
-        kinds = tuple((chunk < PLAIN, (chunk, part) in came) for chunk, part in jobs)
+        kinds = tuple((job[0] > 0, job in came) for job in jobs)
 
         def turn(k):
             return lambda p, s, c: jnp.clip((p - k) * steps + s, 0, steps - 1)
@@ -703,15 +702,16 @@
         order.after(outs[-1])
         return grads
 
-    summed = range(PLAIN)
-    swaps = [swap_flow(grad) for grad in mlp_call([(chunk, 1) for chunk in summed], {}, 26)]
+    summed = range(1, CHUNKS)
+    (grad_other,) = mlp_call([(0, 1)], {}, 13)
+    made_first = []
+    flows = [sum_flow(MLP_WAYS, lambda: made_first[0], grad_other)]
+    order.tick(*flows)
+    grads = mlp_call([(chunk, 1) for chunk in summed], {}, 26)
+    swaps = [swap_flow(grad) for grad in grads]
     order.tick(*swaps)
-    rest = [(chunk, part) for chunk in range(PLAIN, CHUNKS) for part in (1, 0)]
-    grads = mlp_call(rest, {}, 26)
-    flows = [
-        sum_flow(MLP_WAYS, lambda own=own: own, other) for other, own in zip(grads[0::2], grads[1::2])
-    ]
-    order.tick(*swaps, *flows)
+    made_first += mlp_call([(0, 0)], {}, 13)
+    order.tick(*flows, *swaps)
     came = {(chunk, 0): order.results[swap] for chunk, swap in zip(summed, swaps)}
     plain_sums = lax.psum(mlp_call([(chunk, 0) for chunk in summed], came, 26), "dp")
     order.tick(*flows)
@@ -937,8 +937,11 @@
 
     for chunk, flow in enumerate(flows):
         body = functools.partial(final_mlp_kernel, cuts(MLP_WAYS), per)
-        final_mlp(PLAIN + chunk, body, order.finish(flow))
+        final_mlp(chunk, body, order.finish(flow))
     order.tick(last, small)
+    for chunk, total in zip(summed, order.fence(plain_sums)):
+        final_mlp(chunk, functools.partial(final_plain_kernel, per), [total])
+    order.tick(last)
     all_rows = order.fence(order.finish(small)).reshape(16, slots + 5, own_cols)
     all_mod = all_rows[:, :slots].reshape(-1, own_cols)
     all_scaled = all_rows[:, slots + 2 :].reshape(16, -1)[:, : slots * dim].reshape(-1, dim)
@@ -965,9 +968,6 @@
         9,
     )
     grad_w_qkv = jnp.transpose(grad_qkv_rows.reshape(3, cols, dim), (2, 0, 1))
-    order.after(grad_w_proj[0, :1])
-    for chunk, total in enumerate(plain_sums):
-        final_mlp(chunk, functools.partial(final_plain_kernel, per), [total])
     return (
         output,
         grad_tokens,

time: 586 us -> 597 us (1.019)
  waiting for transfers between devices: 107 us -> 120 us
    ppermute x32, waiting for transfers between devices: 86.4 us -> 95 us  [exchange(): lax.ppermute(value, 'dp', bit_pairs(bit))]
    pallas_call x15 -> x16, Pallas kernels: 302 us -> 307 us  [run_kernel(): pl.pallas_call(body, out_shape=out_shape, grid_spec=pltpu.PrefetchScalarG...]
  transfers between devices with their start and end apart: 52 -> 52, of which waited for: 21 -> 17; matrix products, arithmetic and copies ran while one was open for 17% -> 14% of each run, Pallas kernels for 44% -> 48%
where the time goes in v5:
time: 597 us; the launch traced here: 585 us
  Pallas kernels  307 us (51%)
  waiting for transfers between devices  120 us (20%)
  local copies, waits for them, and re-layouts  48.4 us (8%)
  starting transfers between devices  46.5 us (8%)
  other arithmetic  29.1 us (5%)
  matrix products  18.1 us (3%)
  between operations  16.1 us (3%)
    pallas_call x16, Pallas kernels, run_kernel(): pl.pallas_call(body, out_shape=out_shape, grid_spec=pltpu.PrefetchScalarG...  307 us
    ppermute x32, waiting for transfers between devices, exchange(): lax.ppermute(value, 'dp', bit_pairs(bit))  95 us
    ppermute x32, starting transfers between devices, exchange(): lax.ppermute(value, 'dp', bit_pairs(bit))  37.7 us
    ppermute x4, waiting for transfers between devices, rows_flow(): came = lax.ppermute(rows, 'dp', bit_pairs(bit))  21.5 us
    add x21, other arithmetic, reduce_flow(): cut(one, bits, route[stage], side, cols)  15.8 us
    slice x10, local copies, waits for them, and re-layouts, cut(): out = lax.slice(array, lo, hi)  13.4 us
  transfers between devices with their start and end apart: 52, of which 17 were waited for; matrix products, arithmetic and copies ran while one was open for 14% of the time, Pallas kernels for 48%

profile of v5, /device:TPU:0, one launch (start us, length us, event | category | flops | bytes accessed | tf_op | source)
XLA Modules:
  0.0 585.3 jit_solution(6083951489234378414)
XLA Ops:
  22.5 49.0 %shard_map.237 = (bf16[4,3456,256]{2,1,0:T(8,128)(2,1)}, bf16[4,16,256,256]{3,2,1,0:T(8,128)(2,1)}, bf16[4,1152,256]{2,1,0:T(8,128)(2,1)}, f32[4,256,1152]{2,1,0...) custom-call(s32[3]{0:T(128)} %pad_add_fusion.sc, ...), custom_call_target="tpu_custom_call" | custom-call | flops 51749998592 | bytes 45000000 | tf_op jit(solution)/shard_map/pallas_call | solution.py:387
  72.1 15.6 %shard_map.238 = (bf16[2,2304,1024]{2,1,0:T(8,128)(2,1)}, bf16[2,2304,1024]{2,1,0:T(8,128)(2,1)}, bf16[16,96,1152]{2,1,0:T(8,128)(2,1)}, f32[8,768]{1,0:T(8,128)}) custom-call(s32[3]{0:T(128)} %pad_add_fusion.sc, bf16[1024,1152]{1,0:T(8,128)(2,1)} %bitcast.200, bf16[1024,1152]{1,0:T(8,128)(2,1)} %bitcast.204, ...), custom_call_target="tpu_custom_call" | custom-call | flops 14949999616 | bytes 13000000 | tf_op jit(solution)/shard_map/pallas_call | solution.py:387
  87.9 26.5 %shard_map.239 = (bf16[2,2304,1024]{2,1,0:T(8,128)(2,1)}, bf16[2,2304,1024]{2,1,0:T(8,128)(2,1)}, bf16[16,96,1152]{2,1,0:T(8,128)(2,1)}, bf16[16,96,1152]{2,1,0:...) custom-call(s32[3]{0:T(128)} %pad_add_fusion.sc, ...), custom_call_target="tpu_custom_call", output_to_operand_aliasing={{0}: (9, {}), {1}: (10, {})} | custom-call | flops 29899999232 | bytes 26000000 | tf_op jit(solution)/shard_map/pallas_call | solution.py:387
  124.3 15.8 %shard_map.240 = (bf16[2,2304,1024]{2,1,0:T(8,128)(2,1)}, bf16[2,2304,1024]{2,1,0:T(8,128)(2,1)}, bf16[16,96,1152]{2,1,0:T(8,128)(2,1)}, f32[8,768]{1,0:T(8,128)}) custom-call(s32[3]{0:T(128)} %pad_add_fusion.sc, bf16[1024,1152]{1,0:T(8,128)(2,1)} %bitcast.202, bf16[1024,1152]{1,0:T(8,128)(2,1)} %bitcast.206, ...), custom_call_target="tpu_custom_call", output_to_operand_aliasing={{0}: (6, {}), {1}: (7, {})} | custom-call | flops 14949999616 | bytes 13000000 | tf_op jit(solution)/shard_map/pallas_call | solution.py:387
  151.1 26.5 %shard_map.241 = (bf16[2,2304,1024]{2,1,0:T(8,128)(2,1)}, bf16[2,2304,1024]{2,1,0:T(8,128)(2,1)}, bf16[16,96,1152]{2,1,0:T(8,128)(2,1)}, bf16[16,96,1152]{2,1,0:...) custom-call(s32[3]{0:T(128)} %pad_add_fusion.sc, ...), custom_call_target="tpu_custom_call", output_to_operand_aliasing={{0}: (11, {}), {1}: (12, {})} | custom-call | flops 29899999232 | bytes 26000000 | tf_op jit(solution)/shard_map/pallas_call | solution.py:387
  183.5 28.4 %shard_map.242 = (f32[4,256,1152]{2,1,0:T(8,128)}, bf16[4,256,1152]{2,1,0:T(8,128)(2,1)}, f32[4,4,1152]{2,1,0:T(4,128)}) custom-call(s32[3]{0:T(128)} %pad_add_fusion.sc, bf16[2,2304,1024]{2,1,0:T(8,128)(2,1)} %get-tuple-element.311.back, bf16[1152,2304]{1,0:T(8,128)(2,1)} %w_up0.1, bf16[1152,2304]{1,0:T(8,128)(2,1)} %collective-permute-done.4.refs_0_.refs_3_.w_up1, ...), custom_call_target="tpu_custom_call" | custom-call | flops 69000003584 | bytes 41582592 | tf_op jit(solution)/shard_map/pallas_call | solution.py:387
  214.1 20.4 %shard_map.243.refs_0_ = bf16[2,3456,256]{2,1,0:T(8,128)(2,1)} custom-call(s32[3]{0:T(128)} %pad_add_fusion.sc, bf16[4,256,1152]{2,1,0:T(8,128)(2,1)} %get-tuple-element.326.grad_attn.refs_4_, bf16[4,3456,256]{2,1,0:T(8,128)(2,1)} %get-tuple-element.327.qkv, bf16[4,16,256,256]{3,2,1,0:T(8,128)(2,1)} %get-tuple-element.328.prob, bf16[576,1152]{1,0:T(8,128)(2,1)} %refs_0_.7, ...), custom_call_target="tpu_custom_call" | custom-call | flops 69000003584 | bytes 24018944 | tf_op jit(solution)/shard_map/pallas_call | solution.py:387
  234.5 12.9 %collective-permute-done.14 = bf16[2,96,1152]{2,1,0:T(8,128)(2,1)S(1)} collective-permute-done((bf16[2,96,1152]{2,1,0:T(8,128)(2,1)S(1)}, bf16[2,96,1152]{2,1,0:T(8,128)(2,1)S(1)}, u32[]{:S(2)}, u32[]{:S(2)}) %collective-permute-start.14) | collective-permute-done | bytes 442400 | tf_op jit(solution)/shard_map/ppermute | solution.py:445
  249.1 20.8 %shard_map.244.refs_1_ = bf16[2,3456,256]{2,1,0:T(8,128)(2,1)} custom-call(s32[3]{0:T(128)} %pad_add_fusion.sc, bf16[4,256,1152]{2,1,0:T(8,128)(2,1)} %get-tuple-element.326.grad_attn.refs_4_, bf16[4,3456,256]{2,1,0:T(8,128)(2,1)} %get-tuple-element.327.qkv, bf16[4,16,256,256]{3,2,1,0:T(8,128)(2,1)} %get-tuple-element.328.prob, bf16[576,1152]{1,0:T(8,128)(2,1)} %refs_0_.7, ...), custom_call_target="tpu_custom_call" | custom-call | flops 69000003584 | bytes 24018944 | tf_op jit(solution)/shard_map/pallas_call | solution.py:387
  271.3 14.1 %shard_map.245 = (bf16[16,144,1152]{2,1,0:T(8,128)(2,1)}, f32[3,8,576]{2,1,0:T(8,128)}) custom-call(s32[3]{0:T(128)} %pad_add_fusion.sc, bf16[2,3456,256]{2,1,0:T(8,128)(2,1)} %shard_map.243.refs_0_, bf16[2,3456,256]{2,1,0:T(8,128)(2,1)} %shard_map.244.refs_1_, bf16[4,1152,256]{2,1,0:T(8,128)(2,1)} %get-tuple-element.343.refs_2_, ...), custom_call_target="tpu_custom_call" | custom-call | flops 69000003584 | bytes 19519488 | tf_op jit(solution)/shard_map/pallas_call | solution.py:387
  286.8 6.8 %collective-permute-done.16 = bf16[96,1152]{1,0:T(8,128)(2,1)S(1)} collective-permute-done((bf16[96,1152]{1,0:T(8,128)(2,1)S(1)}, bf16[96,1152]{1,0:T(8,128)(2,1)S(1)}, u32[]{:S(2)}, u32[]{:S(2)}) %collective-permute-start.16) | collective-permute-done | bytes 221216 | tf_op jit(solution)/shard_map/ppermute | solution.py:445
  293.8 14.1 %shard_map.246 = (bf16[16,144,1152]{2,1,0:T(8,128)(2,1)}, f32[3,8,576]{2,1,0:T(8,128)}) custom-call(s32[3]{0:T(128)} %pad_add_fusion.sc, bf16[2,3456,256]{2,1,0:T(8,128)(2,1)} %shard_map.243.refs_0_, bf16[2,3456,256]{2,1,0:T(8,128)(2,1)} %shard_map.244.refs_1_, bf16[4,1152,256]{2,1,0:T(8,128)(2,1)} %get-tuple-element.343.refs_2_, ...), custom_call_target="tpu_custom_call" | custom-call | flops 69000003584 | bytes 19519488 | tf_op jit(solution)/shard_map/pallas_call | solution.py:387
  327.2 24.4 %shard_map.247 = (f32[8,256,1152]{2,1,0:T(8,128)}, f32[4,256,1152]{2,1,0:T(8,128)}, f32[4,2,1152]{2,1,0:T(2,128)}) custom-call(s32[3]{0:T(128)} %pad_add_fusion.sc, bf16[2,3456,256]{2,1,0:T(8,128)(2,1)} %shard_map.243.refs_0_, bf16[2,3456,256]{2,1,0:T(8,128)(2,1)} %shard_map.244.refs_1_, bf16[1728,1152]{1,0:T(8,128)(2,1)} %bitcast.198, ...), custom_call_target="tpu_custom_call" | custom-call | flops 69000003584 | bytes 38891520 | tf_op jit(solution)/shard_map/pallas_call | solution.py:387
  351.7 16.1 %collective-permute-done.20 = bf16[2,2,2,144,384]{4,3,0,1,2:T(8,128)(2,1)} collective-permute-done((bf16[2,2,2,144,384]{4,3,0,1,2:T(8,128)(2,1)}, bf16[2,2,2,144,384]{4,3,0,1,2:T(8,128)(2,1)}, u32[]{:S(2)}, u32[]{:S(2)}) %collective-permute-start.20) | collective-permute-done | bytes 884768 | tf_op jit(solution)/shard_map/ppermute | solution.py:445
  383.0 25.7 %shard_map.248 = (bf16[8,256,1152]{2,1,0:T(8,128)(2,1)}, bf16[4,256,1152]{2,1,0:T(8,128)(2,1)}, f32[4,1,1152]{2,1,0:T(1,128)}) custom-call(s32[3]{0:T(128)} %pad_add_fusion.sc, bf16[2,2304,1024]{2,1,0:T(8,128)(2,1)} %get-tuple-element.387.act, bf16[2304,1152]{1,0:T(8,128)(2,1)} %w_down0.1, bf16[2304,1152]{1,0:T(8,128)(2,1)} %collective-permute-done.5.refs_1_.refs_4_.w_down1, ...), custom_call_target="tpu_custom_call" | custom-call | flops 69000003584 | bytes 36813312 | tf_op jit(solution)/shard_map/pallas_call | solution.py:387
  408.9 17.6 %collective-permute-done.28 = bf16[2,2,2,96,512]{4,3,2,1,0:T(8,128)(2,1)} collective-permute-done((bf16[2,2,2,96,512]{4,3,2,1,0:T(8,128)(2,1)}, bf16[2,2,2,96,512]{4,3,2,1,0:T(8,128)(2,1)}, u32[]{:S(2)}, u32[]{:S(2)}) %collective-permute-start.28) | collective-permute-done | bytes 786464 | tf_op jit(solution)/shard_map/ppermute | solution.py:445
  439.3 21.6 %collective-permute-done.30 = bf16[2,144,896]{2,1,0:T(8,128)(2,1)S(1)} collective-permute-done((bf16[2,144,896]{2,1,0:T(8,128)(2,1)}, bf16[2,144,896]{2,1,0:T(8,128)(2,1)S(1)}, u32[]{:S(2)}, u32[]{:S(2)}) %collective-permute-start.30) | collective-permute-done | bytes 516128 | tf_op jit(solution)/shard_map/ppermute | solution.py:445
  484.4 7.5 %collective-permute-done.40 = bf16[26,3456]{1,0:T(8,128)(2,1)S(1)} collective-permute-done((bf16[26,3456]{1,0:T(8,128)(2,1)S(1)}, bf16[26,3456]{1,0:T(8,128)(2,1)S(1)}, u32[]{:S(2)}, u32[]{:S(2)}) %collective-permute-start.40) | collective-permute-done | bytes 179744 | tf_op jit(solution)/shard_map/ppermute | solution.py:519
  505.0 6.3 %shard_map.250 = (f32[2304,1152]{1,0:T(8,128)}, f32[1152,2304]{1,0:T(8,128)}, f32[8,128]{1,0:T(8,128)}) custom-call(s32[3]{0:T(128)} %pad_add_fusion.sc, bf16[8,96,640]{2,1,0:T(8,128)(2,1)} %bitcast.179, bf16[8,96,640]{2,1,0:T(8,128)(2,1)} %bitcast.180, bf16[8,96,512]{2,1,0:T(8,128)(2,1)} %bitcast.90.refs_2_, bf16[8,96,512]{2,1,0:T(8,128)(2,1)} %bitcast.91.refs_3_, ...), custom_call_target="tpu_custom_call" | custom-call | flops 4600000000 | bytes 4000000 | tf_op jit(solution)/shard_map/pallas_call | solution.py:387
  522.0 5.5 shard_map.252
  532.7 10.0 %collective-permute-done.47 = bf16[104,3456]{1,0:T(8,128)(2,1)} collective-permute-done((bf16[104,3456]{1,0:T(8,128)(2,1)S(1)}, bf16[104,3456]{1,0:T(8,128)(2,1)}, u32[]{:S(2)}, u32[]{:S(2)}) %collective-permute-start.47) | collective-permute-done | bytes 718880 | tf_op jit(solution)/shard_map/ppermute | solution.py:519
  547.7 8.1 %fusion.6 = f32[1152,3456]{1,0:T(8,128)} fusion(bf16[128,1152]{1,0:T(8,128)(2,1)S(1)} %reshape.239, bf16[16,13,3456]{2,1,0:T(8,128)(2,1)S(1)} %reshape.233), kind=kOutput, calls=%fused_computation.23 | convolution fusion | flops 1019215872 | bytes 17104896 | tf_op jit(solution)/shard_map/dot_general | solution.py:1006
  555.9 8.8 %collective-permute-done.48 = bf16[2,2,2,144,512]{4,3,1,0,2:T(8,128)(2,1)} collective-permute-done((bf16[2,2,2,144,512]{4,3,1,0,2:T(8,128)(2,1)}, bf16[2,2,2,144,512]{4,3,1,0,2:T(8,128)(2,1)}, u32[]{:S(2)}, u32[]{:S(2)}) %collective-permute-start.48) | collective-permute-done | bytes 1179680 | tf_op jit(solution)/shard_map/ppermute | solution.py:445
  569.5 8.5 %shard_map.249 = (f32[1728,1152]{1,0:T(8,128)}, f32[576,1152]{1,0:T(8,128)}) custom-call(s32[3]{0:T(128)} %pad_add_fusion.sc, bf16[8,144,512]{2,1,0:T(8,128)(2,1)} %bitcast.175, bf16[8,144,512]{2,1,0:T(8,128)(2,1)} %bitcast.176, bf16[8,144,384]{2,1,0:T(8,128)(2,1)} %bitcast.82.refs_2_, bf16[8,144,384]{2,1,0:T(8,128)(2,1)} %bitcast.83.refs_3_, ...), custom_call_target="tpu_custom_call" | custom-call | flops 10350000128 | bytes 9000000 | tf_op jit(solution)/shard_map/pallas_call | solution.py:387
  (276 shorter events, 158.5 us)
Async XLA Ops:
  7.2 504.5 %all-reduce.4.cloned.1.call-start = ((), (), s32[]{:S(2)}) async-start(), calls=%async_computation | async-start | bytes 14155776 | tf_op jit(solution)/shard_map/psum | solution.py:716
  14.6 57.0 %collective-permute-start.4 = (bf16[1152,2304]{1,0:T(8,128)(2,1)}, bf16[1152,2304]{1,0:T(8,128)(2,1)}, u32[]{:S(2)}, u32[]{:S(2)}) collective-permute-start(bf16[1152,2304]{1,0:T(8,128)(2,1)} %w_up0.1), channel_id=1, source_target_pairs={{0,1},{1,0},{2,3},{3,2},{4,5},{5,4},{6,7},{7,6},{8,9},{9,8},{10,11... | collective-permute-start | bytes 15925256 | tf_op jit(solution)/shard_map/ppermute | solution.py:418
  14.9 56.6 %collective-permute-start.5 = (bf16[2304,1152]{1,0:T(8,128)(2,1)}, bf16[2304,1152]{1,0:T(8,128)(2,1)}, u32[]{:S(2)}, u32[]{:S(2)}) collective-permute-start(bf16[2304,1152]{1,0:T(8,128)(2,1)} %w_down0.1), channel_id=1, source_target_pairs={{0,1},{1,0},{2,3},{3,2},{4,5},{5,4},{6,7},{7,6},{8,9},{9,8},{10,11... | collective-permute-start | bytes 15925256 | tf_op jit(solution)/shard_map/ppermute | solution.py:418
  18.1 53.5 %collective-permute-start.6 = (bf16[1,2304]{1,0:T(2,128)(2,1)S(1)}, bf16[1,2304]{1,0:T(2,128)(2,1)S(1)}, u32[]{:S(2)}, u32[]{:S(2)}) collective-permute-start(bf16[1,2304]{1,0:T(2,128)(2,1)S(1)} %broadcast_in_dim.34), channel_id=1, source_target_pairs={{0,1},{1,0},{2,3},{3,2},{4,5},{5,4},{6,7},{7,6},{8,9},{9,8},{10,11... | collective-permute-start | bytes 13832 | tf_op jit(solution)/shard_map/ppermute | solution.py:418
  87.7 55.0 %collective-permute-start.7 = (bf16[16,96,1152]{2,1,0:T(8,128)(2,1)}, bf16[16,96,1152]{2,1,0:T(8,128)(2,1)S(1)}, u32[]{:S(2)}, u32[]{:S(2)}) collective-permute-start(bf16[16,96,1152]{2,1,0:T(8,128)(2,1)} %get-tuple-element.288), channel_id=1, source_target_pairs={{0,1},{1,0},{2,3},{3,2},{4,5},{5,4},{6,7},{7,6},{8,9},{9,8},{10,11... | collective-permute-start | bytes 10616840 | tf_op jit(solution)/shard_map/ppermute | solution.py:418
  114.5 28.2 %collective-permute-start.8 = (bf16[16,96,1152]{2,1,0:T(8,128)(2,1)}, bf16[16,96,1152]{2,1,0:T(8,128)(2,1)}, u32[]{:S(2)}, u32[]{:S(2)}) collective-permute-start(bf16[16,96,1152]{2,1,0:T(8,128)(2,1)} %get-tuple-element.289), channel_id=1, source_target_pairs={{0,1},{1,0},{2,3},{3,2},{4,5},{5,4},{6,7},{7,6},{8,9},{9,8},{10,11... | collective-permute-start | bytes 10616840 | tf_op jit(solution)/shard_map/ppermute | solution.py:418
  146.7 33.7 %collective-permute-start.11 = (bf16[2,2,2,96,512]{4,3,0,1,2:T(8,128)(2,1)S(1)}, bf16[2,2,2,96,512]{4,3,0,1,2:T(8,128)(2,1)}, u32[]{:S(2)}, u32[]{:S(2)}) collective-permute-start(bf16[2,2,2,96,512]{4,3,0,1,2:T(8,128)(2,1)S(1)} %get-tuple-element.304), channel_id=1, source_target_pairs={{0,4},{2,6},{4,0},{6,2},{8,12},{10,14},{12,8},{14,10},{16,20},{18,... | collective-permute-start | bytes 2359304 | tf_op jit(solution)/shard_map/ppermute | solution.py:445
  149.6 30.7 %collective-permute-start.10 = (bf16[2,2,2,96,640]{4,3,0,1,2:T(8,128)(2,1)S(1)}, bf16[2,2,2,96,640]{4,3,0,1,2:T(8,128)(2,1)}, u32[]{:S(2)}, u32[]{:S(2)}) collective-permute-start(bf16[2,2,2,96,640]{4,3,0,1,2:T(8,128)(2,1)S(1)} %get-tuple-element.303), channel_id=1, source_target_pairs={{0,2},{2,0},{4,6},{6,4},{8,10},{10,8},{12,14},{14,12},{16,18},{18,... | collective-permute-start | bytes 2949128 | tf_op jit(solution)/shard_map/ppermute | solution.py:445
  182.9 29.0 %collective-permute-start.13 = (bf16[2,2,96,512]{3,2,0,1:T(8,128)(2,1)S(1)}, bf16[2,2,96,512]{3,2,0,1:T(8,128)(2,1)S(1)}, u32[]{:S(2)}, u32[]{:S(2)}) collective-permute-start(bf16[2,2,96,512]{3,2,0,1:T(8,128)(2,1)S(1)} %get-tuple-element.319), channel_id=1, source_target_pairs={{0,2},{2,0},{4,6},{6,4},{8,10},{10,8},{12,14},{14,12},{16,18},{18,... | collective-permute-start | bytes 1179656 | tf_op jit(solution)/shard_map/ppermute | solution.py:445
  183.5 28.5 %collective-permute-start.12 = (bf16[2,2,96,640]{3,2,0,1:T(8,128)(2,1)S(1)}, bf16[2,2,96,640]{3,2,0,1:T(8,128)(2,1)S(1)}, u32[]{:S(2)}, u32[]{:S(2)}) collective-permute-start(bf16[2,2,96,640]{3,2,0,1:T(8,128)(2,1)S(1)} %get-tuple-element.318), channel_id=1, source_target_pairs={{0,4},{2,6},{4,0},{6,2},{8,12},{10,14},{12,8},{14,10},{16,20},{18,... | collective-permute-start | bytes 1474568 | tf_op jit(solution)/shard_map/ppermute | solution.py:445
  212.1 35.3 %collective-permute-start.14 = (bf16[2,96,1152]{2,1,0:T(8,128)(2,1)S(1)}, bf16[2,96,1152]{2,1,0:T(8,128)(2,1)S(1)}, u32[]{:S(2)}, u32[]{:S(2)}) collective-permute-start(bf16[2,96,1152]{2,1,0:T(8,128)(2,1)S(1)} %pad_maximum_fusion.11), channel_id=1, source_target_pairs={{0,8},{2,10},{4,12},{6,14},{8,0},{10,2},{12,4},{14,6},{16,24},{18,... | collective-permute-start | bytes 1327112 | tf_op jit(solution)/shard_map/ppermute | solution.py:445
  321.3 30.4 %collective-permute-start.23 = (bf16[2,2,96,512]{3,2,1,0:T(8,128)(2,1)S(1)}, bf16[2,2,96,512]{3,2,1,0:T(8,128)(2,1)}, u32[]{:S(2)}, u32[]{:S(2)}) collective-permute-start(bf16[2,2,96,512]{3,2,1,0:T(8,128)(2,1)S(1)} %pad_maximum_fusion.14), channel_id=1, source_target_pairs={{0,2},{2,0},{4,6},{6,4},{8,10},{10,8},{12,14},{14,12},{16,18},{18,... | collective-permute-start | bytes 1179656 | tf_op jit(solution)/shard_map/ppermute | solution.py:445
  322.6 29.1 %collective-permute-start.22 = (bf16[2,2,96,640]{3,2,1,0:T(8,128)(2,1)S(1)}, bf16[2,2,96,640]{3,2,1,0:T(8,128)(2,1)S(1)}, u32[]{:S(2)}, u32[]{:S(2)}) collective-permute-start(bf16[2,2,96,640]{3,2,1,0:T(8,128)(2,1)S(1)} %fusion.14), channel_id=1, source_target_pairs={{0,4},{2,6},{4,0},{6,2},{8,12},{10,14},{12,8},{14,10},{16,20},{18,... | collective-permute-start | bytes 1474568 | tf_op jit(solution)/shard_map/ppermute | solution.py:445
  323.4 28.3 %collective-permute-start.21 = (bf16[2,2,2,144,256]{4,3,1,2,0:T(8,128)(2,1)}, bf16[2,2,2,144,256]{4,3,1,2,0:T(8,128)(2,1)}, u32[]{:S(2)}, u32[]{:S(2)}) collective-permute-start(bf16[2,2,2,144,256]{4,3,1,2,0:T(8,128)(2,1)} %fusion.13), channel_id=1, source_target_pairs={{0,8},{2,10},{4,12},{6,14},{8,0},{10,2},{12,4},{14,6},{16,24},{18,... | collective-permute-start | bytes 1769480 | tf_op jit(solution)/shard_map/ppermute | solution.py:445
  325.3 42.4 %collective-permute-start.20 = (bf16[2,2,2,144,384]{4,3,0,1,2:T(8,128)(2,1)}, bf16[2,2,2,144,384]{4,3,0,1,2:T(8,128)(2,1)}, u32[]{:S(2)}, u32[]{:S(2)}) collective-permute-start(bf16[2,2,2,144,384]{4,3,0,1,2:T(8,128)(2,1)} %fusion.5), channel_id=1, source_target_pairs={{0,4},{2,6},{4,0},{6,2},{8,12},{10,14},{12,8},{14,10},{16,20},{18,... | collective-permute-start | bytes 2654216 | tf_op jit(solution)/shard_map/ppermute | solution.py:445
  326.5 42.4 %collective-permute-start.19 = (bf16[2,2,2,144,512]{4,3,0,1,2:T(8,128)(2,1)}, bf16[2,2,2,144,512]{4,3,0,1,2:T(8,128)(2,1)}, u32[]{:S(2)}, u32[]{:S(2)}) collective-permute-start(bf16[2,2,2,144,512]{4,3,0,1,2:T(8,128)(2,1)} %fusion.1), channel_id=1, source_target_pairs={{0,2},{2,0},{4,6},{6,4},{8,10},{10,8},{12,14},{14,12},{16,18},{18,... | collective-permute-start | bytes 3538952 | tf_op jit(solution)/shard_map/ppermute | solution.py:445
  377.1 31.6 %collective-permute-start.26 = (bf16[2,2,144,256]{3,2,0,1:T(8,128)(2,1)}, bf16[2,2,144,256]{3,2,0,1:T(8,128)(2,1)}, u32[]{:S(2)}, u32[]{:S(2)}) collective-permute-start(bf16[2,2,144,256]{3,2,0,1:T(8,128)(2,1)} %get-tuple-element.396), channel_id=1, source_target_pairs={{0,16},{2,18},{4,20},{6,22},{8,24},{10,26},{12,28},{14,30},{16,0},... | collective-permute-start | bytes 884744 | tf_op jit(solution)/shard_map/ppermute | solution.py:445
  378.5 30.4 %collective-permute-start.25 = (bf16[2,2,144,384]{3,2,0,1:T(8,128)(2,1)}, bf16[2,2,144,384]{3,2,0,1:T(8,128)(2,1)S(1)}, u32[]{:S(2)}, u32[]{:S(2)}) collective-permute-start(bf16[2,2,144,384]{3,2,0,1:T(8,128)(2,1)} %get-tuple-element.395), channel_id=1, source_target_pairs={{0,2},{2,0},{4,6},{6,4},{8,10},{10,8},{12,14},{14,12},{16,18},{18,... | collective-permute-start | bytes 1327112 | tf_op jit(solution)/shard_map/ppermute | solution.py:445
  382.5 44.0 %collective-permute-start.28 = (bf16[2,2,2,96,512]{4,3,2,1,0:T(8,128)(2,1)}, bf16[2,2,2,96,512]{4,3,2,1,0:T(8,128)(2,1)}, u32[]{:S(2)}, u32[]{:S(2)}) collective-permute-start(bf16[2,2,2,96,512]{4,3,2,1,0:T(8,128)(2,1)} %pad_maximum_fusion.4), channel_id=1, source_target_pairs={{0,4},{2,6},{4,0},{6,2},{8,12},{10,14},{12,8},{14,10},{16,20},{18,... | collective-permute-start | bytes 2359304 | tf_op jit(solution)/shard_map/ppermute | solution.py:445
  383.0 43.5 %collective-permute-start.27 = (bf16[2,2,2,96,640]{4,3,1,0,2:T(8,128)(2,1)S(1)}, bf16[2,2,2,96,640]{4,3,1,0,2:T(8,128)(2,1)S(1)}, u32[]{:S(2)}, u32[]{:S(2)}) collective-permute-start(bf16[2,2,2,96,640]{4,3,1,0,2:T(8,128)(2,1)S(1)} %pad_maximum_fusion.2), channel_id=1, source_target_pairs={{0,2},{2,0},{4,6},{6,4},{8,10},{10,8},{12,14},{14,12},{16,18},{18,... | collective-permute-start | bytes 2949128 | tf_op jit(solution)/shard_map/ppermute | solution.py:445
  408.8 74.9 %collective-permute-start.36 = (f32[4,256,1152]{2,1,0:T(8,128)}, f32[4,256,1152]{2,1,0:T(8,128)}, u32[]{:S(2)}, u32[]{:S(2)}) collective-permute-start(f32[4,256,1152]{2,1,0:T(8,128)} %get-tuple-element.444), channel_id=1, source_target_pairs={{0,1},{1,0},{2,3},{3,2},{4,5},{5,4},{6,7},{7,6},{8,9},{9,8},{10,11... | collective-permute-start | bytes 14155784 | tf_op jit(solution)/shard_map/ppermute | solution.py:418
  432.9 37.5 %collective-permute-start.32 = (bf16[4,256,1152]{2,1,0:T(8,128)(2,1)}, bf16[4,256,1152]{2,1,0:T(8,128)(2,1)S(1)}, u32[]{:S(2)}, u32[]{:S(2)}) collective-permute-start(bf16[4,256,1152]{2,1,0:T(8,128)(2,1)} %get-tuple-element.427), channel_id=1, source_target_pairs={{0,1},{1,0},{2,3},{3,2},{4,5},{5,4},{6,7},{7,6},{8,9},{9,8},{10,11... | collective-permute-start | bytes 7077896 | tf_op jit(solution)/shard_map/ppermute | solution.py:418
  514.6 28.0 %collective-permute-start.47 = (bf16[104,3456]{1,0:T(8,128)(2,1)S(1)}, bf16[104,3456]{1,0:T(8,128)(2,1)}, u32[]{:S(2)}, u32[]{:S(2)}) collective-permute-start(bf16[104,3456]{1,0:T(8,128)(2,1)S(1)} %pad_maximum_fusion.5), channel_id=1, source_target_pairs={{0,2},{2,0},{4,6},{6,4},{8,10},{10,8},{12,14},{14,12},{16,18},{18,... | collective-permute-start | bytes 2156552 | tf_op jit(solution)/shard_map/ppermute | solution.py:519
  532.0 32.7 %collective-permute-start.48 = (bf16[2,2,2,144,512]{4,3,1,0,2:T(8,128)(2,1)}, bf16[2,2,2,144,512]{4,3,1,0,2:T(8,128)(2,1)}, u32[]{:S(2)}, u32[]{:S(2)}) collective-permute-start(bf16[2,2,2,144,512]{4,3,1,0,2:T(8,128)(2,1)} %pad_maximum_fusion.1), channel_id=1, source_target_pairs={{0,2},{2,0},{4,6},{6,4},{8,10},{10,8},{12,14},{14,12},{16,18},{18,... | collective-permute-start | bytes 3538952 | tf_op jit(solution)/shard_map/ppermute | solution.py:445
  (57 other events, 813.9 us)
Sparse Core Ops, SparseCore 0:
  180.5 277.8 all-reduce.3

commit v6 on v4

--- a/solution.py
+++ b/solution.py
@@ -336,22 +336,6 @@
             store(high[index].astype(f32), lo, hi)
 
 
-def final_mlp_kernel(cuts, per, sc, *refs):
-    count = 2 * len(cuts)
-    arrays, (_, _, down, up, mark, turned) = refs[:count], refs[count:]
-    here = down.shape[0] // per
-    halves = [(arrays[2 * k], arrays[2 * k + 1]) + cut for k, cut in enumerate(cuts)]
-    for piece in range(here):
-
-        def store(value, lo, hi, piece=piece):
-            down[piece * per : (piece + 1) * per, lo:hi] = value[0:per]
-            turned[piece * per : (piece + 1) * per, lo:hi] = value[per : 2 * per]
-
-        final_piece(sc, halves, pl.program_id(0) * here + piece, store)
-    up[...] = turned[...].T
-    mark[...] = jnp.zeros_like(mark)
-
-
 def final_plain_kernel(per, sc, summed, down_in, up_in, down, up, mark, turned):
     for piece in range(summed.shape[0]):
         lo = piece * per
@@ -422,7 +406,6 @@
     return [(index, index ^ (1 << bit)) for index in range(16)]
 
 
-MLP_WAYS = ((0, 640, (0, 1, 2, 3)), (640, 1152, (1, 0, 2, 3)))
 ATTN_WAYS = ((0, 512, (0, 1, 2, 3)), (512, 896, (1, 0, 2, 3)), (896, 1152, (2, 3, 0, 1)))
 
 
@@ -513,6 +496,14 @@
     return came
 
 
+def both_flow(own, given):
+    (own, given) = yield [own, given]
+    came = swap_cores(given)
+    yield None
+    own, came = yield [own, came]
+    return (yield from rows_flow(own + came))
+
+
 def rows_flow(rows):
     for bit in (3, 2, 1, 0):
         (rows,) = yield [rows]
@@ -556,7 +547,6 @@
 
 
 CHUNKS = 3
-PLAIN = 2
 
 
 def fill_other(both, came, core):
@@ -644,7 +634,7 @@
     def mlp_call(jobs, came, micros):
         nonlocal act, back
         first = act.shape[0] == 8
-        kinds = tuple((chunk < PLAIN, (chunk, part) in came) for chunk, part in jobs)
+        kinds = tuple((True, job in came) for job in jobs)
 
         def turn(k):
             return lambda p, s, c: jnp.clip((p - k) * steps + s, 0, steps - 1)
@@ -703,18 +693,27 @@
         order.after(outs[-1])
         return grads
 
-    summed = range(PLAIN)
-    swaps = [swap_flow(grad) for grad in mlp_call([(chunk, 1) for chunk in summed], {}, 26)]
-    order.tick(*swaps)
-    rest = [(chunk, part) for chunk in range(PLAIN, CHUNKS) for part in (1, 0)]
-    grads = mlp_call(rest, {}, 26)
-    flows = [
-        sum_flow(MLP_WAYS, lambda own=own: own, other) for other, own in zip(grads[0::2], grads[1::2])
-    ]
-    order.tick(*swaps, *flows)
-    came = {(chunk, 0): order.results[swap] for chunk, swap in zip(summed, swaps)}
-    plain_sums = lax.psum(mlp_call([(chunk, 0) for chunk in summed], came, 26), "dp")
-    order.tick(*flows)
+    swaps = {}
+    for chunks in ((0, 1), (2,)):
+        grads = mlp_call([(chunk, 1) for chunk in chunks], {}, 13 * len(chunks))
+        swaps.update({chunk: swap_flow(grad) for chunk, grad in zip(chunks, grads)})
+        order.tick(*[swaps[chunk] for chunk in sorted(swaps)])
+    wide_scaled = jnp.pad(scaled.reshape(-1), (0, 3 * own_cols - slots * dim)).reshape(3, own_cols)
+    early = rows_flow(wide_scaled)
+    sums_in = []
+    for chunks in ((0, 1), (2,)):
+        came = {(chunk, 0): order.finish(swaps[chunk]) for chunk in chunks}
+        if chunks == (2,):
+            order.tick(early)
+        sums_in += mlp_call([(chunk, 0) for chunk in chunks], came, 13 * len(chunks))
+    plain_sums = lax.psum(sums_in, "dp")
+    down_row = jnp.sum(down_sums[:, 0], axis=0, keepdims=True)
+    own_row, other_row = (
+        jnp.concatenate([up_sums[chunk, part] for chunk in range(CHUNKS)] + [down_row], axis=1)
+        for part in range(2)
+    )
+    bias_flow = both_flow(own_row, other_row)
+    order.tick(early, bias_flow)
 
     reach = 768
     turns = ff // reach
@@ -754,7 +753,7 @@
         scratch=[pltpu.VMEM((count, dim), f32)],
     )
     order.after(mid_sums)
-    order.tick(*flows)
+    order.tick(early, bias_flow)
     pieces = 2
     each = images // pieces
     grad_qkv = []
@@ -778,7 +777,7 @@
             )
         grad_qkv.append(grad_piece)
         order.after(grad_piece)
-        order.tick(*flows)
+        order.tick(early, bias_flow)
 
     attn_per = 4 * cols // 16
     qv_sums = [None, None]
@@ -809,9 +808,9 @@
     grad_other = attn_part(1)
     made = []
     last = sum_flow(ATTN_WAYS, lambda: made[0], grad_other)
-    order.tick(last, *flows)
+    order.tick(last, early, bias_flow)
     made.append(attn_part(0))
-    order.tick(last, *flows)
+    order.tick(last, early, bias_flow)
 
     first_spec = lambda part: pl.BlockSpec((cols, dim), lambda s, c: (rows_of(part, 3)(s, c), 0))
     grad_tokens, grad_own_tokens, low_sums = run_kernel(
@@ -828,7 +827,7 @@
         scratch=[pltpu.VMEM((count, dim), f32)],
     )
     order.after(low_sums)
-    order.tick(last, *flows)
+    order.tick(last)
     other_tokens = swap_cores(grad_own_tokens)
     down_spec = lambda part: pl.BlockSpec((reach, dim), lambda s, c: (rows_of(part, turns)(s, c), 0))
     output, own_output, gate_sums = run_kernel(
@@ -851,56 +850,41 @@
         scratch=[pltpu.VMEM((count, dim), f32)],
     )
     order.after(gate_sums)
-    order.tick(last, *flows)
+    order.tick(last)
     other_output = swap_cores(own_output)
 
-    low_sums, mid_sums, gate_sums, down_sums = order.fence((low_sums, mid_sums, gate_sums, down_sums))
+    low_sums, mid_sums, gate_sums = order.fence((low_sums, mid_sums, gate_sums))
     grad_modulation = jnp.concatenate([low_sums, mid_sums[:, 2:3], mid_sums[:, 0:2], gate_sums], axis=1)
     grad_modulation = grad_modulation.reshape(images, 6 * dim).astype(bf16)
-    bias_sums = [
-        jnp.concatenate(
-            [qv_sums[part][0, 0:1], qv_sums[part][2, 0:1]]
-            + [up_sums[chunk, part] for chunk in range(CHUNKS)],
-            axis=1,
-        )
+    proj_row = jnp.sum(mid_sums[:, 3], axis=0, keepdims=True)
+    fill = jnp.zeros((1, own_cols - 2 * cols - dim), f32)
+    rows_kept, rows_given = (
+        jnp.concatenate([qv_sums[part][0, 0:1], qv_sums[part][2, 0:1], proj_row, fill], axis=1)
         for part in range(2)
-    ]
-    shared = jnp.concatenate(
-        [
-            jnp.sum(mid_sums[:, 3], axis=0, keepdims=True),
-            jnp.sum(down_sums[:, 0], axis=0, keepdims=True),
-            jnp.zeros((1, own_cols - 2 * dim), f32),
-        ],
-        axis=1,
     )
     halves = grad_modulation.reshape(images, 2, own_cols)
     kept = lax.dynamic_index_in_dim(halves, core, 1, keepdims=False)
     given = lax.dynamic_index_in_dim(halves, 1 - core, 1, keepdims=False)
-    got = swap_cores(jnp.concatenate([given.astype(f32), bias_sums[1], shared]))
+    got = swap_cores(jnp.concatenate([given.astype(f32), rows_given]))
     came = got[:images].astype(bf16)
     group_mod = jnp.where(core == 0, jnp.concatenate([kept, came]), jnp.concatenate([came, kept]))
-    own_bias_sum = bias_sums[0] + got[images : images + 1]
-    shared_sum = shared + got[images + 1 :]
-    wide_scaled = jnp.pad(scaled.reshape(-1), (0, 3 * own_cols - slots * dim)).reshape(3, own_cols)
-    packed_rows = jnp.concatenate(
-        [group_mod, own_bias_sum.astype(bf16), shared_sum.astype(bf16), wide_scaled]
-    )
+    packed_rows = jnp.concatenate([group_mod, (rows_kept + got[images:]).astype(bf16)])
     (packed_rows,) = order.fence([packed_rows])
     small = rows_flow(packed_rows)
-    order.tick(last, small, *flows)
+    order.tick(last, small)
     (group_mod,) = order.fence([group_mod])
     part_scaled = outer_cols(group_mod, w_mod).astype(bf16)
     came_scaled = swap_cores(part_scaled)
     output = fill_other(output, order.fence(other_output), core)
     order.after((output[0, 0, :1], part_scaled[0, :1]))
-    order.tick(last, small, *flows)
+    order.tick(last, small)
     grad_tokens = fill_other(grad_tokens, order.fence(other_tokens), core)
     part_scaled, came_scaled = order.fence((part_scaled, came_scaled))
     grad_scaled = part_scaled.astype(f32) + came_scaled.astype(f32)
     _, silu_back = jax.vjp(jax.nn.silu, cond_f)
     grad_condition = silu_back(grad_scaled)[0]
     order.after((grad_tokens[0, 0, :1], grad_condition[0, :1]))
-    order.tick(last, small, *flows)
+    order.tick(last, small)
 
     def cuts(ways):
         return tuple((way[0], lo, hi) for lo, hi, way in ways)
@@ -935,21 +919,19 @@
         )
         order.after(mark)
 
-    for chunk, flow in enumerate(flows):
-        body = functools.partial(final_mlp_kernel, cuts(MLP_WAYS), per)
-        final_mlp(PLAIN + chunk, body, order.finish(flow))
     order.tick(last, small)
-    all_rows = order.fence(order.finish(small)).reshape(16, slots + 5, own_cols)
+    all_rows = order.fence(order.finish(small)).reshape(16, slots + 1, own_cols)
     all_mod = all_rows[:, :slots].reshape(-1, own_cols)
-    all_scaled = all_rows[:, slots + 2 :].reshape(16, -1)[:, : slots * dim].reshape(-1, dim)
+    all_scaled = order.finish(early).reshape(16, -1)[:, : slots * dim].reshape(-1, dim)
     grad_w_mod = inner_rows(all_scaled, all_mod)
     grad_b_mod = jnp.sum(all_mod.astype(f32), axis=0)
-    bias_total = jnp.sum(all_rows[:, slots : slots + 2].astype(f32), axis=0)
-    grad_b_qv = bias_total[0, : 2 * cols].reshape(2, cols)
-    grad_b_up = bias_total[0, 2 * cols :]
-    grad_b_proj = bias_total[1, :dim]
-    grad_b_down = bias_total[1, dim : 2 * dim]
-    order.after((grad_w_mod[0, :1], grad_b_mod[:1], bias_total[0, :1]))
+    late_total = jnp.sum(all_rows[:, slots].astype(f32), axis=0)
+    early_total = jnp.sum(order.finish(bias_flow), axis=0)
+    grad_b_qv = late_total[: 2 * cols].reshape(2, cols)
+    grad_b_proj = late_total[2 * cols : 2 * cols + dim]
+    grad_b_up = early_total[:ff]
+    grad_b_down = early_total[ff : ff + dim]
+    order.after((grad_w_mod[0, :1], grad_b_mod[:1], late_total[:1]))
     args = order.finish(last)
     grad_qkv_rows, grad_w_proj = run_kernel(
         functools.partial(final_attn_kernel, cuts(ATTN_WAYS), attn_per),

time: 586 us -> 619 us (1.056)
  waiting for transfers between devices: 107 us -> 145 us
  local copies, waits for them, and re-layouts: 52 us -> 44.4 us
    ppermute x32 -> x20, waiting for transfers between devices: 86.4 us -> 108 us  [exchange(): lax.ppermute(value, 'dp', bit_pairs(bit))]
    ppermute x4 -> x12, starting transfers between devices: 2.94 us -> 21.4 us  [rows_flow(): came = lax.ppermute(rows, 'dp', bit_pairs(bit))]
    ppermute x32 -> x20, starting transfers between devices: 42.5 us -> 25.8 us  [exchange(): lax.ppermute(value, 'dp', bit_pairs(bit))]
    ppermute x4 -> x12, waiting for transfers between devices: 17.3 us -> 31.3 us  [rows_flow(): came = lax.ppermute(rows, 'dp', bit_pairs(bit))]
    add x21 -> x11, other arithmetic: 14.3 us -> 9.33 us  [reduce_flow(): cut(one, bits, route[stage], side, cols)]
    slice x10 -> x6, local copies, waits for them, and re-layouts: 13.6 us -> 9.9 us  [cut(): out = lax.slice(array, lo, hi)]
    pallas_call x15 -> x16, Pallas kernels: 302 us -> 304 us  [run_kernel(): pl.pallas_call(body, out_shape=out_shape, grid_spec=pltpu.PrefetchScalarG...]
  transfers between devices with their start and end apart: 52 -> 49, of which waited for: 21 -> 20; matrix products, arithmetic and copies ran while one was open for 17% -> 15% of each run, Pallas kernels for 44% -> 39%
where the time goes in v6:
time: 619 us; the launch traced here: 610 us
  Pallas kernels  304 us (49%)
  waiting for transfers between devices  145 us (23%)
  starting transfers between devices  50.7 us (8%)
  local copies, waits for them, and re-layouts  44.4 us (7%)
  other arithmetic  32 us (5%)
  matrix products  19.1 us (3%)
  between operations  15.8 us (3%)
    pallas_call x16, Pallas kernels, run_kernel(): pl.pallas_call(body, out_shape=out_shape, grid_spec=pltpu.PrefetchScalarG...  304 us
    ppermute x20, waiting for transfers between devices, exchange(): lax.ppermute(value, 'dp', bit_pairs(bit))  108 us
    ppermute x12, waiting for transfers between devices, rows_flow(): came = lax.ppermute(rows, 'dp', bit_pairs(bit))  31.3 us
    ppermute x20, starting transfers between devices, exchange(): lax.ppermute(value, 'dp', bit_pairs(bit))  25.8 us
    ppermute x12, starting transfers between devices, rows_flow(): came = lax.ppermute(rows, 'dp', bit_pairs(bit))  21.4 us
  transfers between devices with their start and end apart: 49, of which 20 were waited for; matrix products, arithmetic and copies ran while one was open for 15% of the time, Pallas kernels for 39%

profile of v6, /device:TPU:0, one launch (start us, length us, event | category | flops | bytes accessed | tf_op | source)
XLA Modules:
  0.0 610.0 jit_solution(14530301651859869048)
XLA Ops:
  22.5 49.0 %shard_map.237 = (bf16[4,3456,256]{2,1,0:T(8,128)(2,1)}, bf16[4,16,256,256]{3,2,1,0:T(8,128)(2,1)}, bf16[4,1152,256]{2,1,0:T(8,128)(2,1)}, f32[4,256,1152]{2,1,0...) custom-call(s32[3]{0:T(128)} %pad_add_fusion.sc, ...), custom_call_target="tpu_custom_call" | custom-call | flops 51749998592 | bytes 45000000 | tf_op jit(solution)/shard_map/pallas_call | solution.py:371
  72.2 26.4 %shard_map.238 = (bf16[2,2304,1024]{2,1,0:T(8,128)(2,1)}, bf16[2,2304,1024]{2,1,0:T(8,128)(2,1)}, bf16[16,96,1152]{2,1,0:T(8,128)(2,1)}, bf16[16,96,1152]{2,1,0:...) custom-call(s32[3]{0:T(128)} %pad_add_fusion.sc, bf16[1024,1152]{1,0:T(8,128)(2,1)} %bitcast.130, ...), custom_call_target="tpu_custom_call" | custom-call | flops 29899999232 | bytes 26000000 | tf_op jit(solution)/shard_map/pallas_call | solution.py:371
  99.2 14.7 %shard_map.239 = (bf16[2,2304,1024]{2,1,0:T(8,128)(2,1)}, bf16[2,2304,1024]{2,1,0:T(8,128)(2,1)}, bf16[16,96,1152]{2,1,0:T(8,128)(2,1)}, f32[8,768]{1,0:T(8,128)}) custom-call(s32[3]{0:T(128)} %pad_add_fusion.sc, bf16[1024,1152]{1,0:T(8,128)(2,1)} %bitcast.131, bf16[1024,1152]{1,0:T(8,128)(2,1)} %bitcast.135, ...), custom_call_target="tpu_custom_call", output_to_operand_aliasing={{0}: (6, {}), {1}: (7, {})} | custom-call | flops 14949999616 | bytes 13000000 | tf_op jit(solution)/shard_map/pallas_call | solution.py:371
  117.7 26.9 %shard_map.240 = (bf16[2,2304,1024]{2,1,0:T(8,128)(2,1)}, bf16[2,2304,1024]{2,1,0:T(8,128)(2,1)}, bf16[16,96,1152]{2,1,0:T(8,128)(2,1)}, bf16[16,96,1152]{2,1,0:...) custom-call(s32[3]{0:T(128)} %pad_add_fusion.sc, ...), custom_call_target="tpu_custom_call", output_to_operand_aliasing={{0}: (11, {}), {1}: (12, {})} | custom-call | flops 29899999232 | bytes 26000000 | tf_op jit(solution)/shard_map/pallas_call | solution.py:371
  146.1 14.8 %shard_map.241 = (bf16[2,2304,1024]{2,1,0:T(8,128)(2,1)}, bf16[2,2304,1024]{2,1,0:T(8,128)(2,1)}, bf16[16,96,1152]{2,1,0:T(8,128)(2,1)}, f32[8,768]{1,0:T(8,128)}) custom-call(s32[3]{0:T(128)} %pad_add_fusion.sc, bf16[1024,1152]{1,0:T(8,128)(2,1)} %bitcast.133, bf16[1024,1152]{1,0:T(8,128)(2,1)} %bitcast.137, ...), custom_call_target="tpu_custom_call", output_to_operand_aliasing={{0}: (7, {}), {1}: (8, {})} | custom-call | flops 14949999616 | bytes 13000000 | tf_op jit(solution)/shard_map/pallas_call | solution.py:371
  169.5 27.7 %shard_map.242 = (f32[4,256,1152]{2,1,0:T(8,128)}, bf16[4,256,1152]{2,1,0:T(8,128)(2,1)}, f32[4,4,1152]{2,1,0:T(4,128)}) custom-call(s32[3]{0:T(128)} %pad_add_fusion.sc, bf16[2,2304,1024]{2,1,0:T(8,128)(2,1)} %get-tuple-element.287.back, bf16[1152,2304]{1,0:T(8,128)(2,1)} %w_up0.1, bf16[1152,2304]{1,0:T(8,128)(2,1)} %collective-permute-done.4.refs_0_.refs_3_.w_up1, ...), custom_call_target="tpu_custom_call" | custom-call | flops 69000003584 | bytes 41582592 | tf_op jit(solution)/shard_map/pallas_call | solution.py:371
  201.6 20.8 %shard_map.243.refs_0_ = bf16[2,3456,256]{2,1,0:T(8,128)(2,1)} custom-call(s32[3]{0:T(128)} %pad_add_fusion.sc, bf16[4,256,1152]{2,1,0:T(8,128)(2,1)} %get-tuple-element.301.grad_attn.refs_4_, bf16[4,3456,256]{2,1,0:T(8,128)(2,1)} %get-tuple-element.302.qkv, bf16[4,16,256,256]{3,2,1,0:T(8,128)(2,1)} %get-tuple-element.303.prob, bf16[576,1152]{1,0:T(8,128)(2,1)} %refs_0_.7, ...), custom_call_target="tpu_custom_call" | custom-call | flops 69000003584 | bytes 24018944 | tf_op jit(solution)/shard_map/pallas_call | solution.py:371
  225.1 20.5 %shard_map.244.refs_1_ = bf16[2,3456,256]{2,1,0:T(8,128)(2,1)} custom-call(s32[3]{0:T(128)} %pad_add_fusion.sc, bf16[4,256,1152]{2,1,0:T(8,128)(2,1)} %get-tuple-element.301.grad_attn.refs_4_, bf16[4,3456,256]{2,1,0:T(8,128)(2,1)} %get-tuple-element.302.qkv, bf16[4,16,256,256]{3,2,1,0:T(8,128)(2,1)} %get-tuple-element.303.prob, bf16[576,1152]{1,0:T(8,128)(2,1)} %refs_0_.7, ...), custom_call_target="tpu_custom_call" | custom-call | flops 69000003584 | bytes 24018944 | tf_op jit(solution)/shard_map/pallas_call | solution.py:371
  246.2 14.0 %shard_map.245 = (bf16[16,144,1152]{2,1,0:T(8,128)(2,1)}, f32[3,8,576]{2,1,0:T(8,128)}) custom-call(s32[3]{0:T(128)} %pad_add_fusion.sc, bf16[2,3456,256]{2,1,0:T(8,128)(2,1)} %shard_map.243.refs_0_, bf16[2,3456,256]{2,1,0:T(8,128)(2,1)} %shard_map.244.refs_1_, bf16[4,1152,256]{2,1,0:T(8,128)(2,1)} %get-tuple-element.320.refs_2_, ...), custom_call_target="tpu_custom_call" | custom-call | flops 69000003584 | bytes 19519488 | tf_op jit(solution)/shard_map/pallas_call | solution.py:371
  262.1 14.1 %shard_map.246 = (bf16[16,144,1152]{2,1,0:T(8,128)(2,1)}, f32[3,8,576]{2,1,0:T(8,128)}) custom-call(s32[3]{0:T(128)} %pad_add_fusion.sc, bf16[2,3456,256]{2,1,0:T(8,128)(2,1)} %shard_map.243.refs_0_, bf16[2,3456,256]{2,1,0:T(8,128)(2,1)} %shard_map.244.refs_1_, bf16[4,1152,256]{2,1,0:T(8,128)(2,1)} %get-tuple-element.320.refs_2_, ...), custom_call_target="tpu_custom_call" | custom-call | flops 69000003584 | bytes 19519488 | tf_op jit(solution)/shard_map/pallas_call | solution.py:371
  292.6 24.3 %shard_map.247 = (f32[8,256,1152]{2,1,0:T(8,128)}, f32[4,256,1152]{2,1,0:T(8,128)}, f32[4,2,1152]{2,1,0:T(2,128)}) custom-call(s32[3]{0:T(128)} %pad_add_fusion.sc, bf16[2,3456,256]{2,1,0:T(8,128)(2,1)} %shard_map.243.refs_0_, bf16[2,3456,256]{2,1,0:T(8,128)(2,1)} %shard_map.244.refs_1_, bf16[1728,1152]{1,0:T(8,128)(2,1)} %bitcast.127, ...), custom_call_target="tpu_custom_call" | custom-call | flops 69000003584 | bytes 38891520 | tf_op jit(solution)/shard_map/pallas_call | solution.py:371
  317.7 8.0 %collective-permute-done.20 = bf16[2,2,2,144,512]{4,3,0,1,2:T(8,128)(2,1)} collective-permute-done((bf16[2,2,2,144,512]{4,3,0,1,2:T(8,128)(2,1)S(1)}, bf16[2,2,2,144,512]{4,3,0,1,2:T(8,128)(2,1)}, u32[]{:S(2)}, u32[]{:S(2)}) %collective-permute-start.20) | collective-permute-done | bytes 1179680 | tf_op jit(solution)/shard_map/ppermute | solution.py:428
  333.7 25.4 %shard_map.248 = (bf16[8,256,1152]{2,1,0:T(8,128)(2,1)}, bf16[4,256,1152]{2,1,0:T(8,128)(2,1)}, f32[4,1,1152]{2,1,0:T(1,128)}) custom-call(s32[3]{0:T(128)} %pad_add_fusion.sc, bf16[2,2304,1024]{2,1,0:T(8,128)(2,1)} %get-tuple-element.356.act, bf16[2304,1152]{1,0:T(8,128)(2,1)} %w_down0.1, bf16[2304,1152]{1,0:T(8,128)(2,1)} %collective-permute-done.5.refs_1_.refs_4_.w_down1, ...), custom_call_target="tpu_custom_call" | custom-call | flops 69000003584 | bytes 36813312 | tf_op jit(solution)/shard_map/pallas_call | solution.py:371
  374.0 26.8 %collective-permute-done.27 = bf16[2,144,896]{2,1,0:T(8,128)(2,1)S(1)} collective-permute-done((bf16[2,144,896]{2,1,0:T(8,128)(2,1)}, bf16[2,144,896]{2,1,0:T(8,128)(2,1)S(1)}, u32[]{:S(2)}, u32[]{:S(2)}) %collective-permute-start.27) | collective-permute-done | bytes 516128 | tf_op jit(solution)/shard_map/ppermute | solution.py:428
  405.9 18.5 %collective-permute-done.32 = bf16[9,3456]{1,0:T(8,128)(2,1)S(1)} collective-permute-done((bf16[9,3456]{1,0:T(8,128)(2,1)S(1)}, bf16[9,3456]{1,0:T(8,128)(2,1)S(1)}, u32[]{:S(2)}, u32[]{:S(2)}) %collective-permute-start.32) | collective-permute-done | bytes 62240 | tf_op jit(solution)/shard_map/ppermute | solution.py:510
  444.3 13.1 %collective-permute-done.35 = bf16[144,896]{1,0:T(8,128)(2,1)S(1)} collective-permute-done((bf16[144,896]{1,0:T(8,128)(2,1)S(1)}, bf16[144,896]{1,0:T(8,128)(2,1)S(1)}, u32[]{:S(2)}, u32[]{:S(2)}) %collective-permute-start.35) | collective-permute-done | bytes 258080 | tf_op jit(solution)/shard_map/ppermute | solution.py:428
  479.8 17.7 %collective-permute-done.38 = bf16[2,144,896]{2,1,0:T(8,128)(2,1)S(1)} collective-permute-done((bf16[2,144,896]{2,1,0:T(8,128)(2,1)S(1)}, bf16[2,144,896]{2,1,0:T(8,128)(2,1)S(1)}, u32[]{:S(2)}, u32[]{:S(2)}) %collective-permute-start.38) | collective-permute-done | bytes 516128 | tf_op jit(solution)/shard_map/ppermute | solution.py:428
  500.0 7.6 %collective-permute-start.42 = (bf16[2,2,144,512]{3,2,1,0:T(8,128)(2,1)S(1)}, bf16[2,2,144,512]{3,2,1,0:T(8,128)(2,1)}, u32[]{:S(2)}, u32[]{:S(2)}) collective-permute-start(bf16[2,2,144,512]{3,2,1,0:T(8,128)(2,1)S(1)} %fusion.7), channel_id=1, source_target_pairs={{0,4},{2,6},{4,0},{6,2},{8,12},{10,14},{12,8},{14,10},{16,20},{18,... | collective-permute-start | bytes 1769480 | tf_op jit(solution)/shard_map/ppermute | solution.py:428
  519.0 22.3 %collective-permute-done.44 = bf16[2,2,144,256]{3,2,1,0:T(8,128)(2,1)} collective-permute-done((bf16[2,2,144,256]{3,2,1,0:T(8,128)(2,1)}, bf16[2,2,144,256]{3,2,1,0:T(8,128)(2,1)}, u32[]{:S(2)}, u32[]{:S(2)}) %collective-permute-start.44) | collective-permute-done | bytes 294944 | tf_op jit(solution)/shard_map/ppermute | solution.py:428
  549.0 9.1 %fusion.4 = f32[1152,3456]{1,0:T(8,128)} fusion(bf16[128,1152]{1,0:T(8,128)(2,1)} %reshape.186, bf16[16,9,3456]{2,1,0:T(8,128)(2,1)S(1)} %reshape.183), kind=kOutput, calls=%fused_computation.16 | convolution fusion | flops 1019215872 | bytes 17104896 | tf_op jit(solution)/shard_map/dot_general | solution.py:988
  558.1 5.6 collective-permute-done.47
  568.1 5.8 collective-permute-done.45
  583.4 5.5 shard_map.251
  594.4 8.5 %shard_map.249 = (f32[1728,1152]{1,0:T(8,128)}, f32[576,1152]{1,0:T(8,128)}) custom-call(s32[3]{0:T(128)} %pad_add_fusion.sc, bf16[8,144,512]{2,1,0:T(8,128)(2,1)} %bitcast.114, bf16[8,144,512]{2,1,0:T(8,128)(2,1)} %bitcast.115, bf16[8,144,384]{2,1,0:T(8,128)(2,1)} %bitcast.56.refs_2_, bf16[8,144,384]{2,1,0:T(8,128)(2,1)} %bitcast.57.refs_3_, ...), custom_call_target="tpu_custom_call" | custom-call | flops 10350000128 | bytes 9000000 | tf_op jit(solution)/shard_map/pallas_call | solution.py:371
  (257 shorter events, 167.1 us)
Async XLA Ops:
  7.2 570.2 %all-reduce.4.cloned.1.call-start = ((), (), s32[]{:S(2)}) async-start(), calls=%async_computation | async-start | bytes 21233664 | tf_op jit(solution)/shard_map/psum | solution.py:709
  14.6 57.0 %collective-permute-start.4 = (bf16[1152,2304]{1,0:T(8,128)(2,1)}, bf16[1152,2304]{1,0:T(8,128)(2,1)}, u32[]{:S(2)}, u32[]{:S(2)}) collective-permute-start(bf16[1152,2304]{1,0:T(8,128)(2,1)} %w_up0.1), channel_id=1, source_target_pairs={{0,1},{1,0},{2,3},{3,2},{4,5},{5,4},{6,7},{7,6},{8,9},{9,8},{10,11... | collective-permute-start | bytes 15925256 | tf_op jit(solution)/shard_map/ppermute | solution.py:402
  14.9 56.7 %collective-permute-start.5 = (bf16[2304,1152]{1,0:T(8,128)(2,1)}, bf16[2304,1152]{1,0:T(8,128)(2,1)}, u32[]{:S(2)}, u32[]{:S(2)}) collective-permute-start(bf16[2304,1152]{1,0:T(8,128)(2,1)} %w_down0.1), channel_id=1, source_target_pairs={{0,1},{1,0},{2,3},{3,2},{4,5},{5,4},{6,7},{7,6},{8,9},{9,8},{10,11... | collective-permute-start | bytes 15925256 | tf_op jit(solution)/shard_map/ppermute | solution.py:402
  18.0 53.5 %collective-permute-start.6 = (bf16[1,2304]{1,0:T(2,128)(2,1)S(1)}, bf16[1,2304]{1,0:T(2,128)(2,1)S(1)}, u32[]{:S(2)}, u32[]{:S(2)}) collective-permute-start(bf16[1,2304]{1,0:T(2,128)(2,1)S(1)} %broadcast_in_dim.34), channel_id=1, source_target_pairs={{0,1},{1,0},{2,3},{3,2},{4,5},{5,4},{6,7},{7,6},{8,9},{9,8},{10,11... | collective-permute-start | bytes 13832 | tf_op jit(solution)/shard_map/ppermute | solution.py:402
  113.9 32.2 %collective-permute-start.9 = (bf16[16,96,1152]{2,1,0:T(8,128)(2,1)}, bf16[16,96,1152]{2,1,0:T(8,128)(2,1)}, u32[]{:S(2)}, u32[]{:S(2)}) collective-permute-start(bf16[16,96,1152]{2,1,0:T(8,128)(2,1)} %get-tuple-element.272), channel_id=1, source_target_pairs={{0,1},{1,0},{2,3},{3,2},{4,5},{5,4},{6,7},{7,6},{8,9},{9,8},{10,11... | collective-permute-start | bytes 10616840 | tf_op jit(solution)/shard_map/ppermute | solution.py:402
  167.5 29.7 %collective-permute-start.12 = (f32[1,3456]{1,0:T(1,128)S(1)}, f32[1,3456]{1,0:T(1,128)S(1)}, u32[]{:S(2)}, u32[]{:S(2)}) collective-permute-start(f32[1,3456]{1,0:T(1,128)S(1)} %get-tuple-element.294), channel_id=1, source_target_pairs={{0,1},{1,0},{2,3},{3,2},{4,5},{5,4},{6,7},{7,6},{8,9},{9,8},{10,11... | collective-permute-start | bytes 41480 | tf_op jit(solution)/shard_map/ppermute | solution.py:402
  167.5 29.7 %collective-permute-start.11 = (bf16[6,3456]{1,0:T(8,128)(2,1)S(1)}, bf16[6,3456]{1,0:T(8,128)(2,1)S(1)}, u32[]{:S(2)}, u32[]{:S(2)}) collective-permute-start(bf16[6,3456]{1,0:T(8,128)(2,1)S(1)} %pad_maximum_fusion.21), channel_id=1, source_target_pairs={{0,8},{2,10},{4,12},{6,14},{8,0},{10,2},{12,4},{14,6},{16,24},{18,... | collective-permute-start | bytes 124424 | tf_op jit(solution)/shard_map/ppermute | solution.py:510
  197.3 25.1 %collective-permute-start.14 = (f32[1,3456]{1,0:T(1,128)S(1)}, f32[1,3456]{1,0:T(1,128)S(1)}, u32[]{:S(2)}, u32[]{:S(2)}) collective-permute-start(f32[1,3456]{1,0:T(1,128)S(1)} %add.184), channel_id=1, source_target_pairs={{0,16},{2,18},{4,20},{6,22},{8,24},{10,26},{12,28},{14,30},{16,0},... | collective-permute-start | bytes 41480 | tf_op jit(solution)/shard_map/ppermute | solution.py:510
  222.6 23.0 %collective-permute-start.16 = (f32[2,3456]{1,0:T(2,128)S(1)}, f32[2,3456]{1,0:T(2,128)S(1)}, u32[]{:S(2)}, u32[]{:S(2)}) collective-permute-start(f32[2,3456]{1,0:T(2,128)S(1)} %pad_maximum_fusion.23), channel_id=1, source_target_pairs={{0,8},{2,10},{4,12},{6,14},{8,0},{10,2},{12,4},{14,6},{16,24},{18,... | collective-permute-start | bytes 82952 | tf_op jit(solution)/shard_map/ppermute | solution.py:510
  288.4 28.6 %collective-permute-start.22 = (bf16[2,2,2,144,256]{4,3,1,2,0:T(8,128)(2,1)}, bf16[2,2,2,144,256]{4,3,1,2,0:T(8,128)(2,1)}, u32[]{:S(2)}, u32[]{:S(2)}) collective-permute-start(bf16[2,2,2,144,256]{4,3,1,2,0:T(8,128)(2,1)} %get-tuple-element.347), channel_id=1, source_target_pairs={{0,8},{2,10},{4,12},{6,14},{8,0},{10,2},{12,4},{14,6},{16,24},{18,... | collective-permute-start | bytes 1769480 | tf_op jit(solution)/shard_map/ppermute | solution.py:428
  289.7 28.0 %collective-permute-start.21 = (bf16[2,2,2,144,384]{4,3,0,1,2:T(8,128)(2,1)}, bf16[2,2,2,144,384]{4,3,0,1,2:T(8,128)(2,1)}, u32[]{:S(2)}, u32[]{:S(2)}) collective-permute-start(bf16[2,2,2,144,384]{4,3,0,1,2:T(8,128)(2,1)} %get-tuple-element.346), channel_id=1, source_target_pairs={{0,4},{2,6},{4,0},{6,2},{8,12},{10,14},{12,8},{14,10},{16,20},{18,... | collective-permute-start | bytes 2654216 | tf_op jit(solution)/shard_map/ppermute | solution.py:428
  291.1 34.6 %collective-permute-start.20 = (bf16[2,2,2,144,512]{4,3,0,1,2:T(8,128)(2,1)S(1)}, bf16[2,2,2,144,512]{4,3,0,1,2:T(8,128)(2,1)}, u32[]{:S(2)}, u32[]{:S(2)}) collective-permute-start(bf16[2,2,2,144,512]{4,3,0,1,2:T(8,128)(2,1)S(1)} %get-tuple-element.345), channel_id=1, source_target_pairs={{0,2},{2,0},{4,6},{6,4},{8,10},{10,8},{12,14},{14,12},{16,18},{18,... | collective-permute-start | bytes 3538952 | tf_op jit(solution)/shard_map/ppermute | solution.py:428
  317.0 120.7 %collective-permute-start.33 = (f32[4,256,1152]{2,1,0:T(8,128)}, f32[4,256,1152]{2,1,0:T(8,128)}, u32[]{:S(2)}, u32[]{:S(2)}) collective-permute-start(f32[4,256,1152]{2,1,0:T(8,128)} %get-tuple-element.408), channel_id=1, source_target_pairs={{0,1},{1,0},{2,3},{3,2},{4,5},{5,4},{6,7},{7,6},{8,9},{9,8},{10,11... | collective-permute-start | bytes 14155784 | tf_op jit(solution)/shard_map/ppermute | solution.py:402
  330.9 28.2 %collective-permute-start.25 = (bf16[2,2,144,256]{3,2,0,1:T(8,128)(2,1)}, bf16[2,2,144,256]{3,2,0,1:T(8,128)(2,1)S(1)}, u32[]{:S(2)}, u32[]{:S(2)}) collective-permute-start(bf16[2,2,144,256]{3,2,0,1:T(8,128)(2,1)} %get-tuple-element.365), channel_id=1, source_target_pairs={{0,16},{2,18},{4,20},{6,22},{8,24},{10,26},{12,28},{14,30},{16,0},... | collective-permute-start | bytes 884744 | tf_op jit(solution)/shard_map/ppermute | solution.py:428
  332.2 26.9 %collective-permute-start.24 = (bf16[2,2,144,384]{3,2,0,1:T(8,128)(2,1)}, bf16[2,2,144,384]{3,2,0,1:T(8,128)(2,1)S(1)}, u32[]{:S(2)}, u32[]{:S(2)}) collective-permute-start(bf16[2,2,144,384]{3,2,0,1:T(8,128)(2,1)} %get-tuple-element.364), channel_id=1, source_target_pairs={{0,2},{2,0},{4,6},{6,4},{8,10},{10,8},{12,14},{14,12},{16,18},{18,... | collective-permute-start | bytes 1327112 | tf_op jit(solution)/shard_map/ppermute | solution.py:428
  332.2 26.9 %collective-permute-start.23 = (bf16[2,2,144,512]{3,2,0,1:T(8,128)(2,1)S(1)}, bf16[2,2,144,512]{3,2,0,1:T(8,128)(2,1)S(1)}, u32[]{:S(2)}, u32[]{:S(2)}) collective-permute-start(bf16[2,2,144,512]{3,2,0,1:T(8,128)(2,1)S(1)} %get-tuple-element.363), channel_id=1, source_target_pairs={{0,4},{2,6},{4,0},{6,2},{8,12},{10,14},{12,8},{14,10},{16,20},{18,... | collective-permute-start | bytes 1769480 | tf_op jit(solution)/shard_map/ppermute | solution.py:428
  363.5 42.4 %collective-permute-start.29 = (bf16[4,256,1152]{2,1,0:T(8,128)(2,1)}, bf16[4,256,1152]{2,1,0:T(8,128)(2,1)S(1)}, u32[]{:S(2)}, u32[]{:S(2)}) collective-permute-start(bf16[4,256,1152]{2,1,0:T(8,128)(2,1)} %get-tuple-element.391), channel_id=1, source_target_pairs={{0,1},{1,0},{2,3},{3,2},{4,5},{5,4},{6,7},{7,6},{8,9},{9,8},{10,11... | collective-permute-start | bytes 7077896 | tf_op jit(solution)/shard_map/ppermute | solution.py:402
  366.6 34.2 %collective-permute-start.27 = (bf16[2,144,896]{2,1,0:T(8,128)(2,1)}, bf16[2,144,896]{2,1,0:T(8,128)(2,1)S(1)}, u32[]{:S(2)}, u32[]{:S(2)}) collective-permute-start(bf16[2,144,896]{2,1,0:T(8,128)(2,1)} %pad_maximum_fusion.4), channel_id=1, source_target_pairs={{0,8},{2,10},{4,12},{6,14},{8,0},{10,2},{12,4},{14,6},{16,24},{18,... | collective-permute-start | bytes 1548296 | tf_op jit(solution)/shard_map/ppermute | solution.py:428
  427.3 30.0 %collective-permute-start.35 = (bf16[144,896]{1,0:T(8,128)(2,1)S(1)}, bf16[144,896]{1,0:T(8,128)(2,1)S(1)}, u32[]{:S(2)}, u32[]{:S(2)}) collective-permute-start(bf16[144,896]{1,0:T(8,128)(2,1)S(1)} %add.233), channel_id=1, source_target_pairs={{0,16},{2,18},{4,20},{6,22},{8,24},{10,26},{12,28},{14,30},{16,0},... | collective-permute-start | bytes 774152 | tf_op jit(solution)/shard_map/ppermute | solution.py:428
  461.1 36.4 %collective-permute-start.38 = (bf16[2,144,896]{2,1,0:T(8,128)(2,1)S(1)}, bf16[2,144,896]{2,1,0:T(8,128)(2,1)S(1)}, u32[]{:S(2)}, u32[]{:S(2)}) collective-permute-start(bf16[2,144,896]{2,1,0:T(8,128)(2,1)S(1)} %pad_maximum_fusion.6), channel_id=1, source_target_pairs={{0,8},{2,10},{4,12},{6,14},{8,0},{10,2},{12,4},{14,6},{16,24},{18,... | collective-permute-start | bytes 1548296 | tf_op jit(solution)/shard_map/ppermute | solution.py:428
  500.0 41.3 %collective-permute-start.42 = (bf16[2,2,144,512]{3,2,1,0:T(8,128)(2,1)S(1)}, bf16[2,2,144,512]{3,2,1,0:T(8,128)(2,1)}, u32[]{:S(2)}, u32[]{:S(2)}) collective-permute-start(bf16[2,2,144,512]{3,2,1,0:T(8,128)(2,1)S(1)} %fusion.7), channel_id=1, source_target_pairs={{0,4},{2,6},{4,0},{6,2},{8,12},{10,14},{12,8},{14,10},{16,20},{18,... | collective-permute-start | bytes 1769480 | tf_op jit(solution)/shard_map/ppermute | solution.py:428
  512.4 28.9 %collective-permute-start.44 = (bf16[2,2,144,256]{3,2,1,0:T(8,128)(2,1)}, bf16[2,2,144,256]{3,2,1,0:T(8,128)(2,1)}, u32[]{:S(2)}, u32[]{:S(2)}) collective-permute-start(bf16[2,2,144,256]{3,2,1,0:T(8,128)(2,1)} %pad_maximum_fusion.10), channel_id=1, source_target_pairs={{0,16},{2,18},{4,20},{6,22},{8,24},{10,26},{12,28},{14,30},{16,0},... | collective-permute-start | bytes 884744 | tf_op jit(solution)/shard_map/ppermute | solution.py:428
  512.5 28.9 %collective-permute-start.43 = (bf16[2,2,144,384]{3,2,1,0:T(8,128)(2,1)}, bf16[2,2,144,384]{3,2,1,0:T(8,128)(2,1)}, u32[]{:S(2)}, u32[]{:S(2)}) collective-permute-start(bf16[2,2,144,384]{3,2,1,0:T(8,128)(2,1)} %pad_maximum_fusion.8), channel_id=1, source_target_pairs={{0,2},{2,0},{4,6},{6,4},{8,10},{10,8},{12,14},{14,12},{16,18},{18,... | collective-permute-start | bytes 1327112 | tf_op jit(solution)/shard_map/ppermute | solution.py:428
  546.6 27.3 %collective-permute-start.45 = (bf16[2,2,2,144,512]{4,3,1,0,2:T(8,128)(2,1)S(1)}, bf16[2,2,2,144,512]{4,3,1,0,2:T(8,128)(2,1)}, u32[]{:S(2)}, u32[]{:S(2)}) collective-permute-start(bf16[2,2,2,144,512]{4,3,1,0,2:T(8,128)(2,1)S(1)} %pad_maximum_fusion), channel_id=1, source_target_pairs={{0,2},{2,0},{4,6},{6,4},{8,10},{10,8},{12,14},{14,12},{16,18},{18,... | collective-permute-start | bytes 3538952 | tf_op jit(solution)/shard_map/ppermute | solution.py:428
  (54 other events, 665.8 us)
Sparse Core Ops, SparseCore 0:
  165.8 376.3 all-reduce.3

commit v7 on v4

--- a/solution.py
+++ b/solution.py
@@ -111,18 +111,23 @@
         came.append(refs[0] if summed else None)
         refs = refs[1:] if summed else refs
     act, back = refs[2], refs[3]
-    grads, sums = refs[4 : 4 + count], refs[4 + count :]
+    refs = refs[4:]
+    grads = []
+    for cuts, _ in jobs:
+        size = 1 if cuts is None else len(cuts)
+        grads.append(refs[:size])
+        refs = refs[size:]
     job, step = pl.program_id(0), pl.program_id(1)
     for k in range(count):
 
         @pl.when(job == k)
         def _(k=k):
             mlp_block(
-                per, jobs[k][0], step, sc, rows, grad_mlp, *weights[k], act, back, grads[k], sums[k], came[k]
+                per, jobs[k][0], step, sc, rows, grad_mlp, *weights[k], act, back, grads[k], refs[k], came[k]
             )
 
 
-def mlp_block(per, natural, step, sc, rows, grad_mlp, w_up, w_down, bias, act, back, grads, sums, came):
+def mlp_block(per, cuts, step, sc, rows, grad_mlp, w_up, w_down, bias, act, back, grads, sums, came):
     here = w_down.shape[0] // per
     hidden = lax.dot_general(
         w_up[...], rows[...], (((0,), (1,)), ((), ())), preferred_element_type=f32
@@ -137,18 +142,19 @@
     back_b = (dot_nt(w_down[...], grad_mlp[...]) * slope).astype(bf16)
     act[0] = act_b
     back[0] = back_b
-    sums[...] = dot_nt(jnp.ones((8, rows.shape[0]), bf16), back_b)
+    sums[...] = dot_nt(jnp.ones((8, rows.shape[0]), bf16), back_b)[0:1]
     for lo_row, left, right in ((0, act_b, grad_mlp), (per, back_b, rows)):
         grad = dot_nn(left, right[...])
         for piece in range(here):
             value = grad[piece * per : (piece + 1) * per]
-            if natural:
+            if cuts is None:
                 if came is not None:
                     value = value + came[piece, lo_row : lo_row + per, :].astype(f32)
-                grads[piece, lo_row : lo_row + per, :] = value.astype(bf16)
+                grads[0][piece, lo_row : lo_row + per, :] = value.astype(bf16)
             else:
                 at = jnp.bitwise_xor(step * here + piece, sc[2])
-                grads[at, lo_row : lo_row + per, :] = value.astype(bf16)
+                for (lo, hi), into in zip(cuts, grads):
+                    into[at, lo_row : lo_row + per, :] = value[:, lo:hi].astype(bf16)
 
 
 def grow(total, part_steps, left, rights, dims):
@@ -231,9 +237,9 @@
         lax.fori_loop(0, pairs, pair_step, 0, unroll=True)
 
 
-def attn_grad_kernel(pieces, per, sc, *refs):
+def attn_grad_kernel(pieces, per, cuts, sc, *refs):
     grad_qkv, mixed, normed, grad_attn = refs[:pieces], refs[pieces], refs[pieces + 1], refs[pieces + 2]
-    grads, sums = refs[pieces + 3 :]
+    grads, sums = refs[pieces + 3 : -1], refs[-1]
     step = pl.program_id(0)
     here = mixed.shape[1] // per
     images = mixed.shape[0]
@@ -243,7 +249,8 @@
         total = total.astype(bf16)
         for piece in range(here):
             at = jnp.bitwise_xor(step * here + piece, sc[2])
-            grads[at] = total[piece * per : (piece + 1) * per]
+            for (lo, hi), into in zip(cuts, grads):
+                into[at] = total[piece * per : (piece + 1) * per, lo:hi]
 
     @pl.when(step < 3)
     def _():
@@ -254,7 +261,7 @@
             term, one = dot_nn(left, normed[image]), dot_nt(ones, left)
             total = term if image == 0 else total + term
             count = one if image == 0 else count + one
-        sums[0] = count
+        sums[0] = count[0:1]
         spread(total)
 
     @pl.when(step == 3)
@@ -323,15 +330,15 @@
 
 def final_piece(sc, halves, piece, store):
     rel = jnp.bitwise_xor(piece, sc[2])
-    for low, high, bit, lo, hi in halves:
-        index = ((rel >> (bit + 1)) << bit) | (rel & ((1 << bit) - 1))
-        side = (rel >> bit) & 1
-
-        @pl.when(side == 0)
+    for low, high, route, lo, hi in halves:
+        bits = [(rel >> bit) & 1 for bit in route]
+        index = bits[1] * 4 + bits[2] * 2 + bits[3]
+
+        @pl.when(bits[0] == 0)
         def _(low=low, index=index, lo=lo, hi=hi):
             store(low[index].astype(f32), lo, hi)
 
-        @pl.when(side == 1)
+        @pl.when(bits[0] == 1)
         def _(high=high, index=index, lo=lo, hi=hi):
             store(high[index].astype(f32), lo, hi)
 
@@ -426,15 +433,12 @@
 ATTN_WAYS = ((0, 512, (0, 1, 2, 3)), (512, 896, (1, 0, 2, 3)), (896, 1152, (2, 3, 0, 1)))
 
 
-def cut(array, bits, bit, side, cols=None):
-    lo = [0] * array.ndim
-    hi = list(array.shape)
-    place = bits.index(bit)
-    lo[place], hi[place] = side, side + 1
-    if cols is not None:
-        lo[-1], hi[-1] = cols
-    out = lax.slice(array, lo, hi)
-    return out.reshape(out.shape[:place] + out.shape[place + 1 :])
+def columns(ways):
+    return tuple((lo, hi) for lo, hi, _ in ways)
+
+
+def cut(array, bits, bit, side):
+    return lax.index_in_dim(array, side, bits.index(bit), keepdims=False)
 
 
 def left_bits(done):
@@ -445,28 +449,23 @@
     return [lax.ppermute(value, "dp", bit_pairs(bit)) for value, bit in zip(values, bits)]
 
 
-def reduce_flow(ways, get_own, other):
-    shape = (2, 2, 2, 2) + other.shape[1:]
-    (other,) = yield [other]
-    came = swap_cores(other)
+def reduce_flow(ways, get_own, others):
+    others = yield others
+    came = [swap_cores(other) for other in others]
     yield None
     own, came = yield [get_own(), came]
-    firsts, seconds = [own.reshape(shape)] * len(ways), [came.reshape(shape)] * len(ways)
+    firsts, seconds = ([a.reshape((2, 2, 2, 2) + a.shape[1:]) for a in arrays] for arrays in (own, came))
     routes = [way for _, _, way in ways]
     for stage in range(4):
         sends, keeps = [], []
-        for (lo, hi, _), route, one, two in zip(ways, routes, firsts, seconds):
+        for route, one, two in zip(routes, firsts, seconds):
             bits = left_bits(route[:stage])
-            cols = (lo, hi) if stage == 0 else None
             for side, into in ((1, sends), (0, keeps)):
-                into.append(
-                    cut(one, bits, route[stage], side, cols) + cut(two, bits, route[stage], side, cols)
-                )
+                into.append(cut(one, bits, route[stage], side) + cut(two, bits, route[stage], side))
         if stage == 2 and routes[0][2:] == routes[1][2:]:
             sends = [jnp.concatenate(sends[:2], axis=-1)] + sends[2:]
             keeps = [jnp.concatenate(keeps[:2], axis=-1)] + keeps[2:]
             routes = [routes[0]] + routes[2:]
-            ways = [(0, 0, way) for way in routes]
         sends, keeps = yield [sends, keeps]
         comes = exchange(sends, [route[stage] for route in routes])
         yield None
@@ -477,31 +476,26 @@
 def gather_flow(ways, have):
     routes = [ways[0][2]] + [way for _, _, way in ways[2:]]
     middle = ways[0][1]
-    known = [[] for _ in routes]
     (have,) = yield [have]
     comes = exchange(have, [route[3] for route in routes])
+    have = [one[None] for one in have]
+    comes = [one[None] for one in comes]
     yield None
     for stage in (2, 1, 0):
         have, comes = yield [have, comes]
-        joined = []
-        for route, bits, one, two in zip(routes, known, have, comes):
-            bit = route[stage + 1]
-            place = sum(1 for other in bits if other > bit)
-            joined.append(jnp.stack([one, two], axis=place))
-            bits.insert(place, bit)
+        joined = [jnp.concatenate([one, two]) for one, two in zip(have, comes)]
         if stage == 1:
             joined = [joined[0][..., :middle], joined[0][..., middle:]] + joined[1:]
             routes = [way for _, _, way in ways]
-            known = [list(known[0]), list(known[0])] + known[1:]
         (have,) = yield [joined]
         comes = exchange(have, [route[stage] for route in routes])
         yield None
     have, comes = yield [have, comes]
-    return [part.reshape((8,) + part.shape[-2:]) for pair in zip(have, comes) for part in pair]
-
-
-def sum_flow(ways, get_own, other):
-    have = yield from reduce_flow(ways, get_own, other)
+    return [part for pair in zip(have, comes) for part in pair]
+
+
+def sum_flow(ways, get_own, others):
+    have = yield from reduce_flow(ways, get_own, others)
     return (yield from gather_flow(ways, have))
 
 
@@ -644,7 +638,7 @@
     def mlp_call(jobs, came, micros):
         nonlocal act, back
         first = act.shape[0] == 8
-        kinds = tuple((chunk < PLAIN, (chunk, part) in came) for chunk, part in jobs)
+        kinds = tuple((None if job[0] < PLAIN else columns(MLP_WAYS), job in came) for job in jobs)
 
         def turn(k):
             return lambda p, s, c: jnp.clip((p - k) * steps + s, 0, steps - 1)
@@ -666,19 +660,19 @@
                 pl.BlockSpec((block, dim), tall),
                 pl.BlockSpec((1, block), wide),
             ]
-        grad_specs = []
-        for k, (natural, _) in enumerate(kinds):
+        grad_specs, grad_shapes, sizes = [], [], []
+        for k, (split, _) in enumerate(kinds):
             own = lambda p, s, c, k=k: (turn(k)(p, s, c), 0, 0)
             fixed = lambda p, s, c: (0, 0, 0)
-            grad_specs.append(
-                pl.BlockSpec((16 // steps, 2 * per, dim), own)
-                if natural
-                else pl.BlockSpec((16, 2 * per, dim), fixed)
-            )
+            wides = [dim] if split is None else [hi - lo for lo, hi in split]
+            lead = (16 // steps, own) if split is None else (16, fixed)
+            grad_specs.append([pl.BlockSpec((lead[0], 2 * per, wide), lead[1]) for wide in wides])
+            grad_shapes += [shape_of((16, 2 * per, wide), bf16) for wide in wides]
+            sizes.append(len(wides))
         for k, job in enumerate(jobs):
             if job in came:
                 args.append(came[job])
-                specs.append(grad_specs[k])
+                specs += grad_specs[k]
         args += [act, back]
         spot = len(args) + 1
         outs = run_kernel(
@@ -687,33 +681,31 @@
             [rows_flat, grad_flat] + args,
             [whole_block(rows_flat), whole_block(grad_flat)] + specs + [anywhere, anywhere],
             [spread, spread]
-            + grad_specs
-            + [pl.BlockSpec((8, block), lambda p, s, c, k=k: (0, turn(k)(p, s, c))) for k in range(len(jobs))],
-            [shape_of((2, ff, count), bf16)] * 2
-            + [shape_of((16, 2 * per, dim), bf16)] * len(jobs)
-            + [shape_of((8, width), f32)] * len(jobs),
+            + [spec for specs in grad_specs for spec in specs]
+            + [pl.BlockSpec((1, block), lambda p, s, c, k=k: (0, turn(k)(p, s, c))) for k in range(len(jobs))],
+            [shape_of((2, ff, count), bf16)] * 2 + grad_shapes + [shape_of((1, width), f32)] * len(jobs),
             (len(jobs), steps),
             micros,
             alias=None if first else {spot: 0, spot + 1: 1},
         )
         act, back = outs[:2]
-        grads = outs[2 : 2 + len(jobs)]
-        for job, sums in zip(jobs, outs[2 + len(jobs) :]):
-            up_sums[job] = sums[0:1]
+        grads, outs = list(outs[2 : 2 + sum(sizes)]), outs[2 + sum(sizes) :]
+        up_sums.update(zip(jobs, outs))
         order.after(outs[-1])
-        return grads
+        return [[grads.pop(0) for _ in range(size)] for size in sizes]
 
     summed = range(PLAIN)
-    swaps = [swap_flow(grad) for grad in mlp_call([(chunk, 1) for chunk in summed], {}, 26)]
+    swaps = [swap_flow(grad) for (grad,) in mlp_call([(chunk, 1) for chunk in summed], {}, 26)]
     order.tick(*swaps)
     rest = [(chunk, part) for chunk in range(PLAIN, CHUNKS) for part in (1, 0)]
     grads = mlp_call(rest, {}, 26)
     flows = [
-        sum_flow(MLP_WAYS, lambda own=own: own, other) for other, own in zip(grads[0::2], grads[1::2])
+        sum_flow(MLP_WAYS, lambda own=own: own, others) for others, own in zip(grads[0::2], grads[1::2])
     ]
     order.tick(*swaps, *flows)
     came = {(chunk, 0): order.results[swap] for chunk, swap in zip(summed, swaps)}
-    plain_sums = lax.psum(mlp_call([(chunk, 0) for chunk in summed], came, 26), "dp")
+    grads = mlp_call([(chunk, 0) for chunk in summed], came, 26)
+    plain_sums = lax.psum([grad for (grad,) in grads], "dp")
     order.tick(*flows)
 
     reach = 768
@@ -784,8 +776,8 @@
     qv_sums = [None, None]
 
     def attn_part(part):
-        grads, sums = run_kernel(
-            functools.partial(attn_grad_kernel, pieces, attn_per),
+        *grads, sums = run_kernel(
+            functools.partial(attn_grad_kernel, pieces, attn_per, columns(ATTN_WAYS)),
             order.sc,
             grad_qkv + [mixed, normed, grad_attn],
             [
@@ -794,11 +786,10 @@
             ]
             + [pl.BlockSpec((images, cols, seq), lambda s, c: (0, part, 0))]
             + [whole_block(normed), whole_block(grad_attn)],
-            [
-                pl.BlockSpec((16, attn_per, dim), every),
-                pl.BlockSpec((1, 8, cols), lambda s, c: (jnp.minimum(s, 2), 0, 0)),
-            ],
-            [shape_of((16, attn_per, dim), bf16), shape_of((3, 8, cols), f32)],
+            [pl.BlockSpec((16, attn_per, hi - lo), every) for lo, hi in columns(ATTN_WAYS)]
+            + [pl.BlockSpec((1, 1, cols), lambda s, c: (jnp.minimum(s, 2), 0, 0))],
+            [shape_of((16, attn_per, hi - lo), bf16) for lo, hi in columns(ATTN_WAYS)]
+            + [shape_of((3, 1, cols), f32)],
             (4,),
             60,
             )
@@ -859,7 +850,7 @@
     grad_modulation = grad_modulation.reshape(images, 6 * dim).astype(bf16)
     bias_sums = [
         jnp.concatenate(
-            [qv_sums[part][0, 0:1], qv_sums[part][2, 0:1]]
+            [qv_sums[part][0], qv_sums[part][2]]
             + [up_sums[chunk, part] for chunk in range(CHUNKS)],
             axis=1,
         )
@@ -903,7 +894,7 @@
     order.tick(last, small, *flows)
 
     def cuts(ways):
-        return tuple((way[0], lo, hi) for lo, hi, way in ways)
+        return tuple((way, lo, hi) for lo, hi, way in ways)
 
     grad_w_down = grad_w_up = jnp.zeros((8, 128), f32)
 
@@ -939,6 +930,9 @@
         body = functools.partial(final_mlp_kernel, cuts(MLP_WAYS), per)
         final_mlp(PLAIN + chunk, body, order.finish(flow))
     order.tick(last, small)
+    for chunk, total in zip(summed, order.fence(plain_sums)):
+        final_mlp(chunk, functools.partial(final_plain_kernel, per), [total])
+    order.tick(last)
     all_rows = order.fence(order.finish(small)).reshape(16, slots + 5, own_cols)
     all_mod = all_rows[:, :slots].reshape(-1, own_cols)
     all_scaled = all_rows[:, slots + 2 :].reshape(16, -1)[:, : slots * dim].reshape(-1, dim)
@@ -965,9 +959,6 @@
         9,
     )
     grad_w_qkv = jnp.transpose(grad_qkv_rows.reshape(3, cols, dim), (2, 0, 1))
-    order.after(grad_w_proj[0, :1])
-    for chunk, total in enumerate(plain_sums):
-        final_mlp(chunk, functools.partial(final_plain_kernel, per), [total])
     return (
         output,
         grad_tokens,

time: 586 us -> 564 us (0.962)
  local copies, waits for them, and re-layouts: 52 us -> 30.2 us
  waiting for transfers between devices: 107 us -> 120 us
  other arithmetic: 33.3 us -> 25.9 us
    slice x16 -> x14, local copies, waits for them, and re-layouts: 21.5 us -> 6.01 us  [the longest x10 5.84 us: cut(): return lax.index_in_dim(array, side, bits.index(bit), keepdims=False)]
    optimization_barrier x4 -> x0, local copies, waits for them, and re-layouts: 8.07 us -> none  [fence(): self.sc, values = lax.optimization_barrier((self.sc, values))]
    ppermute x32, starting transfers between devices: 42.5 us -> 34.6 us  [exchange(): lax.ppermute(value, 'dp', bit_pairs(bit))]
    another operation x16 -> x3, other arithmetic: 7.49 us -> 0.05 us  [the longest x13 7.45 us: gather_flow(): joined.append(jnp.stack([one, two], axis=place))]
    ppermute x4, waiting for transfers between devices: 17.3 us -> 23.8 us  [rows_flow(): came = lax.ppermute(rows, 'dp', bit_pairs(bit))]
    ppermute x32, waiting for transfers between devices: 86.4 us -> 92.5 us  [exchange(): lax.ppermute(value, 'dp', bit_pairs(bit))]
  transfers between devices with their start and end apart: 52 -> 55, of which waited for: 21 -> 16; matrix products, arithmetic and copies ran while one was open for 17% -> 12% of each run, Pallas kernels for 44% -> 48%
where the time goes in v7:
time: 564 us; the launch traced here: 556 us
  Pallas kernels  301 us (53%)
  waiting for transfers between devices  120 us (21%)
  starting transfers between devices  44.3 us (8%)
  local copies, waits for them, and re-layouts  30.2 us (5%)
  other arithmetic  25.9 us (5%)
  matrix products  18.1 us (3%)
  between operations  15.9 us (3%)
    pallas_call x15, Pallas kernels, run_kernel(): pl.pallas_call(body, out_shape=out_shape, grid_spec=pltpu.PrefetchScalarG...  301 us
    ppermute x32, waiting for transfers between devices, exchange(): lax.ppermute(value, 'dp', bit_pairs(bit))  92.5 us
    ppermute x32, starting transfers between devices, exchange(): lax.ppermute(value, 'dp', bit_pairs(bit))  34.6 us
    ppermute x4, waiting for transfers between devices, rows_flow(): came = lax.ppermute(rows, 'dp', bit_pairs(bit))  23.8 us
    add x21, other arithmetic, reduce_flow(): cut(one, bits, route[stage], side) + cut(two, bits, route[stage], side)  14.1 us
  transfers between devices with their start and end apart: 55, of which 16 were waited for; matrix products, arithmetic and copies ran while one was open for 12% of the time, Pallas kernels for 48%

profile of v7, /device:TPU:0, one launch (start us, length us, event | category | flops | bytes accessed | tf_op | source)
XLA Modules:
  0.0 555.9 jit_solution(798091647268719260)
XLA Ops:
  22.5 49.0 %shard_map.237 = (bf16[4,3456,256]{2,1,0:T(8,128)(2,1)}, bf16[4,16,256,256]{3,2,1,0:T(8,128)(2,1)}, bf16[4,1152,256]{2,1,0:T(8,128)(2,1)}, f32[4,256,1152]{2,1,0...) custom-call(s32[3]{0:T(128)} %pad_add_fusion.sc, ...), custom_call_target="tpu_custom_call" | custom-call | flops 51749998592 | bytes 45000000 | tf_op jit(solution)/shard_map/pallas_call | solution.py:394
  72.2 26.2 %shard_map.238 = (bf16[2,2304,1024]{2,1,0:T(8,128)(2,1)}, bf16[2,2304,1024]{2,1,0:T(8,128)(2,1)}, bf16[16,96,1152]{2,1,0:T(8,128)(2,1)}, bf16[16,96,1152]{2,1,0:...) custom-call(s32[3]{0:T(128)} %pad_add_fusion.sc, bf16[1024,1152]{1,0:T(8,128)(2,1)} %bitcast.146, ...), custom_call_target="tpu_custom_call" | custom-call | flops 29899999232 | bytes 26000000 | tf_op jit(solution)/shard_map/pallas_call | solution.py:394
  100.9 27.3 %shard_map.239 = (bf16[2,2304,1024]{2,1,0:T(8,128)(2,1)}, bf16[2,2304,1024]{2,1,0:T(8,128)(2,1)}, bf16[16,96,640]{2,1,0:T(8,128)(2,1)}, bf16[16,96,512]{2,1,0:T(...) custom-call(s32[3]{0:T(128)} %pad_add_fusion.sc, ...), custom_call_target="tpu_custom_call", output_to_operand_aliasing={{0}: (9, {}), {1}: (10, {})} | custom-call | flops 29899999232 | bytes 26000000 | tf_op jit(solution)/shard_map/pallas_call | solution.py:394
  128.8 27.1 %shard_map.240 = (bf16[2,2304,1024]{2,1,0:T(8,128)(2,1)}, bf16[2,2304,1024]{2,1,0:T(8,128)(2,1)}, bf16[16,96,1152]{2,1,0:T(8,128)(2,1)}, bf16[16,96,1152]{2,1,0:...) custom-call(s32[3]{0:T(128)} %pad_add_fusion.sc, ...), custom_call_target="tpu_custom_call", output_to_operand_aliasing={{0}: (11, {}), {1}: (12, {})} | custom-call | flops 29899999232 | bytes 26000000 | tf_op jit(solution)/shard_map/pallas_call | solution.py:394
  165.6 27.4 %shard_map.241 = (f32[4,256,1152]{2,1,0:T(8,128)}, bf16[4,256,1152]{2,1,0:T(8,128)(2,1)}, f32[4,4,1152]{2,1,0:T(4,128)}) custom-call(s32[3]{0:T(128)} %pad_add_fusion.sc, bf16[2,2304,1024]{2,1,0:T(8,128)(2,1)} %get-tuple-element.312.back, bf16[1152,2304]{1,0:T(8,128)(2,1)} %w_up0.1, bf16[1152,2304]{1,0:T(8,128)(2,1)} %collective-permute-done.4.refs_0_.refs_3_.w_up1, ...), custom_call_target="tpu_custom_call" | custom-call | flops 69000003584 | bytes 41582592 | tf_op jit(solution)/shard_map/pallas_call | solution.py:394
  200.3 20.6 %shard_map.242.refs_0_ = bf16[2,3456,256]{2,1,0:T(8,128)(2,1)} custom-call(s32[3]{0:T(128)} %pad_add_fusion.sc, bf16[4,256,1152]{2,1,0:T(8,128)(2,1)} %get-tuple-element.327.grad_attn.refs_4_, bf16[4,3456,256]{2,1,0:T(8,128)(2,1)} %get-tuple-element.328.qkv, bf16[4,16,256,256]{3,2,1,0:T(8,128)(2,1)} %get-tuple-element.329.prob, bf16[576,1152]{1,0:T(8,128)(2,1)} %refs_0_.5, ...), custom_call_target="tpu_custom_call" | custom-call | flops 69000003584 | bytes 24018944 | tf_op jit(solution)/shard_map/pallas_call | solution.py:394
  223.9 20.2 %shard_map.243.refs_1_ = bf16[2,3456,256]{2,1,0:T(8,128)(2,1)} custom-call(s32[3]{0:T(128)} %pad_add_fusion.sc, bf16[4,256,1152]{2,1,0:T(8,128)(2,1)} %get-tuple-element.327.grad_attn.refs_4_, bf16[4,3456,256]{2,1,0:T(8,128)(2,1)} %get-tuple-element.328.qkv, bf16[4,16,256,256]{3,2,1,0:T(8,128)(2,1)} %get-tuple-element.329.prob, bf16[576,1152]{1,0:T(8,128)(2,1)} %refs_0_.5, ...), custom_call_target="tpu_custom_call" | custom-call | flops 69000003584 | bytes 24018944 | tf_op jit(solution)/shard_map/pallas_call | solution.py:394
  244.2 14.0 %shard_map.244 = (bf16[16,144,512]{2,1,0:T(8,128)(2,1)}, bf16[16,144,384]{2,1,0:T(8,128)(2,1)}, bf16[16,144,256]{2,1,0:T(8,128)(2,1)}, f32[3,1,576]{2,1,0:T(1,128)}) custom-call(s32[3]{0:T(128)} %pad_add_fusion.sc, bf16[2,3456,256]{2,1,0:T(8,128)(2,1)} %shard_map.242.refs_0_, bf16[2,3456,256]{2,1,0:T(8,128)(2,1)} %shard_map.243.refs_1_, ...), custom_call_target="tpu_custom_call" | custom-call | flops 69000003584 | bytes 19471104 | tf_op jit(solution)/shard_map/pallas_call | solution.py:394
  262.7 8.6 %collective-permute-done.16 = bf16[96,1152]{1,0:T(8,128)(2,1)S(1)} collective-permute-done((bf16[96,1152]{1,0:T(8,128)(2,1)S(1)}, bf16[96,1152]{1,0:T(8,128)(2,1)S(1)}, u32[]{:S(2)}, u32[]{:S(2)}) %collective-permute-start.16) | collective-permute-done | bytes 221216 | tf_op jit(solution)/shard_map/ppermute | solution.py:449
  272.6 14.3 %shard_map.245 = (bf16[16,144,512]{2,1,0:T(8,128)(2,1)}, bf16[16,144,384]{2,1,0:T(8,128)(2,1)}, bf16[16,144,256]{2,1,0:T(8,128)(2,1)}, f32[3,1,576]{2,1,0:T(1,128)}) custom-call(s32[3]{0:T(128)} %pad_add_fusion.sc, bf16[2,3456,256]{2,1,0:T(8,128)(2,1)} %shard_map.242.refs_0_, bf16[2,3456,256]{2,1,0:T(8,128)(2,1)} %shard_map.243.refs_1_, ...), custom_call_target="tpu_custom_call" | custom-call | flops 69000003584 | bytes 19471104 | tf_op jit(solution)/shard_map/pallas_call | solution.py:394
  303.1 24.4 %shard_map.246 = (f32[8,256,1152]{2,1,0:T(8,128)}, f32[4,256,1152]{2,1,0:T(8,128)}, f32[4,2,1152]{2,1,0:T(2,128)}) custom-call(s32[3]{0:T(128)} %pad_add_fusion.sc, bf16[2,3456,256]{2,1,0:T(8,128)(2,1)} %shard_map.242.refs_0_, bf16[2,3456,256]{2,1,0:T(8,128)(2,1)} %shard_map.243.refs_1_, bf16[1728,1152]{1,0:T(8,128)(2,1)} %bitcast.144, ...), custom_call_target="tpu_custom_call" | custom-call | flops 69000003584 | bytes 38891520 | tf_op jit(solution)/shard_map/pallas_call | solution.py:394
  327.4 10.0 %collective-permute-done.24 = bf16[2,96,1152]{2,1,0:T(8,128)(2,1)} collective-permute-done((bf16[2,96,1152]{2,1,0:T(8,128)(2,1)S(1)}, bf16[2,96,1152]{2,1,0:T(8,128)(2,1)}, u32[]{:S(2)}, u32[]{:S(2)}) %collective-permute-start.24) | collective-permute-done | bytes 442400 | tf_op jit(solution)/shard_map/ppermute | solution.py:449
  349.1 25.3 %shard_map.247 = (bf16[8,256,1152]{2,1,0:T(8,128)(2,1)}, bf16[4,256,1152]{2,1,0:T(8,128)(2,1)}, f32[4,1,1152]{2,1,0:T(1,128)}) custom-call(s32[3]{0:T(128)} %pad_add_fusion.sc, bf16[2,2304,1024]{2,1,0:T(8,128)(2,1)} %get-tuple-element.400.act, bf16[2304,1152]{1,0:T(8,128)(2,1)} %w_down0.1, bf16[2304,1152]{1,0:T(8,128)(2,1)} %collective-permute-done.5.refs_1_.refs_4_.w_down1, ...), custom_call_target="tpu_custom_call" | custom-call | flops 69000003584 | bytes 36813312 | tf_op jit(solution)/shard_map/pallas_call | solution.py:394
  374.4 6.7 %collective-permute-done.27 = bf16[2,2,144,256]{3,2,0,1:T(8,128)(2,1)} collective-permute-done((bf16[2,2,144,256]{3,2,0,1:T(8,128)(2,1)}, bf16[2,2,144,256]{3,2,0,1:T(8,128)(2,1)}, u32[]{:S(2)}, u32[]{:S(2)}) %collective-permute-start.27) | collective-permute-done | bytes 294944 | tf_op jit(solution)/shard_map/ppermute | solution.py:449
  392.5 33.5 %collective-permute-done.32 = bf16[2,144,256]{2,1,0:T(8,128)(2,1)S(1)} collective-permute-done((bf16[2,144,256]{2,1,0:T(8,128)(2,1)S(1)}, bf16[2,144,256]{2,1,0:T(8,128)(2,1)S(1)}, u32[]{:S(2)}, u32[]{:S(2)}) %collective-permute-start.32) | collective-permute-done | bytes 147488 | tf_op jit(solution)/shard_map/ppermute | solution.py:449
  426.1 13.5 %collective-permute-done.31 = bf16[2,144,896]{2,1,0:T(8,128)(2,1)S(1)} collective-permute-done((bf16[2,144,896]{2,1,0:T(8,128)(2,1)}, bf16[2,144,896]{2,1,0:T(8,128)(2,1)S(1)}, u32[]{:S(2)}, u32[]{:S(2)}) %collective-permute-start.31) | collective-permute-done | bytes 516128 | tf_op jit(solution)/shard_map/ppermute | solution.py:449
  451.3 8.7 %collective-permute-done.38 = bf16[13,3456]{1,0:T(8,128)(2,1)S(1)} collective-permute-done((bf16[13,3456]{1,0:T(8,128)(2,1)S(1)}, bf16[13,3456]{1,0:T(8,128)(2,1)S(1)}, u32[]{:S(2)}, u32[]{:S(2)}) %collective-permute-start.38) | collective-permute-done | bytes 89888 | tf_op jit(solution)/shard_map/ppermute | solution.py:513
  465.4 7.7 %collective-permute-done.43 = bf16[26,3456]{1,0:T(8,128)(2,1)S(1)} collective-permute-done((bf16[26,3456]{1,0:T(8,128)(2,1)S(1)}, bf16[26,3456]{1,0:T(8,128)(2,1)S(1)}, u32[]{:S(2)}, u32[]{:S(2)}) %collective-permute-start.43) | collective-permute-done | bytes 179744 | tf_op jit(solution)/shard_map/ppermute | solution.py:513
  482.0 6.2 %shard_map.249 = (f32[2304,1152]{1,0:T(8,128)}, f32[1152,2304]{1,0:T(8,128)}, f32[8,128]{1,0:T(8,128)}) custom-call(s32[3]{0:T(128)} %pad_add_fusion.sc, bf16[8,96,640]{2,1,0:T(8,128)(2,1)} %copy-done.4, bf16[8,96,640]{2,1,0:T(8,128)(2,1)} %copy-done.29, bf16[8,96,512]{2,1,0:T(8,128)(2,1)} %pad_maximum_fusion.4.refs_2_, bf16[8,96,512]{2,1,0:T(8,128)(2,1)} %copy-done.30, ...), custom_call_target="tpu_custom_call" | custom-call | flops 4600000000 | bytes 4000000 | tf_op jit(solution)/shard_map/pallas_call | solution.py:394
  497.7 5.5 shard_map.251
  510.0 7.4 %collective-permute-done.50 = bf16[104,3456]{1,0:T(8,128)(2,1)} collective-permute-done((bf16[104,3456]{1,0:T(8,128)(2,1)S(1)}, bf16[104,3456]{1,0:T(8,128)(2,1)}, u32[]{:S(2)}, u32[]{:S(2)}) %collective-permute-start.50) | collective-permute-done | bytes 718880 | tf_op jit(solution)/shard_map/ppermute | solution.py:513
  522.5 8.1 %fusion.6 = f32[1152,3456]{1,0:T(8,128)} fusion(bf16[128,1152]{1,0:T(8,128)(2,1)S(1)} %reshape.151, bf16[16,13,3456]{2,1,0:T(8,128)(2,1)S(1)} %reshape.149), kind=kOutput, calls=%fused_computation.19 | convolution fusion | flops 1019215872 | bytes 17104896 | tf_op jit(solution)/shard_map/dot_general | solution.py:997
  530.7 9.6 %collective-permute-done.51.refs_1_ = bf16[8,144,512]{2,1,0:T(8,128)(2,1)} collective-permute-done((bf16[8,144,512]{2,1,0:T(8,128)(2,1)}, bf16[8,144,512]{2,1,0:T(8,128)(2,1)}, u32[]{:S(2)}, u32[]{:S(2)}) %collective-permute-start.51) | collective-permute-done | bytes 1179680 | tf_op jit(solution)/shard_map/ppermute | solution.py:449
  540.3 8.5 %shard_map.248 = (f32[1728,1152]{1,0:T(8,128)}, f32[576,1152]{1,0:T(8,128)}) custom-call(s32[3]{0:T(128)} %pad_add_fusion.sc, bf16[8,144,512]{2,1,0:T(8,128)(2,1)} %pad_maximum_fusion.1.refs_0_, bf16[8,144,512]{2,1,0:T(8,128)(2,1)} %collective-permute-done.51.refs_1_, bf16[8,144,384]{2,1,0:T(8,128)(2,1)} %pad_maximum_fusion.3.refs_2_, ...), custom_call_target="tpu_custom_call" | custom-call | flops 10350000128 | bytes 9000000 | tf_op jit(solution)/shard_map/pallas_call | solution.py:394
  (289 shorter events, 130.2 us)
Async XLA Ops:
  7.2 484.6 %all-reduce.4.cloned.1.call-start = ((), (), s32[]{:S(2)}) async-start(), calls=%async_computation | async-start | bytes 14155776 | tf_op jit(solution)/shard_map/psum | solution.py:708
  14.6 57.0 %collective-permute-start.4 = (bf16[1152,2304]{1,0:T(8,128)(2,1)}, bf16[1152,2304]{1,0:T(8,128)(2,1)}, u32[]{:S(2)}, u32[]{:S(2)}) collective-permute-start(bf16[1152,2304]{1,0:T(8,128)(2,1)} %w_up0.1), channel_id=1, source_target_pairs={{0,1},{1,0},{2,3},{3,2},{4,5},{5,4},{6,7},{7,6},{8,9},{9,8},{10,11... | collective-permute-start | bytes 15925256 | tf_op jit(solution)/shard_map/ppermute | solution.py:425
  14.9 56.6 %collective-permute-start.5 = (bf16[2304,1152]{1,0:T(8,128)(2,1)}, bf16[2304,1152]{1,0:T(8,128)(2,1)}, u32[]{:S(2)}, u32[]{:S(2)}) collective-permute-start(bf16[2304,1152]{1,0:T(8,128)(2,1)} %w_down0.1), channel_id=1, source_target_pairs={{0,1},{1,0},{2,3},{3,2},{4,5},{5,4},{6,7},{7,6},{8,9},{9,8},{10,11... | collective-permute-start | bytes 15925256 | tf_op jit(solution)/shard_map/ppermute | solution.py:425
  18.1 53.5 %collective-permute-start.6 = (bf16[1,2304]{1,0:T(2,128)(2,1)S(1)}, bf16[1,2304]{1,0:T(2,128)(2,1)S(1)}, u32[]{:S(2)}, u32[]{:S(2)}) collective-permute-start(bf16[1,2304]{1,0:T(2,128)(2,1)S(1)} %broadcast_in_dim.52), channel_id=1, source_target_pairs={{0,1},{1,0},{2,3},{3,2},{4,5},{5,4},{6,7},{7,6},{8,9},{9,8},{10,11... | collective-permute-start | bytes 13832 | tf_op jit(solution)/shard_map/ppermute | solution.py:425
  98.4 29.8 %collective-permute-start.7 = (bf16[16,96,1152]{2,1,0:T(8,128)(2,1)}, bf16[16,96,1152]{2,1,0:T(8,128)(2,1)}, u32[]{:S(2)}, u32[]{:S(2)}) collective-permute-start(bf16[16,96,1152]{2,1,0:T(8,128)(2,1)} %get-tuple-element.291), channel_id=1, source_target_pairs={{0,1},{1,0},{2,3},{3,2},{4,5},{5,4},{6,7},{7,6},{8,9},{9,8},{10,11... | collective-permute-start | bytes 10616840 | tf_op jit(solution)/shard_map/ppermute | solution.py:425
  98.6 29.6 %collective-permute-start.8 = (bf16[16,96,1152]{2,1,0:T(8,128)(2,1)}, bf16[16,96,1152]{2,1,0:T(8,128)(2,1)}, u32[]{:S(2)}, u32[]{:S(2)}) collective-permute-start(bf16[16,96,1152]{2,1,0:T(8,128)(2,1)} %get-tuple-element.292), channel_id=1, source_target_pairs={{0,1},{1,0},{2,3},{3,2},{4,5},{5,4},{6,7},{7,6},{8,9},{9,8},{10,11... | collective-permute-start | bytes 10616840 | tf_op jit(solution)/shard_map/ppermute | solution.py:425
  128.2 27.8 %collective-permute-start.9 = (bf16[16,96,640]{2,1,0:T(8,128)(2,1)}, bf16[16,96,640]{2,1,0:T(8,128)(2,1)S(1)}, u32[]{:S(2)}, u32[]{:S(2)}) collective-permute-start(bf16[16,96,640]{2,1,0:T(8,128)(2,1)} %get-tuple-element.304), channel_id=1, source_target_pairs={{0,1},{1,0},{2,3},{3,2},{4,5},{5,4},{6,7},{7,6},{8,9},{9,8},{10,11... | collective-permute-start | bytes 5898248 | tf_op jit(solution)/shard_map/ppermute | solution.py:425
  161.3 34.5 %collective-permute-start.11 = (bf16[2,2,2,96,640]{4,3,0,1,2:T(8,128)(2,1)S(1)}, bf16[2,2,2,96,640]{4,3,0,1,2:T(8,128)(2,1)S(1)}, u32[]{:S(2)}, u32[]{:S(2)}) collective-permute-start(bf16[2,2,2,96,640]{4,3,0,1,2:T(8,128)(2,1)S(1)} %get-tuple-element.319), channel_id=1, source_target_pairs={{0,2},{2,0},{4,6},{6,4},{8,10},{10,8},{12,14},{14,12},{16,18},{18,... | collective-permute-start | bytes 2949128 | tf_op jit(solution)/shard_map/ppermute | solution.py:449
  164.0 28.9 %collective-permute-start.12 = (bf16[2,2,2,96,512]{4,3,0,1,2:T(8,128)(2,1)}, bf16[2,2,2,96,512]{4,3,0,1,2:T(8,128)(2,1)}, u32[]{:S(2)}, u32[]{:S(2)}) collective-permute-start(bf16[2,2,2,96,512]{4,3,0,1,2:T(8,128)(2,1)} %get-tuple-element.320), channel_id=1, source_target_pairs={{0,4},{2,6},{4,0},{6,2},{8,12},{10,14},{12,8},{14,10},{16,20},{18,... | collective-permute-start | bytes 2359304 | tf_op jit(solution)/shard_map/ppermute | solution.py:449
  299.1 38.3 %collective-permute-start.21 = (bf16[2,2,2,144,512]{4,3,0,1,2:T(8,128)(2,1)}, bf16[2,2,2,144,512]{4,3,0,1,2:T(8,128)(2,1)}, u32[]{:S(2)}, u32[]{:S(2)}) collective-permute-start(bf16[2,2,2,144,512]{4,3,0,1,2:T(8,128)(2,1)} %fusion.1), channel_id=1, source_target_pairs={{0,2},{2,0},{4,6},{6,4},{8,10},{10,8},{12,14},{14,12},{16,18},{18,... | collective-permute-start | bytes 3538952 | tf_op jit(solution)/shard_map/ppermute | solution.py:449
  300.6 36.9 %collective-permute-start.22 = (bf16[2,2,2,144,384]{4,3,0,1,2:T(8,128)(2,1)}, bf16[2,2,2,144,384]{4,3,0,1,2:T(8,128)(2,1)}, u32[]{:S(2)}, u32[]{:S(2)}) collective-permute-start(bf16[2,2,2,144,384]{4,3,0,1,2:T(8,128)(2,1)} %fusion.5), channel_id=1, source_target_pairs={{0,4},{2,6},{4,0},{6,2},{8,12},{10,14},{12,8},{14,10},{16,20},{18,... | collective-permute-start | bytes 2654216 | tf_op jit(solution)/shard_map/ppermute | solution.py:449
  301.1 36.3 %collective-permute-start.23 = (bf16[2,2,2,144,256]{4,3,1,2,0:T(8,128)(2,1)S(1)}, bf16[2,2,2,144,256]{4,3,1,2,0:T(8,128)(2,1)}, u32[]{:S(2)}, u32[]{:S(2)}) collective-permute-start(bf16[2,2,2,144,256]{4,3,1,2,0:T(8,128)(2,1)S(1)} %fusion.12), channel_id=1, source_target_pairs={{0,8},{2,10},{4,12},{6,14},{8,0},{10,2},{12,4},{14,6},{16,24},{18,... | collective-permute-start | bytes 1769480 | tf_op jit(solution)/shard_map/ppermute | solution.py:449
  302.2 35.2 %collective-permute-start.24 = (bf16[2,96,1152]{2,1,0:T(8,128)(2,1)S(1)}, bf16[2,96,1152]{2,1,0:T(8,128)(2,1)}, u32[]{:S(2)}, u32[]{:S(2)}) collective-permute-start(bf16[2,96,1152]{2,1,0:T(8,128)(2,1)S(1)} %pad_maximum_fusion.12), channel_id=1, source_target_pairs={{0,8},{2,10},{4,12},{6,14},{8,0},{10,2},{12,4},{14,6},{16,24},{18,... | collective-permute-start | bytes 1327112 | tf_op jit(solution)/shard_map/ppermute | solution.py:449
  344.7 36.5 %collective-permute-start.25 = (bf16[2,2,144,512]{3,2,0,1:T(8,128)(2,1)}, bf16[2,2,144,512]{3,2,0,1:T(8,128)(2,1)S(1)}, u32[]{:S(2)}, u32[]{:S(2)}) collective-permute-start(bf16[2,2,144,512]{3,2,0,1:T(8,128)(2,1)} %get-tuple-element.407), channel_id=1, source_target_pairs={{0,4},{2,6},{4,0},{6,2},{8,12},{10,14},{12,8},{14,10},{16,20},{18,... | collective-permute-start | bytes 1769480 | tf_op jit(solution)/shard_map/ppermute | solution.py:449
  345.9 35.2 %collective-permute-start.28 = (bf16[4,96,640]{2,1,0:T(8,128)(2,1)S(1)}, bf16[4,96,640]{2,1,0:T(8,128)(2,1)S(1)}, u32[]{:S(2)}, u32[]{:S(2)}) collective-permute-start(bf16[4,96,640]{2,1,0:T(8,128)(2,1)S(1)} %slice.406), channel_id=1, source_target_pairs={{0,4},{2,6},{4,0},{6,2},{8,12},{10,14},{12,8},{14,10},{16,20},{18,... | collective-permute-start | bytes 1474568 | tf_op jit(solution)/shard_map/ppermute | solution.py:449
  346.7 34.4 %collective-permute-start.26 = (bf16[2,2,144,384]{3,2,0,1:T(8,128)(2,1)}, bf16[2,2,144,384]{3,2,0,1:T(8,128)(2,1)}, u32[]{:S(2)}, u32[]{:S(2)}) collective-permute-start(bf16[2,2,144,384]{3,2,0,1:T(8,128)(2,1)} %get-tuple-element.408), channel_id=1, source_target_pairs={{0,2},{2,0},{4,6},{6,4},{8,10},{10,8},{12,14},{14,12},{16,18},{18,... | collective-permute-start | bytes 1327112 | tf_op jit(solution)/shard_map/ppermute | solution.py:449
  348.8 32.3 %collective-permute-start.29 = (bf16[4,96,512]{2,1,0:T(8,128)(2,1)S(1)}, bf16[4,96,512]{2,1,0:T(8,128)(2,1)S(1)}, u32[]{:S(2)}, u32[]{:S(2)}) collective-permute-start(bf16[4,96,512]{2,1,0:T(8,128)(2,1)S(1)} %slice.407), channel_id=1, source_target_pairs={{0,2},{2,0},{4,6},{6,4},{8,10},{10,8},{12,14},{14,12},{16,18},{18,... | collective-permute-start | bytes 1179656 | tf_op jit(solution)/shard_map/ppermute | solution.py:449
  348.8 32.3 %collective-permute-start.27 = (bf16[2,2,144,256]{3,2,0,1:T(8,128)(2,1)}, bf16[2,2,144,256]{3,2,0,1:T(8,128)(2,1)}, u32[]{:S(2)}, u32[]{:S(2)}) collective-permute-start(bf16[2,2,144,256]{3,2,0,1:T(8,128)(2,1)} %get-tuple-element.409), channel_id=1, source_target_pairs={{0,16},{2,18},{4,20},{6,22},{8,24},{10,26},{12,28},{14,30},{16,0},... | collective-permute-start | bytes 884744 | tf_op jit(solution)/shard_map/ppermute | solution.py:449
  381.1 81.4 %collective-permute-start.39 = (f32[4,256,1152]{2,1,0:T(8,128)}, f32[4,256,1152]{2,1,0:T(8,128)}, u32[]{:S(2)}, u32[]{:S(2)}) collective-permute-start(f32[4,256,1152]{2,1,0:T(8,128)} %get-tuple-element.464), channel_id=1, source_target_pairs={{0,1},{1,0},{2,3},{3,2},{4,5},{5,4},{6,7},{7,6},{8,9},{9,8},{10,11... | collective-permute-start | bytes 14155784 | tf_op jit(solution)/shard_map/ppermute | solution.py:425
  388.9 62.3 %collective-permute-start.35 = (bf16[4,256,1152]{2,1,0:T(8,128)(2,1)}, bf16[4,256,1152]{2,1,0:T(8,128)(2,1)S(1)}, u32[]{:S(2)}, u32[]{:S(2)}) collective-permute-start(bf16[4,256,1152]{2,1,0:T(8,128)(2,1)} %get-tuple-element.447), channel_id=1, source_target_pairs={{0,1},{1,0},{2,3},{3,2},{4,5},{5,4},{6,7},{7,6},{8,9},{9,8},{10,11... | collective-permute-start | bytes 7077896 | tf_op jit(solution)/shard_map/ppermute | solution.py:425
  389.0 50.6 %collective-permute-start.33 = (bf16[8,96,640]{2,1,0:T(8,128)(2,1)S(1)}, bf16[8,96,640]{2,1,0:T(8,128)(2,1)S(1)}, u32[]{:S(2)}, u32[]{:S(2)}) collective-permute-start(bf16[8,96,640]{2,1,0:T(8,128)(2,1)S(1)} %pad_maximum_fusion.2.refs_0_), channel_id=1, source_target_pairs={{0,2},{2,0},{4,6},{6,4},{8,10},{10,8},{12,14},{14,12},{16,18},{18,... | collective-permute-start | bytes 2949128 | tf_op jit(solution)/shard_map/ppermute | solution.py:449
  389.8 49.8 %collective-permute-start.34 = (bf16[8,96,512]{2,1,0:T(8,128)(2,1)S(1)}, bf16[8,96,512]{2,1,0:T(8,128)(2,1)S(1)}, u32[]{:S(2)}, u32[]{:S(2)}) collective-permute-start(bf16[8,96,512]{2,1,0:T(8,128)(2,1)S(1)} %copy-done.5), channel_id=1, source_target_pairs={{0,4},{2,6},{4,0},{6,2},{8,12},{10,14},{12,8},{14,10},{16,20},{18,... | collective-permute-start | bytes 2359304 | tf_op jit(solution)/shard_map/ppermute | solution.py:449
  391.5 34.5 %collective-permute-start.32 = (bf16[2,144,256]{2,1,0:T(8,128)(2,1)S(1)}, bf16[2,144,256]{2,1,0:T(8,128)(2,1)S(1)}, u32[]{:S(2)}, u32[]{:S(2)}) collective-permute-start(bf16[2,144,256]{2,1,0:T(8,128)(2,1)S(1)} %get-tuple-element.436), channel_id=1, source_target_pairs={{0,2},{2,0},{4,6},{6,4},{8,10},{10,8},{12,14},{14,12},{16,18},{18,... | collective-permute-start | bytes 442376 | tf_op jit(solution)/shard_map/ppermute | solution.py:449
  507.6 32.7 %collective-permute-start.51 = (bf16[8,144,512]{2,1,0:T(8,128)(2,1)}, bf16[8,144,512]{2,1,0:T(8,128)(2,1)}, u32[]{:S(2)}, u32[]{:S(2)}) collective-permute-start(bf16[8,144,512]{2,1,0:T(8,128)(2,1)} %pad_maximum_fusion.1.refs_0_), channel_id=1, source_target_pairs={{0,2},{2,0},{4,6},{6,4},{8,10},{10,8},{12,14},{14,12},{16,18},{18,... | collective-permute-start | bytes 3538952 | tf_op jit(solution)/shard_map/ppermute | solution.py:449
  (67 other events, 770.3 us)
Sparse Core Ops, SparseCore 0:
  156.1 268.5 all-reduce.3

commit v8 on v7

--- a/solution.py
+++ b/solution.py
@@ -820,7 +820,6 @@
     )
     order.after(low_sums)
     order.tick(last, *flows)
-    other_tokens = swap_cores(grad_own_tokens)
     down_spec = lambda part: pl.BlockSpec((reach, dim), lambda s, c: (rows_of(part, turns)(s, c), 0))
     output, own_output, gate_sums = run_kernel(
         functools.partial(output_kernel, turns, images),
@@ -843,9 +842,10 @@
     )
     order.after(gate_sums)
     order.tick(last, *flows)
-    other_output = swap_cores(own_output)
-
-    low_sums, mid_sums, gate_sums, down_sums = order.fence((low_sums, mid_sums, gate_sums, down_sums))
+
+    low_sums, mid_sums, gate_sums, down_sums, qv_sums, up_sums, scaled_rows = order.fence(
+        (low_sums, mid_sums, gate_sums, down_sums, qv_sums, up_sums, scaled)
+    )
     grad_modulation = jnp.concatenate([low_sums, mid_sums[:, 2:3], mid_sums[:, 0:2], gate_sums], axis=1)
     grad_modulation = grad_modulation.reshape(images, 6 * dim).astype(bf16)
     bias_sums = [
@@ -872,26 +872,19 @@
     group_mod = jnp.where(core == 0, jnp.concatenate([kept, came]), jnp.concatenate([came, kept]))
     own_bias_sum = bias_sums[0] + got[images : images + 1]
     shared_sum = shared + got[images + 1 :]
-    wide_scaled = jnp.pad(scaled.reshape(-1), (0, 3 * own_cols - slots * dim)).reshape(3, own_cols)
+    wide_scaled = jnp.pad(scaled_rows.reshape(-1), (0, 3 * own_cols - slots * dim)).reshape(3, own_cols)
     packed_rows = jnp.concatenate(
         [group_mod, own_bias_sum.astype(bf16), shared_sum.astype(bf16), wide_scaled]
     )
     (packed_rows,) = order.fence([packed_rows])
     small = rows_flow(packed_rows)
-    order.tick(last, small, *flows)
+    order.tick(last, small)
     (group_mod,) = order.fence([group_mod])
     part_scaled = outer_cols(group_mod, w_mod).astype(bf16)
-    came_scaled = swap_cores(part_scaled)
-    output = fill_other(output, order.fence(other_output), core)
-    order.after((output[0, 0, :1], part_scaled[0, :1]))
+    order.after(part_scaled[0, :1])
     order.tick(last, small, *flows)
-    grad_tokens = fill_other(grad_tokens, order.fence(other_tokens), core)
-    part_scaled, came_scaled = order.fence((part_scaled, came_scaled))
-    grad_scaled = part_scaled.astype(f32) + came_scaled.astype(f32)
-    _, silu_back = jax.vjp(jax.nn.silu, cond_f)
-    grad_condition = silu_back(grad_scaled)[0]
-    order.after((grad_tokens[0, 0, :1], grad_condition[0, :1]))
-    order.tick(last, small, *flows)
+    own_output, part_scaled = order.fence((own_output, part_scaled))
+    other_output, came_scaled = swap_cores(own_output), swap_cores(part_scaled)
 
     def cuts(ways):
         return tuple((way, lo, hi) for lo, hi, way in ways)
@@ -930,9 +923,19 @@
         body = functools.partial(final_mlp_kernel, cuts(MLP_WAYS), per)
         final_mlp(PLAIN + chunk, body, order.finish(flow))
     order.tick(last, small)
+    other_output, came_scaled, grad_own_tokens = order.fence((other_output, came_scaled, grad_own_tokens))
+    other_tokens = swap_cores(grad_own_tokens)
     for chunk, total in zip(summed, order.fence(plain_sums)):
         final_mlp(chunk, functools.partial(final_plain_kernel, per), [total])
+    order.tick(last, small)
+    output = fill_other(output, other_output, core)
+    grad_scaled = part_scaled.astype(f32) + came_scaled.astype(f32)
+    _, silu_back = jax.vjp(jax.nn.silu, cond_f)
+    grad_condition = silu_back(grad_scaled)[0]
+    order.after((output[0, 0, :1], grad_condition[0, :1]))
     order.tick(last)
+    grad_tokens = fill_other(grad_tokens, order.fence(other_tokens), core)
+    order.after(grad_tokens[0, 0, :1])
     all_rows = order.fence(order.finish(small)).reshape(16, slots + 5, own_cols)
     all_mod = all_rows[:, :slots].reshape(-1, own_cols)
     all_scaled = all_rows[:, slots + 2 :].reshape(16, -1)[:, : slots * dim].reshape(-1, dim)

time: 564 us -> 563 us (level)
  waiting for transfers between devices: 120 us -> 113 us
  other arithmetic: 25.9 us -> 32.6 us
    concatenate x9, other arithmetic: 5.3 us -> 12 us  [gather_flow(): joined = [jnp.concatenate([one, two]) for one, two in zip(have, comes)]]
    ppermute x4, waiting for transfers between devices: 23.8 us -> 17.5 us  [rows_flow(): came = lax.ppermute(rows, 'dp', bit_pairs(bit))]
  transfers between devices with their start and end apart: 55 -> 55, of which waited for: 16 -> 19; matrix products, arithmetic and copies ran while one was open for 12% -> 12% of each run, Pallas kernels for 48% -> 48%
where the time goes in v8:
time: 563 us; the launch traced here: 555 us
  Pallas kernels  301 us (53%)
  waiting for transfers between devices  113 us (20%)
  starting transfers between devices  45.9 us (8%)
  other arithmetic  32.6 us (6%)
  local copies, waits for them, and re-layouts  28.2 us (5%)
  matrix products  18.1 us (3%)
  between operations  16 us (3%)
    pallas_call x15, Pallas kernels, run_kernel(): pl.pallas_call(body, out_shape=out_shape, grid_spec=pltpu.PrefetchScalarG...  301 us
    ppermute x32, waiting for transfers between devices, exchange(): lax.ppermute(value, 'dp', bit_pairs(bit))  91.5 us
    ppermute x32, starting transfers between devices, exchange(): lax.ppermute(value, 'dp', bit_pairs(bit))  33.7 us
    ppermute x4, waiting for transfers between devices, rows_flow(): came = lax.ppermute(rows, 'dp', bit_pairs(bit))  17.5 us
    add x21, other arithmetic, reduce_flow(): cut(one, bits, route[stage], side) + cut(two, bits, route[stage], side)  12.4 us
    concatenate x9, other arithmetic, gather_flow(): joined = [jnp.concatenate([one, two]) for one, two in zip(have, comes)]  12 us
  transfers between devices with their start and end apart: 55, of which 19 were waited for; matrix products, arithmetic and copies ran while one was open for 12% of the time, Pallas kernels for 48%

profile of v8, /device:TPU:0, one launch (start us, length us, event | category | flops | bytes accessed | tf_op | source)
XLA Modules:
  0.0 554.5 jit_solution(14174612897890823779)
XLA Ops:
  22.5 49.0 %shard_map.237 = (bf16[4,3456,256]{2,1,0:T(8,128)(2,1)}, bf16[4,16,256,256]{3,2,1,0:T(8,128)(2,1)}, bf16[4,1152,256]{2,1,0:T(8,128)(2,1)}, f32[4,256,1152]{2,1,0...) custom-call(s32[3]{0:T(128)} %pad_add_fusion.sc, ...), custom_call_target="tpu_custom_call" | custom-call | flops 51749998592 | bytes 45000000 | tf_op jit(solution)/shard_map/pallas_call | solution.py:394
  72.1 26.3 %shard_map.238 = (bf16[2,2304,1024]{2,1,0:T(8,128)(2,1)}, bf16[2,2304,1024]{2,1,0:T(8,128)(2,1)}, bf16[16,96,1152]{2,1,0:T(8,128)(2,1)}, bf16[16,96,1152]{2,1,0:...) custom-call(s32[3]{0:T(128)} %pad_add_fusion.sc, bf16[1024,1152]{1,0:T(8,128)(2,1)} %bitcast.144, ...), custom_call_target="tpu_custom_call" | custom-call | flops 29899999232 | bytes 26000000 | tf_op jit(solution)/shard_map/pallas_call | solution.py:394
  100.9 27.3 %shard_map.239 = (bf16[2,2304,1024]{2,1,0:T(8,128)(2,1)}, bf16[2,2304,1024]{2,1,0:T(8,128)(2,1)}, bf16[16,96,640]{2,1,0:T(8,128)(2,1)}, bf16[16,96,512]{2,1,0:T(...) custom-call(s32[3]{0:T(128)} %pad_add_fusion.sc, ...), custom_call_target="tpu_custom_call", output_to_operand_aliasing={{0}: (9, {}), {1}: (10, {})} | custom-call | flops 29899999232 | bytes 26000000 | tf_op jit(solution)/shard_map/pallas_call | solution.py:394
  128.8 27.1 %shard_map.240 = (bf16[2,2304,1024]{2,1,0:T(8,128)(2,1)}, bf16[2,2304,1024]{2,1,0:T(8,128)(2,1)}, bf16[16,96,1152]{2,1,0:T(8,128)(2,1)}, bf16[16,96,1152]{2,1,0:...) custom-call(s32[3]{0:T(128)} %pad_add_fusion.sc, ...), custom_call_target="tpu_custom_call", output_to_operand_aliasing={{0}: (11, {}), {1}: (12, {})} | custom-call | flops 29899999232 | bytes 26000000 | tf_op jit(solution)/shard_map/pallas_call | solution.py:394
  165.5 27.4 %shard_map.241 = (f32[4,256,1152]{2,1,0:T(8,128)}, bf16[4,256,1152]{2,1,0:T(8,128)(2,1)}, f32[4,4,1152]{2,1,0:T(4,128)}) custom-call(s32[3]{0:T(128)} %pad_add_fusion.sc, bf16[2,2304,1024]{2,1,0:T(8,128)(2,1)} %get-tuple-element.323.back, bf16[1152,2304]{1,0:T(8,128)(2,1)} %w_up0.1, bf16[1152,2304]{1,0:T(8,128)(2,1)} %collective-permute-done.4.refs_0_.refs_3_.w_up1, ...), custom_call_target="tpu_custom_call" | custom-call | flops 69000003584 | bytes 41582592 | tf_op jit(solution)/shard_map/pallas_call | solution.py:394
  200.4 20.6 %shard_map.242.refs_0_ = bf16[2,3456,256]{2,1,0:T(8,128)(2,1)} custom-call(s32[3]{0:T(128)} %pad_add_fusion.sc, bf16[4,256,1152]{2,1,0:T(8,128)(2,1)} %get-tuple-element.338.grad_attn.refs_4_, bf16[4,3456,256]{2,1,0:T(8,128)(2,1)} %get-tuple-element.339.qkv, bf16[4,16,256,256]{3,2,1,0:T(8,128)(2,1)} %get-tuple-element.340.prob, bf16[576,1152]{1,0:T(8,128)(2,1)} %refs_0_.5, ...), custom_call_target="tpu_custom_call" | custom-call | flops 69000003584 | bytes 24018944 | tf_op jit(solution)/shard_map/pallas_call | solution.py:394
  223.8 20.2 %shard_map.243.refs_1_ = bf16[2,3456,256]{2,1,0:T(8,128)(2,1)} custom-call(s32[3]{0:T(128)} %pad_add_fusion.sc, bf16[4,256,1152]{2,1,0:T(8,128)(2,1)} %get-tuple-element.338.grad_attn.refs_4_, bf16[4,3456,256]{2,1,0:T(8,128)(2,1)} %get-tuple-element.339.qkv, bf16[4,16,256,256]{3,2,1,0:T(8,128)(2,1)} %get-tuple-element.340.prob, bf16[576,1152]{1,0:T(8,128)(2,1)} %refs_0_.5, ...), custom_call_target="tpu_custom_call" | custom-call | flops 69000003584 | bytes 24018944 | tf_op jit(solution)/shard_map/pallas_call | solution.py:394
  247.2 14.0 %shard_map.244 = (bf16[16,144,512]{2,1,0:T(8,128)(2,1)}, bf16[16,144,384]{2,1,0:T(8,128)(2,1)}, bf16[16,144,256]{2,1,0:T(8,128)(2,1)}, f32[3,1,576]{2,1,0:T(1,128)}) custom-call(s32[3]{0:T(128)} %pad_add_fusion.sc, bf16[2,3456,256]{2,1,0:T(8,128)(2,1)} %shard_map.242.refs_0_, bf16[2,3456,256]{2,1,0:T(8,128)(2,1)} %shard_map.243.refs_1_, ...), custom_call_target="tpu_custom_call" | custom-call | flops 69000003584 | bytes 19471104 | tf_op jit(solution)/shard_map/pallas_call | solution.py:394
  261.2 5.2 collective-permute-done.16
  267.7 14.3 %shard_map.245 = (bf16[16,144,512]{2,1,0:T(8,128)(2,1)}, bf16[16,144,384]{2,1,0:T(8,128)(2,1)}, bf16[16,144,256]{2,1,0:T(8,128)(2,1)}, f32[3,1,576]{2,1,0:T(1,128)}) custom-call(s32[3]{0:T(128)} %pad_add_fusion.sc, bf16[2,3456,256]{2,1,0:T(8,128)(2,1)} %shard_map.242.refs_0_, bf16[2,3456,256]{2,1,0:T(8,128)(2,1)} %shard_map.243.refs_1_, ...), custom_call_target="tpu_custom_call" | custom-call | flops 69000003584 | bytes 19471104 | tf_op jit(solution)/shard_map/pallas_call | solution.py:394
  282.0 5.8 %collective-permute-done.20 = bf16[96,1152]{1,0:T(8,128)(2,1)} collective-permute-done((bf16[96,1152]{1,0:T(8,128)(2,1)}, bf16[96,1152]{1,0:T(8,128)(2,1)}, u32[]{:S(2)}, u32[]{:S(2)}) %collective-permute-start.20) | collective-permute-done | bytes 221216 | tf_op jit(solution)/shard_map/ppermute | solution.py:449
  301.9 24.5 %shard_map.246 = (f32[8,256,1152]{2,1,0:T(8,128)}, f32[4,256,1152]{2,1,0:T(8,128)}, f32[4,2,1152]{2,1,0:T(2,128)}) custom-call(s32[3]{0:T(128)} %pad_add_fusion.sc, bf16[2,3456,256]{2,1,0:T(8,128)(2,1)} %shard_map.242.refs_0_, bf16[2,3456,256]{2,1,0:T(8,128)(2,1)} %shard_map.243.refs_1_, bf16[1728,1152]{1,0:T(8,128)(2,1)} %bitcast.142, ...), custom_call_target="tpu_custom_call" | custom-call | flops 69000003584 | bytes 38891520 | tf_op jit(solution)/shard_map/pallas_call | solution.py:394
  326.4 14.2 %collective-permute-done.24 = bf16[2,96,1152]{2,1,0:T(8,128)(2,1)} collective-permute-done((bf16[2,96,1152]{2,1,0:T(8,128)(2,1)S(1)}, bf16[2,96,1152]{2,1,0:T(8,128)(2,1)}, u32[]{:S(2)}, u32[]{:S(2)}) %collective-permute-start.24) | collective-permute-done | bytes 442400 | tf_op jit(solution)/shard_map/ppermute | solution.py:449
  351.7 24.7 %shard_map.247 = (bf16[8,256,1152]{2,1,0:T(8,128)(2,1)}, bf16[4,256,1152]{2,1,0:T(8,128)(2,1)}, f32[4,1,1152]{2,1,0:T(1,128)}) custom-call(s32[3]{0:T(128)} %pad_add_fusion.sc, bf16[2,2304,1024]{2,1,0:T(8,128)(2,1)} %get-tuple-element.411.act, bf16[2304,1152]{1,0:T(8,128)(2,1)} %w_down0.1, bf16[2304,1152]{1,0:T(8,128)(2,1)} %collective-permute-done.5.refs_1_.refs_4_.w_down1, ...), custom_call_target="tpu_custom_call" | custom-call | flops 69000003584 | bytes 36813312 | tf_op jit(solution)/shard_map/pallas_call | solution.py:394
  389.9 6.2 %collective-permute-done.32 = bf16[2,144,256]{2,1,0:T(8,128)(2,1)S(1)} collective-permute-done((bf16[2,144,256]{2,1,0:T(8,128)(2,1)S(1)}, bf16[2,144,256]{2,1,0:T(8,128)(2,1)S(1)}, u32[]{:S(2)}, u32[]{:S(2)}) %collective-permute-start.32) | collective-permute-done | bytes 147488 | tf_op jit(solution)/shard_map/ppermute | solution.py:449
  396.1 32.1 %collective-permute-done.31 = bf16[2,144,896]{2,1,0:T(8,128)(2,1)S(1)} collective-permute-done((bf16[2,144,896]{2,1,0:T(8,128)(2,1)S(1)}, bf16[2,144,896]{2,1,0:T(8,128)(2,1)S(1)}, u32[]{:S(2)}, u32[]{:S(2)}) %collective-permute-start.31) | collective-permute-done | bytes 516128 | tf_op jit(solution)/shard_map/ppermute | solution.py:449
  432.3 5.4 convolution_convert_fusion
  437.7 9.1 %collective-permute-done.35 = bf16[13,3456]{1,0:T(8,128)(2,1)S(1)} collective-permute-done((bf16[13,3456]{1,0:T(8,128)(2,1)S(1)}, bf16[13,3456]{1,0:T(8,128)(2,1)S(1)}, u32[]{:S(2)}, u32[]{:S(2)}) %collective-permute-start.35) | collective-permute-done | bytes 89888 | tf_op jit(solution)/shard_map/ppermute | solution.py:513
  464.9 6.2 %shard_map.249 = (f32[2304,1152]{1,0:T(8,128)}, f32[1152,2304]{1,0:T(8,128)}, f32[8,128]{1,0:T(8,128)}) custom-call(s32[3]{0:T(128)} %pad_add_fusion.sc, bf16[8,96,640]{2,1,0:T(8,128)(2,1)} %pad_maximum_fusion.2.refs_0_, bf16[8,96,640]{2,1,0:T(8,128)(2,1)} %copy-done.30, bf16[8,96,512]{2,1,0:T(8,128)(2,1)} %pad_maximum_fusion.4.refs_2_, ...), custom_call_target="tpu_custom_call" | custom-call | flops 4600000000 | bytes 4000000 | tf_op jit(solution)/shard_map/pallas_call | solution.py:394
  484.8 5.4 shard_map.250
  491.6 5.5 shard_map.251
  514.2 8.1 %fusion.6 = f32[1152,3456]{1,0:T(8,128)} fusion(bf16[128,1152]{1,0:T(8,128)(2,1)S(1)} %reshape.151, bf16[16,13,3456]{2,1,0:T(8,128)(2,1)S(1)} %reshape.149), kind=kOutput, calls=%fused_computation.19 | convolution fusion | flops 1019215872 | bytes 17104896 | tf_op jit(solution)/shard_map/dot_general | solution.py:1000
  526.5 6.9 %collective-permute-done.51.refs_1_ = bf16[8,144,512]{2,1,0:T(8,128)(2,1)} collective-permute-done((bf16[8,144,512]{2,1,0:T(8,128)(2,1)}, bf16[8,144,512]{2,1,0:T(8,128)(2,1)}, u32[]{:S(2)}, u32[]{:S(2)}) %collective-permute-start.51) | collective-permute-done | bytes 1179680 | tf_op jit(solution)/shard_map/ppermute | solution.py:449
  538.9 8.5 %shard_map.248 = (f32[1728,1152]{1,0:T(8,128)}, f32[576,1152]{1,0:T(8,128)}) custom-call(s32[3]{0:T(128)} %pad_add_fusion.sc, bf16[8,144,512]{2,1,0:T(8,128)(2,1)} %pad_maximum_fusion.1.refs_0_, bf16[8,144,512]{2,1,0:T(8,128)(2,1)} %collective-permute-done.51.refs_1_, bf16[8,144,384]{2,1,0:T(8,128)(2,1)} %pad_maximum_fusion.3.refs_2_, ...), custom_call_target="tpu_custom_call" | custom-call | flops 10350000128 | bytes 9000000 | tf_op jit(solution)/shard_map/pallas_call | solution.py:394
  (284 shorter events, 144.4 us)
Async XLA Ops:
  7.2 464.0 %all-reduce.4.cloned.1.call-start = ((), (), s32[]{:S(2)}) async-start(), calls=%async_computation | async-start | bytes 14155776 | tf_op jit(solution)/shard_map/psum | solution.py:708
  14.6 57.0 %collective-permute-start.4 = (bf16[1152,2304]{1,0:T(8,128)(2,1)}, bf16[1152,2304]{1,0:T(8,128)(2,1)}, u32[]{:S(2)}, u32[]{:S(2)}) collective-permute-start(bf16[1152,2304]{1,0:T(8,128)(2,1)} %w_up0.1), channel_id=1, source_target_pairs={{0,1},{1,0},{2,3},{3,2},{4,5},{5,4},{6,7},{7,6},{8,9},{9,8},{10,11... | collective-permute-start | bytes 15925256 | tf_op jit(solution)/shard_map/ppermute | solution.py:425
  14.9 56.6 %collective-permute-start.5 = (bf16[2304,1152]{1,0:T(8,128)(2,1)}, bf16[2304,1152]{1,0:T(8,128)(2,1)}, u32[]{:S(2)}, u32[]{:S(2)}) collective-permute-start(bf16[2304,1152]{1,0:T(8,128)(2,1)} %w_down0.1), channel_id=1, source_target_pairs={{0,1},{1,0},{2,3},{3,2},{4,5},{5,4},{6,7},{7,6},{8,9},{9,8},{10,11... | collective-permute-start | bytes 15925256 | tf_op jit(solution)/shard_map/ppermute | solution.py:425
  18.1 53.4 %collective-permute-start.6 = (bf16[1,2304]{1,0:T(2,128)(2,1)S(1)}, bf16[1,2304]{1,0:T(2,128)(2,1)S(1)}, u32[]{:S(2)}, u32[]{:S(2)}) collective-permute-start(bf16[1,2304]{1,0:T(2,128)(2,1)S(1)} %broadcast_in_dim.52), channel_id=1, source_target_pairs={{0,1},{1,0},{2,3},{3,2},{4,5},{5,4},{6,7},{7,6},{8,9},{9,8},{10,11... | collective-permute-start | bytes 13832 | tf_op jit(solution)/shard_map/ppermute | solution.py:425
  98.5 29.7 %collective-permute-start.7 = (bf16[16,96,1152]{2,1,0:T(8,128)(2,1)}, bf16[16,96,1152]{2,1,0:T(8,128)(2,1)}, u32[]{:S(2)}, u32[]{:S(2)}) collective-permute-start(bf16[16,96,1152]{2,1,0:T(8,128)(2,1)} %get-tuple-element.302), channel_id=1, source_target_pairs={{0,1},{1,0},{2,3},{3,2},{4,5},{5,4},{6,7},{7,6},{8,9},{9,8},{10,11... | collective-permute-start | bytes 10616840 | tf_op jit(solution)/shard_map/ppermute | solution.py:425
  98.7 29.5 %collective-permute-start.8 = (bf16[16,96,1152]{2,1,0:T(8,128)(2,1)}, bf16[16,96,1152]{2,1,0:T(8,128)(2,1)}, u32[]{:S(2)}, u32[]{:S(2)}) collective-permute-start(bf16[16,96,1152]{2,1,0:T(8,128)(2,1)} %get-tuple-element.303), channel_id=1, source_target_pairs={{0,1},{1,0},{2,3},{3,2},{4,5},{5,4},{6,7},{7,6},{8,9},{9,8},{10,11... | collective-permute-start | bytes 10616840 | tf_op jit(solution)/shard_map/ppermute | solution.py:425
  128.2 27.8 %collective-permute-start.9 = (bf16[16,96,640]{2,1,0:T(8,128)(2,1)}, bf16[16,96,640]{2,1,0:T(8,128)(2,1)S(1)}, u32[]{:S(2)}, u32[]{:S(2)}) collective-permute-start(bf16[16,96,640]{2,1,0:T(8,128)(2,1)} %get-tuple-element.315), channel_id=1, source_target_pairs={{0,1},{1,0},{2,3},{3,2},{4,5},{5,4},{6,7},{7,6},{8,9},{9,8},{10,11... | collective-permute-start | bytes 5898248 | tf_op jit(solution)/shard_map/ppermute | solution.py:425
  128.4 27.5 %collective-permute-start.10 = (bf16[16,96,512]{2,1,0:T(8,128)(2,1)}, bf16[16,96,512]{2,1,0:T(8,128)(2,1)}, u32[]{:S(2)}, u32[]{:S(2)}) collective-permute-start(bf16[16,96,512]{2,1,0:T(8,128)(2,1)} %get-tuple-element.316), channel_id=1, source_target_pairs={{0,1},{1,0},{2,3},{3,2},{4,5},{5,4},{6,7},{7,6},{8,9},{9,8},{10,11... | collective-permute-start | bytes 4718600 | tf_op jit(solution)/shard_map/ppermute | solution.py:425
  161.2 34.6 %collective-permute-start.11 = (bf16[2,2,2,96,640]{4,3,0,1,2:T(8,128)(2,1)S(1)}, bf16[2,2,2,96,640]{4,3,0,1,2:T(8,128)(2,1)S(1)}, u32[]{:S(2)}, u32[]{:S(2)}) collective-permute-start(bf16[2,2,2,96,640]{4,3,0,1,2:T(8,128)(2,1)S(1)} %get-tuple-element.330), channel_id=1, source_target_pairs={{0,2},{2,0},{4,6},{6,4},{8,10},{10,8},{12,14},{14,12},{16,18},{18,... | collective-permute-start | bytes 2949128 | tf_op jit(solution)/shard_map/ppermute | solution.py:449
  163.9 28.9 %collective-permute-start.12 = (bf16[2,2,2,96,512]{4,3,0,1,2:T(8,128)(2,1)}, bf16[2,2,2,96,512]{4,3,0,1,2:T(8,128)(2,1)}, u32[]{:S(2)}, u32[]{:S(2)}) collective-permute-start(bf16[2,2,2,96,512]{4,3,0,1,2:T(8,128)(2,1)} %get-tuple-element.331), channel_id=1, source_target_pairs={{0,4},{2,6},{4,0},{6,2},{8,12},{10,14},{12,8},{14,10},{16,20},{18,... | collective-permute-start | bytes 2359304 | tf_op jit(solution)/shard_map/ppermute | solution.py:449
  297.3 43.3 %collective-permute-start.21 = (bf16[2,2,2,144,512]{4,3,0,1,2:T(8,128)(2,1)}, bf16[2,2,2,144,512]{4,3,0,1,2:T(8,128)(2,1)}, u32[]{:S(2)}, u32[]{:S(2)}) collective-permute-start(bf16[2,2,2,144,512]{4,3,0,1,2:T(8,128)(2,1)} %fusion.1), channel_id=1, source_target_pairs={{0,2},{2,0},{4,6},{6,4},{8,10},{10,8},{12,14},{14,12},{16,18},{18,... | collective-permute-start | bytes 3538952 | tf_op jit(solution)/shard_map/ppermute | solution.py:449
  298.7 41.9 %collective-permute-start.22 = (bf16[2,2,2,144,384]{4,3,0,1,2:T(8,128)(2,1)}, bf16[2,2,2,144,384]{4,3,0,1,2:T(8,128)(2,1)S(1)}, u32[]{:S(2)}, u32[]{:S(2)}) collective-permute-start(bf16[2,2,2,144,384]{4,3,0,1,2:T(8,128)(2,1)} %fusion.5), channel_id=1, source_target_pairs={{0,4},{2,6},{4,0},{6,2},{8,12},{10,14},{12,8},{14,10},{16,20},{18,... | collective-permute-start | bytes 2654216 | tf_op jit(solution)/shard_map/ppermute | solution.py:449
  299.9 40.7 %collective-permute-start.23 = (bf16[2,2,2,144,256]{4,3,1,2,0:T(8,128)(2,1)}, bf16[2,2,2,144,256]{4,3,1,2,0:T(8,128)(2,1)}, u32[]{:S(2)}, u32[]{:S(2)}) collective-permute-start(bf16[2,2,2,144,256]{4,3,1,2,0:T(8,128)(2,1)} %fusion.12), channel_id=1, source_target_pairs={{0,8},{2,10},{4,12},{6,14},{8,0},{10,2},{12,4},{14,6},{16,24},{18,... | collective-permute-start | bytes 1769480 | tf_op jit(solution)/shard_map/ppermute | solution.py:449
  299.9 40.7 %collective-permute-start.24 = (bf16[2,96,1152]{2,1,0:T(8,128)(2,1)S(1)}, bf16[2,96,1152]{2,1,0:T(8,128)(2,1)}, u32[]{:S(2)}, u32[]{:S(2)}) collective-permute-start(bf16[2,96,1152]{2,1,0:T(8,128)(2,1)S(1)} %pad_maximum_fusion.12), channel_id=1, source_target_pairs={{0,8},{2,10},{4,12},{6,14},{8,0},{10,2},{12,4},{14,6},{16,24},{18,... | collective-permute-start | bytes 1327112 | tf_op jit(solution)/shard_map/ppermute | solution.py:449
  347.6 33.3 %collective-permute-start.25 = (bf16[2,2,144,512]{3,2,0,1:T(8,128)(2,1)}, bf16[2,2,144,512]{3,2,0,1:T(8,128)(2,1)S(1)}, u32[]{:S(2)}, u32[]{:S(2)}) collective-permute-start(bf16[2,2,144,512]{3,2,0,1:T(8,128)(2,1)} %get-tuple-element.418), channel_id=1, source_target_pairs={{0,4},{2,6},{4,0},{6,2},{8,12},{10,14},{12,8},{14,10},{16,20},{18,... | collective-permute-start | bytes 1769480 | tf_op jit(solution)/shard_map/ppermute | solution.py:449
  348.3 32.6 %collective-permute-start.28 = (bf16[4,96,640]{2,1,0:T(8,128)(2,1)S(1)}, bf16[4,96,640]{2,1,0:T(8,128)(2,1)S(1)}, u32[]{:S(2)}, u32[]{:S(2)}) collective-permute-start(bf16[4,96,640]{2,1,0:T(8,128)(2,1)S(1)} %slice.406), channel_id=1, source_target_pairs={{0,4},{2,6},{4,0},{6,2},{8,12},{10,14},{12,8},{14,10},{16,20},{18,... | collective-permute-start | bytes 1474568 | tf_op jit(solution)/shard_map/ppermute | solution.py:449
  349.7 31.3 %collective-permute-start.26 = (bf16[2,2,144,384]{3,2,0,1:T(8,128)(2,1)}, bf16[2,2,144,384]{3,2,0,1:T(8,128)(2,1)}, u32[]{:S(2)}, u32[]{:S(2)}) collective-permute-start(bf16[2,2,144,384]{3,2,0,1:T(8,128)(2,1)} %get-tuple-element.419), channel_id=1, source_target_pairs={{0,2},{2,0},{4,6},{6,4},{8,10},{10,8},{12,14},{14,12},{16,18},{18,... | collective-permute-start | bytes 1327112 | tf_op jit(solution)/shard_map/ppermute | solution.py:449
  350.7 30.2 %collective-permute-start.29 = (bf16[4,96,512]{2,1,0:T(8,128)(2,1)S(1)}, bf16[4,96,512]{2,1,0:T(8,128)(2,1)}, u32[]{:S(2)}, u32[]{:S(2)}) collective-permute-start(bf16[4,96,512]{2,1,0:T(8,128)(2,1)S(1)} %slice.407), channel_id=1, source_target_pairs={{0,2},{2,0},{4,6},{6,4},{8,10},{10,8},{12,14},{14,12},{16,18},{18,... | collective-permute-start | bytes 1179656 | tf_op jit(solution)/shard_map/ppermute | solution.py:449
  351.7 29.2 %collective-permute-start.27 = (bf16[2,2,144,256]{3,2,0,1:T(8,128)(2,1)}, bf16[2,2,144,256]{3,2,0,1:T(8,128)(2,1)S(1)}, u32[]{:S(2)}, u32[]{:S(2)}) collective-permute-start(bf16[2,2,144,256]{3,2,0,1:T(8,128)(2,1)} %get-tuple-element.420), channel_id=1, source_target_pairs={{0,16},{2,18},{4,20},{6,22},{8,24},{10,26},{12,28},{14,30},{16,0},... | collective-permute-start | bytes 884744 | tf_op jit(solution)/shard_map/ppermute | solution.py:449
  386.5 41.8 %collective-permute-start.31 = (bf16[2,144,896]{2,1,0:T(8,128)(2,1)S(1)}, bf16[2,144,896]{2,1,0:T(8,128)(2,1)S(1)}, u32[]{:S(2)}, u32[]{:S(2)}) collective-permute-start(bf16[2,144,896]{2,1,0:T(8,128)(2,1)S(1)} %pad_maximum_fusion.7), channel_id=1, source_target_pairs={{0,8},{2,10},{4,12},{6,14},{8,0},{10,2},{12,4},{14,6},{16,24},{18,... | collective-permute-start | bytes 1548296 | tf_op jit(solution)/shard_map/ppermute | solution.py:449
  387.4 59.4 %collective-permute-start.36 = (bf16[8,96,640]{2,1,0:T(8,128)(2,1)}, bf16[8,96,640]{2,1,0:T(8,128)(2,1)S(1)}, u32[]{:S(2)}, u32[]{:S(2)}) collective-permute-start(bf16[8,96,640]{2,1,0:T(8,128)(2,1)} %pad_maximum_fusion.2.refs_0_), channel_id=1, source_target_pairs={{0,2},{2,0},{4,6},{6,4},{8,10},{10,8},{12,14},{14,12},{16,18},{18,... | collective-permute-start | bytes 2949128 | tf_op jit(solution)/shard_map/ppermute | solution.py:449
  388.6 58.2 %collective-permute-start.37 = (bf16[8,96,512]{2,1,0:T(8,128)(2,1)}, bf16[8,96,512]{2,1,0:T(8,128)(2,1)}, u32[]{:S(2)}, u32[]{:S(2)}) collective-permute-start(bf16[8,96,512]{2,1,0:T(8,128)(2,1)} %pad_maximum_fusion.4.refs_2_), channel_id=1, source_target_pairs={{0,4},{2,6},{4,0},{6,2},{8,12},{10,14},{12,8},{14,10},{16,20},{18,... | collective-permute-start | bytes 2359304 | tf_op jit(solution)/shard_map/ppermute | solution.py:449
  462.0 45.9 %collective-permute-start.49 = (f32[4,256,1152]{2,1,0:T(8,128)}, f32[4,256,1152]{2,1,0:T(8,128)}, u32[]{:S(2)}, u32[]{:S(2)}) collective-permute-start(f32[4,256,1152]{2,1,0:T(8,128)} %get-tuple-element.525), channel_id=1, source_target_pairs={{0,1},{1,0},{2,3},{3,2},{4,5},{5,4},{6,7},{7,6},{8,9},{9,8},{10,11... | collective-permute-start | bytes 14155784 | tf_op jit(solution)/shard_map/ppermute | solution.py:425
  504.9 28.6 %collective-permute-start.51 = (bf16[8,144,512]{2,1,0:T(8,128)(2,1)}, bf16[8,144,512]{2,1,0:T(8,128)(2,1)}, u32[]{:S(2)}, u32[]{:S(2)}) collective-permute-start(bf16[8,144,512]{2,1,0:T(8,128)(2,1)} %pad_maximum_fusion.1.refs_0_), channel_id=1, source_target_pairs={{0,2},{2,0},{4,6},{6,4},{8,10},{10,8},{12,14},{14,12},{16,18},{18,... | collective-permute-start | bytes 3538952 | tf_op jit(solution)/shard_map/ppermute | solution.py:449
  (65 other events, 658.7 us)
Sparse Core Ops, SparseCore 0:
  156.0 275.8 all-reduce.3

commit v9 on v8

--- a/solution.py
+++ b/solution.py
@@ -8,6 +8,7 @@
 from jax.sharding import PartitionSpec as P
 
 HEAD_DIM = 72
+LOG2_E = 1.4426950408889634
 
 
 epsilon = 1e-06
@@ -43,6 +44,10 @@
 
 def column(row):
     return jnp.broadcast_to(row[...].astype(f32), (8, row.shape[1])).T[:, 0:1]
+
+
+def head_rows(values, one):
+    return values[one * HEAD_DIM : (one + 1) * HEAD_DIM].astype(bf16)
 
 
 def token_sum(values):
@@ -62,9 +67,8 @@
     cols = w_proj[0].shape[0]
     pairs = cols // (2 * HEAD_DIM)
     span = 2 * HEAD_DIM
-    factor = HEAD_DIM ** (-0.5)
+    scale = HEAD_DIM ** (-0.5) * LOG2_E
     rows = normed[0]
-    total = b_proj[...]
     for part in range(parts):
         base = part * 3 * cols
         shift = bias[part][...].astype(f32).T
@@ -75,25 +79,44 @@
                 value = value + shift[:, proj // 2 : proj // 2 + 1]
             qkv[0, base + lo : base + lo + cols, :] = value.astype(bf16)
 
-        def pair_step(pair, carry, base=base, part=part):
-            at = pl.multiple_of(base + pair * span, 16)
-            query = qkv[0, pl.ds(at, span), :].astype(f32)
-            key = qkv[0, pl.ds(at + cols, span), :].astype(f32)
-            value = qkv[0, pl.ds(at + 2 * cols, span), :].astype(f32)
-            outs = []
-            for one in range(2):
-                rows_of = slice(one * HEAD_DIM, (one + 1) * HEAD_DIM)
-                scores = dot_tn(key[rows_of].astype(bf16), query[rows_of].astype(bf16)) * factor
-                raised = jnp.exp(scores - jnp.max(scores, axis=0, keepdims=True))
-                share = 1.0 / jnp.sum(raised, axis=0, keepdims=True)
-                prob_b = (raised * share).astype(bf16)
-                prob[0, part * 2 * pairs + 2 * pair + one] = prob_b
-                outs.append(dot_nn(value[rows_of].astype(bf16), prob_b))
-            to = pl.multiple_of(part * cols + pair * span, 16)
-            mixed[0, pl.ds(to, span), :] = jnp.concatenate(outs, axis=0).astype(bf16)
-            return carry
-
-        lax.fori_loop(0, pairs, pair_step, 0, unroll=True)
+    def load(part, pair):
+        at = part * 3 * cols + pair * span
+        return [qkv[0, at + k * cols : at + k * cols + span, :].astype(f32) for k in range(3)]
+
+    def score(loaded):
+        query, key, _ = loaded
+        return [dot_tn(head_rows(key, one), head_rows(query, one)) for one in range(2)]
+
+    def spread(scores, head):
+        raised = jnp.exp2((scores - jnp.max(scores, axis=0, keepdims=True)) * scale)
+        share = 1.0 / jnp.sum(raised, axis=0, keepdims=True)
+        prob_b = (raised * share).astype(bf16)
+        prob[0, head] = prob_b
+        return prob_b
+
+    def mix(part, pair, loaded, probs):
+        outs = [dot_nn(head_rows(loaded[2], one), probs[one]) for one in range(2)]
+        to = part * cols + pair * span
+        mixed[0, to : to + span, :] = jnp.concatenate(outs, axis=0).astype(bf16)
+
+    work = [(part, pair) for part in range(parts) for pair in range(pairs)]
+    loaded = load(*work[0])
+    scores = score(loaded)
+    waiting = None
+    for turn, (part, pair) in enumerate(work):
+        after = turn + 1 < len(work)
+        if after:
+            next_loaded = load(*work[turn + 1])
+            next_scores = score(next_loaded)
+        probs = [spread(scores[one], part * 2 * pairs + 2 * pair + one) for one in range(2)]
+        if waiting is not None:
+            mix(*waiting)
+        waiting = (part, pair, loaded, probs)
+        if after:
+            loaded, scores = next_loaded, next_scores
+    mix(*waiting)
+    total = b_proj[...]
+    for part in range(parts):
         total = total + dot_tn(mixed[0, part * cols : (part + 1) * cols, :], w_proj[part][...])
     attn_out[0] = total
     summed = tok[0].astype(f32) + mod[0, 2:3, :] * total
@@ -208,33 +231,43 @@
     factor = HEAD_DIM ** (-0.5)
     grad_att = grad_attn[0]
     for part in range(parts):
-        base = part * 3 * cols
-        grad_mixed[part * cols : (part + 1) * cols, :] = dot_nt(w_proj[part][...], grad_att).astype(bf16)
-
-        def pair_step(pair, carry, base=base, part=part):
-            at = pl.multiple_of(base + pair * span, 16)
-            query = qkv[0, pl.ds(at, span), :].astype(f32)
-            key = qkv[0, pl.ds(at + cols, span), :].astype(f32)
-            value = qkv[0, pl.ds(at + 2 * cols, span), :].astype(f32)
-            grads = grad_mixed[pl.ds(pl.multiple_of(part * cols + pair * span, 16), span), :].astype(f32)
-            to_query, to_key, to_value = [], [], []
-            for one in range(2):
-                rows_of = slice(one * HEAD_DIM, (one + 1) * HEAD_DIM)
-                prob_b = prob[0, part * 2 * pairs + 2 * pair + one]
-                prob_f = prob_b.astype(f32)
-                grad_b = grads[rows_of].astype(bf16)
-                grad_prob = dot_tn(value[rows_of].astype(bf16), grad_b)
-                delta = jnp.sum(prob_f * grad_prob, axis=0, keepdims=True)
-                grad_scores = (prob_f * (grad_prob - delta)).astype(bf16)
-                to_query.append(dot_nn(key[rows_of].astype(bf16), grad_scores) * factor)
-                to_key.append(dot_nt(query[rows_of].astype(bf16), grad_scores) * factor)
-                to_value.append(dot_nt(grad_b, prob_b))
-            grad_qkv[0, pl.ds(at, span), :] = jnp.concatenate(to_query, axis=0).astype(bf16)
-            grad_qkv[0, pl.ds(at + cols, span), :] = jnp.concatenate(to_key, axis=0).astype(bf16)
-            grad_qkv[0, pl.ds(at + 2 * cols, span), :] = jnp.concatenate(to_value, axis=0).astype(bf16)
-            return carry
-
-        lax.fori_loop(0, pairs, pair_step, 0, unroll=True)
+        rows = slice(part * cols, (part + 1) * cols)
+        grad_mixed[rows, :] = dot_nt(w_proj[part][...], grad_att).astype(bf16)
+
+    def load(part, pair):
+        at = part * 3 * cols + pair * span
+        mix_at = part * cols + pair * span
+        loaded = [qkv[0, at + k * cols : at + k * cols + span, :].astype(f32) for k in range(3)]
+        return loaded + [grad_mixed[mix_at : mix_at + span, :].astype(f32)]
+
+    def back_prob(loaded):
+        return [dot_tn(head_rows(loaded[2], one), head_rows(loaded[3], one)) for one in range(2)]
+
+    def back_scores(grad_prob, head):
+        prob_b = prob[0, head]
+        prob_f = prob_b.astype(f32)
+        delta = jnp.sum(prob_f * grad_prob, axis=0, keepdims=True)
+        return prob_b, (prob_f * (grad_prob - delta)).astype(bf16)
+
+    work = [(part, pair) for part in range(parts) for pair in range(pairs)]
+    loaded = load(*work[0])
+    grad_probs = back_prob(loaded)
+    for turn, (part, pair) in enumerate(work):
+        after = turn + 1 < len(work)
+        if after:
+            next_loaded = load(*work[turn + 1])
+            next_probs = back_prob(next_loaded)
+        middle = [back_scores(grad_probs[one], part * 2 * pairs + 2 * pair + one) for one in range(2)]
+        query, key, _, grads = loaded
+        to_query = [dot_nn(head_rows(key, one), middle[one][1]) * factor for one in range(2)]
+        to_key = [dot_nt(head_rows(query, one), middle[one][1]) * factor for one in range(2)]
+        to_value = [dot_nt(head_rows(grads, one), middle[one][0]) for one in range(2)]
+        at = part * 3 * cols + pair * span
+        for k, outs in enumerate((to_query, to_key, to_value)):
+            into = slice(at + k * cols, at + k * cols + span)
+            grad_qkv[0, into, :] = jnp.concatenate(outs, axis=0).astype(bf16)
+        if after:
+            loaded, grad_probs = next_loaded, next_probs
 
 
 def attn_grad_kernel(pieces, per, cuts, sc, *refs):
@@ -621,7 +654,7 @@
             shape_of((images, 1, dim), f32),
         ],
         (images,),
-        45,
+        33,
     )
     order.after(down_sums)
 

time: 563 us -> 547 us (0.972)
  Pallas kernels: 301 us -> 270 us
  waiting for transfers between devices: 113 us -> 130 us
    pallas_call x15, Pallas kernels: 301 us -> 270 us  [run_kernel(): pl.pallas_call(body, out_shape=out_shape, grid_spec=pltpu.PrefetchScalarG...]
    ppermute x4, waiting for transfers between devices: 17.5 us -> 39.1 us  [rows_flow(): came = lax.ppermute(rows, 'dp', bit_pairs(bit))]
    ppermute x32, waiting for transfers between devices: 91.5 us -> 83.2 us  [exchange(): lax.ppermute(value, 'dp', bit_pairs(bit))]
  transfers between devices with their start and end apart: 55 -> 55, of which waited for: 19 -> 23; matrix products, arithmetic and copies ran while one was open for 12% -> 12% of each run, Pallas kernels for 48% -> 44%
where the time goes in v9:
time: 547 us; the launch traced here: 540 us
  Pallas kernels  270 us (49%)
  waiting for transfers between devices  130 us (24%)
  starting transfers between devices  44.8 us (8%)
  other arithmetic  32.7 us (6%)
  local copies, waits for them, and re-layouts  28.3 us (5%)
  matrix products  18.3 us (3%)
  between operations  16 us (3%)
    pallas_call x15, Pallas kernels, run_kernel(): pl.pallas_call(body, out_shape=out_shape, grid_spec=pltpu.PrefetchScalarG...  270 us
    ppermute x32, waiting for transfers between devices, exchange(): lax.ppermute(value, 'dp', bit_pairs(bit))  83.2 us
    ppermute x4, waiting for transfers between devices, rows_flow(): came = lax.ppermute(rows, 'dp', bit_pairs(bit))  39.1 us
    ppermute x32, starting transfers between devices, exchange(): lax.ppermute(value, 'dp', bit_pairs(bit))  36.8 us
    add x21, other arithmetic, reduce_flow(): cut(one, bits, route[stage], side) + cut(two, bits, route[stage], side)  12.6 us
    concatenate x9, other arithmetic, gather_flow(): joined = [jnp.concatenate([one, two]) for one, two in zip(have, comes)]  12 us
  transfers between devices with their start and end apart: 55, of which 23 were waited for; matrix products, arithmetic and copies ran while one was open for 12% of the time, Pallas kernels for 44%

profile of v9, /device:TPU:0, one launch (start us, length us, event | category | flops | bytes accessed | tf_op | source)
XLA Modules:
  0.0 540.0 jit_solution(7696535255878904349)
XLA Ops:
  18.7 6.0 %collective-permute-done.3.refs_5_ = bf16[2,576]{1,0:T(2,128)(2,1)S(1)} collective-permute-done((bf16[2,576]{1,0:T(2,128)(2,1)S(1)}, bf16[2,576]{1,0:T(2,128)(2,1)S(1)}, u32[]{:S(2)}, u32[]{:S(2)}) %collective-permute-start.3) | collective-permute-done | bytes 2336 | tf_op jit(solution)/shard_map/ppermute | solution.py:458
  26.3 32.8 %shard_map.237 = (bf16[4,3456,256]{2,1,0:T(8,128)(2,1)}, bf16[4,16,256,256]{3,2,1,0:T(8,128)(2,1)}, bf16[4,1152,256]{2,1,0:T(8,128)(2,1)}, f32[4,256,1152]{2,1,0...) custom-call(s32[3]{0:T(128)} %pad_add_fusion.sc, ...), custom_call_target="tpu_custom_call" | custom-call | flops 37950001152 | bytes 33000000 | tf_op jit(solution)/shard_map/pallas_call | solution.py:427
  59.7 26.4 %shard_map.238 = (bf16[2,2304,1024]{2,1,0:T(8,128)(2,1)}, bf16[2,2304,1024]{2,1,0:T(8,128)(2,1)}, bf16[16,96,1152]{2,1,0:T(8,128)(2,1)}, bf16[16,96,1152]{2,1,0:...) custom-call(s32[3]{0:T(128)} %pad_add_fusion.sc, bf16[1024,1152]{1,0:T(8,128)(2,1)} %bitcast.144, ...), custom_call_target="tpu_custom_call" | custom-call | flops 29899999232 | bytes 26000000 | tf_op jit(solution)/shard_map/pallas_call | solution.py:427
  88.6 27.6 %shard_map.239 = (bf16[2,2304,1024]{2,1,0:T(8,128)(2,1)}, bf16[2,2304,1024]{2,1,0:T(8,128)(2,1)}, bf16[16,96,640]{2,1,0:T(8,128)(2,1)}, bf16[16,96,512]{2,1,0:T(...) custom-call(s32[3]{0:T(128)} %pad_add_fusion.sc, ...), custom_call_target="tpu_custom_call", output_to_operand_aliasing={{0}: (9, {}), {1}: (10, {})} | custom-call | flops 29899999232 | bytes 26000000 | tf_op jit(solution)/shard_map/pallas_call | solution.py:427
  116.8 26.9 %shard_map.240 = (bf16[2,2304,1024]{2,1,0:T(8,128)(2,1)}, bf16[2,2304,1024]{2,1,0:T(8,128)(2,1)}, bf16[16,96,1152]{2,1,0:T(8,128)(2,1)}, bf16[16,96,1152]{2,1,0:...) custom-call(s32[3]{0:T(128)} %pad_add_fusion.sc, ...), custom_call_target="tpu_custom_call", output_to_operand_aliasing={{0}: (11, {}), {1}: (12, {})} | custom-call | flops 29899999232 | bytes 26000000 | tf_op jit(solution)/shard_map/pallas_call | solution.py:427
  153.4 27.4 %shard_map.241 = (f32[4,256,1152]{2,1,0:T(8,128)}, bf16[4,256,1152]{2,1,0:T(8,128)(2,1)}, f32[4,4,1152]{2,1,0:T(4,128)}) custom-call(s32[3]{0:T(128)} %pad_add_fusion.sc, bf16[2,2304,1024]{2,1,0:T(8,128)(2,1)} %get-tuple-element.323.back, bf16[1152,2304]{1,0:T(8,128)(2,1)} %w_up0.1, bf16[1152,2304]{1,0:T(8,128)(2,1)} %collective-permute-done.4.refs_0_.refs_3_.w_up1, ...), custom_call_target="tpu_custom_call" | custom-call | flops 69000003584 | bytes 41582592 | tf_op jit(solution)/shard_map/pallas_call | solution.py:427
  188.3 12.6 %shard_map.242.refs_0_ = bf16[2,3456,256]{2,1,0:T(8,128)(2,1)} custom-call(s32[3]{0:T(128)} %pad_add_fusion.sc, bf16[4,256,1152]{2,1,0:T(8,128)(2,1)} %get-tuple-element.338.grad_attn.refs_4_, bf16[4,3456,256]{2,1,0:T(8,128)(2,1)} %get-tuple-element.339.qkv, bf16[4,16,256,256]{3,2,1,0:T(8,128)(2,1)} %get-tuple-element.340.prob, bf16[576,1152]{1,0:T(8,128)(2,1)} %refs_0_.5, ...), custom_call_target="tpu_custom_call" | custom-call | flops 69000003584 | bytes 24018944 | tf_op jit(solution)/shard_map/pallas_call | solution.py:427
  205.7 12.9 %shard_map.243.refs_1_ = bf16[2,3456,256]{2,1,0:T(8,128)(2,1)} custom-call(s32[3]{0:T(128)} %pad_add_fusion.sc, bf16[4,256,1152]{2,1,0:T(8,128)(2,1)} %get-tuple-element.338.grad_attn.refs_4_, bf16[4,3456,256]{2,1,0:T(8,128)(2,1)} %get-tuple-element.339.qkv, bf16[4,16,256,256]{3,2,1,0:T(8,128)(2,1)} %get-tuple-element.340.prob, bf16[576,1152]{1,0:T(8,128)(2,1)} %refs_0_.5, ...), custom_call_target="tpu_custom_call" | custom-call | flops 69000003584 | bytes 24018944 | tf_op jit(solution)/shard_map/pallas_call | solution.py:427
  218.6 7.5 %collective-permute-done.15 = bf16[2,96,1152]{2,1,0:T(8,128)(2,1)S(1)} collective-permute-done((bf16[2,96,1152]{2,1,0:T(8,128)(2,1)S(1)}, bf16[2,96,1152]{2,1,0:T(8,128)(2,1)S(1)}, u32[]{:S(2)}, u32[]{:S(2)}) %collective-permute-start.15) | collective-permute-done | bytes 442400 | tf_op jit(solution)/shard_map/ppermute | solution.py:482
  228.4 14.5 %shard_map.244 = (bf16[16,144,512]{2,1,0:T(8,128)(2,1)}, bf16[16,144,384]{2,1,0:T(8,128)(2,1)}, bf16[16,144,256]{2,1,0:T(8,128)(2,1)}, f32[3,1,576]{2,1,0:T(1,128)}) custom-call(s32[3]{0:T(128)} %pad_add_fusion.sc, bf16[2,3456,256]{2,1,0:T(8,128)(2,1)} %shard_map.242.refs_0_, bf16[2,3456,256]{2,1,0:T(8,128)(2,1)} %shard_map.243.refs_1_, ...), custom_call_target="tpu_custom_call" | custom-call | flops 69000003584 | bytes 19471104 | tf_op jit(solution)/shard_map/pallas_call | solution.py:427
  248.3 14.0 %shard_map.245 = (bf16[16,144,512]{2,1,0:T(8,128)(2,1)}, bf16[16,144,384]{2,1,0:T(8,128)(2,1)}, bf16[16,144,256]{2,1,0:T(8,128)(2,1)}, f32[3,1,576]{2,1,0:T(1,128)}) custom-call(s32[3]{0:T(128)} %pad_add_fusion.sc, bf16[2,3456,256]{2,1,0:T(8,128)(2,1)} %shard_map.242.refs_0_, bf16[2,3456,256]{2,1,0:T(8,128)(2,1)} %shard_map.243.refs_1_, ...), custom_call_target="tpu_custom_call" | custom-call | flops 69000003584 | bytes 19471104 | tf_op jit(solution)/shard_map/pallas_call | solution.py:427
  278.0 24.5 %shard_map.246 = (f32[8,256,1152]{2,1,0:T(8,128)}, f32[4,256,1152]{2,1,0:T(8,128)}, f32[4,2,1152]{2,1,0:T(2,128)}) custom-call(s32[3]{0:T(128)} %pad_add_fusion.sc, bf16[2,3456,256]{2,1,0:T(8,128)(2,1)} %shard_map.242.refs_0_, bf16[2,3456,256]{2,1,0:T(8,128)(2,1)} %shard_map.243.refs_1_, bf16[1728,1152]{1,0:T(8,128)(2,1)} %bitcast.142, ...), custom_call_target="tpu_custom_call" | custom-call | flops 69000003584 | bytes 38891520 | tf_op jit(solution)/shard_map/pallas_call | solution.py:427
  302.6 5.7 %collective-permute-done.24 = bf16[2,96,1152]{2,1,0:T(8,128)(2,1)} collective-permute-done((bf16[2,96,1152]{2,1,0:T(8,128)(2,1)S(1)}, bf16[2,96,1152]{2,1,0:T(8,128)(2,1)}, u32[]{:S(2)}, u32[]{:S(2)}) %collective-permute-start.24) | collective-permute-done | bytes 442400 | tf_op jit(solution)/shard_map/ppermute | solution.py:482
  320.2 24.8 %shard_map.247 = (bf16[8,256,1152]{2,1,0:T(8,128)(2,1)}, bf16[4,256,1152]{2,1,0:T(8,128)(2,1)}, f32[4,1,1152]{2,1,0:T(1,128)}) custom-call(s32[3]{0:T(128)} %pad_add_fusion.sc, bf16[2,2304,1024]{2,1,0:T(8,128)(2,1)} %get-tuple-element.411.act, bf16[2304,1152]{1,0:T(8,128)(2,1)} %w_down0.1, bf16[2304,1152]{1,0:T(8,128)(2,1)} %collective-permute-done.5.refs_1_.refs_4_.w_down1, ...), custom_call_target="tpu_custom_call" | custom-call | flops 69000003584 | bytes 36813312 | tf_op jit(solution)/shard_map/pallas_call | solution.py:427
  356.3 7.0 %collective-permute-done.32 = bf16[2,144,256]{2,1,0:T(8,128)(2,1)S(1)} collective-permute-done((bf16[2,144,256]{2,1,0:T(8,128)(2,1)S(1)}, bf16[2,144,256]{2,1,0:T(8,128)(2,1)S(1)}, u32[]{:S(2)}, u32[]{:S(2)}) %collective-permute-start.32) | collective-permute-done | bytes 147488 | tf_op jit(solution)/shard_map/ppermute | solution.py:482
  363.3 28.0 %collective-permute-done.31 = bf16[2,144,896]{2,1,0:T(8,128)(2,1)S(1)} collective-permute-done((bf16[2,144,896]{2,1,0:T(8,128)(2,1)S(1)}, bf16[2,144,896]{2,1,0:T(8,128)(2,1)S(1)}, u32[]{:S(2)}, u32[]{:S(2)}) %collective-permute-start.31) | collective-permute-done | bytes 516128 | tf_op jit(solution)/shard_map/ppermute | solution.py:482
  394.4 5.6 %convolution_convert_fusion = bf16[8,1152]{1,0:T(8,128)(2,1)S(1)} fusion(bf16[8,3456]{1,0:T(8,128)(2,1)S(1)} %maximum_select_fusion, bf16[1152,3456]{1,0:T(8,128)(2,1)} %param.25), kind=kOutput, calls=%fused_computation.1 | convolution fusion | flops 63710208 | bytes 8036352 | tf_op jit(solution)/shard_map/dot_general | solution.py:1039
  400.0 32.3 %collective-permute-done.35 = bf16[13,3456]{1,0:T(8,128)(2,1)S(1)} collective-permute-done((bf16[13,3456]{1,0:T(8,128)(2,1)S(1)}, bf16[13,3456]{1,0:T(8,128)(2,1)S(1)}, u32[]{:S(2)}, u32[]{:S(2)}) %collective-permute-start.35) | collective-permute-done | bytes 89888 | tf_op jit(solution)/shard_map/ppermute | solution.py:546
  451.1 6.3 %shard_map.249 = (f32[2304,1152]{1,0:T(8,128)}, f32[1152,2304]{1,0:T(8,128)}, f32[8,128]{1,0:T(8,128)}) custom-call(s32[3]{0:T(128)} %pad_add_fusion.sc, bf16[8,96,640]{2,1,0:T(8,128)(2,1)} %pad_maximum_fusion.2.refs_0_, bf16[8,96,640]{2,1,0:T(8,128)(2,1)} %copy-done.30, bf16[8,96,512]{2,1,0:T(8,128)(2,1)} %pad_maximum_fusion.4.refs_2_, ...), custom_call_target="tpu_custom_call" | custom-call | flops 4600000000 | bytes 4000000 | tf_op jit(solution)/shard_map/pallas_call | solution.py:427
  469.0 5.4 %shard_map.250 = (f32[2304,1152]{1,0:T(8,128)}, f32[1152,2304]{1,0:T(8,128)}, f32[8,128]{1,0:T(8,128)}) custom-call(s32[3]{0:T(128)} %pad_add_fusion.sc, bf16[16,96,1152]{2,1,0:T(8,128)(2,1)} %get-tuple-element.548.summed, f32[2304,1152]{1,0:T(8,128)} %get-tuple-element.553.down_in, ...), custom_call_target="tpu_custom_call", output_to_operand_aliasing={{0}: (2, {}), {1}: (3, {})} | custom-call | flops 4600000000 | bytes 4000000 | tf_op jit(solution)/shard_map/pallas_call | solution.py:427
  475.9 5.5 %shard_map.251 = (f32[2304,1152]{1,0:T(8,128)}, f32[1152,2304]{1,0:T(8,128)}, f32[8,128]{1,0:T(8,128)}) custom-call(s32[3]{0:T(128)} %pad_add_fusion.sc, bf16[16,96,1152]{2,1,0:T(8,128)(2,1)} %get-tuple-element.547.summed, f32[2304,1152]{1,0:T(8,128)} %get-tuple-element.555.down_in, ...), custom_call_target="tpu_custom_call", output_to_operand_aliasing={{0}: (2, {}), {1}: (3, {})} | custom-call | flops 4600000000 | bytes 4000000 | tf_op jit(solution)/shard_map/pallas_call | solution.py:427
  498.8 8.1 %fusion.6 = f32[1152,3456]{1,0:T(8,128)} fusion(bf16[128,1152]{1,0:T(8,128)(2,1)S(1)} %reshape.151, bf16[16,13,3456]{2,1,0:T(8,128)(2,1)S(1)} %reshape.149), kind=kOutput, calls=%fused_computation.19 | convolution fusion | flops 1019215872 | bytes 17104896 | tf_op jit(solution)/shard_map/dot_general | solution.py:1033
  511.9 6.9 %collective-permute-done.51.refs_1_ = bf16[8,144,512]{2,1,0:T(8,128)(2,1)} collective-permute-done((bf16[8,144,512]{2,1,0:T(8,128)(2,1)}, bf16[8,144,512]{2,1,0:T(8,128)(2,1)}, u32[]{:S(2)}, u32[]{:S(2)}) %collective-permute-start.51) | collective-permute-done | bytes 1179680 | tf_op jit(solution)/shard_map/ppermute | solution.py:482
  524.3 8.5 %shard_map.248 = (f32[1728,1152]{1,0:T(8,128)}, f32[576,1152]{1,0:T(8,128)}) custom-call(s32[3]{0:T(128)} %pad_add_fusion.sc, bf16[8,144,512]{2,1,0:T(8,128)(2,1)} %pad_maximum_fusion.1.refs_0_, bf16[8,144,512]{2,1,0:T(8,128)(2,1)} %collective-permute-done.51.refs_1_, bf16[8,144,384]{2,1,0:T(8,128)(2,1)} %pad_maximum_fusion.3.refs_2_, ...), custom_call_target="tpu_custom_call" | custom-call | flops 10350000128 | bytes 9000000 | tf_op jit(solution)/shard_map/pallas_call | solution.py:427
  (284 shorter events, 146.7 us)
Async XLA Ops:
  7.2 450.2 %all-reduce.4.cloned.1.call-start = ((), (), s32[]{:S(2)}) async-start(), calls=%async_computation | async-start | bytes 14155776 | tf_op jit(solution)/shard_map/psum | solution.py:741
  14.6 44.5 %collective-permute-start.4 = (bf16[1152,2304]{1,0:T(8,128)(2,1)}, bf16[1152,2304]{1,0:T(8,128)(2,1)}, u32[]{:S(2)}, u32[]{:S(2)}) collective-permute-start(bf16[1152,2304]{1,0:T(8,128)(2,1)} %w_up0.1), channel_id=1, source_target_pairs={{0,1},{1,0},{2,3},{3,2},{4,5},{5,4},{6,7},{7,6},{8,9},{9,8},{10,11... | collective-permute-start | bytes 15925256 | tf_op jit(solution)/shard_map/ppermute | solution.py:458
  14.9 44.2 %collective-permute-start.5 = (bf16[2304,1152]{1,0:T(8,128)(2,1)}, bf16[2304,1152]{1,0:T(8,128)(2,1)}, u32[]{:S(2)}, u32[]{:S(2)}) collective-permute-start(bf16[2304,1152]{1,0:T(8,128)(2,1)} %w_down0.1), channel_id=1, source_target_pairs={{0,1},{1,0},{2,3},{3,2},{4,5},{5,4},{6,7},{7,6},{8,9},{9,8},{10,11... | collective-permute-start | bytes 15925256 | tf_op jit(solution)/shard_map/ppermute | solution.py:458
  18.2 40.8 %collective-permute-start.6 = (bf16[1,2304]{1,0:T(2,128)(2,1)S(1)}, bf16[1,2304]{1,0:T(2,128)(2,1)S(1)}, u32[]{:S(2)}, u32[]{:S(2)}) collective-permute-start(bf16[1,2304]{1,0:T(2,128)(2,1)S(1)} %broadcast_in_dim.52), channel_id=1, source_target_pairs={{0,1},{1,0},{2,3},{3,2},{4,5},{5,4},{6,7},{7,6},{8,9},{9,8},{10,11... | collective-permute-start | bytes 13832 | tf_op jit(solution)/shard_map/ppermute | solution.py:458
  86.1 30.0 %collective-permute-start.7 = (bf16[16,96,1152]{2,1,0:T(8,128)(2,1)}, bf16[16,96,1152]{2,1,0:T(8,128)(2,1)}, u32[]{:S(2)}, u32[]{:S(2)}) collective-permute-start(bf16[16,96,1152]{2,1,0:T(8,128)(2,1)} %get-tuple-element.302), channel_id=1, source_target_pairs={{0,1},{1,0},{2,3},{3,2},{4,5},{5,4},{6,7},{7,6},{8,9},{9,8},{10,11... | collective-permute-start | bytes 10616840 | tf_op jit(solution)/shard_map/ppermute | solution.py:458
  86.6 29.6 %collective-permute-start.8 = (bf16[16,96,1152]{2,1,0:T(8,128)(2,1)}, bf16[16,96,1152]{2,1,0:T(8,128)(2,1)}, u32[]{:S(2)}, u32[]{:S(2)}) collective-permute-start(bf16[16,96,1152]{2,1,0:T(8,128)(2,1)} %get-tuple-element.303), channel_id=1, source_target_pairs={{0,1},{1,0},{2,3},{3,2},{4,5},{5,4},{6,7},{7,6},{8,9},{9,8},{10,11... | collective-permute-start | bytes 10616840 | tf_op jit(solution)/shard_map/ppermute | solution.py:458
  116.2 27.5 %collective-permute-start.9 = (bf16[16,96,640]{2,1,0:T(8,128)(2,1)}, bf16[16,96,640]{2,1,0:T(8,128)(2,1)S(1)}, u32[]{:S(2)}, u32[]{:S(2)}) collective-permute-start(bf16[16,96,640]{2,1,0:T(8,128)(2,1)} %get-tuple-element.315), channel_id=1, source_target_pairs={{0,1},{1,0},{2,3},{3,2},{4,5},{5,4},{6,7},{7,6},{8,9},{9,8},{10,11... | collective-permute-start | bytes 5898248 | tf_op jit(solution)/shard_map/ppermute | solution.py:458
  116.6 27.1 %collective-permute-start.10 = (bf16[16,96,512]{2,1,0:T(8,128)(2,1)}, bf16[16,96,512]{2,1,0:T(8,128)(2,1)}, u32[]{:S(2)}, u32[]{:S(2)}) collective-permute-start(bf16[16,96,512]{2,1,0:T(8,128)(2,1)} %get-tuple-element.316), channel_id=1, source_target_pairs={{0,1},{1,0},{2,3},{3,2},{4,5},{5,4},{6,7},{7,6},{8,9},{9,8},{10,11... | collective-permute-start | bytes 4718600 | tf_op jit(solution)/shard_map/ppermute | solution.py:458
  149.0 34.5 %collective-permute-start.11 = (bf16[2,2,2,96,640]{4,3,0,1,2:T(8,128)(2,1)S(1)}, bf16[2,2,2,96,640]{4,3,0,1,2:T(8,128)(2,1)S(1)}, u32[]{:S(2)}, u32[]{:S(2)}) collective-permute-start(bf16[2,2,2,96,640]{4,3,0,1,2:T(8,128)(2,1)S(1)} %get-tuple-element.330), channel_id=1, source_target_pairs={{0,2},{2,0},{4,6},{6,4},{8,10},{10,8},{12,14},{14,12},{16,18},{18,... | collective-permute-start | bytes 2949128 | tf_op jit(solution)/shard_map/ppermute | solution.py:482
  151.9 28.9 %collective-permute-start.12 = (bf16[2,2,2,96,512]{4,3,0,1,2:T(8,128)(2,1)}, bf16[2,2,2,96,512]{4,3,0,1,2:T(8,128)(2,1)}, u32[]{:S(2)}, u32[]{:S(2)}) collective-permute-start(bf16[2,2,2,96,512]{4,3,0,1,2:T(8,128)(2,1)} %get-tuple-element.331), channel_id=1, source_target_pairs={{0,4},{2,6},{4,0},{6,2},{8,12},{10,14},{12,8},{14,10},{16,20},{18,... | collective-permute-start | bytes 2359304 | tf_op jit(solution)/shard_map/ppermute | solution.py:482
  272.7 35.6 %collective-permute-start.21 = (bf16[2,2,2,144,512]{4,3,0,1,2:T(8,128)(2,1)}, bf16[2,2,2,144,512]{4,3,0,1,2:T(8,128)(2,1)}, u32[]{:S(2)}, u32[]{:S(2)}) collective-permute-start(bf16[2,2,2,144,512]{4,3,0,1,2:T(8,128)(2,1)} %fusion.1), channel_id=1, source_target_pairs={{0,2},{2,0},{4,6},{6,4},{8,10},{10,8},{12,14},{14,12},{16,18},{18,... | collective-permute-start | bytes 3538952 | tf_op jit(solution)/shard_map/ppermute | solution.py:482
  273.8 34.5 %collective-permute-start.22 = (bf16[2,2,2,144,384]{4,3,0,1,2:T(8,128)(2,1)}, bf16[2,2,2,144,384]{4,3,0,1,2:T(8,128)(2,1)S(1)}, u32[]{:S(2)}, u32[]{:S(2)}) collective-permute-start(bf16[2,2,2,144,384]{4,3,0,1,2:T(8,128)(2,1)} %fusion.5), channel_id=1, source_target_pairs={{0,4},{2,6},{4,0},{6,2},{8,12},{10,14},{12,8},{14,10},{16,20},{18,... | collective-permute-start | bytes 2654216 | tf_op jit(solution)/shard_map/ppermute | solution.py:482
  274.5 33.7 %collective-permute-start.23 = (bf16[2,2,2,144,256]{4,3,1,2,0:T(8,128)(2,1)}, bf16[2,2,2,144,256]{4,3,1,2,0:T(8,128)(2,1)}, u32[]{:S(2)}, u32[]{:S(2)}) collective-permute-start(bf16[2,2,2,144,256]{4,3,1,2,0:T(8,128)(2,1)} %fusion.12), channel_id=1, source_target_pairs={{0,8},{2,10},{4,12},{6,14},{8,0},{10,2},{12,4},{14,6},{16,24},{18,... | collective-permute-start | bytes 1769480 | tf_op jit(solution)/shard_map/ppermute | solution.py:482
  278.0 30.3 %collective-permute-start.24 = (bf16[2,96,1152]{2,1,0:T(8,128)(2,1)S(1)}, bf16[2,96,1152]{2,1,0:T(8,128)(2,1)}, u32[]{:S(2)}, u32[]{:S(2)}) collective-permute-start(bf16[2,96,1152]{2,1,0:T(8,128)(2,1)S(1)} %pad_maximum_fusion.12), channel_id=1, source_target_pairs={{0,8},{2,10},{4,12},{6,14},{8,0},{10,2},{12,4},{14,6},{16,24},{18,... | collective-permute-start | bytes 1327112 | tf_op jit(solution)/shard_map/ppermute | solution.py:482
  315.4 30.8 %collective-permute-start.25 = (bf16[2,2,144,512]{3,2,0,1:T(8,128)(2,1)}, bf16[2,2,144,512]{3,2,0,1:T(8,128)(2,1)S(1)}, u32[]{:S(2)}, u32[]{:S(2)}) collective-permute-start(bf16[2,2,144,512]{3,2,0,1:T(8,128)(2,1)} %get-tuple-element.418), channel_id=1, source_target_pairs={{0,4},{2,6},{4,0},{6,2},{8,12},{10,14},{12,8},{14,10},{16,20},{18,... | collective-permute-start | bytes 1769480 | tf_op jit(solution)/shard_map/ppermute | solution.py:482
  317.2 29.0 %collective-permute-start.28 = (bf16[4,96,640]{2,1,0:T(8,128)(2,1)S(1)}, bf16[4,96,640]{2,1,0:T(8,128)(2,1)S(1)}, u32[]{:S(2)}, u32[]{:S(2)}) collective-permute-start(bf16[4,96,640]{2,1,0:T(8,128)(2,1)S(1)} %slice.406), channel_id=1, source_target_pairs={{0,4},{2,6},{4,0},{6,2},{8,12},{10,14},{12,8},{14,10},{16,20},{18,... | collective-permute-start | bytes 1474568 | tf_op jit(solution)/shard_map/ppermute | solution.py:482
  317.5 27.5 %collective-permute-start.26 = (bf16[2,2,144,384]{3,2,0,1:T(8,128)(2,1)}, bf16[2,2,144,384]{3,2,0,1:T(8,128)(2,1)}, u32[]{:S(2)}, u32[]{:S(2)}) collective-permute-start(bf16[2,2,144,384]{3,2,0,1:T(8,128)(2,1)} %get-tuple-element.419), channel_id=1, source_target_pairs={{0,2},{2,0},{4,6},{6,4},{8,10},{10,8},{12,14},{14,12},{16,18},{18,... | collective-permute-start | bytes 1327112 | tf_op jit(solution)/shard_map/ppermute | solution.py:482
  351.9 39.4 %collective-permute-start.31 = (bf16[2,144,896]{2,1,0:T(8,128)(2,1)S(1)}, bf16[2,144,896]{2,1,0:T(8,128)(2,1)S(1)}, u32[]{:S(2)}, u32[]{:S(2)}) collective-permute-start(bf16[2,144,896]{2,1,0:T(8,128)(2,1)S(1)} %pad_maximum_fusion.7), channel_id=1, source_target_pairs={{0,8},{2,10},{4,12},{6,14},{8,0},{10,2},{12,4},{14,6},{16,24},{18,... | collective-permute-start | bytes 1548296 | tf_op jit(solution)/shard_map/ppermute | solution.py:482
  354.9 77.4 %collective-permute-start.36 = (bf16[8,96,640]{2,1,0:T(8,128)(2,1)}, bf16[8,96,640]{2,1,0:T(8,128)(2,1)S(1)}, u32[]{:S(2)}, u32[]{:S(2)}) collective-permute-start(bf16[8,96,640]{2,1,0:T(8,128)(2,1)} %pad_maximum_fusion.2.refs_0_), channel_id=1, source_target_pairs={{0,2},{2,0},{4,6},{6,4},{8,10},{10,8},{12,14},{14,12},{16,18},{18,... | collective-permute-start | bytes 2949128 | tf_op jit(solution)/shard_map/ppermute | solution.py:482
  355.5 76.8 %collective-permute-start.37 = (bf16[8,96,512]{2,1,0:T(8,128)(2,1)}, bf16[8,96,512]{2,1,0:T(8,128)(2,1)}, u32[]{:S(2)}, u32[]{:S(2)}) collective-permute-start(bf16[8,96,512]{2,1,0:T(8,128)(2,1)} %pad_maximum_fusion.4.refs_2_), channel_id=1, source_target_pairs={{0,4},{2,6},{4,0},{6,2},{8,12},{10,14},{12,8},{14,10},{16,20},{18,... | collective-permute-start | bytes 2359304 | tf_op jit(solution)/shard_map/ppermute | solution.py:482
  391.4 40.9 %collective-permute-start.33 = (bf16[144,896]{1,0:T(8,128)(2,1)S(1)}, bf16[144,896]{1,0:T(8,128)(2,1)S(1)}, u32[]{:S(2)}, u32[]{:S(2)}) collective-permute-start(bf16[144,896]{1,0:T(8,128)(2,1)S(1)} %get-tuple-element.467), channel_id=1, source_target_pairs={{0,16},{2,18},{4,20},{6,22},{8,24},{10,26},{12,28},{14,30},{16,0},... | collective-permute-start | bytes 774152 | tf_op jit(solution)/shard_map/ppermute | solution.py:482
  394.1 38.2 %collective-permute-start.35 = (bf16[13,3456]{1,0:T(8,128)(2,1)S(1)}, bf16[13,3456]{1,0:T(8,128)(2,1)S(1)}, u32[]{:S(2)}, u32[]{:S(2)}) collective-permute-start(bf16[13,3456]{1,0:T(8,128)(2,1)S(1)} %pad_maximum_fusion.18), channel_id=1, source_target_pairs={{0,16},{2,18},{4,20},{6,22},{8,24},{10,26},{12,28},{14,30},{16,0},... | collective-permute-start | bytes 269576 | tf_op jit(solution)/shard_map/ppermute | solution.py:546
  446.9 46.9 %collective-permute-start.49 = (f32[4,256,1152]{2,1,0:T(8,128)}, f32[4,256,1152]{2,1,0:T(8,128)}, u32[]{:S(2)}, u32[]{:S(2)}) collective-permute-start(f32[4,256,1152]{2,1,0:T(8,128)} %get-tuple-element.525), channel_id=1, source_target_pairs={{0,1},{1,0},{2,3},{3,2},{4,5},{5,4},{6,7},{7,6},{8,9},{9,8},{10,11... | collective-permute-start | bytes 14155784 | tf_op jit(solution)/shard_map/ppermute | solution.py:458
  489.8 29.0 %collective-permute-start.51 = (bf16[8,144,512]{2,1,0:T(8,128)(2,1)}, bf16[8,144,512]{2,1,0:T(8,128)(2,1)}, u32[]{:S(2)}, u32[]{:S(2)}) collective-permute-start(bf16[8,144,512]{2,1,0:T(8,128)(2,1)} %pad_maximum_fusion.1.refs_0_), channel_id=1, source_target_pairs={{0,2},{2,0},{4,6},{6,4},{8,10},{10,8},{12,14},{14,12},{16,18},{18,... | collective-permute-start | bytes 3538952 | tf_op jit(solution)/shard_map/ppermute | solution.py:482
  (65 other events, 692.8 us)
Sparse Core Ops, SparseCore 0:
  143.8 298.5 all-reduce.3

commit v10 on v9

--- a/solution.py
+++ b/solution.py
@@ -125,7 +125,7 @@
     normed_mlp[0] = (unit * (1.0 + mod[0, 4:5, :]) + mod[0, 3:4, :]).astype(bf16)
 
 
-def mlp_kernel(per, jobs, sc, rows, grad_mlp, *refs):
+def mlp_kernel(per, cuts, jobs, sc, rows, grad_mlp, *refs):
     count = len(jobs)
     weights = [refs[3 * k : 3 * k + 3] for k in range(count)]
     refs = refs[3 * count :]
@@ -136,8 +136,8 @@
     act, back = refs[2], refs[3]
     refs = refs[4:]
     grads = []
-    for cuts, _ in jobs:
-        size = 1 if cuts is None else len(cuts)
+    for kind, _ in jobs:
+        size = (kind != "cut") + (kind != "plain") * len(cuts)
         grads.append(refs[:size])
         refs = refs[size:]
     job, step = pl.program_id(0), pl.program_id(1)
@@ -146,11 +146,13 @@
         @pl.when(job == k)
         def _(k=k):
             mlp_block(
-                per, jobs[k][0], step, sc, rows, grad_mlp, *weights[k], act, back, grads[k], refs[k], came[k]
+                per, cuts, jobs[k][0], step, sc, rows, grad_mlp, *weights[k], act, back, grads[k], refs[k], came[k]
             )
 
 
-def mlp_block(per, cuts, step, sc, rows, grad_mlp, w_up, w_down, bias, act, back, grads, sums, came):
+def mlp_block(
+    per, cuts, kind, step, sc, rows, grad_mlp, w_up, w_down, bias, act, back, grads, sums, came
+):
     here = w_down.shape[0] // per
     hidden = lax.dot_general(
         w_up[...], rows[...], (((0,), (1,)), ((), ())), preferred_element_type=f32
@@ -166,17 +168,19 @@
     act[0] = act_b
     back[0] = back_b
     sums[...] = dot_nt(jnp.ones((8, rows.shape[0]), bf16), back_b)[0:1]
-    for lo_row, left, right in ((0, act_b, grad_mlp), (per, back_b, rows)):
+    for which, (left, right) in enumerate(((act_b, grad_mlp), (back_b, rows))):
         grad = dot_nn(left, right[...])
+        lo_row = 0 if kind == "mixed" else which * per
+        plain = kind == "plain" or (kind == "mixed" and which == 0)
         for piece in range(here):
             value = grad[piece * per : (piece + 1) * per]
-            if cuts is None:
+            if plain:
                 if came is not None:
                     value = value + came[piece, lo_row : lo_row + per, :].astype(f32)
                 grads[0][piece, lo_row : lo_row + per, :] = value.astype(bf16)
             else:
                 at = jnp.bitwise_xor(step * here + piece, sc[2])
-                for (lo, hi), into in zip(cuts, grads):
+                for (lo, hi), into in zip(cuts, grads[-len(cuts) :]):
                     into[at, lo_row : lo_row + per, :] = value[:, lo:hi].astype(bf16)
 
 
@@ -401,6 +405,23 @@
     mark[...] = jnp.zeros_like(mark)
 
 
+def final_mixed_kernel(cuts, per, sc, *refs):
+    count = 2 * len(cuts)
+    arrays, (summed, _, _, down, up, mark, turned) = refs[:count], refs[count:]
+    here = down.shape[0] // per
+    halves = [(arrays[2 * k], arrays[2 * k + 1]) + cut for k, cut in enumerate(cuts)]
+    for piece in range(here):
+        rows = slice(piece * per, (piece + 1) * per)
+        down[rows, :] = summed[piece].astype(f32)
+
+        def store(value, lo, hi, rows=rows):
+            turned[rows, lo:hi] = value[2 * per :]
+
+        final_piece(sc, halves, pl.program_id(0) * here + piece, store)
+    up[...] = turned[...].T
+    mark[...] = jnp.zeros_like(mark)
+
+
 def final_attn_kernel(cuts, per, sc, *refs):
     count = 2 * len(cuts)
     arrays, (qkv, proj) = refs[:count], refs[count:]
@@ -484,17 +505,19 @@
 
 def reduce_flow(ways, get_own, others):
     others = yield others
-    came = [swap_cores(other) for other in others]
+    came = jax.tree.map(swap_cores, others)
     yield None
     own, came = yield [get_own(), came]
-    firsts, seconds = ([a.reshape((2, 2, 2, 2) + a.shape[1:]) for a in arrays] for arrays in (own, came))
+    firsts, seconds = jax.tree.map(lambda a: a.reshape((2, 2, 2, 2) + a.shape[1:]), (own, came))
     routes = [way for _, _, way in ways]
     for stage in range(4):
         sends, keeps = [], []
         for route, one, two in zip(routes, firsts, seconds):
             bits = left_bits(route[:stage])
+            one, two = (value if isinstance(value, list) else [value] for value in (one, two))
             for side, into in ((1, sends), (0, keeps)):
-                into.append(cut(one, bits, route[stage], side) + cut(two, bits, route[stage], side))
+                sums = [cut(a, bits, route[stage], side) + cut(b, bits, route[stage], side) for a, b in zip(one, two)]
+                into.append(sums[0] if len(sums) == 1 else jnp.concatenate(sums, axis=-2))
         if stage == 2 and routes[0][2:] == routes[1][2:]:
             sends = [jnp.concatenate(sends[:2], axis=-1)] + sends[2:]
             keeps = [jnp.concatenate(keeps[:2], axis=-1)] + keeps[2:]
@@ -583,7 +606,6 @@
 
 
 CHUNKS = 3
-PLAIN = 2
 
 
 def fill_other(both, came, core):
@@ -671,7 +693,7 @@
     def mlp_call(jobs, came, micros):
         nonlocal act, back
         first = act.shape[0] == 8
-        kinds = tuple((None if job[0] < PLAIN else columns(MLP_WAYS), job in came) for job in jobs)
+        kinds = tuple((("plain", "mixed", "cut")[job[0]], job in came) for job in jobs)
 
         def turn(k):
             return lambda p, s, c: jnp.clip((p - k) * steps + s, 0, steps - 1)
@@ -694,22 +716,26 @@
                 pl.BlockSpec((1, block), wide),
             ]
         grad_specs, grad_shapes, sizes = [], [], []
-        for k, (split, _) in enumerate(kinds):
+        for k, (kind, _) in enumerate(kinds):
             own = lambda p, s, c, k=k: (turn(k)(p, s, c), 0, 0)
             fixed = lambda p, s, c: (0, 0, 0)
-            wides = [dim] if split is None else [hi - lo for lo, hi in split]
-            lead = (16 // steps, own) if split is None else (16, fixed)
-            grad_specs.append([pl.BlockSpec((lead[0], 2 * per, wide), lead[1]) for wide in wides])
-            grad_shapes += [shape_of((16, 2 * per, wide), bf16) for wide in wides]
-            sizes.append(len(wides))
+            tall = per if kind == "mixed" else 2 * per
+            plain = [] if kind == "cut" else [dim]
+            split = [] if kind == "plain" else [hi - lo for lo, hi in columns(MLP_WAYS)]
+            grad_specs.append(
+                [pl.BlockSpec((16 // steps, tall, wide), own) for wide in plain]
+                + [pl.BlockSpec((16, tall, wide), fixed) for wide in split]
+            )
+            grad_shapes += [shape_of((16, tall, wide), bf16) for wide in plain + split]
+            sizes.append(len(plain + split))
         for k, job in enumerate(jobs):
             if job in came:
                 args.append(came[job])
-                specs += grad_specs[k]
+                specs.append(grad_specs[k][0])
         args += [act, back]
         spot = len(args) + 1
         outs = run_kernel(
-            functools.partial(mlp_kernel, per, kinds),
+            functools.partial(mlp_kernel, per, columns(MLP_WAYS), kinds),
             order.sc,
             [rows_flat, grad_flat] + args,
             [whole_block(rows_flat), whole_block(grad_flat)] + specs + [anywhere, anywhere],
@@ -727,19 +753,19 @@
         order.after(outs[-1])
         return [[grads.pop(0) for _ in range(size)] for size in sizes]
 
-    summed = range(PLAIN)
-    swaps = [swap_flow(grad) for (grad,) in mlp_call([(chunk, 1) for chunk in summed], {}, 26)]
+    (other_0,), (other_1, *rest_1) = mlp_call([(0, 1), (1, 1)], {}, 26)
+    swaps = [swap_flow(other_0), swap_flow(other_1)]
     order.tick(*swaps)
-    rest = [(chunk, part) for chunk in range(PLAIN, CHUNKS) for part in (1, 0)]
-    grads = mlp_call(rest, {}, 26)
-    flows = [
-        sum_flow(MLP_WAYS, lambda own=own: own, others) for others, own in zip(grads[0::2], grads[1::2])
-    ]
-    order.tick(*swaps, *flows)
-    came = {(chunk, 0): order.results[swap] for chunk, swap in zip(summed, swaps)}
-    grads = mlp_call([(chunk, 0) for chunk in summed], came, 26)
-    plain_sums = lax.psum([grad for (grad,) in grads], "dp")
-    order.tick(*flows)
+    others, own_2 = mlp_call([(2, 1), (2, 0)], {}, 26)
+    made_rest = []
+    flow = sum_flow(MLP_WAYS, lambda: made_rest, [list(pair) for pair in zip(others, rest_1)])
+    flows = [flow]
+    order.tick(*swaps, flow)
+    came = {(chunk, 0): order.results[swap] for chunk, swap in enumerate(swaps)}
+    (sum_0,), (sum_1, *own_1) = mlp_call([(0, 0), (1, 0)], came, 26)
+    made_rest += [list(pair) for pair in zip(own_2, own_1)]
+    plain_sums = lax.psum([sum_0, sum_1], "dp")
+    order.tick(flow)
 
     reach = 768
     turns = ff // reach
@@ -832,7 +858,7 @@
 
     grad_other = attn_part(1)
     made = []
-    last = sum_flow(ATTN_WAYS, lambda: made[0], grad_other)
+    last = sum_flow(ATTN_WAYS, lambda: [[a] for a in made[0]], [[a] for a in grad_other])
     order.tick(last, *flows)
     made.append(attn_part(0))
     order.tick(last, *flows)
@@ -952,14 +978,14 @@
         )
         order.after(mark)
 
-    for chunk, flow in enumerate(flows):
-        body = functools.partial(final_mlp_kernel, cuts(MLP_WAYS), per)
-        final_mlp(PLAIN + chunk, body, order.finish(flow))
+    final_mlp(2, functools.partial(final_mlp_kernel, cuts(MLP_WAYS), per), order.finish(flow))
     order.tick(last, small)
     other_output, came_scaled, grad_own_tokens = order.fence((other_output, came_scaled, grad_own_tokens))
     other_tokens = swap_cores(grad_own_tokens)
-    for chunk, total in zip(summed, order.fence(plain_sums)):
-        final_mlp(chunk, functools.partial(final_plain_kernel, per), [total])
+    sum_0, sum_1 = order.fence(plain_sums)
+    final_mlp(0, functools.partial(final_plain_kernel, per), [sum_0])
+    body = functools.partial(final_mixed_kernel, cuts(MLP_WAYS), per)
+    final_mlp(1, body, list(order.finish(flow)) + [sum_1])
     order.tick(last, small)
     output = fill_other(output, other_output, core)
     grad_scaled = part_scaled.astype(f32) + came_scaled.astype(f32)

time: 547 us -> 589 us (1.077)
  waiting for transfers between devices: 130 us -> 147 us
  local copies, waits for them, and re-layouts: 28.3 us -> 39.3 us
  other arithmetic: 32.7 us -> 41 us
    ppermute x32, waiting for transfers between devices: 83.2 us -> 129 us  [exchange(): lax.ppermute(value, 'dp', bit_pairs(bit))]
    ppermute x4, waiting for transfers between devices: 39.1 us -> 10 us  [rows_flow(): came = lax.ppermute(rows, 'dp', bit_pairs(bit))]
    add x21 -> x23, other arithmetic: 12.6 us -> 16.8 us  [reduce_flow(): cut(a, bits, route[stage], side) + cut(b, bits, route[stage], side)]
  transfers between devices with their start and end apart: 55 -> 57, of which waited for: 23 -> 25; matrix products, arithmetic and copies ran while one was open for 12% -> 14% of each run, Pallas kernels for 44% -> 41%
where the time goes in v10:
time: 589 us; the launch traced here: 581 us
  Pallas kernels  272 us (46%)
  waiting for transfers between devices  147 us (25%)
  starting transfers between devices  48.2 us (8%)
  other arithmetic  41 us (7%)
  local copies, waits for them, and re-layouts  39.3 us (7%)
  matrix products  18.1 us (3%)
  between operations  16.1 us (3%)
    pallas_call x15, Pallas kernels, run_kernel(): pl.pallas_call(body, out_shape=out_shape, grid_spec=pltpu.PrefetchScalarG...  272 us
    ppermute x32, waiting for transfers between devices, exchange(): lax.ppermute(value, 'dp', bit_pairs(bit))  129 us
    ppermute x32, starting transfers between devices, exchange(): lax.ppermute(value, 'dp', bit_pairs(bit))  39.6 us
    add x23, other arithmetic, reduce_flow(): cut(a, bits, route[stage], side) + cut(b, bits, route[stage], side)  16.8 us
    concatenate x9, other arithmetic, gather_flow(): joined = [jnp.concatenate([one, two]) for one, two in zip(have, comes)]  11.9 us
  transfers between devices with their start and end apart: 57, of which 25 were waited for; matrix products, arithmetic and copies ran while one was open for 14% of the time, Pallas kernels for 41%

profile of v10, /device:TPU:0, one launch (start us, length us, event | category | flops | bytes accessed | tf_op | source)
XLA Modules:
  0.0 581.4 jit_solution(2409664630878891079)
XLA Ops:
  26.3 32.8 %shard_map.237 = (bf16[4,3456,256]{2,1,0:T(8,128)(2,1)}, bf16[4,16,256,256]{3,2,1,0:T(8,128)(2,1)}, bf16[4,1152,256]{2,1,0:T(8,128)(2,1)}, f32[4,256,1152]{2,1,0...) custom-call(s32[3]{0:T(128)} %pad_add_fusion.sc, ...), custom_call_target="tpu_custom_call" | custom-call | flops 37950001152 | bytes 33000000 | tf_op jit(solution)/shard_map/pallas_call | solution.py:448
  59.7 26.7 %shard_map.238 = (bf16[2,2304,1024]{2,1,0:T(8,128)(2,1)}, bf16[2,2304,1024]{2,1,0:T(8,128)(2,1)}, bf16[16,96,1152]{2,1,0:T(8,128)(2,1)}, bf16[16,48,1152]{2,1,0:...) custom-call(s32[3]{0:T(128)} %pad_add_fusion.sc, ...), custom_call_target="tpu_custom_call" | custom-call | flops 29899999232 | bytes 26000000 | tf_op jit(solution)/shard_map/pallas_call | solution.py:448
  88.8 27.6 %shard_map.239 = (bf16[2,2304,1024]{2,1,0:T(8,128)(2,1)}, bf16[2,2304,1024]{2,1,0:T(8,128)(2,1)}, bf16[16,96,640]{2,1,0:T(8,128)(2,1)}, bf16[16,96,512]{2,1,0:T(...) custom-call(s32[3]{0:T(128)} %pad_add_fusion.sc, ...), custom_call_target="tpu_custom_call", output_to_operand_aliasing={{0}: (9, {}), {1}: (10, {})} | custom-call | flops 29899999232 | bytes 26000000 | tf_op jit(solution)/shard_map/pallas_call | solution.py:448
  118.7 27.5 %shard_map.240 = (bf16[2,2304,1024]{2,1,0:T(8,128)(2,1)}, bf16[2,2304,1024]{2,1,0:T(8,128)(2,1)}, bf16[16,96,1152]{2,1,0:T(8,128)(2,1)}, bf16[16,48,1152]{2,1,0:...) custom-call(s32[3]{0:T(128)} %pad_add_fusion.sc, ...), custom_call_target="tpu_custom_call", output_to_operand_aliasing={{0}: (11, {}), {1}: (12, {})} | custom-call | flops 29899999232 | bytes 26000000 | tf_op jit(solution)/shard_map/pallas_call | solution.py:448
  160.9 27.5 %shard_map.241 = (f32[4,256,1152]{2,1,0:T(8,128)}, bf16[4,256,1152]{2,1,0:T(8,128)(2,1)}, f32[4,4,1152]{2,1,0:T(4,128)}) custom-call(s32[3]{0:T(128)} %pad_add_fusion.sc, bf16[2,2304,1024]{2,1,0:T(8,128)(2,1)} %get-tuple-element.343.back, bf16[1152,2304]{1,0:T(8,128)(2,1)} %w_up0.1, bf16[1152,2304]{1,0:T(8,128)(2,1)} %collective-permute-done.4.refs_0_.refs_3_.w_up1, ...), custom_call_target="tpu_custom_call" | custom-call | flops 69000003584 | bytes 41582592 | tf_op jit(solution)/shard_map/pallas_call | solution.py:448
  188.3 8.1 %collective-permute-done.14 = bf16[2,2,2,144,512]{4,3,0,1,2:T(8,128)(2,1)} collective-permute-done((bf16[2,2,2,144,512]{4,3,0,1,2:T(8,128)(2,1)}, bf16[2,2,2,144,512]{4,3,0,1,2:T(8,128)(2,1)}, u32[]{:S(2)}, u32[]{:S(2)}) %collective-permute-start.14) | collective-permute-done | bytes 1179680 | tf_op jit(solution)/shard_map/ppermute | solution.py:503
  196.5 6.3 %collective-permute-done.13 = bf16[2,2,2,144,640]{4,3,0,1,2:T(8,128)(2,1)} collective-permute-done((bf16[2,2,2,144,640]{4,3,0,1,2:T(8,128)(2,1)S(1)}, bf16[2,2,2,144,640]{4,3,0,1,2:T(8,128)(2,1)}, u32[]{:S(2)}, u32[]{:S(2)}) %collective-permute-start.13) | collective-permute-done | bytes 1474592 | tf_op jit(solution)/shard_map/ppermute | solution.py:503
  208.2 12.3 %shard_map.242.refs_0_ = bf16[2,3456,256]{2,1,0:T(8,128)(2,1)} custom-call(s32[3]{0:T(128)} %pad_add_fusion.sc, bf16[4,256,1152]{2,1,0:T(8,128)(2,1)} %get-tuple-element.358.grad_attn.refs_4_, bf16[4,3456,256]{2,1,0:T(8,128)(2,1)} %get-tuple-element.359.qkv, bf16[4,16,256,256]{3,2,1,0:T(8,128)(2,1)} %get-tuple-element.360.prob, bf16[576,1152]{1,0:T(8,128)(2,1)} %refs_0_.5, ...), custom_call_target="tpu_custom_call" | custom-call | flops 69000003584 | bytes 24018944 | tf_op jit(solution)/shard_map/pallas_call | solution.py:448
  220.5 9.5 %collective-permute-done.16 = bf16[2,2,144,512]{3,2,0,1:T(8,128)(2,1)S(1)} collective-permute-done((bf16[2,2,144,512]{3,2,0,1:T(8,128)(2,1)}, bf16[2,2,144,512]{3,2,0,1:T(8,128)(2,1)S(1)}, u32[]{:S(2)}, u32[]{:S(2)}) %collective-permute-start.16) | collective-permute-done | bytes 589856 | tf_op jit(solution)/shard_map/ppermute | solution.py:503
  235.0 12.9 %shard_map.243.refs_1_ = bf16[2,3456,256]{2,1,0:T(8,128)(2,1)} custom-call(s32[3]{0:T(128)} %pad_add_fusion.sc, bf16[4,256,1152]{2,1,0:T(8,128)(2,1)} %get-tuple-element.358.grad_attn.refs_4_, bf16[4,3456,256]{2,1,0:T(8,128)(2,1)} %get-tuple-element.359.qkv, bf16[4,16,256,256]{3,2,1,0:T(8,128)(2,1)} %get-tuple-element.360.prob, bf16[576,1152]{1,0:T(8,128)(2,1)} %refs_0_.5, ...), custom_call_target="tpu_custom_call" | custom-call | flops 69000003584 | bytes 24018944 | tf_op jit(solution)/shard_map/pallas_call | solution.py:448
  247.9 7.3 %collective-permute-done.17 = bf16[2,144,1152]{2,1,0:T(8,128)(2,1)S(1)} collective-permute-done((bf16[2,144,1152]{2,1,0:T(8,128)(2,1)S(1)}, bf16[2,144,1152]{2,1,0:T(8,128)(2,1)S(1)}, u32[]{:S(2)}, u32[]{:S(2)}) %collective-permute-start.17) | collective-permute-done | bytes 663584 | tf_op jit(solution)/shard_map/ppermute | solution.py:503
  257.4 14.1 %shard_map.244 = (bf16[16,144,512]{2,1,0:T(8,128)(2,1)}, bf16[16,144,384]{2,1,0:T(8,128)(2,1)}, bf16[16,144,256]{2,1,0:T(8,128)(2,1)}, f32[3,1,576]{2,1,0:T(1,128)}) custom-call(s32[3]{0:T(128)} %pad_add_fusion.sc, bf16[2,3456,256]{2,1,0:T(8,128)(2,1)} %shard_map.242.refs_0_, bf16[2,3456,256]{2,1,0:T(8,128)(2,1)} %shard_map.243.refs_1_, ...), custom_call_target="tpu_custom_call" | custom-call | flops 69000003584 | bytes 19471104 | tf_op jit(solution)/shard_map/pallas_call | solution.py:448
  278.0 13.9 %shard_map.245 = (bf16[16,144,512]{2,1,0:T(8,128)(2,1)}, bf16[16,144,384]{2,1,0:T(8,128)(2,1)}, bf16[16,144,256]{2,1,0:T(8,128)(2,1)}, f32[3,1,576]{2,1,0:T(1,128)}) custom-call(s32[3]{0:T(128)} %pad_add_fusion.sc, bf16[2,3456,256]{2,1,0:T(8,128)(2,1)} %shard_map.242.refs_0_, bf16[2,3456,256]{2,1,0:T(8,128)(2,1)} %shard_map.243.refs_1_, ...), custom_call_target="tpu_custom_call" | custom-call | flops 69000003584 | bytes 19471104 | tf_op jit(solution)/shard_map/pallas_call | solution.py:448
  291.9 15.5 %collective-permute-done.22 = bf16[144,1152]{1,0:T(8,128)(2,1)} collective-permute-done((bf16[144,1152]{1,0:T(8,128)(2,1)}, bf16[144,1152]{1,0:T(8,128)(2,1)}, u32[]{:S(2)}, u32[]{:S(2)}) %collective-permute-start.22) | collective-permute-done | bytes 331808 | tf_op jit(solution)/shard_map/ppermute | solution.py:503
  323.8 24.6 %shard_map.246 = (f32[8,256,1152]{2,1,0:T(8,128)}, f32[4,256,1152]{2,1,0:T(8,128)}, f32[4,2,1152]{2,1,0:T(2,128)}) custom-call(s32[3]{0:T(128)} %pad_add_fusion.sc, bf16[2,3456,256]{2,1,0:T(8,128)(2,1)} %shard_map.242.refs_0_, bf16[2,3456,256]{2,1,0:T(8,128)(2,1)} %shard_map.243.refs_1_, bf16[1728,1152]{1,0:T(8,128)(2,1)} %bitcast.156, ...), custom_call_target="tpu_custom_call" | custom-call | flops 69000003584 | bytes 38891520 | tf_op jit(solution)/shard_map/pallas_call | solution.py:448
  348.5 36.0 %collective-permute-done.25 = bf16[2,2,2,144,256]{4,3,1,2,0:T(8,128)(2,1)} collective-permute-done((bf16[2,2,2,144,256]{4,3,1,2,0:T(8,128)(2,1)}, bf16[2,2,2,144,256]{4,3,1,2,0:T(8,128)(2,1)}, u32[]{:S(2)}, u32[]{:S(2)}) %collective-permute-start.25) | collective-permute-done | bytes 589856 | tf_op jit(solution)/shard_map/ppermute | solution.py:503
  397.3 24.8 %shard_map.247 = (bf16[8,256,1152]{2,1,0:T(8,128)(2,1)}, bf16[4,256,1152]{2,1,0:T(8,128)(2,1)}, f32[4,1,1152]{2,1,0:T(1,128)}) custom-call(s32[3]{0:T(128)} %pad_add_fusion.sc, bf16[2,2304,1024]{2,1,0:T(8,128)(2,1)} %get-tuple-element.431.act, bf16[2304,1152]{1,0:T(8,128)(2,1)} %w_down0.1, bf16[2304,1152]{1,0:T(8,128)(2,1)} %collective-permute-done.5.refs_1_.refs_4_.w_down1, ...), custom_call_target="tpu_custom_call" | custom-call | flops 69000003584 | bytes 36813312 | tf_op jit(solution)/shard_map/pallas_call | solution.py:448
  440.8 6.6 %collective-permute-done.33 = bf16[2,144,896]{2,1,0:T(8,128)(2,1)} collective-permute-done((bf16[2,144,896]{2,1,0:T(8,128)(2,1)}, bf16[2,144,896]{2,1,0:T(8,128)(2,1)}, u32[]{:S(2)}, u32[]{:S(2)}) %collective-permute-start.33) | collective-permute-done | bytes 516128 | tf_op jit(solution)/shard_map/ppermute | solution.py:503
  458.5 6.5 %collective-permute-done.36 = bf16[144,256]{1,0:T(8,128)(2,1)S(1)} collective-permute-done((bf16[144,256]{1,0:T(8,128)(2,1)S(1)}, bf16[144,256]{1,0:T(8,128)(2,1)S(1)}, u32[]{:S(2)}, u32[]{:S(2)}) %collective-permute-start.36) | collective-permute-done | bytes 73760 | tf_op jit(solution)/shard_map/ppermute | solution.py:503
  491.8 6.8 %shard_map.249 = (f32[2304,1152]{1,0:T(8,128)}, f32[1152,2304]{1,0:T(8,128)}, f32[8,128]{1,0:T(8,128)}) custom-call(s32[3]{0:T(128)} %pad_add_fusion.sc, bf16[8,144,640]{2,1,0:T(8,128)(2,1)} %copy-done, bf16[8,144,640]{2,1,0:T(8,128)(2,1)} %collective-permute-done.38.refs_1_, bf16[8,144,512]{2,1,0:T(8,128)(2,1)} %copy-done.1, ...), custom_call_target="tpu_custom_call" | custom-call | flops 4600000000 | bytes 4000000 | tf_op jit(solution)/shard_map/pallas_call | solution.py:448
  517.4 6.8 %shard_map.251 = (f32[2304,1152]{1,0:T(8,128)}, f32[1152,2304]{1,0:T(8,128)}, f32[8,128]{1,0:T(8,128)}) custom-call(s32[3]{0:T(128)} %pad_add_fusion.sc, bf16[8,144,640]{2,1,0:T(8,128)(2,1)} %copy-done, bf16[8,144,640]{2,1,0:T(8,128)(2,1)} %collective-permute-done.38.refs_1_, ...), custom_call_target="tpu_custom_call", output_to_operand_aliasing={{0}: (6, {}), {1}: (7, {})} | custom-call | flops 4600000000 | bytes 4000000 | tf_op jit(solution)/shard_map/pallas_call | solution.py:448
  540.3 8.1 %fusion.6 = f32[1152,3456]{1,0:T(8,128)} fusion(bf16[128,1152]{1,0:T(8,128)(2,1)S(1)} %reshape.171, bf16[16,13,3456]{2,1,0:T(8,128)(2,1)S(1)} %reshape.169), kind=kOutput, calls=%fused_computation.24 | convolution fusion | flops 1019215872 | bytes 17104896 | tf_op jit(solution)/shard_map/dot_general | solution.py:1059
  553.5 6.7 %collective-permute-done.53.refs_1_ = bf16[8,144,512]{2,1,0:T(8,128)(2,1)} collective-permute-done((bf16[8,144,512]{2,1,0:T(8,128)(2,1)}, bf16[8,144,512]{2,1,0:T(8,128)(2,1)}, u32[]{:S(2)}, u32[]{:S(2)}) %collective-permute-start.53) | collective-permute-done | bytes 1179680 | tf_op jit(solution)/shard_map/ppermute | solution.py:503
  565.7 8.5 %shard_map.248 = (f32[1728,1152]{1,0:T(8,128)}, f32[576,1152]{1,0:T(8,128)}) custom-call(s32[3]{0:T(128)} %pad_add_fusion.sc, bf16[8,144,512]{2,1,0:T(8,128)(2,1)} %pad_maximum_fusion.7.refs_0_, bf16[8,144,512]{2,1,0:T(8,128)(2,1)} %collective-permute-done.53.refs_1_, bf16[8,144,384]{2,1,0:T(8,128)(2,1)} %pad_maximum_fusion.8.refs_2_, ...), custom_call_target="tpu_custom_call" | custom-call | flops 10350000128 | bytes 9000000 | tf_op jit(solution)/shard_map/pallas_call | solution.py:448
  (322 shorter events, 187.8 us)
Async XLA Ops:
  7.2 491.4 %all-reduce.4.cloned.1.call-start = ((), (), s32[]{:S(2)}) async-start(), calls=%async_computation | async-start | bytes 10616832 | tf_op jit(solution)/shard_map/psum | solution.py:767
  14.6 44.6 %collective-permute-start.4 = (bf16[1152,2304]{1,0:T(8,128)(2,1)}, bf16[1152,2304]{1,0:T(8,128)(2,1)}, u32[]{:S(2)}, u32[]{:S(2)}) collective-permute-start(bf16[1152,2304]{1,0:T(8,128)(2,1)} %w_up0.1), channel_id=1, source_target_pairs={{0,1},{1,0},{2,3},{3,2},{4,5},{5,4},{6,7},{7,6},{8,9},{9,8},{10,11... | collective-permute-start | bytes 15925256 | tf_op jit(solution)/shard_map/ppermute | solution.py:479
  14.9 44.2 %collective-permute-start.5 = (bf16[2304,1152]{1,0:T(8,128)(2,1)}, bf16[2304,1152]{1,0:T(8,128)(2,1)}, u32[]{:S(2)}, u32[]{:S(2)}) collective-permute-start(bf16[2304,1152]{1,0:T(8,128)(2,1)} %w_down0.1), channel_id=1, source_target_pairs={{0,1},{1,0},{2,3},{3,2},{4,5},{5,4},{6,7},{7,6},{8,9},{9,8},{10,11... | collective-permute-start | bytes 15925256 | tf_op jit(solution)/shard_map/ppermute | solution.py:479
  18.3 40.8 %collective-permute-start.6 = (bf16[1,2304]{1,0:T(2,128)(2,1)S(1)}, bf16[1,2304]{1,0:T(2,128)(2,1)S(1)}, u32[]{:S(2)}, u32[]{:S(2)}) collective-permute-start(bf16[1,2304]{1,0:T(2,128)(2,1)S(1)} %broadcast_in_dim.52), channel_id=1, source_target_pairs={{0,1},{1,0},{2,3},{3,2},{4,5},{5,4},{6,7},{7,6},{8,9},{9,8},{10,11... | collective-permute-start | bytes 13832 | tf_op jit(solution)/shard_map/ppermute | solution.py:479
  86.4 30.1 %collective-permute-start.7 = (bf16[16,96,1152]{2,1,0:T(8,128)(2,1)}, bf16[16,96,1152]{2,1,0:T(8,128)(2,1)}, u32[]{:S(2)}, u32[]{:S(2)}) collective-permute-start(bf16[16,96,1152]{2,1,0:T(8,128)(2,1)} %get-tuple-element.312), channel_id=1, source_target_pairs={{0,1},{1,0},{2,3},{3,2},{4,5},{5,4},{6,7},{7,6},{8,9},{9,8},{10,11... | collective-permute-start | bytes 10616840 | tf_op jit(solution)/shard_map/ppermute | solution.py:479
  117.7 28.6 %collective-permute-start.9 = (bf16[16,96,640]{2,1,0:T(8,128)(2,1)}, bf16[16,96,640]{2,1,0:T(8,128)(2,1)S(1)}, u32[]{:S(2)}, u32[]{:S(2)}) collective-permute-start(bf16[16,96,640]{2,1,0:T(8,128)(2,1)} %get-tuple-element.329), channel_id=1, source_target_pairs={{0,1},{1,0},{2,3},{3,2},{4,5},{5,4},{6,7},{7,6},{8,9},{9,8},{10,11... | collective-permute-start | bytes 5898248 | tf_op jit(solution)/shard_map/ppermute | solution.py:479
  118.1 28.2 %collective-permute-start.11 = (bf16[16,96,512]{2,1,0:T(8,128)(2,1)}, bf16[16,96,512]{2,1,0:T(8,128)(2,1)}, u32[]{:S(2)}, u32[]{:S(2)}) collective-permute-start(bf16[16,96,512]{2,1,0:T(8,128)(2,1)} %get-tuple-element.331), channel_id=1, source_target_pairs={{0,1},{1,0},{2,3},{3,2},{4,5},{5,4},{6,7},{7,6},{8,9},{9,8},{10,11... | collective-permute-start | bytes 4718600 | tf_op jit(solution)/shard_map/ppermute | solution.py:479
  156.1 46.6 %collective-permute-start.13 = (bf16[2,2,2,144,640]{4,3,0,1,2:T(8,128)(2,1)S(1)}, bf16[2,2,2,144,640]{4,3,0,1,2:T(8,128)(2,1)}, u32[]{:S(2)}, u32[]{:S(2)}) collective-permute-start(bf16[2,2,2,144,640]{4,3,0,1,2:T(8,128)(2,1)S(1)} %pad_maximum_fusion), channel_id=1, source_target_pairs={{0,2},{2,0},{4,6},{6,4},{8,10},{10,8},{12,14},{14,12},{16,18},{18,... | collective-permute-start | bytes 4423688 | tf_op jit(solution)/shard_map/ppermute | solution.py:503
  159.3 37.1 %collective-permute-start.14 = (bf16[2,2,2,144,512]{4,3,0,1,2:T(8,128)(2,1)}, bf16[2,2,2,144,512]{4,3,0,1,2:T(8,128)(2,1)}, u32[]{:S(2)}, u32[]{:S(2)}) collective-permute-start(bf16[2,2,2,144,512]{4,3,0,1,2:T(8,128)(2,1)} %pad_maximum_fusion.4), channel_id=1, source_target_pairs={{0,4},{2,6},{4,0},{6,2},{8,12},{10,14},{12,8},{14,10},{16,20},{18,... | collective-permute-start | bytes 3538952 | tf_op jit(solution)/shard_map/ppermute | solution.py:503
  277.5 29.9 %collective-permute-start.19 = (bf16[16,144,512]{2,1,0:T(8,128)(2,1)}, bf16[16,144,512]{2,1,0:T(8,128)(2,1)S(1)}, u32[]{:S(2)}, u32[]{:S(2)}) collective-permute-start(bf16[16,144,512]{2,1,0:T(8,128)(2,1)} %get-tuple-element.397), channel_id=1, source_target_pairs={{0,1},{1,0},{2,3},{3,2},{4,5},{5,4},{6,7},{7,6},{8,9},{9,8},{10,11... | collective-permute-start | bytes 7077896 | tf_op jit(solution)/shard_map/ppermute | solution.py:479
  277.5 29.9 %collective-permute-start.20 = (bf16[16,144,384]{2,1,0:T(8,128)(2,1)}, bf16[16,144,384]{2,1,0:T(8,128)(2,1)S(1)}, u32[]{:S(2)}, u32[]{:S(2)}) collective-permute-start(bf16[16,144,384]{2,1,0:T(8,128)(2,1)} %get-tuple-element.398), channel_id=1, source_target_pairs={{0,1},{1,0},{2,3},{3,2},{4,5},{5,4},{6,7},{7,6},{8,9},{9,8},{10,11... | collective-permute-start | bytes 5308424 | tf_op jit(solution)/shard_map/ppermute | solution.py:479
  278.0 29.4 %collective-permute-start.21 = (bf16[16,144,256]{2,1,0:T(8,128)(2,1)}, bf16[16,144,256]{2,1,0:T(8,128)(2,1)}, u32[]{:S(2)}, u32[]{:S(2)}) collective-permute-start(bf16[16,144,256]{2,1,0:T(8,128)(2,1)} %get-tuple-element.399), channel_id=1, source_target_pairs={{0,1},{1,0},{2,3},{3,2},{4,5},{5,4},{6,7},{7,6},{8,9},{9,8},{10,11... | collective-permute-start | bytes 3538952 | tf_op jit(solution)/shard_map/ppermute | solution.py:479
  278.0 29.4 %collective-permute-start.22 = (bf16[144,1152]{1,0:T(8,128)(2,1)}, bf16[144,1152]{1,0:T(8,128)(2,1)}, u32[]{:S(2)}, u32[]{:S(2)}) collective-permute-start(bf16[144,1152]{1,0:T(8,128)(2,1)} %add.329), channel_id=1, source_target_pairs={{0,16},{2,18},{4,20},{6,22},{8,24},{10,26},{12,28},{14,30},{16,0},... | collective-permute-start | bytes 995336 | tf_op jit(solution)/shard_map/ppermute | solution.py:503
  318.5 66.1 %collective-permute-start.23 = (bf16[2,2,2,144,512]{4,3,0,1,2:T(8,128)(2,1)}, bf16[2,2,2,144,512]{4,3,0,1,2:T(8,128)(2,1)S(1)}, u32[]{:S(2)}, u32[]{:S(2)}) collective-permute-start(bf16[2,2,2,144,512]{4,3,0,1,2:T(8,128)(2,1)} %fusion.1), channel_id=1, source_target_pairs={{0,2},{2,0},{4,6},{6,4},{8,10},{10,8},{12,14},{14,12},{16,18},{18,... | collective-permute-start | bytes 3538952 | tf_op jit(solution)/shard_map/ppermute | solution.py:503
  318.5 66.1 %collective-permute-start.24 = (bf16[2,2,2,144,384]{4,3,0,1,2:T(8,128)(2,1)}, bf16[2,2,2,144,384]{4,3,0,1,2:T(8,128)(2,1)}, u32[]{:S(2)}, u32[]{:S(2)}) collective-permute-start(bf16[2,2,2,144,384]{4,3,0,1,2:T(8,128)(2,1)} %fusion.5), channel_id=1, source_target_pairs={{0,4},{2,6},{4,0},{6,2},{8,12},{10,14},{12,8},{14,10},{16,20},{18,... | collective-permute-start | bytes 2654216 | tf_op jit(solution)/shard_map/ppermute | solution.py:503
  321.8 62.7 %collective-permute-start.26 = (bf16[2,144,1152]{2,1,0:T(8,128)(2,1)S(1)}, bf16[2,144,1152]{2,1,0:T(8,128)(2,1)}, u32[]{:S(2)}, u32[]{:S(2)}) collective-permute-start(bf16[2,144,1152]{2,1,0:T(8,128)(2,1)S(1)} %pad_maximum_fusion.12), channel_id=1, source_target_pairs={{0,8},{2,10},{4,12},{6,14},{8,0},{10,2},{12,4},{14,6},{16,24},{18,... | collective-permute-start | bytes 1990664 | tf_op jit(solution)/shard_map/ppermute | solution.py:503
  321.8 62.7 %collective-permute-start.25 = (bf16[2,2,2,144,256]{4,3,1,2,0:T(8,128)(2,1)}, bf16[2,2,2,144,256]{4,3,1,2,0:T(8,128)(2,1)}, u32[]{:S(2)}, u32[]{:S(2)}) collective-permute-start(bf16[2,2,2,144,256]{4,3,1,2,0:T(8,128)(2,1)} %fusion.12), channel_id=1, source_target_pairs={{0,8},{2,10},{4,12},{6,14},{8,0},{10,2},{12,4},{14,6},{16,24},{18,... | collective-permute-start | bytes 1769480 | tf_op jit(solution)/shard_map/ppermute | solution.py:503
  392.8 31.0 %collective-permute-start.30 = (bf16[4,144,640]{2,1,0:T(8,128)(2,1)S(1)}, bf16[4,144,640]{2,1,0:T(8,128)(2,1)}, u32[]{:S(2)}, u32[]{:S(2)}) collective-permute-start(bf16[4,144,640]{2,1,0:T(8,128)(2,1)S(1)} %slice.446), channel_id=1, source_target_pairs={{0,4},{2,6},{4,0},{6,2},{8,12},{10,14},{12,8},{14,10},{16,20},{18,... | collective-permute-start | bytes 2211848 | tf_op jit(solution)/shard_map/ppermute | solution.py:503
  394.3 29.5 %collective-permute-start.27 = (bf16[2,2,144,512]{3,2,0,1:T(8,128)(2,1)S(1)}, bf16[2,2,144,512]{3,2,0,1:T(8,128)(2,1)S(1)}, u32[]{:S(2)}, u32[]{:S(2)}) collective-permute-start(bf16[2,2,144,512]{3,2,0,1:T(8,128)(2,1)S(1)} %get-tuple-element.438), channel_id=1, source_target_pairs={{0,4},{2,6},{4,0},{6,2},{8,12},{10,14},{12,8},{14,10},{16,20},{18,... | collective-permute-start | bytes 1769480 | tf_op jit(solution)/shard_map/ppermute | solution.py:503
  394.8 29.0 %collective-permute-start.31 = (bf16[4,144,512]{2,1,0:T(8,128)(2,1)}, bf16[4,144,512]{2,1,0:T(8,128)(2,1)S(1)}, u32[]{:S(2)}, u32[]{:S(2)}) collective-permute-start(bf16[4,144,512]{2,1,0:T(8,128)(2,1)} %slice.447), channel_id=1, source_target_pairs={{0,2},{2,0},{4,6},{6,4},{8,10},{10,8},{12,14},{14,12},{16,18},{18,... | collective-permute-start | bytes 1769480 | tf_op jit(solution)/shard_map/ppermute | solution.py:503
  435.4 36.4 %collective-permute-start.38 = (bf16[8,144,640]{2,1,0:T(8,128)(2,1)S(1)}, bf16[8,144,640]{2,1,0:T(8,128)(2,1)}, u32[]{:S(2)}, u32[]{:S(2)}) collective-permute-start(bf16[8,144,640]{2,1,0:T(8,128)(2,1)S(1)} %pad_maximum_fusion.2.refs_0_), channel_id=1, source_target_pairs={{0,2},{2,0},{4,6},{6,4},{8,10},{10,8},{12,14},{14,12},{16,18},{18,... | collective-permute-start | bytes 4423688 | tf_op jit(solution)/shard_map/ppermute | solution.py:503
  436.0 31.7 %collective-permute-start.39 = (bf16[8,144,512]{2,1,0:T(8,128)(2,1)S(1)}, bf16[8,144,512]{2,1,0:T(8,128)(2,1)}, u32[]{:S(2)}, u32[]{:S(2)}) collective-permute-start(bf16[8,144,512]{2,1,0:T(8,128)(2,1)S(1)} %pad_maximum_fusion.6.refs_2_), channel_id=1, source_target_pairs={{0,4},{2,6},{4,0},{6,2},{8,12},{10,14},{12,8},{14,10},{16,20},{18,... | collective-permute-start | bytes 3538952 | tf_op jit(solution)/shard_map/ppermute | solution.py:503
  488.0 47.6 %collective-permute-start.51 = (f32[4,256,1152]{2,1,0:T(8,128)}, f32[4,256,1152]{2,1,0:T(8,128)}, u32[]{:S(2)}, u32[]{:S(2)}) collective-permute-start(f32[4,256,1152]{2,1,0:T(8,128)} %get-tuple-element.545), channel_id=1, source_target_pairs={{0,1},{1,0},{2,3},{3,2},{4,5},{5,4},{6,7},{7,6},{8,9},{9,8},{10,11... | collective-permute-start | bytes 14155784 | tf_op jit(solution)/shard_map/ppermute | solution.py:479
  531.9 28.3 %collective-permute-start.53 = (bf16[8,144,512]{2,1,0:T(8,128)(2,1)}, bf16[8,144,512]{2,1,0:T(8,128)(2,1)}, u32[]{:S(2)}, u32[]{:S(2)}) collective-permute-start(bf16[8,144,512]{2,1,0:T(8,128)(2,1)} %pad_maximum_fusion.7.refs_0_), channel_id=1, source_target_pairs={{0,2},{2,0},{4,6},{6,4},{8,10},{10,8},{12,14},{14,12},{16,18},{18,... | collective-permute-start | bytes 3538952 | tf_op jit(solution)/shard_map/ppermute | solution.py:503
  (79 other events, 775.5 us)
Sparse Core Ops, SparseCore 0:
  146.4 238.1 all-reduce.3

commit v11 on v9

--- a/solution.py
+++ b/solution.py
@@ -730,16 +730,21 @@
     summed = range(PLAIN)
     swaps = [swap_flow(grad) for (grad,) in mlp_call([(chunk, 1) for chunk in summed], {}, 26)]
     order.tick(*swaps)
-    rest = [(chunk, part) for chunk in range(PLAIN, CHUNKS) for part in (1, 0)]
-    grads = mlp_call(rest, {}, 26)
+    rest = range(PLAIN, CHUNKS)
+    made_rest = []
     flows = [
-        sum_flow(MLP_WAYS, lambda own=own: own, others) for others, own in zip(grads[0::2], grads[1::2])
+        sum_flow(MLP_WAYS, lambda k=k: made_rest[k], others)
+        for k, others in enumerate(mlp_call([(chunk, 1) for chunk in rest], {}, 13))
     ]
-    order.tick(*swaps, *flows)
+    wide_scaled = jnp.pad(scaled.reshape(-1), (0, 3 * own_cols - slots * dim)).reshape(3, own_cols)
+    early = rows_flow(wide_scaled)
+    order.tick(*swaps, *flows, early)
     came = {(chunk, 0): order.results[swap] for chunk, swap in zip(summed, swaps)}
     grads = mlp_call([(chunk, 0) for chunk in summed], came, 26)
     plain_sums = lax.psum([grad for (grad,) in grads], "dp")
-    order.tick(*flows)
+    order.tick(early)
+    made_rest += mlp_call([(chunk, 0) for chunk in rest], {}, 13)
+    order.tick(*flows, early)
 
     reach = 768
     turns = ff // reach
@@ -779,7 +784,7 @@
         scratch=[pltpu.VMEM((count, dim), f32)],
     )
     order.after(mid_sums)
-    order.tick(*flows)
+    order.tick(*flows, early)
     pieces = 2
     each = images // pieces
     grad_qkv = []
@@ -803,7 +808,7 @@
             )
         grad_qkv.append(grad_piece)
         order.after(grad_piece)
-        order.tick(*flows)
+        order.tick(*flows, early)
 
     attn_per = 4 * cols // 16
     qv_sums = [None, None]
@@ -876,8 +881,8 @@
     order.after(gate_sums)
     order.tick(last, *flows)
 
-    low_sums, mid_sums, gate_sums, down_sums, qv_sums, up_sums, scaled_rows = order.fence(
-        (low_sums, mid_sums, gate_sums, down_sums, qv_sums, up_sums, scaled)
+    low_sums, mid_sums, gate_sums, down_sums, qv_sums, up_sums = order.fence(
+        (low_sums, mid_sums, gate_sums, down_sums, qv_sums, up_sums)
     )
     grad_modulation = jnp.concatenate([low_sums, mid_sums[:, 2:3], mid_sums[:, 0:2], gate_sums], axis=1)
     grad_modulation = grad_modulation.reshape(images, 6 * dim).astype(bf16)
@@ -905,20 +910,11 @@
     group_mod = jnp.where(core == 0, jnp.concatenate([kept, came]), jnp.concatenate([came, kept]))
     own_bias_sum = bias_sums[0] + got[images : images + 1]
     shared_sum = shared + got[images + 1 :]
-    wide_scaled = jnp.pad(scaled_rows.reshape(-1), (0, 3 * own_cols - slots * dim)).reshape(3, own_cols)
     packed_rows = jnp.concatenate(
-        [group_mod, own_bias_sum.astype(bf16), shared_sum.astype(bf16), wide_scaled]
+        [group_mod, own_bias_sum.astype(bf16), shared_sum.astype(bf16)]
     )
     (packed_rows,) = order.fence([packed_rows])
     small = rows_flow(packed_rows)
-    order.tick(last, small)
-    (group_mod,) = order.fence([group_mod])
-    part_scaled = outer_cols(group_mod, w_mod).astype(bf16)
-    order.after(part_scaled[0, :1])
-    order.tick(last, small, *flows)
-    own_output, part_scaled = order.fence((own_output, part_scaled))
-    other_output, came_scaled = swap_cores(own_output), swap_cores(part_scaled)
-
     def cuts(ways):
         return tuple((way, lo, hi) for lo, hi, way in ways)
 
@@ -928,7 +924,7 @@
         nonlocal grad_w_down, grad_w_up
         first = grad_w_down.shape[0] == 8
         spot = len(args) + 1
-        grad_w_down, grad_w_up, mark = run_kernel(
+        grad_w_down, grad_w_up, _ = run_kernel(
             body,
             order.sc,
             list(args) + [grad_w_down, grad_w_up],
@@ -950,28 +946,35 @@
             scratch=[pltpu.VMEM((block, dim), f32)],
             alias=None if first else {spot: 0, spot + 1: 1},
         )
-        order.after(mark)
-
+        grad_w_down, grad_w_up = order.fence((grad_w_down, grad_w_up))
+
+    order.tick(last, small, *flows)
+    own_output, grad_own_tokens, group_mod = order.fence((own_output, grad_own_tokens, group_mod))
+    other_output, other_tokens = swap_cores(own_output), swap_cores(grad_own_tokens)
+    part_scaled = outer_cols(group_mod, w_mod).astype(bf16)
+    part_scaled = order.fence(part_scaled)
     for chunk, flow in enumerate(flows):
         body = functools.partial(final_mlp_kernel, cuts(MLP_WAYS), per)
         final_mlp(PLAIN + chunk, body, order.finish(flow))
     order.tick(last, small)
-    other_output, came_scaled, grad_own_tokens = order.fence((other_output, came_scaled, grad_own_tokens))
-    other_tokens = swap_cores(grad_own_tokens)
-    for chunk, total in zip(summed, order.fence(plain_sums)):
-        final_mlp(chunk, functools.partial(final_plain_kernel, per), [total])
+    came_scaled = swap_cores(order.fence(part_scaled))
+    other_output, other_tokens = order.fence((other_output, other_tokens))
+    output = fill_other(output, other_output, core)
+    grad_tokens = fill_other(grad_tokens, other_tokens, core)
+    output, grad_tokens = order.fence((output, grad_tokens))
     order.tick(last, small)
-    output = fill_other(output, other_output, core)
-    grad_scaled = part_scaled.astype(f32) + came_scaled.astype(f32)
+    grad_scaled = part_scaled.astype(f32) + order.fence(came_scaled).astype(f32)
     _, silu_back = jax.vjp(jax.nn.silu, cond_f)
     grad_condition = silu_back(grad_scaled)[0]
-    order.after((output[0, 0, :1], grad_condition[0, :1]))
+    grad_condition = order.fence(grad_condition)
+    plain_sums = order.fence(plain_sums)
+    final_mlp(0, functools.partial(final_plain_kernel, per), [plain_sums[0]])
+    order.tick(last, small)
+    final_mlp(1, functools.partial(final_plain_kernel, per), [plain_sums[1]])
     order.tick(last)
-    grad_tokens = fill_other(grad_tokens, order.fence(other_tokens), core)
-    order.after(grad_tokens[0, 0, :1])
-    all_rows = order.fence(order.finish(small)).reshape(16, slots + 5, own_cols)
+    all_rows = order.fence(order.finish(small)).reshape(16, slots + 2, own_cols)
     all_mod = all_rows[:, :slots].reshape(-1, own_cols)
-    all_scaled = all_rows[:, slots + 2 :].reshape(16, -1)[:, : slots * dim].reshape(-1, dim)
+    all_scaled = order.finish(early).reshape(16, -1)[:, : slots * dim].reshape(-1, dim)
     grad_w_mod = inner_rows(all_scaled, all_mod)
     grad_b_mod = jnp.sum(all_mod.astype(f32), axis=0)
     bias_total = jnp.sum(all_rows[:, slots : slots + 2].astype(f32), axis=0)
@@ -979,7 +982,7 @@
     grad_b_up = bias_total[0, 2 * cols :]
     grad_b_proj = bias_total[1, :dim]
     grad_b_down = bias_total[1, dim : 2 * dim]
-    order.after((grad_w_mod[0, :1], grad_b_mod[:1], bias_total[0, :1]))
+    grad_w_mod = order.fence(grad_w_mod)
     args = order.finish(last)
     grad_qkv_rows, grad_w_proj = run_kernel(
         functools.partial(final_attn_kernel, cuts(ATTN_WAYS), attn_per),

time: 547 us -> 533 us (0.974)
  waiting for transfers between devices: 130 us -> 109 us
    ppermute x4 -> x8, waiting for transfers between devices: 39.1 us -> 12.7 us  [rows_flow(): came = lax.ppermute(rows, 'dp', bit_pairs(bit))]
    ppermute x4 -> x8, starting transfers between devices: 3.86 us -> 13.6 us  [rows_flow(): came = lax.ppermute(rows, 'dp', bit_pairs(bit))]
    ppermute x32, starting transfers between devices: 36.8 us -> 30.9 us  [exchange(): lax.ppermute(value, 'dp', bit_pairs(bit))]
    pallas_call x15 -> x16, Pallas kernels: 270 us -> 274 us  [run_kernel(): pl.pallas_call(body, out_shape=out_shape, grid_spec=pltpu.PrefetchScalarG...]
  transfers between devices with their start and end apart: 55 -> 59, of which waited for: 23 -> 21; matrix products, arithmetic and copies ran while one was open for 12% -> 13% of each run, Pallas kernels for 44% -> 45%
where the time goes in v11:
time: 533 us; the launch traced here: 526 us
  Pallas kernels  274 us (51%)
  waiting for transfers between devices  109 us (20%)
  starting transfers between devices  48.9 us (9%)
  local copies, waits for them, and re-layouts  30.3 us (6%)
  other arithmetic  30.2 us (6%)
  matrix products  18.1 us (3%)
  between operations  16.1 us (3%)
    pallas_call x16, Pallas kernels, run_kernel(): pl.pallas_call(body, out_shape=out_shape, grid_spec=pltpu.PrefetchScalarG...  274 us
    ppermute x32, waiting for transfers between devices, exchange(): lax.ppermute(value, 'dp', bit_pairs(bit))  88.4 us
    ppermute x32, starting transfers between devices, exchange(): lax.ppermute(value, 'dp', bit_pairs(bit))  30.9 us
    add x21, other arithmetic, reduce_flow(): cut(one, bits, route[stage], side) + cut(two, bits, route[stage], side)  14.2 us
    ppermute x8, starting transfers between devices, rows_flow(): came = lax.ppermute(rows, 'dp', bit_pairs(bit))  13.6 us
    ppermute x8, waiting for transfers between devices, rows_flow(): came = lax.ppermute(rows, 'dp', bit_pairs(bit))  12.7 us
  transfers between devices with their start and end apart: 59, of which 21 were waited for; matrix products, arithmetic and copies ran while one was open for 13% of the time, Pallas kernels for 45%

profile of v11, /device:TPU:0, one launch (start us, length us, event | category | flops | bytes accessed | tf_op | source)
XLA Modules:
  0.0 526.2 jit_solution(6557283434732598499)
XLA Ops:
  18.7 6.0 %collective-permute-done.3.refs_5_ = bf16[2,576]{1,0:T(2,128)(2,1)S(1)} collective-permute-done((bf16[2,576]{1,0:T(2,128)(2,1)S(1)}, bf16[2,576]{1,0:T(2,128)(2,1)S(1)}, u32[]{:S(2)}, u32[]{:S(2)}) %collective-permute-start.3) | collective-permute-done | bytes 2336 | tf_op jit(solution)/shard_map/ppermute | solution.py:458
  26.4 32.8 %shard_map.237 = (bf16[4,3456,256]{2,1,0:T(8,128)(2,1)}, bf16[4,16,256,256]{3,2,1,0:T(8,128)(2,1)}, bf16[4,1152,256]{2,1,0:T(8,128)(2,1)}, f32[4,256,1152]{2,1,0...) custom-call(s32[3]{0:T(128)} %pad_add_fusion.sc, ...), custom_call_target="tpu_custom_call" | custom-call | flops 37950001152 | bytes 33000000 | tf_op jit(solution)/shard_map/pallas_call | solution.py:427
  59.8 26.6 %shard_map.238 = (bf16[2,2304,1024]{2,1,0:T(8,128)(2,1)}, bf16[2,2304,1024]{2,1,0:T(8,128)(2,1)}, bf16[16,96,1152]{2,1,0:T(8,128)(2,1)}, bf16[16,96,1152]{2,1,0:...) custom-call(s32[3]{0:T(128)} %pad_add_fusion.sc, bf16[1024,1152]{1,0:T(8,128)(2,1)} %bitcast.143, ...), custom_call_target="tpu_custom_call" | custom-call | flops 29899999232 | bytes 26000000 | tf_op jit(solution)/shard_map/pallas_call | solution.py:427
  88.9 15.6 %shard_map.239 = (bf16[2,2304,1024]{2,1,0:T(8,128)(2,1)}, bf16[2,2304,1024]{2,1,0:T(8,128)(2,1)}, bf16[16,96,640]{2,1,0:T(8,128)(2,1)}, bf16[16,96,512]{2,1,0:T(8,128)(2,1)}, f32[1,768]{1,0:T(1,128)}) custom-call(s32[3]{0:T(128)} %pad_add_fusion.sc, bf16[1024,1152]{1,0:T(8,128)(2,1)} %bitcast.144, ...), custom_call_target="tpu_custom_call", output_to_operand_aliasing={{0}: (6, {}), {1}: (7, {})} | custom-call | flops 14949999616 | bytes 13000000 | tf_op jit(solution)/shard_map/pallas_call | solution.py:427
  108.5 27.0 %shard_map.240 = (bf16[2,2304,1024]{2,1,0:T(8,128)(2,1)}, bf16[2,2304,1024]{2,1,0:T(8,128)(2,1)}, bf16[16,96,1152]{2,1,0:T(8,128)(2,1)}, bf16[16,96,1152]{2,1,0:...) custom-call(s32[3]{0:T(128)} %pad_add_fusion.sc, ...), custom_call_target="tpu_custom_call", output_to_operand_aliasing={{0}: (11, {}), {1}: (12, {})} | custom-call | flops 29899999232 | bytes 26000000 | tf_op jit(solution)/shard_map/pallas_call | solution.py:427
  138.6 16.7 %shard_map.241 = (bf16[2,2304,1024]{2,1,0:T(8,128)(2,1)}, bf16[2,2304,1024]{2,1,0:T(8,128)(2,1)}, bf16[16,96,640]{2,1,0:T(8,128)(2,1)}, bf16[16,96,512]{2,1,0:T(8,128)(2,1)}, f32[1,768]{1,0:T(1,128)}) custom-call(s32[3]{0:T(128)} %pad_add_fusion.sc, bf16[1024,1152]{1,0:T(8,128)(2,1)} %bitcast.146, ...), custom_call_target="tpu_custom_call", output_to_operand_aliasing={{0}: (6, {}), {1}: (7, {})} | custom-call | flops 14949999616 | bytes 13000000 | tf_op jit(solution)/shard_map/pallas_call | solution.py:427
  163.9 27.4 %shard_map.242 = (f32[4,256,1152]{2,1,0:T(8,128)}, bf16[4,256,1152]{2,1,0:T(8,128)(2,1)}, f32[4,4,1152]{2,1,0:T(4,128)}) custom-call(s32[3]{0:T(128)} %pad_add_fusion.sc, bf16[2,2304,1024]{2,1,0:T(8,128)(2,1)} %get-tuple-element.369.back, bf16[1152,2304]{1,0:T(8,128)(2,1)} %w_up0.1, bf16[1152,2304]{1,0:T(8,128)(2,1)} %collective-permute-done.4.refs_0_.refs_3_.w_up1, ...), custom_call_target="tpu_custom_call" | custom-call | flops 69000003584 | bytes 41582592 | tf_op jit(solution)/shard_map/pallas_call | solution.py:427
  198.9 12.3 %shard_map.243.refs_0_ = bf16[2,3456,256]{2,1,0:T(8,128)(2,1)} custom-call(s32[3]{0:T(128)} %pad_add_fusion.sc, bf16[4,256,1152]{2,1,0:T(8,128)(2,1)} %get-tuple-element.387.grad_attn.refs_4_, bf16[4,3456,256]{2,1,0:T(8,128)(2,1)} %get-tuple-element.388.qkv, bf16[4,16,256,256]{3,2,1,0:T(8,128)(2,1)} %get-tuple-element.389.prob, bf16[576,1152]{1,0:T(8,128)(2,1)} %refs_0_.7, ...), custom_call_target="tpu_custom_call" | custom-call | flops 69000003584 | bytes 24018944 | tf_op jit(solution)/shard_map/pallas_call | solution.py:427
  213.3 12.7 %shard_map.244.refs_1_ = bf16[2,3456,256]{2,1,0:T(8,128)(2,1)} custom-call(s32[3]{0:T(128)} %pad_add_fusion.sc, bf16[4,256,1152]{2,1,0:T(8,128)(2,1)} %get-tuple-element.387.grad_attn.refs_4_, bf16[4,3456,256]{2,1,0:T(8,128)(2,1)} %get-tuple-element.388.qkv, bf16[4,16,256,256]{3,2,1,0:T(8,128)(2,1)} %get-tuple-element.389.prob, bf16[576,1152]{1,0:T(8,128)(2,1)} %refs_0_.7, ...), custom_call_target="tpu_custom_call" | custom-call | flops 69000003584 | bytes 24018944 | tf_op jit(solution)/shard_map/pallas_call | solution.py:427
  226.0 7.2 %collective-permute-done.19 = bf16[2,96,1152]{2,1,0:T(8,128)(2,1)S(1)} collective-permute-done((bf16[2,96,1152]{2,1,0:T(8,128)(2,1)S(1)}, bf16[2,96,1152]{2,1,0:T(8,128)(2,1)S(1)}, u32[]{:S(2)}, u32[]{:S(2)}) %collective-permute-start.19) | collective-permute-done | bytes 442400 | tf_op jit(solution)/shard_map/ppermute | solution.py:482
  233.8 13.9 %shard_map.245 = (bf16[16,144,512]{2,1,0:T(8,128)(2,1)}, bf16[16,144,384]{2,1,0:T(8,128)(2,1)}, bf16[16,144,256]{2,1,0:T(8,128)(2,1)}, f32[3,1,576]{2,1,0:T(1,128)}) custom-call(s32[3]{0:T(128)} %pad_add_fusion.sc, bf16[2,3456,256]{2,1,0:T(8,128)(2,1)} %shard_map.243.refs_0_, bf16[2,3456,256]{2,1,0:T(8,128)(2,1)} %shard_map.244.refs_1_, ...), custom_call_target="tpu_custom_call" | custom-call | flops 69000003584 | bytes 19471104 | tf_op jit(solution)/shard_map/pallas_call | solution.py:427
  251.5 13.9 %shard_map.246 = (bf16[16,144,512]{2,1,0:T(8,128)(2,1)}, bf16[16,144,384]{2,1,0:T(8,128)(2,1)}, bf16[16,144,256]{2,1,0:T(8,128)(2,1)}, f32[3,1,576]{2,1,0:T(1,128)}) custom-call(s32[3]{0:T(128)} %pad_add_fusion.sc, bf16[2,3456,256]{2,1,0:T(8,128)(2,1)} %shard_map.243.refs_0_, bf16[2,3456,256]{2,1,0:T(8,128)(2,1)} %shard_map.244.refs_1_, ...), custom_call_target="tpu_custom_call" | custom-call | flops 69000003584 | bytes 19471104 | tf_op jit(solution)/shard_map/pallas_call | solution.py:427
  280.1 24.5 %shard_map.247 = (f32[8,256,1152]{2,1,0:T(8,128)}, f32[4,256,1152]{2,1,0:T(8,128)}, f32[4,2,1152]{2,1,0:T(2,128)}) custom-call(s32[3]{0:T(128)} %pad_add_fusion.sc, bf16[2,3456,256]{2,1,0:T(8,128)(2,1)} %shard_map.243.refs_0_, bf16[2,3456,256]{2,1,0:T(8,128)(2,1)} %shard_map.244.refs_1_, bf16[1728,1152]{1,0:T(8,128)(2,1)} %bitcast.141, ...), custom_call_target="tpu_custom_call" | custom-call | flops 69000003584 | bytes 38891520 | tf_op jit(solution)/shard_map/pallas_call | solution.py:427
  304.6 12.1 %collective-permute-done.28 = bf16[2,96,1152]{2,1,0:T(8,128)(2,1)} collective-permute-done((bf16[2,96,1152]{2,1,0:T(8,128)(2,1)S(1)}, bf16[2,96,1152]{2,1,0:T(8,128)(2,1)}, u32[]{:S(2)}, u32[]{:S(2)}) %collective-permute-start.28) | collective-permute-done | bytes 442400 | tf_op jit(solution)/shard_map/ppermute | solution.py:482
  328.2 24.8 %shard_map.248 = (bf16[8,256,1152]{2,1,0:T(8,128)(2,1)}, bf16[4,256,1152]{2,1,0:T(8,128)(2,1)}, f32[4,1,1152]{2,1,0:T(1,128)}) custom-call(s32[3]{0:T(128)} %pad_add_fusion.sc, bf16[2,2304,1024]{2,1,0:T(8,128)(2,1)} %get-tuple-element.461.act, bf16[2304,1152]{1,0:T(8,128)(2,1)} %w_down0.1, bf16[2304,1152]{1,0:T(8,128)(2,1)} %collective-permute-done.5.refs_1_.refs_4_.w_down1, ...), custom_call_target="tpu_custom_call" | custom-call | flops 69000003584 | bytes 36813312 | tf_op jit(solution)/shard_map/pallas_call | solution.py:427
  372.0 25.7 %collective-permute-done.36 = bf16[2,144,256]{2,1,0:T(8,128)(2,1)S(1)} collective-permute-done((bf16[2,144,256]{2,1,0:T(8,128)(2,1)S(1)}, bf16[2,144,256]{2,1,0:T(8,128)(2,1)S(1)}, u32[]{:S(2)}, u32[]{:S(2)}) %collective-permute-start.36) | collective-permute-done | bytes 147488 | tf_op jit(solution)/shard_map/ppermute | solution.py:482
  397.7 7.6 %collective-permute-done.35 = bf16[2,144,896]{2,1,0:T(8,128)(2,1)S(1)} collective-permute-done((bf16[2,144,896]{2,1,0:T(8,128)(2,1)}, bf16[2,144,896]{2,1,0:T(8,128)(2,1)S(1)}, u32[]{:S(2)}, u32[]{:S(2)}) %collective-permute-start.35) | collective-permute-done | bytes 516128 | tf_op jit(solution)/shard_map/ppermute | solution.py:482
  416.6 6.3 %shard_map.249 = (f32[2304,1152]{1,0:T(8,128)}, f32[1152,2304]{1,0:T(8,128)}, f32[8,128]{1,0:T(8,128)}) custom-call(s32[3]{0:T(128)} %pad_add_fusion.sc, bf16[8,96,640]{2,1,0:T(8,128)(2,1)} %copy-done.4, bf16[8,96,640]{2,1,0:T(8,128)(2,1)} %collective-permute-done.37.refs_1_, bf16[8,96,512]{2,1,0:T(8,128)(2,1)} %copy-done.7, ...), custom_call_target="tpu_custom_call" | custom-call | flops 4600000000 | bytes 4000000 | tf_op jit(solution)/shard_map/pallas_call | solution.py:427
  422.8 7.7 %collective-permute-done.41 = bf16[10,3456]{1,0:T(8,128)(2,1)S(1)} collective-permute-done((bf16[10,3456]{1,0:T(8,128)(2,1)S(1)}, bf16[10,3456]{1,0:T(8,128)(2,1)S(1)}, u32[]{:S(2)}, u32[]{:S(2)}) %collective-permute-start.41) | collective-permute-done | bytes 69152 | tf_op jit(solution)/shard_map/ppermute | solution.py:546
  469.2 7.6 %collective-permute-done.53 = bf16[4,144,256]{2,1,0:T(8,128)(2,1)S(1)} collective-permute-done((bf16[4,144,256]{2,1,0:T(8,128)(2,1)S(1)}, bf16[4,144,256]{2,1,0:T(8,128)(2,1)S(1)}, u32[]{:S(2)}, u32[]{:S(2)}) %collective-permute-start.53) | collective-permute-done | bytes 294944 | tf_op jit(solution)/shard_map/ppermute | solution.py:482
  486.6 8.1 %fusion.6 = f32[1152,3456]{1,0:T(8,128)} fusion(bf16[128,1152]{1,0:T(8,128)(2,1)S(1)} %reshape.149, bf16[16,10,3456]{2,1,0:T(8,128)(2,1)S(1)} %reshape.150), kind=kOutput, calls=%fused_computation.19 | convolution fusion | flops 1019215872 | bytes 17104896 | tf_op jit(solution)/shard_map/dot_general | solution.py:1036
  499.0 5.6 %collective-permute-done.56.refs_3_ = bf16[8,144,384]{2,1,0:T(8,128)(2,1)S(1)} collective-permute-done((bf16[8,144,384]{2,1,0:T(8,128)(2,1)}, bf16[8,144,384]{2,1,0:T(8,128)(2,1)S(1)}, u32[]{:S(2)}, u32[]{:S(2)}) %collective-permute-start.56) | collective-permute-done | bytes 884768 | tf_op jit(solution)/shard_map/ppermute | solution.py:482
  504.6 5.9 %collective-permute-done.55.refs_1_ = bf16[8,144,512]{2,1,0:T(8,128)(2,1)} collective-permute-done((bf16[8,144,512]{2,1,0:T(8,128)(2,1)}, bf16[8,144,512]{2,1,0:T(8,128)(2,1)}, u32[]{:S(2)}, u32[]{:S(2)}) %collective-permute-start.55) | collective-permute-done | bytes 1179680 | tf_op jit(solution)/shard_map/ppermute | solution.py:482
  510.6 8.5 %shard_map.252 = (f32[1728,1152]{1,0:T(8,128)}, f32[576,1152]{1,0:T(8,128)}) custom-call(s32[3]{0:T(128)} %pad_add_fusion.sc, bf16[8,144,512]{2,1,0:T(8,128)(2,1)} %pad_maximum_fusion.refs_0_, bf16[8,144,512]{2,1,0:T(8,128)(2,1)} %collective-permute-done.55.refs_1_, bf16[8,144,384]{2,1,0:T(8,128)(2,1)} %pad_maximum_fusion.3.refs_2_, ...), custom_call_target="tpu_custom_call" | custom-call | flops 10350000128 | bytes 9000000 | tf_op jit(solution)/shard_map/pallas_call | solution.py:427
  (319 shorter events, 153.3 us)
Async XLA Ops:
  7.2 438.6 %all-reduce.4.cloned.1.call-start = ((), (), s32[]{:S(2)}) async-start(), calls=%async_computation | async-start | bytes 14155776 | tf_op jit(solution)/shard_map/psum | solution.py:744
  14.6 44.6 %collective-permute-start.4 = (bf16[1152,2304]{1,0:T(8,128)(2,1)}, bf16[1152,2304]{1,0:T(8,128)(2,1)}, u32[]{:S(2)}, u32[]{:S(2)}) collective-permute-start(bf16[1152,2304]{1,0:T(8,128)(2,1)} %w_up0.1), channel_id=1, source_target_pairs={{0,1},{1,0},{2,3},{3,2},{4,5},{5,4},{6,7},{7,6},{8,9},{9,8},{10,11... | collective-permute-start | bytes 15925256 | tf_op jit(solution)/shard_map/ppermute | solution.py:458
  14.9 44.2 %collective-permute-start.5 = (bf16[2304,1152]{1,0:T(8,128)(2,1)}, bf16[2304,1152]{1,0:T(8,128)(2,1)}, u32[]{:S(2)}, u32[]{:S(2)}) collective-permute-start(bf16[2304,1152]{1,0:T(8,128)(2,1)} %w_down0.1), channel_id=1, source_target_pairs={{0,1},{1,0},{2,3},{3,2},{4,5},{5,4},{6,7},{7,6},{8,9},{9,8},{10,11... | collective-permute-start | bytes 15925256 | tf_op jit(solution)/shard_map/ppermute | solution.py:458
  18.3 40.9 %collective-permute-start.6 = (bf16[1,2304]{1,0:T(2,128)(2,1)S(1)}, bf16[1,2304]{1,0:T(2,128)(2,1)S(1)}, u32[]{:S(2)}, u32[]{:S(2)}) collective-permute-start(bf16[1,2304]{1,0:T(2,128)(2,1)S(1)} %broadcast_in_dim.52), channel_id=1, source_target_pairs={{0,1},{1,0},{2,3},{3,2},{4,5},{5,4},{6,7},{7,6},{8,9},{9,8},{10,11... | collective-permute-start | bytes 13832 | tf_op jit(solution)/shard_map/ppermute | solution.py:458
  104.5 31.6 %collective-permute-start.9 = (bf16[3,3456]{1,0:T(4,128)(2,1)}, bf16[3,3456]{1,0:T(4,128)(2,1)}, u32[]{:S(2)}, u32[]{:S(2)}) collective-permute-start(bf16[3,3456]{1,0:T(4,128)(2,1)} %reshape.137), channel_id=1, source_target_pairs={{0,16},{2,18},{4,20},{6,22},{8,24},{10,26},{12,28},{14,30},{16,0},... | collective-permute-start | bytes 62216 | tf_op jit(solution)/shard_map/ppermute | solution.py:546
  108.5 46.8 %collective-permute-start.10 = (bf16[16,96,640]{2,1,0:T(8,128)(2,1)}, bf16[16,96,640]{2,1,0:T(8,128)(2,1)S(1)}, u32[]{:S(2)}, u32[]{:S(2)}) collective-permute-start(bf16[16,96,640]{2,1,0:T(8,128)(2,1)} %get-tuple-element.358), channel_id=1, source_target_pairs={{0,1},{1,0},{2,3},{3,2},{4,5},{5,4},{6,7},{7,6},{8,9},{9,8},{10,11... | collective-permute-start | bytes 5898248 | tf_op jit(solution)/shard_map/ppermute | solution.py:458
  160.3 32.9 %collective-permute-start.13 = (bf16[2,2,2,96,640]{4,3,0,1,2:T(8,128)(2,1)S(1)}, bf16[2,2,2,96,640]{4,3,0,1,2:T(8,128)(2,1)S(1)}, u32[]{:S(2)}, u32[]{:S(2)}) collective-permute-start(bf16[2,2,2,96,640]{4,3,0,1,2:T(8,128)(2,1)S(1)} %get-tuple-element.376), channel_id=1, source_target_pairs={{0,2},{2,0},{4,6},{6,4},{8,10},{10,8},{12,14},{14,12},{16,18},{18,... | collective-permute-start | bytes 2949128 | tf_op jit(solution)/shard_map/ppermute | solution.py:482
  161.9 30.7 %collective-permute-start.14 = (bf16[2,2,2,96,512]{4,3,0,1,2:T(8,128)(2,1)}, bf16[2,2,2,96,512]{4,3,0,1,2:T(8,128)(2,1)}, u32[]{:S(2)}, u32[]{:S(2)}) collective-permute-start(bf16[2,2,2,96,512]{4,3,0,1,2:T(8,128)(2,1)} %get-tuple-element.377), channel_id=1, source_target_pairs={{0,4},{2,6},{4,0},{6,2},{8,12},{10,14},{12,8},{14,10},{16,20},{18,... | collective-permute-start | bytes 2359304 | tf_op jit(solution)/shard_map/ppermute | solution.py:482
  163.4 29.2 %collective-permute-start.15 = (bf16[12,3456]{1,0:T(8,128)(2,1)S(1)}, bf16[12,3456]{1,0:T(8,128)(2,1)S(1)}, u32[]{:S(2)}, u32[]{:S(2)}) collective-permute-start(bf16[12,3456]{1,0:T(8,128)(2,1)S(1)} %pad_maximum_fusion.20), channel_id=1, source_target_pairs={{0,4},{2,6},{4,0},{6,2},{8,12},{10,14},{12,8},{14,10},{16,20},{18,... | collective-permute-start | bytes 248840 | tf_op jit(solution)/shard_map/ppermute | solution.py:546
  275.0 41.7 %collective-permute-start.25 = (bf16[2,2,2,144,512]{4,3,0,1,2:T(8,128)(2,1)}, bf16[2,2,2,144,512]{4,3,0,1,2:T(8,128)(2,1)}, u32[]{:S(2)}, u32[]{:S(2)}) collective-permute-start(bf16[2,2,2,144,512]{4,3,0,1,2:T(8,128)(2,1)} %fusion.1), channel_id=1, source_target_pairs={{0,2},{2,0},{4,6},{6,4},{8,10},{10,8},{12,14},{14,12},{16,18},{18,... | collective-permute-start | bytes 3538952 | tf_op jit(solution)/shard_map/ppermute | solution.py:482
  276.5 40.2 %collective-permute-start.26 = (bf16[2,2,2,144,384]{4,3,0,1,2:T(8,128)(2,1)}, bf16[2,2,2,144,384]{4,3,0,1,2:T(8,128)(2,1)S(1)}, u32[]{:S(2)}, u32[]{:S(2)}) collective-permute-start(bf16[2,2,2,144,384]{4,3,0,1,2:T(8,128)(2,1)} %fusion.5), channel_id=1, source_target_pairs={{0,4},{2,6},{4,0},{6,2},{8,12},{10,14},{12,8},{14,10},{16,20},{18,... | collective-permute-start | bytes 2654216 | tf_op jit(solution)/shard_map/ppermute | solution.py:482
  278.0 38.7 %collective-permute-start.27 = (bf16[2,2,2,144,256]{4,3,1,2,0:T(8,128)(2,1)}, bf16[2,2,2,144,256]{4,3,1,2,0:T(8,128)(2,1)}, u32[]{:S(2)}, u32[]{:S(2)}) collective-permute-start(bf16[2,2,2,144,256]{4,3,1,2,0:T(8,128)(2,1)} %fusion.12), channel_id=1, source_target_pairs={{0,8},{2,10},{4,12},{6,14},{8,0},{10,2},{12,4},{14,6},{16,24},{18,... | collective-permute-start | bytes 1769480 | tf_op jit(solution)/shard_map/ppermute | solution.py:482
  280.0 36.7 %collective-permute-start.28 = (bf16[2,96,1152]{2,1,0:T(8,128)(2,1)S(1)}, bf16[2,96,1152]{2,1,0:T(8,128)(2,1)}, u32[]{:S(2)}, u32[]{:S(2)}) collective-permute-start(bf16[2,96,1152]{2,1,0:T(8,128)(2,1)S(1)} %pad_maximum_fusion.12), channel_id=1, source_target_pairs={{0,8},{2,10},{4,12},{6,14},{8,0},{10,2},{12,4},{14,6},{16,24},{18,... | collective-permute-start | bytes 1327112 | tf_op jit(solution)/shard_map/ppermute | solution.py:482
  324.1 36.1 %collective-permute-start.29 = (bf16[2,2,144,512]{3,2,0,1:T(8,128)(2,1)}, bf16[2,2,144,512]{3,2,0,1:T(8,128)(2,1)S(1)}, u32[]{:S(2)}, u32[]{:S(2)}) collective-permute-start(bf16[2,2,144,512]{3,2,0,1:T(8,128)(2,1)} %get-tuple-element.467), channel_id=1, source_target_pairs={{0,4},{2,6},{4,0},{6,2},{8,12},{10,14},{12,8},{14,10},{16,20},{18,... | collective-permute-start | bytes 1769480 | tf_op jit(solution)/shard_map/ppermute | solution.py:482
  324.3 34.2 %collective-permute-start.32 = (bf16[4,96,640]{2,1,0:T(8,128)(2,1)S(1)}, bf16[4,96,640]{2,1,0:T(8,128)(2,1)S(1)}, u32[]{:S(2)}, u32[]{:S(2)}) collective-permute-start(bf16[4,96,640]{2,1,0:T(8,128)(2,1)S(1)} %slice.395), channel_id=1, source_target_pairs={{0,4},{2,6},{4,0},{6,2},{8,12},{10,14},{12,8},{14,10},{16,20},{18,... | collective-permute-start | bytes 1474568 | tf_op jit(solution)/shard_map/ppermute | solution.py:482
  326.1 32.3 %collective-permute-start.30 = (bf16[2,2,144,384]{3,2,0,1:T(8,128)(2,1)}, bf16[2,2,144,384]{3,2,0,1:T(8,128)(2,1)S(1)}, u32[]{:S(2)}, u32[]{:S(2)}) collective-permute-start(bf16[2,2,144,384]{3,2,0,1:T(8,128)(2,1)} %get-tuple-element.468), channel_id=1, source_target_pairs={{0,2},{2,0},{4,6},{6,4},{8,10},{10,8},{12,14},{14,12},{16,18},{18,... | collective-permute-start | bytes 1327112 | tf_op jit(solution)/shard_map/ppermute | solution.py:482
  326.1 32.3 %collective-permute-start.33 = (bf16[4,96,512]{2,1,0:T(8,128)(2,1)S(1)}, bf16[4,96,512]{2,1,0:T(8,128)(2,1)S(1)}, u32[]{:S(2)}, u32[]{:S(2)}) collective-permute-start(bf16[4,96,512]{2,1,0:T(8,128)(2,1)S(1)} %slice.396), channel_id=1, source_target_pairs={{0,2},{2,0},{4,6},{6,4},{8,10},{10,8},{12,14},{14,12},{16,18},{18,... | collective-permute-start | bytes 1179656 | tf_op jit(solution)/shard_map/ppermute | solution.py:482
  328.1 30.3 %collective-permute-start.31 = (bf16[2,2,144,256]{3,2,0,1:T(8,128)(2,1)}, bf16[2,2,144,256]{3,2,0,1:T(8,128)(2,1)}, u32[]{:S(2)}, u32[]{:S(2)}) collective-permute-start(bf16[2,2,144,256]{3,2,0,1:T(8,128)(2,1)} %get-tuple-element.469), channel_id=1, source_target_pairs={{0,16},{2,18},{4,20},{6,22},{8,24},{10,26},{12,28},{14,30},{16,0},... | collective-permute-start | bytes 884744 | tf_op jit(solution)/shard_map/ppermute | solution.py:482
  366.8 38.6 %collective-permute-start.37 = (bf16[8,96,640]{2,1,0:T(8,128)(2,1)S(1)}, bf16[8,96,640]{2,1,0:T(8,128)(2,1)}, u32[]{:S(2)}, u32[]{:S(2)}) collective-permute-start(bf16[8,96,640]{2,1,0:T(8,128)(2,1)S(1)} %pad_maximum_fusion.2.refs_0_), channel_id=1, source_target_pairs={{0,2},{2,0},{4,6},{6,4},{8,10},{10,8},{12,14},{14,12},{16,18},{18,... | collective-permute-start | bytes 2949128 | tf_op jit(solution)/shard_map/ppermute | solution.py:482
  367.6 37.7 %collective-permute-start.38 = (bf16[8,96,512]{2,1,0:T(8,128)(2,1)S(1)}, bf16[8,96,512]{2,1,0:T(8,128)(2,1)}, u32[]{:S(2)}, u32[]{:S(2)}) collective-permute-start(bf16[8,96,512]{2,1,0:T(8,128)(2,1)S(1)} %pad_maximum_fusion.4.refs_2_), channel_id=1, source_target_pairs={{0,4},{2,6},{4,0},{6,2},{8,12},{10,14},{12,8},{14,10},{16,20},{18,... | collective-permute-start | bytes 2359304 | tf_op jit(solution)/shard_map/ppermute | solution.py:482
  368.7 36.6 %collective-permute-start.35 = (bf16[2,144,896]{2,1,0:T(8,128)(2,1)}, bf16[2,144,896]{2,1,0:T(8,128)(2,1)S(1)}, u32[]{:S(2)}, u32[]{:S(2)}) collective-permute-start(bf16[2,144,896]{2,1,0:T(8,128)(2,1)} %pad_maximum_fusion.7), channel_id=1, source_target_pairs={{0,8},{2,10},{4,12},{6,14},{8,0},{10,2},{12,4},{14,6},{16,24},{18,... | collective-permute-start | bytes 1548296 | tf_op jit(solution)/shard_map/ppermute | solution.py:482
  368.8 29.0 %collective-permute-start.36 = (bf16[2,144,256]{2,1,0:T(8,128)(2,1)S(1)}, bf16[2,144,256]{2,1,0:T(8,128)(2,1)S(1)}, u32[]{:S(2)}, u32[]{:S(2)}) collective-permute-start(bf16[2,144,256]{2,1,0:T(8,128)(2,1)S(1)} %get-tuple-element.503), channel_id=1, source_target_pairs={{0,2},{2,0},{4,6},{6,4},{8,10},{10,8},{12,14},{14,12},{16,18},{18,... | collective-permute-start | bytes 442376 | tf_op jit(solution)/shard_map/ppermute | solution.py:482
  406.2 28.4 %collective-permute-start.43 = (f32[4,256,1152]{2,1,0:T(8,128)}, f32[4,256,1152]{2,1,0:T(8,128)}, u32[]{:S(2)}, u32[]{:S(2)}) collective-permute-start(f32[4,256,1152]{2,1,0:T(8,128)} %get-tuple-element.541), channel_id=1, source_target_pairs={{0,1},{1,0},{2,3},{3,2},{4,5},{5,4},{6,7},{7,6},{8,9},{9,8},{10,11... | collective-permute-start | bytes 14155784 | tf_op jit(solution)/shard_map/ppermute | solution.py:458
  406.2 28.4 %collective-permute-start.42 = (bf16[4,256,1152]{2,1,0:T(8,128)(2,1)}, bf16[4,256,1152]{2,1,0:T(8,128)(2,1)S(1)}, u32[]{:S(2)}, u32[]{:S(2)}) collective-permute-start(bf16[4,256,1152]{2,1,0:T(8,128)(2,1)} %get-tuple-element.540), channel_id=1, source_target_pairs={{0,1},{1,0},{2,3},{3,2},{4,5},{5,4},{6,7},{7,6},{8,9},{9,8},{10,11... | collective-permute-start | bytes 7077896 | tf_op jit(solution)/shard_map/ppermute | solution.py:458
  (80 other events, 717.2 us)
Sparse Core Ops, SparseCore 0:
  136.3 269.4 all-reduce.3

commit v12 on v11

--- a/solution.py
+++ b/solution.py
@@ -619,7 +619,8 @@
     proj_bias = b_proj.astype(f32)[None]
     down_bias = b_down.astype(f32)[None]
 
-    late_up, late_down, late_bias = lax.optimization_barrier((wq[1], w_up, w_down, b_up, modulation))[1:4]
+    crossed = (wq[1], wp[1], qkv_bias[1], modulation)
+    late_up, late_down, late_bias = lax.optimization_barrier((w_up, w_down, b_up, crossed))[:3]
     wu = [w_up, swap_cores(late_up)]
     wd = [w_down, swap_cores(late_down)]
     up_bias = [b_up[None], swap_cores(late_bias[None])]

time: 533 us -> 526 us (0.987)
  waiting for transfers between devices: 109 us -> 101 us
  transfers between devices with their start and end apart: 59 -> 59, of which waited for: 21 -> 20; matrix products, arithmetic and copies ran while one was open for 13% -> 13% of each run, Pallas kernels for 45% -> 46%
where the time goes in v12:
time: 526 us; the launch traced here: 519 us
  Pallas kernels  274 us (52%)
  waiting for transfers between devices  101 us (19%)
  starting transfers between devices  51.8 us (10%)
  other arithmetic  29.9 us (6%)
  local copies, waits for them, and re-layouts  28.7 us (5%)
  matrix products  18.1 us (3%)
  between operations  16.1 us (3%)
    pallas_call x16, Pallas kernels, run_kernel(): pl.pallas_call(body, out_shape=out_shape, grid_spec=pltpu.PrefetchScalarG...  274 us
    ppermute x32, waiting for transfers between devices, exchange(): lax.ppermute(value, 'dp', bit_pairs(bit))  85.2 us
    ppermute x32, starting transfers between devices, exchange(): lax.ppermute(value, 'dp', bit_pairs(bit))  33.3 us
    ppermute x8, starting transfers between devices, rows_flow(): came = lax.ppermute(rows, 'dp', bit_pairs(bit))  14.1 us
    add x21, other arithmetic, reduce_flow(): cut(one, bits, route[stage], side) + cut(two, bits, route[stage], side)  13.9 us
    ppermute x8, waiting for transfers between devices, rows_flow(): came = lax.ppermute(rows, 'dp', bit_pairs(bit))  13 us
  transfers between devices with their start and end apart: 59, of which 20 were waited for; matrix products, arithmetic and copies ran while one was open for 13% of the time, Pallas kernels for 46%

profile of v12, /device:TPU:0, one launch (start us, length us, event | category | flops | bytes accessed | tf_op | source)
XLA Modules:
  0.0 519.5 jit_solution(13442164789717642152)
XLA Ops:
  20.0 32.8 %shard_map.237 = (bf16[4,3456,256]{2,1,0:T(8,128)(2,1)}, bf16[4,16,256,256]{3,2,1,0:T(8,128)(2,1)}, bf16[4,1152,256]{2,1,0:T(8,128)(2,1)}, f32[4,256,1152]{2,1,0...) custom-call(s32[3]{0:T(128)} %pad_add_fusion.sc, ...), custom_call_target="tpu_custom_call" | custom-call | flops 37950001152 | bytes 33000000 | tf_op jit(solution)/shard_map/pallas_call | solution.py:427
  53.4 26.6 %shard_map.238 = (bf16[2,2304,1024]{2,1,0:T(8,128)(2,1)}, bf16[2,2304,1024]{2,1,0:T(8,128)(2,1)}, bf16[16,96,1152]{2,1,0:T(8,128)(2,1)}, bf16[16,96,1152]{2,1,0:...) custom-call(s32[3]{0:T(128)} %pad_add_fusion.sc, bf16[1024,1152]{1,0:T(8,128)(2,1)} %bitcast.143, ...), custom_call_target="tpu_custom_call" | custom-call | flops 29899999232 | bytes 26000000 | tf_op jit(solution)/shard_map/pallas_call | solution.py:427
  82.5 15.6 %shard_map.239 = (bf16[2,2304,1024]{2,1,0:T(8,128)(2,1)}, bf16[2,2304,1024]{2,1,0:T(8,128)(2,1)}, bf16[16,96,640]{2,1,0:T(8,128)(2,1)}, bf16[16,96,512]{2,1,0:T(8,128)(2,1)}, f32[1,768]{1,0:T(1,128)}) custom-call(s32[3]{0:T(128)} %pad_add_fusion.sc, bf16[1024,1152]{1,0:T(8,128)(2,1)} %bitcast.144, ...), custom_call_target="tpu_custom_call", output_to_operand_aliasing={{0}: (6, {}), {1}: (7, {})} | custom-call | flops 14949999616 | bytes 13000000 | tf_op jit(solution)/shard_map/pallas_call | solution.py:427
  102.0 27.0 %shard_map.240 = (bf16[2,2304,1024]{2,1,0:T(8,128)(2,1)}, bf16[2,2304,1024]{2,1,0:T(8,128)(2,1)}, bf16[16,96,1152]{2,1,0:T(8,128)(2,1)}, bf16[16,96,1152]{2,1,0:...) custom-call(s32[3]{0:T(128)} %pad_add_fusion.sc, ...), custom_call_target="tpu_custom_call", output_to_operand_aliasing={{0}: (11, {}), {1}: (12, {})} | custom-call | flops 29899999232 | bytes 26000000 | tf_op jit(solution)/shard_map/pallas_call | solution.py:427
  132.0 16.7 %shard_map.241 = (bf16[2,2304,1024]{2,1,0:T(8,128)(2,1)}, bf16[2,2304,1024]{2,1,0:T(8,128)(2,1)}, bf16[16,96,640]{2,1,0:T(8,128)(2,1)}, bf16[16,96,512]{2,1,0:T(8,128)(2,1)}, f32[1,768]{1,0:T(1,128)}) custom-call(s32[3]{0:T(128)} %pad_add_fusion.sc, bf16[1024,1152]{1,0:T(8,128)(2,1)} %bitcast.146, ...), custom_call_target="tpu_custom_call", output_to_operand_aliasing={{0}: (6, {}), {1}: (7, {})} | custom-call | flops 14949999616 | bytes 13000000 | tf_op jit(solution)/shard_map/pallas_call | solution.py:427
  157.3 27.4 %shard_map.242 = (f32[4,256,1152]{2,1,0:T(8,128)}, bf16[4,256,1152]{2,1,0:T(8,128)(2,1)}, f32[4,4,1152]{2,1,0:T(4,128)}) custom-call(s32[3]{0:T(128)} %pad_add_fusion.sc, bf16[2,2304,1024]{2,1,0:T(8,128)(2,1)} %get-tuple-element.369.back, bf16[1152,2304]{1,0:T(8,128)(2,1)} %w_up0.1, bf16[1152,2304]{1,0:T(8,128)(2,1)} %collective-permute-done.4.refs_0_.refs_3_.w_up1, ...), custom_call_target="tpu_custom_call" | custom-call | flops 69000003584 | bytes 41582592 | tf_op jit(solution)/shard_map/pallas_call | solution.py:427
  192.4 12.3 %shard_map.243.refs_0_ = bf16[2,3456,256]{2,1,0:T(8,128)(2,1)} custom-call(s32[3]{0:T(128)} %pad_add_fusion.sc, bf16[4,256,1152]{2,1,0:T(8,128)(2,1)} %get-tuple-element.387.grad_attn.refs_4_, bf16[4,3456,256]{2,1,0:T(8,128)(2,1)} %get-tuple-element.388.qkv, bf16[4,16,256,256]{3,2,1,0:T(8,128)(2,1)} %get-tuple-element.389.prob, bf16[576,1152]{1,0:T(8,128)(2,1)} %refs_0_.7, ...), custom_call_target="tpu_custom_call" | custom-call | flops 69000003584 | bytes 24018944 | tf_op jit(solution)/shard_map/pallas_call | solution.py:427
  207.7 12.7 %shard_map.244.refs_1_ = bf16[2,3456,256]{2,1,0:T(8,128)(2,1)} custom-call(s32[3]{0:T(128)} %pad_add_fusion.sc, bf16[4,256,1152]{2,1,0:T(8,128)(2,1)} %get-tuple-element.387.grad_attn.refs_4_, bf16[4,3456,256]{2,1,0:T(8,128)(2,1)} %get-tuple-element.388.qkv, bf16[4,16,256,256]{3,2,1,0:T(8,128)(2,1)} %get-tuple-element.389.prob, bf16[576,1152]{1,0:T(8,128)(2,1)} %refs_0_.7, ...), custom_call_target="tpu_custom_call" | custom-call | flops 69000003584 | bytes 24018944 | tf_op jit(solution)/shard_map/pallas_call | solution.py:427
  220.4 6.2 %collective-permute-done.19 = bf16[2,96,1152]{2,1,0:T(8,128)(2,1)S(1)} collective-permute-done((bf16[2,96,1152]{2,1,0:T(8,128)(2,1)S(1)}, bf16[2,96,1152]{2,1,0:T(8,128)(2,1)S(1)}, u32[]{:S(2)}, u32[]{:S(2)}) %collective-permute-start.19) | collective-permute-done | bytes 442400 | tf_op jit(solution)/shard_map/ppermute | solution.py:482
  227.2 13.9 %shard_map.245 = (bf16[16,144,512]{2,1,0:T(8,128)(2,1)}, bf16[16,144,384]{2,1,0:T(8,128)(2,1)}, bf16[16,144,256]{2,1,0:T(8,128)(2,1)}, f32[3,1,576]{2,1,0:T(1,128)}) custom-call(s32[3]{0:T(128)} %pad_add_fusion.sc, bf16[2,3456,256]{2,1,0:T(8,128)(2,1)} %shard_map.243.refs_0_, bf16[2,3456,256]{2,1,0:T(8,128)(2,1)} %shard_map.244.refs_1_, ...), custom_call_target="tpu_custom_call" | custom-call | flops 69000003584 | bytes 19471104 | tf_op jit(solution)/shard_map/pallas_call | solution.py:427
  244.8 13.9 %shard_map.246 = (bf16[16,144,512]{2,1,0:T(8,128)(2,1)}, bf16[16,144,384]{2,1,0:T(8,128)(2,1)}, bf16[16,144,256]{2,1,0:T(8,128)(2,1)}, f32[3,1,576]{2,1,0:T(1,128)}) custom-call(s32[3]{0:T(128)} %pad_add_fusion.sc, bf16[2,3456,256]{2,1,0:T(8,128)(2,1)} %shard_map.243.refs_0_, bf16[2,3456,256]{2,1,0:T(8,128)(2,1)} %shard_map.244.refs_1_, ...), custom_call_target="tpu_custom_call" | custom-call | flops 69000003584 | bytes 19471104 | tf_op jit(solution)/shard_map/pallas_call | solution.py:427
  273.4 24.5 %shard_map.247 = (f32[8,256,1152]{2,1,0:T(8,128)}, f32[4,256,1152]{2,1,0:T(8,128)}, f32[4,2,1152]{2,1,0:T(2,128)}) custom-call(s32[3]{0:T(128)} %pad_add_fusion.sc, bf16[2,3456,256]{2,1,0:T(8,128)(2,1)} %shard_map.243.refs_0_, bf16[2,3456,256]{2,1,0:T(8,128)(2,1)} %shard_map.244.refs_1_, bf16[1728,1152]{1,0:T(8,128)(2,1)} %bitcast.141, ...), custom_call_target="tpu_custom_call" | custom-call | flops 69000003584 | bytes 38891520 | tf_op jit(solution)/shard_map/pallas_call | solution.py:427
  297.9 9.4 %collective-permute-done.28 = bf16[2,96,1152]{2,1,0:T(8,128)(2,1)} collective-permute-done((bf16[2,96,1152]{2,1,0:T(8,128)(2,1)S(1)}, bf16[2,96,1152]{2,1,0:T(8,128)(2,1)}, u32[]{:S(2)}, u32[]{:S(2)}) %collective-permute-start.28) | collective-permute-done | bytes 442400 | tf_op jit(solution)/shard_map/ppermute | solution.py:482
  319.7 24.8 %shard_map.248 = (bf16[8,256,1152]{2,1,0:T(8,128)(2,1)}, bf16[4,256,1152]{2,1,0:T(8,128)(2,1)}, f32[4,1,1152]{2,1,0:T(1,128)}) custom-call(s32[3]{0:T(128)} %pad_add_fusion.sc, bf16[2,2304,1024]{2,1,0:T(8,128)(2,1)} %get-tuple-element.461.act, bf16[2304,1152]{1,0:T(8,128)(2,1)} %w_down0.1, bf16[2304,1152]{1,0:T(8,128)(2,1)} %collective-permute-done.5.refs_1_.refs_4_.w_down1, ...), custom_call_target="tpu_custom_call" | custom-call | flops 69000003584 | bytes 36813312 | tf_op jit(solution)/shard_map/pallas_call | solution.py:427
  364.0 26.0 %collective-permute-done.36 = bf16[2,144,256]{2,1,0:T(8,128)(2,1)S(1)} collective-permute-done((bf16[2,144,256]{2,1,0:T(8,128)(2,1)S(1)}, bf16[2,144,256]{2,1,0:T(8,128)(2,1)S(1)}, u32[]{:S(2)}, u32[]{:S(2)}) %collective-permute-start.36) | collective-permute-done | bytes 147488 | tf_op jit(solution)/shard_map/ppermute | solution.py:482
  390.0 8.5 %collective-permute-done.35 = bf16[2,144,896]{2,1,0:T(8,128)(2,1)S(1)} collective-permute-done((bf16[2,144,896]{2,1,0:T(8,128)(2,1)}, bf16[2,144,896]{2,1,0:T(8,128)(2,1)S(1)}, u32[]{:S(2)}, u32[]{:S(2)}) %collective-permute-start.35) | collective-permute-done | bytes 516128 | tf_op jit(solution)/shard_map/ppermute | solution.py:482
  399.8 5.5 %convolution_convert_fusion = bf16[8,1152]{1,0:T(8,128)(2,1)S(1)} fusion(bf16[8,3456]{1,0:T(8,128)(2,1)S(1)} %maximum_select_fusion, bf16[1152,3456]{1,0:T(8,128)(2,1)} %param.25), kind=kOutput, calls=%fused_computation.1 | convolution fusion | flops 63710208 | bytes 8036352 | tf_op jit(solution)/shard_map/dot_general | solution.py:1043
  410.3 6.3 %shard_map.249 = (f32[2304,1152]{1,0:T(8,128)}, f32[1152,2304]{1,0:T(8,128)}, f32[8,128]{1,0:T(8,128)}) custom-call(s32[3]{0:T(128)} %pad_add_fusion.sc, bf16[8,96,640]{2,1,0:T(8,128)(2,1)} %copy-done.4, bf16[8,96,640]{2,1,0:T(8,128)(2,1)} %collective-permute-done.37.refs_1_, bf16[8,96,512]{2,1,0:T(8,128)(2,1)} %copy-done.7, ...), custom_call_target="tpu_custom_call" | custom-call | flops 4600000000 | bytes 4000000 | tf_op jit(solution)/shard_map/pallas_call | solution.py:427
  416.5 7.3 %collective-permute-done.41 = bf16[10,3456]{1,0:T(8,128)(2,1)S(1)} collective-permute-done((bf16[10,3456]{1,0:T(8,128)(2,1)S(1)}, bf16[10,3456]{1,0:T(8,128)(2,1)S(1)}, u32[]{:S(2)}, u32[]{:S(2)}) %collective-permute-start.41) | collective-permute-done | bytes 69152 | tf_op jit(solution)/shard_map/ppermute | solution.py:546
  462.2 7.8 %collective-permute-done.53 = bf16[4,144,256]{2,1,0:T(8,128)(2,1)S(1)} collective-permute-done((bf16[4,144,256]{2,1,0:T(8,128)(2,1)S(1)}, bf16[4,144,256]{2,1,0:T(8,128)(2,1)S(1)}, u32[]{:S(2)}, u32[]{:S(2)}) %collective-permute-start.53) | collective-permute-done | bytes 294944 | tf_op jit(solution)/shard_map/ppermute | solution.py:482
  480.0 8.1 %fusion.6 = f32[1152,3456]{1,0:T(8,128)} fusion(bf16[128,1152]{1,0:T(8,128)(2,1)S(1)} %reshape.149, bf16[16,10,3456]{2,1,0:T(8,128)(2,1)S(1)} %reshape.150), kind=kOutput, calls=%fused_computation.19 | convolution fusion | flops 1019215872 | bytes 17104896 | tf_op jit(solution)/shard_map/dot_general | solution.py:1037
  492.4 5.7 %collective-permute-done.56.refs_3_ = bf16[8,144,384]{2,1,0:T(8,128)(2,1)S(1)} collective-permute-done((bf16[8,144,384]{2,1,0:T(8,128)(2,1)}, bf16[8,144,384]{2,1,0:T(8,128)(2,1)S(1)}, u32[]{:S(2)}, u32[]{:S(2)}) %collective-permute-start.56) | collective-permute-done | bytes 884768 | tf_op jit(solution)/shard_map/ppermute | solution.py:482
  498.1 5.8 %collective-permute-done.55.refs_1_ = bf16[8,144,512]{2,1,0:T(8,128)(2,1)} collective-permute-done((bf16[8,144,512]{2,1,0:T(8,128)(2,1)}, bf16[8,144,512]{2,1,0:T(8,128)(2,1)}, u32[]{:S(2)}, u32[]{:S(2)}) %collective-permute-start.55) | collective-permute-done | bytes 1179680 | tf_op jit(solution)/shard_map/ppermute | solution.py:482
  503.8 8.5 %shard_map.252 = (f32[1728,1152]{1,0:T(8,128)}, f32[576,1152]{1,0:T(8,128)}) custom-call(s32[3]{0:T(128)} %pad_add_fusion.sc, bf16[8,144,512]{2,1,0:T(8,128)(2,1)} %pad_maximum_fusion.refs_0_, bf16[8,144,512]{2,1,0:T(8,128)(2,1)} %collective-permute-done.55.refs_1_, bf16[8,144,384]{2,1,0:T(8,128)(2,1)} %pad_maximum_fusion.3.refs_2_, ...), custom_call_target="tpu_custom_call" | custom-call | flops 10350000128 | bytes 9000000 | tf_op jit(solution)/shard_map/pallas_call | solution.py:427
  (319 shorter events, 150.1 us)
Async XLA Ops:
  7.2 431.6 %all-reduce.4.cloned.1.call-start = ((), (), s32[]{:S(2)}) async-start(), calls=%async_computation | async-start | bytes 14155776 | tf_op jit(solution)/shard_map/psum | solution.py:745
  16.3 36.5 %collective-permute-start.4 = (bf16[1152,2304]{1,0:T(8,128)(2,1)}, bf16[1152,2304]{1,0:T(8,128)(2,1)}, u32[]{:S(2)}, u32[]{:S(2)}) collective-permute-start(bf16[1152,2304]{1,0:T(8,128)(2,1)} %w_up0.1), channel_id=1, source_target_pairs={{0,1},{1,0},{2,3},{3,2},{4,5},{5,4},{6,7},{7,6},{8,9},{9,8},{10,11... | collective-permute-start | bytes 15925256 | tf_op jit(solution)/shard_map/ppermute | solution.py:458
  16.7 36.1 %collective-permute-start.5 = (bf16[2304,1152]{1,0:T(8,128)(2,1)}, bf16[2304,1152]{1,0:T(8,128)(2,1)}, u32[]{:S(2)}, u32[]{:S(2)}) collective-permute-start(bf16[2304,1152]{1,0:T(8,128)(2,1)} %w_down0.1), channel_id=1, source_target_pairs={{0,1},{1,0},{2,3},{3,2},{4,5},{5,4},{6,7},{7,6},{8,9},{9,8},{10,11... | collective-permute-start | bytes 15925256 | tf_op jit(solution)/shard_map/ppermute | solution.py:458
  19.5 33.2 %collective-permute-start.6 = (bf16[1,2304]{1,0:T(2,128)(2,1)S(1)}, bf16[1,2304]{1,0:T(2,128)(2,1)S(1)}, u32[]{:S(2)}, u32[]{:S(2)}) collective-permute-start(bf16[1,2304]{1,0:T(2,128)(2,1)S(1)} %broadcast_in_dim.52), channel_id=1, source_target_pairs={{0,1},{1,0},{2,3},{3,2},{4,5},{5,4},{6,7},{7,6},{8,9},{9,8},{10,11... | collective-permute-start | bytes 13832 | tf_op jit(solution)/shard_map/ppermute | solution.py:458
  98.1 31.4 %collective-permute-start.9 = (bf16[3,3456]{1,0:T(4,128)(2,1)}, bf16[3,3456]{1,0:T(4,128)(2,1)}, u32[]{:S(2)}, u32[]{:S(2)}) collective-permute-start(bf16[3,3456]{1,0:T(4,128)(2,1)} %reshape.137), channel_id=1, source_target_pairs={{0,16},{2,18},{4,20},{6,22},{8,24},{10,26},{12,28},{14,30},{16,0},... | collective-permute-start | bytes 62216 | tf_op jit(solution)/shard_map/ppermute | solution.py:546
  101.9 46.8 %collective-permute-start.10 = (bf16[16,96,640]{2,1,0:T(8,128)(2,1)}, bf16[16,96,640]{2,1,0:T(8,128)(2,1)S(1)}, u32[]{:S(2)}, u32[]{:S(2)}) collective-permute-start(bf16[16,96,640]{2,1,0:T(8,128)(2,1)} %get-tuple-element.358), channel_id=1, source_target_pairs={{0,1},{1,0},{2,3},{3,2},{4,5},{5,4},{6,7},{7,6},{8,9},{9,8},{10,11... | collective-permute-start | bytes 5898248 | tf_op jit(solution)/shard_map/ppermute | solution.py:458
  153.7 33.1 %collective-permute-start.13 = (bf16[2,2,2,96,640]{4,3,0,1,2:T(8,128)(2,1)S(1)}, bf16[2,2,2,96,640]{4,3,0,1,2:T(8,128)(2,1)S(1)}, u32[]{:S(2)}, u32[]{:S(2)}) collective-permute-start(bf16[2,2,2,96,640]{4,3,0,1,2:T(8,128)(2,1)S(1)} %get-tuple-element.376), channel_id=1, source_target_pairs={{0,2},{2,0},{4,6},{6,4},{8,10},{10,8},{12,14},{14,12},{16,18},{18,... | collective-permute-start | bytes 2949128 | tf_op jit(solution)/shard_map/ppermute | solution.py:482
  155.3 30.9 %collective-permute-start.14 = (bf16[2,2,2,96,512]{4,3,0,1,2:T(8,128)(2,1)}, bf16[2,2,2,96,512]{4,3,0,1,2:T(8,128)(2,1)}, u32[]{:S(2)}, u32[]{:S(2)}) collective-permute-start(bf16[2,2,2,96,512]{4,3,0,1,2:T(8,128)(2,1)} %get-tuple-element.377), channel_id=1, source_target_pairs={{0,4},{2,6},{4,0},{6,2},{8,12},{10,14},{12,8},{14,10},{16,20},{18,... | collective-permute-start | bytes 2359304 | tf_op jit(solution)/shard_map/ppermute | solution.py:482
  156.8 29.4 %collective-permute-start.15 = (bf16[12,3456]{1,0:T(8,128)(2,1)S(1)}, bf16[12,3456]{1,0:T(8,128)(2,1)S(1)}, u32[]{:S(2)}, u32[]{:S(2)}) collective-permute-start(bf16[12,3456]{1,0:T(8,128)(2,1)S(1)} %pad_maximum_fusion.20), channel_id=1, source_target_pairs={{0,4},{2,6},{4,0},{6,2},{8,12},{10,14},{12,8},{14,10},{16,20},{18,... | collective-permute-start | bytes 248840 | tf_op jit(solution)/shard_map/ppermute | solution.py:546
  268.5 38.9 %collective-permute-start.25 = (bf16[2,2,2,144,512]{4,3,0,1,2:T(8,128)(2,1)}, bf16[2,2,2,144,512]{4,3,0,1,2:T(8,128)(2,1)}, u32[]{:S(2)}, u32[]{:S(2)}) collective-permute-start(bf16[2,2,2,144,512]{4,3,0,1,2:T(8,128)(2,1)} %fusion.1), channel_id=1, source_target_pairs={{0,2},{2,0},{4,6},{6,4},{8,10},{10,8},{12,14},{14,12},{16,18},{18,... | collective-permute-start | bytes 3538952 | tf_op jit(solution)/shard_map/ppermute | solution.py:482
  269.9 37.4 %collective-permute-start.26 = (bf16[2,2,2,144,384]{4,3,0,1,2:T(8,128)(2,1)}, bf16[2,2,2,144,384]{4,3,0,1,2:T(8,128)(2,1)S(1)}, u32[]{:S(2)}, u32[]{:S(2)}) collective-permute-start(bf16[2,2,2,144,384]{4,3,0,1,2:T(8,128)(2,1)} %fusion.5), channel_id=1, source_target_pairs={{0,4},{2,6},{4,0},{6,2},{8,12},{10,14},{12,8},{14,10},{16,20},{18,... | collective-permute-start | bytes 2654216 | tf_op jit(solution)/shard_map/ppermute | solution.py:482
  271.4 36.0 %collective-permute-start.27 = (bf16[2,2,2,144,256]{4,3,1,2,0:T(8,128)(2,1)}, bf16[2,2,2,144,256]{4,3,1,2,0:T(8,128)(2,1)}, u32[]{:S(2)}, u32[]{:S(2)}) collective-permute-start(bf16[2,2,2,144,256]{4,3,1,2,0:T(8,128)(2,1)} %fusion.12), channel_id=1, source_target_pairs={{0,8},{2,10},{4,12},{6,14},{8,0},{10,2},{12,4},{14,6},{16,24},{18,... | collective-permute-start | bytes 1769480 | tf_op jit(solution)/shard_map/ppermute | solution.py:482
  272.7 34.6 %collective-permute-start.28 = (bf16[2,96,1152]{2,1,0:T(8,128)(2,1)S(1)}, bf16[2,96,1152]{2,1,0:T(8,128)(2,1)}, u32[]{:S(2)}, u32[]{:S(2)}) collective-permute-start(bf16[2,96,1152]{2,1,0:T(8,128)(2,1)S(1)} %pad_maximum_fusion.12), channel_id=1, source_target_pairs={{0,8},{2,10},{4,12},{6,14},{8,0},{10,2},{12,4},{14,6},{16,24},{18,... | collective-permute-start | bytes 1327112 | tf_op jit(solution)/shard_map/ppermute | solution.py:482
  314.4 36.7 %collective-permute-start.29 = (bf16[2,2,144,512]{3,2,0,1:T(8,128)(2,1)}, bf16[2,2,144,512]{3,2,0,1:T(8,128)(2,1)S(1)}, u32[]{:S(2)}, u32[]{:S(2)}) collective-permute-start(bf16[2,2,144,512]{3,2,0,1:T(8,128)(2,1)} %get-tuple-element.467), channel_id=1, source_target_pairs={{0,4},{2,6},{4,0},{6,2},{8,12},{10,14},{12,8},{14,10},{16,20},{18,... | collective-permute-start | bytes 1769480 | tf_op jit(solution)/shard_map/ppermute | solution.py:482
  314.5 35.0 %collective-permute-start.32 = (bf16[4,96,640]{2,1,0:T(8,128)(2,1)S(1)}, bf16[4,96,640]{2,1,0:T(8,128)(2,1)S(1)}, u32[]{:S(2)}, u32[]{:S(2)}) collective-permute-start(bf16[4,96,640]{2,1,0:T(8,128)(2,1)S(1)} %slice.395), channel_id=1, source_target_pairs={{0,4},{2,6},{4,0},{6,2},{8,12},{10,14},{12,8},{14,10},{16,20},{18,... | collective-permute-start | bytes 1474568 | tf_op jit(solution)/shard_map/ppermute | solution.py:482
  316.5 33.0 %collective-permute-start.30 = (bf16[2,2,144,384]{3,2,0,1:T(8,128)(2,1)}, bf16[2,2,144,384]{3,2,0,1:T(8,128)(2,1)S(1)}, u32[]{:S(2)}, u32[]{:S(2)}) collective-permute-start(bf16[2,2,144,384]{3,2,0,1:T(8,128)(2,1)} %get-tuple-element.468), channel_id=1, source_target_pairs={{0,2},{2,0},{4,6},{6,4},{8,10},{10,8},{12,14},{14,12},{16,18},{18,... | collective-permute-start | bytes 1327112 | tf_op jit(solution)/shard_map/ppermute | solution.py:482
  317.0 32.5 %collective-permute-start.33 = (bf16[4,96,512]{2,1,0:T(8,128)(2,1)S(1)}, bf16[4,96,512]{2,1,0:T(8,128)(2,1)S(1)}, u32[]{:S(2)}, u32[]{:S(2)}) collective-permute-start(bf16[4,96,512]{2,1,0:T(8,128)(2,1)S(1)} %slice.396), channel_id=1, source_target_pairs={{0,2},{2,0},{4,6},{6,4},{8,10},{10,8},{12,14},{14,12},{16,18},{18,... | collective-permute-start | bytes 1179656 | tf_op jit(solution)/shard_map/ppermute | solution.py:482
  318.5 31.0 %collective-permute-start.31 = (bf16[2,2,144,256]{3,2,0,1:T(8,128)(2,1)}, bf16[2,2,144,256]{3,2,0,1:T(8,128)(2,1)}, u32[]{:S(2)}, u32[]{:S(2)}) collective-permute-start(bf16[2,2,144,256]{3,2,0,1:T(8,128)(2,1)} %get-tuple-element.469), channel_id=1, source_target_pairs={{0,16},{2,18},{4,20},{6,22},{8,24},{10,26},{12,28},{14,30},{16,0},... | collective-permute-start | bytes 884744 | tf_op jit(solution)/shard_map/ppermute | solution.py:482
  357.7 40.7 %collective-permute-start.37 = (bf16[8,96,640]{2,1,0:T(8,128)(2,1)S(1)}, bf16[8,96,640]{2,1,0:T(8,128)(2,1)}, u32[]{:S(2)}, u32[]{:S(2)}) collective-permute-start(bf16[8,96,640]{2,1,0:T(8,128)(2,1)S(1)} %pad_maximum_fusion.2.refs_0_), channel_id=1, source_target_pairs={{0,2},{2,0},{4,6},{6,4},{8,10},{10,8},{12,14},{14,12},{16,18},{18,... | collective-permute-start | bytes 2949128 | tf_op jit(solution)/shard_map/ppermute | solution.py:482
  358.6 39.9 %collective-permute-start.38 = (bf16[8,96,512]{2,1,0:T(8,128)(2,1)S(1)}, bf16[8,96,512]{2,1,0:T(8,128)(2,1)}, u32[]{:S(2)}, u32[]{:S(2)}) collective-permute-start(bf16[8,96,512]{2,1,0:T(8,128)(2,1)S(1)} %pad_maximum_fusion.4.refs_2_), channel_id=1, source_target_pairs={{0,4},{2,6},{4,0},{6,2},{8,12},{10,14},{12,8},{14,10},{16,20},{18,... | collective-permute-start | bytes 2359304 | tf_op jit(solution)/shard_map/ppermute | solution.py:482
  359.8 38.6 %collective-permute-start.35 = (bf16[2,144,896]{2,1,0:T(8,128)(2,1)}, bf16[2,144,896]{2,1,0:T(8,128)(2,1)S(1)}, u32[]{:S(2)}, u32[]{:S(2)}) collective-permute-start(bf16[2,144,896]{2,1,0:T(8,128)(2,1)} %pad_maximum_fusion.7), channel_id=1, source_target_pairs={{0,8},{2,10},{4,12},{6,14},{8,0},{10,2},{12,4},{14,6},{16,24},{18,... | collective-permute-start | bytes 1548296 | tf_op jit(solution)/shard_map/ppermute | solution.py:482
  360.2 29.8 %collective-permute-start.36 = (bf16[2,144,256]{2,1,0:T(8,128)(2,1)S(1)}, bf16[2,144,256]{2,1,0:T(8,128)(2,1)S(1)}, u32[]{:S(2)}, u32[]{:S(2)}) collective-permute-start(bf16[2,144,256]{2,1,0:T(8,128)(2,1)S(1)} %get-tuple-element.503), channel_id=1, source_target_pairs={{0,2},{2,0},{4,6},{6,4},{8,10},{10,8},{12,14},{14,12},{16,18},{18,... | collective-permute-start | bytes 442376 | tf_op jit(solution)/shard_map/ppermute | solution.py:482
  399.3 28.8 %collective-permute-start.43 = (f32[4,256,1152]{2,1,0:T(8,128)}, f32[4,256,1152]{2,1,0:T(8,128)}, u32[]{:S(2)}, u32[]{:S(2)}) collective-permute-start(f32[4,256,1152]{2,1,0:T(8,128)} %get-tuple-element.541), channel_id=1, source_target_pairs={{0,1},{1,0},{2,3},{3,2},{4,5},{5,4},{6,7},{7,6},{8,9},{9,8},{10,11... | collective-permute-start | bytes 14155784 | tf_op jit(solution)/shard_map/ppermute | solution.py:458
  399.3 28.8 %collective-permute-start.42 = (bf16[4,256,1152]{2,1,0:T(8,128)(2,1)}, bf16[4,256,1152]{2,1,0:T(8,128)(2,1)S(1)}, u32[]{:S(2)}, u32[]{:S(2)}) collective-permute-start(bf16[4,256,1152]{2,1,0:T(8,128)(2,1)} %get-tuple-element.540), channel_id=1, source_target_pairs={{0,1},{1,0},{2,3},{3,2},{4,5},{5,4},{6,7},{7,6},{8,9},{9,8},{10,11... | collective-permute-start | bytes 7077896 | tf_op jit(solution)/shard_map/ppermute | solution.py:458
  (80 other events, 714.8 us)
Sparse Core Ops, SparseCore 0:
  129.7 269.7 all-reduce.3
